TPU v7x, 32 devices: a whole 2x2x4 slice. The times are simulated.
32 devices in a mesh: row: 4 (over y, x), col: 8 (over z, core).
Axes of the slice: x: 2, y: 2, z: 4, core: 2. Of those that a mesh axis runs over, the one named last changes fastest.
Arguments:
- tokens: bfloat16 [10240, 2048], P('col', 'row'), may hold values from -6 to 6
- cotangent: bfloat16 [10240, 2048], P('col', 'row'), may hold values from -6 to 6
- query_weight: bfloat16 [2048, 2048], P('col', 'row'), may hold values from -0.125 to 0.125
- key_weight: bfloat16 [2048, 2048], P('col', 'row'), may hold values from -0.125 to 0.125
- value_weight: bfloat16 [2048, 4096], P('col', 'row'), may hold values from -0.125 to 0.125
- gate_weight: bfloat16 [2048, 4096], P('col', 'row'), may hold values from -0.125 to 0.125
- out_weight: bfloat16 [4096, 2048], P('row', 'col'), may hold values from -0.1875 to 0.1875
- up_weight: bfloat16 [2048, 4096], P('col', 'row'), may hold values from -0.125 to 0.125
- down_weight: bfloat16 [4096, 2048], P('row', 'col'), may hold values from -0.09375 to 0.09375
- first_gain: float32 [2048], P('row'), may hold values from 0.5 to 1.5
- first_bias: float32 [2048], P('row'), may hold values from -1 to 1
- group_gain: float32 [4096], P('row'), may hold values from 0.5 to 1.5
- group_bias: float32 [4096], P('row'), may hold values from -1 to 1
- second_gain: float32 [2048], P('row'), may hold values from 0.5 to 1.5
- second_bias: float32 [2048], P('row'), may hold values from -1 to 1
- up_bias: float32 [4096], P('row'), may hold values from -1 to 1
- down_bias: float32 [2048], P('row'), may hold values from -1 to 1
- segment_lengths: int32 [1, 13], replicated, may hold values from 128 to 4096, as said below
- leaf_parents: int32 [1, 8], replicated, may hold values from 0 to 3
Outputs:
- block_out: bfloat16 [10240, 2048], P('col', 'row')
- tokens_grad: float32 [10240, 2048], P('col', 'row')
- query_grad: float32 [2048, 2048], P('col', 'row')
- key_grad: float32 [2048, 2048], P('col', 'row')
- value_grad: float32 [2048, 4096], P('col', 'row')
- gate_grad: float32 [2048, 4096], P('col', 'row')
- out_grad: float32 [4096, 2048], P('row', 'col')
- up_grad: float32 [2048, 4096], P('col', 'row')
- down_grad: float32 [4096, 2048], P('row', 'col')
- first_gain_grad: float32 [2048], P(('row', 'col'))
- first_bias_grad: float32 [2048], P(('row', 'col'))
- group_gain_grad: float32 [4096], P(('row', 'col'))
- group_bias_grad: float32 [4096], P(('row', 'col'))
- second_gain_grad: float32 [2048], P(('row', 'col'))
- second_bias_grad: float32 [2048], P(('row', 'col'))
- up_bias_grad: float32 [4096], P(('row', 'col'))
- down_bias_grad: float32 [2048], P(('row', 'col'))
- norm_values: float32 [3], replicated
Inputs may be any that keep to these rules, and one draw needn't show every extreme that they name: segment_lengths[t, 0] is tree t's trunk length, at most 4096; entries 1 to 4 are its branches' and 5 to 12 its leaves' lengths, each at most 512; every entry is at least a quarter of its slot; in tree 0 the trunk, the first branch and the first leaf fill their slots. leaf_parents[t, j] names the branch of tree t on which leaf j hangs.
All inputs are finite; a program needn't handle non-finite values.
Results may differ from a plain program's by a relative error of at most 0.014.
Values may be sent and summed in bfloat16 or wider, within the bound.
A program may use at most 256 MiB of HBM per device.

v0:
```python
import jax
import jax.numpy as jnp
from jax import lax
from jax.sharding import PartitionSpec as P

D = 2048
QK = 256
HV = 512
TRUNK = 4096
SEG = 512


EPSILON = 1e-05


def lookup(values_table, positions):
    matches = positions[..., None] == jnp.arange(values_table.shape[0], dtype=jnp.int32)
    return jnp.sum(jnp.where(matches, values_table, 0), axis=-1)


def token_info(token_index, segment_lengths, leaf_parents):
    tree_count = segment_lengths.shape[0]
    tree_width = TRUNK + 12 * SEG
    tree_id = jnp.floor_divide(token_index, tree_width)
    inside = (tree_id >= 0) & (tree_id < tree_count)
    tree_safe = jnp.clip(tree_id, 0, tree_count - 1)
    offset_in = token_index - tree_id * tree_width
    in_trunk = offset_in < TRUNK
    beyond = jnp.maximum(offset_in - TRUNK, 0)
    segment = jnp.where(in_trunk, 0, 1 + beyond // SEG)
    position = jnp.where(in_trunk, offset_in, beyond % SEG)
    flat_lengths = segment_lengths.reshape(-1)
    own_length = lookup(flat_lengths, tree_safe * 13 + segment)
    trunk_length = lookup(flat_lengths, tree_safe * 13)
    leaf_slot = jnp.clip(segment - 5, 0, 7)
    branch = 1 + lookup(leaf_parents.reshape(-1), tree_safe * 8 + leaf_slot)
    parent = jnp.where(segment >= 5, branch, jnp.where(segment >= 1, 0, -1))
    branch_length = lookup(flat_lengths, tree_safe * 13 + branch)
    path_depth = jnp.where(
        segment == 0,
        position,
        jnp.where(segment < 5, trunk_length + position, trunk_length + branch_length + position),
    )
    is_valid = inside & (position < own_length)
    return (jnp.where(inside, tree_id, -1), segment, position, path_depth, is_valid, parent)


def coefficients(query_info, key_info, log_decay):
    query_tree, query_segment, query_position, query_depth, query_valid, query_parent = query_info
    key_tree, key_segment, key_position, key_depth, key_valid, key_parent = key_info
    same_tree = (query_tree[:, None] == key_tree[None, :]) & key_valid[None, :]
    own_segment = (key_segment[None, :] == query_segment[:, None]) & (
        key_position[None, :] <= query_position[:, None]
    )
    trunk_key = (key_segment[None, :] == 0) & (query_segment[:, None] > 0)
    parent_key = (query_segment[:, None] >= 5) & (key_segment[None, :] == query_parent[:, None])
    visible = same_tree & (own_segment | trunk_key | parent_key)
    distance = jnp.maximum(query_depth[:, None] - key_depth[None, :], 0).astype(jnp.float32)
    decayed = jnp.exp(distance[None, :, :] * log_decay[:, None, None]) * QK ** (-0.5)
    return (jnp.where(visible[None, :, :], decayed, 0.0), jnp.any(visible))


def rotation_tables(path_depth):
    half_width = QK // 2
    frequency = 10000.0 ** (-jnp.arange(half_width, dtype=jnp.float32) / (half_width - 1))
    angles = path_depth.astype(jnp.float32)[:, None] * frequency[None, :]
    return (jnp.cos(angles)[:, None, :], jnp.sin(angles)[:, None, :])


def rotate(values, cosine_table, sine_table):
    half_width = values.shape[-1] // 2
    leading = values[..., :half_width]
    trailing = values[..., half_width:]
    return jnp.concatenate(
        [
            leading * cosine_table - trailing * sine_table,
            trailing * cosine_table + leading * sine_table,
        ],
        axis=-1,
    )


def unrotate(values, cosine_table, sine_table):
    half_width = values.shape[-1] // 2
    leading = values[..., :half_width]
    trailing = values[..., half_width:]
    return jnp.concatenate(
        [
            leading * cosine_table + trailing * sine_table,
            trailing * cosine_table - leading * sine_table,
        ],
        axis=-1,
    )


def gate_piece(retained, gate_raw, gain_vector, bias_vector):
    average = jnp.mean(retained, axis=-1, keepdims=True)
    centred = retained - average
    spread = jnp.mean(centred * centred, axis=-1, keepdims=True)
    normed = (centred * lax.rsqrt(spread + EPSILON)).reshape(
        retained.shape[0], -1
    ) * gain_vector + bias_vector
    return normed * jax.nn.silu(gate_raw)


def spread_rows(activation):
    return lax.all_gather(activation, "row", axis=1, tiled=True)


def collect_rows(partial_sums):
    return lax.psum_scatter(partial_sums, "row", scatter_dimension=1, tiled=True)


def row_sums(first_terms, second_terms):
    return lax.psum((first_terms, second_terms), "row")


def norm_forward(values):
    feature_count = values.shape[1] * lax.axis_size("row")
    totals, squares = row_sums(jnp.sum(values, axis=1), jnp.sum(values * values, axis=1))
    average = totals / feature_count
    inverse = lax.rsqrt(squares / feature_count - average * average + EPSILON)
    return ((values - average[:, None]) * inverse[:, None], inverse)


def norm_backward(grad_out, normal, inverse, gain_vector):
    feature_count = normal.shape[1] * lax.axis_size("row")
    scaled = grad_out * gain_vector
    totals, crossed = row_sums(jnp.sum(scaled, axis=1), jnp.sum(scaled * normal, axis=1))
    grad_in = inverse[:, None] * (
        scaled - totals[:, None] / feature_count - normal * (crossed[:, None] / feature_count)
    )
    return (grad_in, jnp.sum(grad_out * normal, axis=0), jnp.sum(grad_out, axis=0))


def by_blocks(block_fn, row_count):

    def folded(running, portion, first_index):
        block_count = portion.shape[0] // row_count
        stacked = portion.reshape((block_count, row_count) + portion.shape[1:])

        def scan_step(state_now, scan_item):
            sub_block, offset = scan_item
            return (block_fn(state_now, sub_block, offset * row_count), None)

        result, _ = lax.scan(
            scan_step, running, (stacked, jnp.arange(block_count, dtype=jnp.int32))
        )
        return result

    return folded


def visit_keys(stacked_pairs, block_fn, initial):
    return block_fn(initial, lax.all_gather(stacked_pairs, "col", axis=0, tiled=True), jnp.int32(0))


def visit_queries(stacked_pairs, block_fn, initial):
    return block_fn(initial, lax.all_gather(stacked_pairs, "col", axis=0, tiled=True), jnp.int32(0))


def body(
    tokens,
    cotangent,
    query_weight,
    key_weight,
    value_weight,
    gate_weight,
    out_weight,
    up_weight,
    down_weight,
    first_gain,
    first_bias,
    group_gain,
    group_bias,
    second_gain,
    second_bias,
    up_bias,
    down_bias,
    segment_lengths,
    leaf_parents,
):
    row_count = tokens.shape[0]
    query_full, key_full, value_full, gate_full, out_full, up_full, down_full = (
        lax.all_gather(query_weight, "col", axis=0, tiled=True),
        lax.all_gather(key_weight, "col", axis=0, tiled=True),
        lax.all_gather(value_weight, "col", axis=0, tiled=True),
        lax.all_gather(gate_weight, "col", axis=0, tiled=True),
        lax.all_gather(out_weight, "col", axis=1, tiled=True),
        lax.all_gather(up_weight, "col", axis=0, tiled=True),
        lax.all_gather(down_weight, "col", axis=1, tiled=True),
    )
    local_heads = query_full.shape[1] // QK
    head_numbers = (
        lax.axis_index("row") * local_heads + jnp.arange(local_heads, dtype=jnp.int32)
    ).astype(jnp.float32)
    log_decay = jnp.log(1.0 - 2.0 ** (-5.0 - head_numbers))
    own_first = lax.axis_index("col") * row_count
    own_info = token_info(
        own_first + jnp.arange(row_count, dtype=jnp.int32), segment_lengths, leaf_parents
    )
    valid_rows = own_info[4].astype(jnp.float32)
    cosine_table, sine_table = rotation_tables(own_info[3])
    inputs = tokens.astype(jnp.float32)
    normal_one, inverse_one = norm_forward(inputs)
    first_low = (normal_one * first_gain + first_bias).astype(jnp.bfloat16)
    first_wide = spread_rows(first_low)
    query_raw = jnp.dot(first_wide, query_full, preferred_element_type=jnp.float32)
    key_raw = jnp.dot(first_wide, key_full, preferred_element_type=jnp.float32)
    value_raw = jnp.dot(first_wide, value_full, preferred_element_type=jnp.float32)
    gate_raw = jnp.dot(first_wide, gate_full, preferred_element_type=jnp.float32)
    query_rot = rotate(
        query_raw.reshape(row_count, local_heads, QK), cosine_table, sine_table
    ).astype(jnp.bfloat16)
    key_rot = rotate(key_raw.reshape(row_count, local_heads, QK), cosine_table, sine_table).astype(
        jnp.bfloat16
    )
    value_low = value_raw.astype(jnp.bfloat16).reshape(row_count, local_heads, HV)
    keys_values = jnp.concatenate([key_rot, value_low], axis=2).reshape(row_count, -1)

    def forward_block(running, portion, first_index):
        portion_rows = portion.shape[0]
        portion = portion.reshape(portion_rows, local_heads, QK + HV)
        key_part = portion[:, :, :QK]
        value_part = portion[:, :, QK:]
        key_info = token_info(
            first_index + jnp.arange(portion_rows, dtype=jnp.int32), segment_lengths, leaf_parents
        )
        weights, any_seen = coefficients(own_info, key_info, log_decay)

        def forward_compute(state_now):
            products = jnp.einsum(
                "qhd,khd->hqk", query_rot, key_part, preferred_element_type=jnp.float32
            )
            scores = (products * weights).astype(jnp.bfloat16)
            return state_now + jnp.einsum(
                "hqk,khe->qhe", scores, value_part, preferred_element_type=jnp.float32
            )

        return lax.cond(any_seen, forward_compute, lambda state_now: state_now, running)

    retained = visit_keys(
        keys_values,
        by_blocks(forward_block, row_count),
        jnp.zeros((row_count, local_heads, HV), jnp.float32),
    )
    gated_f32, gate_back = jax.vjp(gate_piece, retained, gate_raw, group_gain, group_bias)
    gated_out = gated_f32.astype(jnp.bfloat16)
    attended = collect_rows(jnp.dot(gated_out, out_full, preferred_element_type=jnp.float32))
    middle = inputs + attended
    normal_two, inverse_two = norm_forward(middle)
    second_low = (normal_two * second_gain + second_bias).astype(jnp.bfloat16)
    second_wide = spread_rows(second_low)
    before = jnp.dot(second_wide, up_full, preferred_element_type=jnp.float32) + up_bias
    hidden = jax.nn.gelu(before, approximate=False).astype(jnp.bfloat16)
    fed_out = (
        collect_rows(jnp.dot(hidden, down_full, preferred_element_type=jnp.float32)) + down_bias
    )
    layer_out = middle + fed_out
    grad_fed = cotangent.astype(jnp.float32) * valid_rows[:, None]
    fed_wide = spread_rows(grad_fed.astype(jnp.bfloat16))
    grad_hidden = jnp.einsum("rd,fd->rf", fed_wide, down_full, preferred_element_type=jnp.float32)
    down_grad = jnp.einsum("rf,rd->fd", hidden, fed_wide, preferred_element_type=jnp.float32)
    down_bias_grad = jnp.sum(grad_fed, axis=0)
    _, gelu_back = jax.vjp(lambda values: jax.nn.gelu(values, approximate=False), before)
    grad_before = gelu_back(grad_hidden)[0].astype(jnp.bfloat16)
    up_grad = jnp.einsum("rd,rf->df", second_wide, grad_before, preferred_element_type=jnp.float32)
    up_bias_grad = jnp.sum(grad_before.astype(jnp.float32), axis=0)
    second_back = collect_rows(
        jnp.einsum("rf,df->rd", grad_before, up_full, preferred_element_type=jnp.float32)
    )
    grad_middle_norm, second_gain_grad, second_bias_grad = norm_backward(
        second_back, normal_two, inverse_two, second_gain
    )
    grad_middle = grad_fed + grad_middle_norm
    middle_wide = spread_rows(grad_middle.astype(jnp.bfloat16))
    grad_gated = jnp.einsum("rd,vd->rv", middle_wide, out_full, preferred_element_type=jnp.float32)
    out_grad = jnp.einsum("rv,rd->vd", gated_out, middle_wide, preferred_element_type=jnp.float32)
    grad_retained, grad_gate, group_gain_grad, group_bias_grad = gate_back(grad_gated)
    grad_gate_low = grad_gate.astype(jnp.bfloat16)
    retained_low = grad_retained.astype(jnp.bfloat16)

    def query_block(running, portion, first_index):
        portion_rows = portion.shape[0]
        portion = portion.reshape(portion_rows, local_heads, QK + HV)
        key_part = portion[:, :, :QK]
        value_part = portion[:, :, QK:]
        key_info = token_info(
            first_index + jnp.arange(portion_rows, dtype=jnp.int32), segment_lengths, leaf_parents
        )
        weights, any_seen = coefficients(own_info, key_info, log_decay)

        def query_compute(state_now):
            slopes = jnp.einsum(
                "qhe,khe->hqk", retained_low, value_part, preferred_element_type=jnp.float32
            )
            grad_raw = (slopes * weights).astype(jnp.bfloat16)
            return state_now + jnp.einsum(
                "hqk,khd->qhd", grad_raw, key_part, preferred_element_type=jnp.float32
            )

        return lax.cond(any_seen, query_compute, lambda state_now: state_now, running)

    grad_query_rot = visit_keys(
        keys_values,
        by_blocks(query_block, row_count),
        jnp.zeros((row_count, local_heads, QK), jnp.float32),
    )
    queries_grads = jnp.concatenate([query_rot, retained_low], axis=2).reshape(row_count, -1)

    def key_block(running, portion, first_index):
        portion_rows = portion.shape[0]
        portion = portion.reshape(portion_rows, local_heads, QK + HV)
        query_part = portion[:, :, :QK]
        grad_part = portion[:, :, QK:]
        query_info = token_info(
            first_index + jnp.arange(portion_rows, dtype=jnp.int32), segment_lengths, leaf_parents
        )
        weights, any_seen = coefficients(query_info, own_info, log_decay)

        def key_compute(state_now):
            key_sums, value_sums = state_now
            products = jnp.einsum(
                "qhd,khd->hqk", query_part, key_rot, preferred_element_type=jnp.float32
            )
            scores = (products * weights).astype(jnp.bfloat16)
            value_sums = value_sums + jnp.einsum(
                "hqk,qhe->khe", scores, grad_part, preferred_element_type=jnp.float32
            )
            slopes = jnp.einsum(
                "qhe,khe->hqk", grad_part, value_low, preferred_element_type=jnp.float32
            )
            grad_raw = (slopes * weights).astype(jnp.bfloat16)
            key_sums = key_sums + jnp.einsum(
                "hqk,qhd->khd", grad_raw, query_part, preferred_element_type=jnp.float32
            )
            return (key_sums, value_sums)

        return lax.cond(any_seen, key_compute, lambda state_now: state_now, running)

    grad_key_rot, grad_values = visit_queries(
        queries_grads,
        by_blocks(key_block, row_count),
        (
            jnp.zeros((row_count, local_heads, QK), jnp.float32),
            jnp.zeros((row_count, local_heads, HV), jnp.float32),
        ),
    )
    grad_query = (
        unrotate(grad_query_rot, cosine_table, sine_table)
        .reshape(row_count, -1)
        .astype(jnp.bfloat16)
    )
    grad_key = (
        unrotate(grad_key_rot, cosine_table, sine_table).reshape(row_count, -1).astype(jnp.bfloat16)
    )
    grad_value = grad_values.reshape(row_count, -1).astype(jnp.bfloat16)
    query_grad = jnp.einsum("rd,rq->dq", first_wide, grad_query, preferred_element_type=jnp.float32)
    key_grad = jnp.einsum("rd,rq->dq", first_wide, grad_key, preferred_element_type=jnp.float32)
    value_grad = jnp.einsum("rd,rv->dv", first_wide, grad_value, preferred_element_type=jnp.float32)
    gate_grad = jnp.einsum(
        "rd,rv->dv", first_wide, grad_gate_low, preferred_element_type=jnp.float32
    )
    first_part = jnp.einsum("rq,dq->rd", grad_query, query_full, preferred_element_type=jnp.float32)
    first_part = first_part + jnp.einsum(
        "rq,dq->rd", grad_key, key_full, preferred_element_type=jnp.float32
    )
    first_part = first_part + jnp.einsum(
        "rv,dv->rd", grad_value, value_full, preferred_element_type=jnp.float32
    )
    first_part = first_part + jnp.einsum(
        "rv,dv->rd", grad_gate_low, gate_full, preferred_element_type=jnp.float32
    )
    first_back = collect_rows(first_part)
    grad_first, first_gain_grad, first_bias_grad = norm_backward(
        first_back, normal_one, inverse_one, first_gain
    )
    tokens_grad = grad_middle + grad_first
    summed = (
        lax.psum_scatter(query_grad, "col", scatter_dimension=0, tiled=True),
        lax.psum_scatter(key_grad, "col", scatter_dimension=0, tiled=True),
        lax.psum_scatter(value_grad, "col", scatter_dimension=0, tiled=True),
        lax.psum_scatter(gate_grad, "col", scatter_dimension=0, tiled=True),
        lax.psum_scatter(out_grad, "col", scatter_dimension=1, tiled=True),
        lax.psum_scatter(up_grad, "col", scatter_dimension=0, tiled=True),
        lax.psum_scatter(down_grad, "col", scatter_dimension=1, tiled=True),
        lax.psum_scatter(first_gain_grad, "col", scatter_dimension=0, tiled=True),
        lax.psum_scatter(first_bias_grad, "col", scatter_dimension=0, tiled=True),
        lax.psum_scatter(group_gain_grad, "col", scatter_dimension=0, tiled=True),
        lax.psum_scatter(group_bias_grad, "col", scatter_dimension=0, tiled=True),
        lax.psum_scatter(second_gain_grad, "col", scatter_dimension=0, tiled=True),
        lax.psum_scatter(second_bias_grad, "col", scatter_dimension=0, tiled=True),
        lax.psum_scatter(up_bias_grad, "col", scatter_dimension=0, tiled=True),
        lax.psum_scatter(down_bias_grad, "col", scatter_dimension=0, tiled=True),
    )
    column = valid_rows[:, None]
    totals = lax.psum(
        (
            jnp.sum(column * layer_out * layer_out),
            jnp.sum(column * attended * attended),
            jnp.sum(column * fed_out * fed_out),
        ),
        ("row", "col"),
    )
    valid_count = jnp.sum(segment_lengths).astype(jnp.float32) * D
    norm_values = jnp.sqrt(jnp.stack([totals[0], totals[1], totals[2]]) / valid_count)
    return (
        layer_out.astype(jnp.bfloat16),
        tokens_grad,
        summed[0],
        summed[1],
        summed[2],
        summed[3],
        summed[4],
        summed[5],
        summed[6],
        summed[7],
        summed[8],
        summed[9],
        summed[10],
        summed[11],
        summed[12],
        summed[13],
        summed[14],
        norm_values,
    )


def solution(mesh):
    in_specs = (
        P("col", "row"),
        P("col", "row"),
        P("col", "row"),
        P("col", "row"),
        P("col", "row"),
        P("col", "row"),
        P("row", "col"),
        P("col", "row"),
        P("row", "col"),
        P("row"),
        P("row"),
        P("row"),
        P("row"),
        P("row"),
        P("row"),
        P("row"),
        P("row"),
        P(),
        P(),
    )
    out_specs = (
        P("col", "row"),
        P("col", "row"),
        P("col", "row"),
        P("col", "row"),
        P("col", "row"),
        P("col", "row"),
        P("row", "col"),
        P("col", "row"),
        P("row", "col"),
        P(("row", "col")),
        P(("row", "col")),
        P(("row", "col")),
        P(("row", "col")),
        P(("row", "col")),
        P(("row", "col")),
        P(("row", "col")),
        P(("row", "col")),
        P(),
    )
    return jax.shard_map(body, mesh=mesh, in_specs=in_specs, out_specs=out_specs, check_vma=False)
```

profile of v0, /device:TPU:0, one launch (start us, length us, event | category | flops | bytes accessed | tf_op | source)
XLA Modules:
  0.0 2893.7 jit_solution(17352729068299227666)
XLA Ops:
  9.7 17.5 all-reduce.13
  41.5 63.2 %all-gather.14.cloned.1.call-done = bf16[1280,2048]{1,0:T(8,128)(2,1)} async-done(((bf16[1280,512]{1,0:T(8,128)(2,1)}), bf16[1280,2048]{1,0:T(8,128)(2,1)}) %all-gather.14.cloned.1.call-update) | async-done | bytes 5242896 | tf_op jit(solution)/shard_map/all_gather | solution.py:107
  112.3 23.2 all-gather.22.cloned.1.call-done
  143.5 40.0 %all-gather.18.cloned.1.call-done = bf16[2048,1024]{1,0:T(8,128)(2,1)} async-done(((bf16[256,1024]{1,0:T(8,128)(2,1)}), bf16[2048,1024]{1,0:T(8,128)(2,1)}) %all-gather.18.cloned.1.call-update) | async-done | bytes 4194320 | tf_op jit(solution)/shard_map/all_gather | solution.py:187
  205.0 268.2 %all-gather.20.cloned.1.call-done = bf16[10240,1536]{1,0:T(8,128)(2,1)} async-done(((bf16[1280,1536]{1,0:T(8,128)(2,1)}), bf16[10240,1536]{1,0:T(8,128)(2,1)}) %all-gather.20.cloned.1.call-update) | async-done | bytes 31457296 | tf_op jit(solution)/shard_map/all_gather | solution.py:155
  473.2 37.8 %copy.150 = bf16[8,1280,1536]{1,2,0:T(8,128)(2,1)} copy(bf16[8,1280,1536]{2,1,0:T(8,128)(2,1)} %bitcast.156) | data formatting | bytes 62914560
  514.0 108.1 %while.53 = (s32[]{:T(128)}, f32[1280,2,512]{2,0,1:T(8,128)}, s32[8]{0:T(128)S(1)}, s32[1,13]{1,0:T(1,128)S(1)}, s32[1280]{0:T(1024)S(1)}, /*index=5*/s32[1280]{...) while((s32[]{:T(128)}, f32[1280,2,512]{2,0,1:T(8,128)}, ...), condition=%wide.region_15.16_spmd.clone.clone, body=%wide.region_7.15_spmd.clone.clone.sunk | while | flops 5093961216 | bytes 40192464 | solution.py:146
  524.7 22.6 conditional.12
  663.1 236.1 %reduce-scatter.12.cloned.1.call-done = f32[1280,512]{1,0:T(8,128)} async-done(((f32[1280,2048]{1,0:T(8,128)}), f32[1280,512]{1,0:T(8,128)}) %reduce-scatter.12.cloned.1.call-update) | async-done | bytes 2621456 | tf_op jit(solution)/shard_map/reduce_scatter | solution.py:111
  901.9 15.1 all-reduce.12
  922.7 25.3 all-gather.30.cloned.1.call-done
  948.0 62.3 %all-gather.28.cloned.1.call-done = bf16[1280,2048]{1,0:T(8,128)(2,1)} async-done(((bf16[1280,512]{1,0:T(8,128)(2,1)}), bf16[1280,2048]{1,0:T(8,128)(2,1)}) %all-gather.28.cloned.1.call-update) | async-done | bytes 5242896 | tf_op jit(solution)/shard_map/all_gather | solution.py:107
  1021.0 38.7 %all-gather.32.cloned.1.call-done = bf16[1024,2048]{1,0:T(8,128)(2,1)} async-done(((bf16[1024,256]{1,0:T(8,128)(2,1)}), bf16[1024,2048]{1,0:T(8,128)(2,1)}) %all-gather.32.cloned.1.call-update) | async-done | bytes 4194320 | tf_op jit(solution)/shard_map/all_gather | solution.py:191
  1059.7 61.8 %all-gather.34.cloned.1.call-done = bf16[1280,2048]{1,0:T(8,128)(2,1)} async-done(((bf16[1280,512]{1,0:T(8,128)(2,1)}), bf16[1280,2048]{1,0:T(8,128)(2,1)}) %all-gather.34.cloned.1.call-update) | async-done | bytes 5242896 | tf_op jit(solution)/shard_map/all_gather | solution.py:107
  1121.6 22.5 convert_reduce_fusion
  1166.7 92.8 %reduce-scatter.14.cloned.1.call-done = f32[1280,512]{1,0:T(8,128)} async-done(((f32[1280,2048]{1,0:T(8,128)}), f32[1280,512]{1,0:T(8,128)}) %reduce-scatter.14.cloned.1.call-update) | async-done | bytes 2621456 | tf_op jit(solution)/shard_map/reduce_scatter | solution.py:111
  1259.5 106.5 %reduce-scatter.16.cloned.1.call-done = f32[1280,512]{1,0:T(8,128)} async-done(((f32[1280,2048]{1,0:T(8,128)}), f32[1280,512]{1,0:T(8,128)}) %reduce-scatter.16.cloned.1.call-update) | async-done | bytes 2621456 | tf_op jit(solution)/shard_map/reduce_scatter | solution.py:111
  1372.5 15.1 all-reduce.11
  1393.8 59.5 %all-gather.36.cloned.1.call-done = bf16[1280,2048]{1,0:T(8,128)(2,1)} async-done(((bf16[1280,512]{1,0:T(8,128)(2,1)}), bf16[1280,2048]{1,0:T(8,128)(2,1)}) %all-gather.36.cloned.1.call-update) | async-done | bytes 5242896 | tf_op jit(solution)/shard_map/all_gather | solution.py:107
  1453.3 15.2 fusion.151
  1498.6 107.9 %while.54 = (s32[]{:T(128)}, f32[1280,2,256]{2,0,1:T(8,128)}, s32[8]{0:T(128)S(1)}, s32[1,13]{1,0:T(1,128)S(1)}, s32[1280]{0:T(1024)S(1)}, /*index=5*/s32[1280]{...) while((s32[]{:T(128)}, f32[1280,2,256]{2,0,1:T(8,128)}, ...), condition=%wide.region_40.41_spmd.clone.clone, body=%wide.region_32.40_spmd.clone.clone.sunk | while | flops 5093305856 | bytes 36260304 | solution.py:146
  1510.0 22.5 conditional.13
  1620.6 142.5 %all-gather.38.cloned.1.call-done = bf16[10240,1536]{1,0:T(8,128)(2,1)} async-done(((bf16[1280,1536]{1,0:T(8,128)(2,1)}), bf16[10240,1536]{1,0:T(8,128)(2,1)}) %all-gather.38.cloned.1.call-update) | async-done | bytes 31457296 | tf_op jit(solution)/shard_map/all_gather | solution.py:159
  1763.1 37.4 %copy.164 = bf16[8,1280,1536]{1,2,0:T(8,128)(2,1)} copy(bf16[8,1280,1536]{2,1,0:T(8,128)(2,1)} %bitcast.155) | data formatting | bytes 62914560
  1805.1 378.4 %while.55 = (s32[]{:T(128)}, f32[1280,2,256]{2,0,1:T(8,128)}, f32[1280,2,512]{2,0,1:T(8,128)}, s32[8]{0:T(128)S(1)}, pred[1280]{0:T(1024)(128)(4,1)S(1)}, /*inde...) while((s32[]{:T(128)}, f32[1280,2,256]{2,0,1:T(8,128)}, ...), condition=%wide.region_48.49_spmd.clone.clone, body=%wide.region_41.48_spmd.clone.clone.sunk | while | flops 10144092160 | bytes 60164368 | solution.py:146
  1816.1 36.6 %conditional.14 = ((f32[1280,2,256]{2,0,1:T(8,128)}, f32[1280,2,512]{2,0,1:T(8,128)})) conditional(s32[]{:T(128)} %convert_element_type.307, (f32[1280,2,256]{2,0,1:T(8,128)}, f32[1280,2,512]{2,0,1:T(8,128)}) %tuple.471, (bf16[8,1280,1536]{1,2,0:T(8,128)(2,1)}, s32[]{:T(128)}, bf16[1280,2,512]{2,0,1:T(8,128)(2,1)}, s32[1280]{0:T(1024)S(1)}, ...), branch_computations={%region_46.46_spmd, %region_47.47_spmd.clone} | conditional | flops 10119086080 | bytes 53452860 | solution.py:339
  1825.0 14.1 bitcast_add_fusion.1
  1863.4 36.6 %conditional.14 = ((f32[1280,2,256]{2,0,1:T(8,128)}, f32[1280,2,512]{2,0,1:T(8,128)})) conditional(s32[]{:T(128)} %convert_element_type.307, (f32[1280,2,256]{2,0,1:T(8,128)}, f32[1280,2,512]{2,0,1:T(8,128)}) %tuple.471, (bf16[8,1280,1536]{1,2,0:T(8,128)(2,1)}, s32[]{:T(128)}, bf16[1280,2,512]{2,0,1:T(8,128)(2,1)}, s32[1280]{0:T(1024)S(1)}, ...), branch_computations={%region_46.46_spmd, %region_47.47_spmd.clone} | conditional | flops 10119086080 | bytes 53452860 | solution.py:339
  1910.6 36.6 %conditional.14 = ((f32[1280,2,256]{2,0,1:T(8,128)}, f32[1280,2,512]{2,0,1:T(8,128)})) conditional(s32[]{:T(128)} %convert_element_type.307, (f32[1280,2,256]{2,0,1:T(8,128)}, f32[1280,2,512]{2,0,1:T(8,128)}) %tuple.471, (bf16[8,1280,1536]{1,2,0:T(8,128)(2,1)}, s32[]{:T(128)}, bf16[1280,2,512]{2,0,1:T(8,128)(2,1)}, s32[1280]{0:T(1024)S(1)}, ...), branch_computations={%region_46.46_spmd, %region_47.47_spmd.clone} | conditional | flops 10119086080 | bytes 53452860 | solution.py:339
  1919.5 14.1 bitcast_add_fusion.1
  1957.9 36.6 %conditional.14 = ((f32[1280,2,256]{2,0,1:T(8,128)}, f32[1280,2,512]{2,0,1:T(8,128)})) conditional(s32[]{:T(128)} %convert_element_type.307, (f32[1280,2,256]{2,0,1:T(8,128)}, f32[1280,2,512]{2,0,1:T(8,128)}) %tuple.471, (bf16[8,1280,1536]{1,2,0:T(8,128)(2,1)}, s32[]{:T(128)}, bf16[1280,2,512]{2,0,1:T(8,128)(2,1)}, s32[1280]{0:T(1024)S(1)}, ...), branch_computations={%region_46.46_spmd, %region_47.47_spmd.clone} | conditional | flops 10119086080 | bytes 53452860 | solution.py:339
  2005.1 36.6 %conditional.14 = ((f32[1280,2,256]{2,0,1:T(8,128)}, f32[1280,2,512]{2,0,1:T(8,128)})) conditional(s32[]{:T(128)} %convert_element_type.307, (f32[1280,2,256]{2,0,1:T(8,128)}, f32[1280,2,512]{2,0,1:T(8,128)}) %tuple.471, (bf16[8,1280,1536]{1,2,0:T(8,128)(2,1)}, s32[]{:T(128)}, bf16[1280,2,512]{2,0,1:T(8,128)(2,1)}, s32[1280]{0:T(1024)S(1)}, ...), branch_computations={%region_46.46_spmd, %region_47.47_spmd.clone} | conditional | flops 10119086080 | bytes 53452860 | solution.py:339
  2014.0 14.1 bitcast_add_fusion.1
  2052.4 36.6 %conditional.14 = ((f32[1280,2,256]{2,0,1:T(8,128)}, f32[1280,2,512]{2,0,1:T(8,128)})) conditional(s32[]{:T(128)} %convert_element_type.307, (f32[1280,2,256]{2,0,1:T(8,128)}, f32[1280,2,512]{2,0,1:T(8,128)}) %tuple.471, (bf16[8,1280,1536]{1,2,0:T(8,128)(2,1)}, s32[]{:T(128)}, bf16[1280,2,512]{2,0,1:T(8,128)(2,1)}, s32[1280]{0:T(1024)S(1)}, ...), branch_computations={%region_46.46_spmd, %region_47.47_spmd.clone} | conditional | flops 10119086080 | bytes 53452860 | solution.py:339
  2099.6 36.6 %conditional.14 = ((f32[1280,2,256]{2,0,1:T(8,128)}, f32[1280,2,512]{2,0,1:T(8,128)})) conditional(s32[]{:T(128)} %convert_element_type.307, (f32[1280,2,256]{2,0,1:T(8,128)}, f32[1280,2,512]{2,0,1:T(8,128)}) %tuple.471, (bf16[8,1280,1536]{1,2,0:T(8,128)(2,1)}, s32[]{:T(128)}, bf16[1280,2,512]{2,0,1:T(8,128)(2,1)}, s32[1280]{0:T(1024)S(1)}, ...), branch_computations={%region_46.46_spmd, %region_47.47_spmd.clone} | conditional | flops 10119086080 | bytes 53452860 | solution.py:339
  2108.5 14.1 bitcast_add_fusion.1
  2146.9 36.6 %conditional.14 = ((f32[1280,2,256]{2,0,1:T(8,128)}, f32[1280,2,512]{2,0,1:T(8,128)})) conditional(s32[]{:T(128)} %convert_element_type.307, (f32[1280,2,256]{2,0,1:T(8,128)}, f32[1280,2,512]{2,0,1:T(8,128)}) %tuple.471, (bf16[8,1280,1536]{1,2,0:T(8,128)(2,1)}, s32[]{:T(128)}, bf16[1280,2,512]{2,0,1:T(8,128)(2,1)}, s32[1280]{0:T(1024)S(1)}, ...), branch_computations={%region_46.46_spmd, %region_47.47_spmd.clone} | conditional | flops 10119086080 | bytes 53452860 | solution.py:339
  2210.0 15.9 add_add_fusion.3
  2300.4 37.8 %all-reduce.8 = (f32[1]{0:T(128)}, f32[1]{0:T(128)}, f32[1]{0:T(128)}) all-reduce(f32[1]{0:T(128)} %bitcast.27, f32[1]{0:T(128)} %bitcast.26, f32[1]{0:T(128)} %bitcast.25), channel_id=1, replica_groups=mesh['row'=4,'col'=8] {'row','col'}, use_global_device_ids=true, to_apply=%region_82.83 | all-reduce | flops 3 | bytes 24 | tf_op jit(solution)/shard_map/psum | solution.py:397
  2343.6 28.5 all-reduce.9
  2376.8 15.9 all-reduce.10
  2396.8 24.4 reduce-scatter.30.cloned.1.call-done
  2421.2 90.9 %reduce-scatter.32.cloned.1.call-done = f32[1024,256]{1,0:T(8,128)} async-done(((f32[1024,2048]{1,0:T(8,128)}), f32[1024,256]{1,0:T(8,128)}) %reduce-scatter.32.cloned.1.call-update) | async-done | bytes 1048592 | tf_op jit(solution)/shard_map/reduce_scatter | solution.py:386
  2512.0 90.7 %reduce-scatter.28.cloned.1.call-done = f32[1024,256]{1,0:T(8,128)} async-done(((f32[1024,2048]{1,0:T(8,128)}), f32[1024,256]{1,0:T(8,128)}) %reduce-scatter.28.cloned.1.call-update) | async-done | bytes 1048592 | tf_op jit(solution)/shard_map/reduce_scatter | solution.py:384
  2602.7 90.9 %reduce-scatter.26.cloned.1.call-done = f32[256,1024]{1,0:T(8,128)} async-done(((f32[2048,1024]{1,0:T(8,128)}), f32[256,1024]{1,0:T(8,128)}) %reduce-scatter.26.cloned.1.call-update) | async-done | bytes 1048592 | tf_op jit(solution)/shard_map/reduce_scatter | solution.py:383
  2693.6 51.3 %reduce-scatter.22.cloned.1.call-done = f32[256,512]{1,0:T(8,128)} async-done(((f32[2048,512]{1,0:T(8,128)}), f32[256,512]{1,0:T(8,128)}) %reduce-scatter.22.cloned.1.call-update) | async-done | bytes 524304 | tf_op jit(solution)/shard_map/reduce_scatter | solution.py:381
  2744.9 51.0 %reduce-scatter.20.cloned.1.call-done = f32[256,512]{1,0:T(8,128)} async-done(((f32[2048,512]{1,0:T(8,128)}), f32[256,512]{1,0:T(8,128)}) %reduce-scatter.20.cloned.1.call-update) | async-done | bytes 524304 | tf_op jit(solution)/shard_map/reduce_scatter | solution.py:380
  2795.9 90.5 %reduce-scatter.24.cloned.1.call-done = f32[256,1024]{1,0:T(8,128)} async-done(((f32[2048,1024]{1,0:T(8,128)}), f32[256,1024]{1,0:T(8,128)}) %reduce-scatter.24.cloned.1.call-update) | async-done | bytes 1048592 | tf_op jit(solution)/shard_map/reduce_scatter | solution.py:382
  (703 shorter events, 817.4 us)
Async XLA Ops:
  7.2 25.1 copy-start.36
  7.2 25.2 copy-start.30
  7.2 34.3 %all-gather.16.cloned.1.call-start = ((), (), s32[]{:S(2)}) async-start(), calls=%async_computation.12 | async-start | bytes 2359296 | tf_op jit(solution)/shard_map/all_gather | solution.py:186
  7.9 96.7 %all-gather.14.cloned.1.call-start = ((), (), s32[]{:S(2)}) async-start(), calls=%async_computation.11 | async-start | bytes 6553600 | tf_op jit(solution)/shard_map/all_gather | solution.py:107
  30.8 104.6 %all-gather.22.cloned.1.call-start = ((), (), s32[]{:S(2)}) async-start(), calls=%async_computation.15 | async-start | bytes 2359296 | tf_op jit(solution)/shard_map/all_gather | solution.py:185
  31.6 152.0 %all-gather.18.cloned.1.call-start = ((), (), s32[]{:S(2)}) async-start(), calls=%async_computation.13 | async-start | bytes 4718592 | tf_op jit(solution)/shard_map/all_gather | solution.py:187
  32.1 441.1 %all-gather.20.cloned.1.call-start = ((), (), s32[]{:S(2)}) async-start(), calls=%async_computation.14 | async-start | bytes 35389440 | tf_op jit(solution)/shard_map/all_gather | solution.py:155
  35.5 106.3 %copy-start.7 = (f32[1280,128]{0,1:T(8,128)}, f32[1280,128]{0,1:T(8,128)S(1)}, u32[]{:S(2)}) copy-start(f32[1280,128]{0,1:T(8,128)S(1)} %get-tuple-element.1993) | copy-start | bytes 1966084
  35.5 106.3 %copy-start.9 = (f32[1280,128]{0,1:T(8,128)}, f32[1280,128]{0,1:T(8,128)S(1)}, u32[]{:S(2)}) copy-start(f32[1280,128]{0,1:T(8,128)S(1)} %get-tuple-element.1994) | copy-start | bytes 1966084
  143.5 49.6 %copy-start.13 = (bf16[1280,2,128]{0,2,1:T(8,128)(2,1)}, bf16[1280,2,128]{0,2,1:T(8,128)(2,1)S(1)}, u32[]{:S(2)}) copy-start(bf16[1280,2,128]{0,2,1:T(8,128)(2,1)S(1)} %get-tuple-element.1991) | copy-start | bytes 1966084
  143.5 60.7 %copy-start.10 = (bf16[1280,2,128]{0,2,1:T(8,128)(2,1)}, bf16[1280,2,128]{0,2,1:T(8,128)(2,1)S(1)}, u32[]{:S(2)}) copy-start(bf16[1280,2,128]{0,2,1:T(8,128)(2,1)S(1)} %get-tuple-element.1986) | copy-start | bytes 1966084
  143.5 60.8 %copy-start.12 = (bf16[1280,2,128]{0,2,1:T(8,128)(2,1)}, bf16[1280,2,128]{0,2,1:T(8,128)(2,1)S(1)}, u32[]{:S(2)}) copy-start(bf16[1280,2,128]{0,2,1:T(8,128)(2,1)S(1)} %get-tuple-element.1985) | copy-start | bytes 1966084
  143.5 51.0 %copy-start.15 = (bf16[1280,2,128]{0,2,1:T(8,128)(2,1)S(1)}, bf16[1280,2,128]{0,2,1:T(8,128)(2,1)}, u32[]{:S(2)}) copy-start(bf16[1280,2,128]{0,2,1:T(8,128)(2,1)} %get-tuple-element.1992) | copy-start | bytes 1966084
  202.9 435.5 %all-gather.24.cloned.1.call-start = ((), (), s32[]{:S(2)}) async-start(), calls=%async_computation.16 | async-start | bytes 4718592 | tf_op jit(solution)/shard_map/all_gather | solution.py:188
  203.5 447.5 %all-gather.26.cloned.1.call-start = ((), (), s32[]{:S(2)}) async-start(), calls=%async_computation.17 | async-start | bytes 4718592 | tf_op jit(solution)/shard_map/all_gather | solution.py:189
  204.2 695.0 %reduce-scatter.12.cloned.1.call-start = ((), (), s32[]{:S(2)}) async-start(), calls=%async_computation.18 | async-start | bytes 13107200 | tf_op jit(solution)/shard_map/reduce_scatter | solution.py:111
  662.3 254.6 %copy-start.42 = (f32[512]{0:T(512)S(1)}, f32[512]{0:T(512)}, u32[]{:S(2)}) copy-start(f32[512]{0:T(512)} %param.44) | copy-start | bytes 6148
  662.3 254.6 %copy-start.52 = (f32[512]{0:T(512)S(1)}, f32[512]{0:T(512)}, u32[]{:S(2)}) copy-start(f32[512]{0:T(512)} %param.45) | copy-start | bytes 6148
  662.3 285.7 %all-gather.30.cloned.1.call-start = ((), (), s32[]{:S(2)}) async-start(), calls=%async_computation.20 | async-start | bytes 4718592 | tf_op jit(solution)/shard_map/all_gather | solution.py:190
  663.1 347.2 %all-gather.28.cloned.1.call-start = ((), (), s32[]{:S(2)}) async-start(), calls=%async_computation.19 | async-start | bytes 6553600 | tf_op jit(solution)/shard_map/all_gather | solution.py:107
  901.9 17.4 copy-start.41
  918.5 141.2 %all-gather.32.cloned.1.call-start = ((), (), s32[]{:S(2)}) async-start(), calls=%async_computation.21 | async-start | bytes 4718592 | tf_op jit(solution)/shard_map/all_gather | solution.py:191
  919.2 202.3 %all-gather.34.cloned.1.call-start = ((), (), s32[]{:S(2)}) async-start(), calls=%async_computation.23 | async-start | bytes 6553600 | tf_op jit(solution)/shard_map/all_gather | solution.py:107
  922.7 198.9 %copy-start.47 = (f32[1024]{0:T(1024)S(1)}, f32[1024]{0:T(1024)}, u32[]{:S(2)}) copy-start(f32[1024]{0:T(1024)} %param.46) | copy-start | bytes 12292
  922.7 336.9 %reduce-scatter.14.cloned.1.call-start = ((), (), s32[]{:S(2)}) async-start(), calls=%async_computation.22 | async-start | bytes 13107200 | tf_op jit(solution)/shard_map/reduce_scatter | solution.py:111
  1121.6 22.5 copy-start.16
  1155.8 210.2 %reduce-scatter.16.cloned.1.call-start = ((), (), s32[]{:S(2)}) async-start(), calls=%async_computation.24 | async-start | bytes 13107200 | tf_op jit(solution)/shard_map/reduce_scatter | solution.py:111
  1166.6 199.4 %copy-start.53 = (f32[512]{0:T(512)S(1)}, f32[512]{0:T(512)}, u32[]{:S(2)}) copy-start(f32[512]{0:T(512)} %param.47) | copy-start | bytes 6148
  1166.7 286.6 %all-gather.36.cloned.1.call-start = ((), (), s32[]{:S(2)}) async-start(), calls=%async_computation.25 | async-start | bytes 6553600 | tf_op jit(solution)/shard_map/all_gather | solution.py:107
  1392.0 371.1 %all-gather.38.cloned.1.call-start = ((), (), s32[]{:S(2)}) async-start(), calls=%async_computation.26 | async-start | bytes 35389440 | tf_op jit(solution)/shard_map/all_gather | solution.py:159
  1491.5 849.2 %reduce-scatter.18.cloned.1.call-start = ((), (), s32[]{:S(2)}) async-start(), calls=%async_computation.27 | async-start | bytes 13107200 | tf_op jit(solution)/shard_map/reduce_scatter | solution.py:111
  2225.9 195.3 %reduce-scatter.30.cloned.1.call-start = ((), (), s32[]{:S(2)}) async-start(), calls=%async_computation.33 | async-start | bytes 9437184 | tf_op jit(solution)/shard_map/reduce_scatter | solution.py:385
  2236.9 275.1 %reduce-scatter.32.cloned.1.call-start = ((), (), s32[]{:S(2)}) async-start(), calls=%async_computation.34 | async-start | bytes 9437184 | tf_op jit(solution)/shard_map/reduce_scatter | solution.py:386
  2248.1 354.6 %reduce-scatter.28.cloned.1.call-start = ((), (), s32[]{:S(2)}) async-start(), calls=%async_computation.32 | async-start | bytes 9437184 | tf_op jit(solution)/shard_map/reduce_scatter | solution.py:384
  2259.0 434.6 %reduce-scatter.26.cloned.1.call-start = ((), (), s32[]{:S(2)}) async-start(), calls=%async_computation.31 | async-start | bytes 9437184 | tf_op jit(solution)/shard_map/reduce_scatter | solution.py:383
  2270.0 474.9 %reduce-scatter.22.cloned.1.call-start = ((), (), s32[]{:S(2)}) async-start(), calls=%async_computation.29 | async-start | bytes 4718592 | tf_op jit(solution)/shard_map/reduce_scatter | solution.py:381
  2277.2 518.7 %reduce-scatter.20.cloned.1.call-start = ((), (), s32[]{:S(2)}) async-start(), calls=%async_computation.28 | async-start | bytes 4718592 | tf_op jit(solution)/shard_map/reduce_scatter | solution.py:380
  2284.4 602.0 %reduce-scatter.24.cloned.1.call-start = ((), (), s32[]{:S(2)}) async-start(), calls=%async_computation.30 | async-start | bytes 9437184 | tf_op jit(solution)/shard_map/reduce_scatter | solution.py:382
  2297.1 43.7 %copy-start.2 = (bf16[1280,512]{1,0:T(8,128)(2,1)S(1)}, bf16[1280,512]{1,0:T(8,128)(2,1)}, u32[]{:S(2)}) copy-start(bf16[1280,512]{1,0:T(8,128)(2,1)} %param.31) | copy-start | bytes 3932164
  2297.1 43.7 %copy-start.33 = (f32[1280]{0:T(1024)S(1)}, f32[1280]{0:T(1024)}, u32[]{:S(2)}) copy-start(f32[1280]{0:T(1024)} %copy-done.32) | copy-start | bytes 15364
  2297.1 43.7 %copy-start.35 = (f32[1280]{0:T(1024)S(1)}, f32[1280]{0:T(1024)}, u32[]{:S(2)}) copy-start(f32[1280]{0:T(1024)} %copy-done.34) | copy-start | bytes 15364
  2297.1 43.7 %copy-start.43 = (f32[512]{0:T(512)S(1)}, f32[512]{0:T(512)}, u32[]{:S(2)}) copy-start(f32[512]{0:T(512)} %param.40) | copy-start | bytes 6148
  2297.1 46.4 %copy-start.44 = (f32[512]{0:T(512)S(1)}, f32[512]{0:T(512)}, u32[]{:S(2)}) copy-start(f32[512]{0:T(512)} %get-tuple-element.1837) | copy-start | bytes 6148
  2297.1 46.4 %copy-start.45 = (f32[512]{0:T(512)S(1)}, f32[512]{0:T(512)}, u32[]{:S(2)}) copy-start(f32[512]{0:T(512)} %get-tuple-element.1838) | copy-start | bytes 6148
  2297.1 46.4 %copy-start.46 = (f32[512]{0:T(512)S(1)}, f32[512]{0:T(512)}, u32[]{:S(2)}) copy-start(f32[512]{0:T(512)} %get-tuple-element.1845) | copy-start | bytes 6148
  2297.1 46.4 %copy-start.49 = (f32[1024]{0:T(1024)S(1)}, f32[1024]{0:T(1024)}, u32[]{:S(2)}) copy-start(f32[1024]{0:T(1024)} %get-tuple-element.1938) | copy-start | bytes 12292
  2297.1 46.4 %copy-start.50 = (f32[1024]{0:T(1024)S(1)}, f32[1024]{0:T(1024)}, u32[]{:S(2)}) copy-start(f32[1024]{0:T(1024)} %get-tuple-element.1827) | copy-start | bytes 12292
  2297.2 46.4 %copy-start.51 = (f32[1024]{0:T(1024)S(1)}, f32[1024]{0:T(1024)}, u32[]{:S(2)}) copy-start(f32[1024]{0:T(1024)} %get-tuple-element.1828) | copy-start | bytes 12292
  (38 other events, 167.5 us)
Sparse Core Ops, SparseCore 0:
  9.6 31.7 all-gather.15
  43.9 60.7 all-gather.13
  106.3 29.0 all-gather.21
  136.9 46.6 all-gather.17
  203.0 270.1 all-gather.19
  474.7 45.3 all-gather.23
  521.6 46.5 all-gather.25
  662.4 236.7 reduce-scatter.11
  900.9 47.1 all-gather.29
  950.3 59.9 all-gather.27
  1011.9 47.7 all-gather.31
  1062.0 59.5 all-gather.33
  1156.0 103.5 reduce-scatter.13
  1262.5 103.5 reduce-scatter.15
  1392.1 61.1 all-gather.35
  1491.6 271.4 all-gather.37
  2226.0 102.8 reduce-scatter.17
  2331.6 89.5 reduce-scatter.29
  2424.0 87.9 reduce-scatter.31
  2514.7 87.9 reduce-scatter.27
  2605.6 87.9 reduce-scatter.25
  2696.5 48.3 reduce-scatter.21
  2747.7 48.1 reduce-scatter.19
  2798.6 87.7 reduce-scatter.23
where the time goes:
time: 2910 us; the launch traced here: 2890 us
  waiting for transfers between devices  1720 us (59%)
  matrix products  474 us (16%)
  other arithmetic  319 us (11%)
  local copies, waits for them, and re-layouts  198 us (7%)
  blocking collectives  130 us (4%)
  loops' own time  34 us (1%)
    reduce_scatter x4, waiting for transfers between devices, collect_rows(): lax.psum_scatter(partial_sums, 'row', scatter_dimension=1, tiled=True)  436 us
    all_gather x1, waiting for transfers between devices, visit_keys(): lax.all_gather(stacked_pairs, 'col', axis=0, tiled=True)  268 us
    all_gather x4, waiting for transfers between devices, spread_rows(): return lax.all_gather(activation, 'row', axis=1, tiled=True)  247 us
    all_gather x1, waiting for transfers between devices, visit_queries(): lax.all_gather(stacked_pairs, 'col', axis=0, tiled=True)  143 us
    dot_general x8, matrix products, key_compute(): jnp.einsum('hqk,qhe->khe', scores, grad_part, preferred_element_type=jnp....  113 us
    dot_general x8, matrix products, key_compute(): jnp.einsum('hqk,qhd->khd', grad_raw, query_part, preferred_element_type=j...  109 us
    reduce_or x24, other arithmetic, coefficients(): return (jnp.where(visible[None, :, :], decayed, 0.0), jnp.any(visible))  109 us
    unnamed x138, local copies, waits for them, and re-layouts  97.2 us
  transfers between devices with their start and end apart: 24, of which 21 were waited for; matrix products, arithmetic and copies ran while one was open for 15% of the time, Pallas kernels for 0%

commit v1 on v0

v1 whole, which is shorter than its diff:
```python
import functools

import jax
import jax.numpy as jnp
from jax import lax
from jax.experimental import pallas as pl
from jax.experimental.pallas import tpu as pltpu
from jax.sharding import PartitionSpec as P

D = 2048
QK = 256
HV = 512
TRUNK = 4096
SEG = 512
TREE_LEN = TRUNK + 12 * SEG
CHUNK = 256
TRUNK_CHUNKS = TRUNK // CHUNK
SLOTS = 8

EPSILON = 1e-05
SCALE = QK**-0.5
F32 = jnp.float32
BF16 = jnp.bfloat16

X_PAIRS = [(0, 1), (1, 0), (2, 3), (3, 2)]
Y_PAIRS = [(0, 2), (2, 0), (1, 3), (3, 1)]
D_PAIRS = [(0, 3), (3, 0), (1, 2), (2, 1)]


def mm(a, b):
    return lax.dot_general(a, b, (((1,), (0,)), ((), ())), preferred_element_type=F32)


def mm_nt(a, b):
    return lax.dot_general(a, b, (((1,), (1,)), ((), ())), preferred_element_type=F32)


def mm_tn(a, b):
    return lax.dot_general(a, b, (((0,), (0,)), ((), ())), preferred_element_type=F32)


def params(semantics, limit=None):
    return pltpu.CompilerParams(
        dimension_semantics=semantics, vmem_limit_bytes=limit or 60 * 1024 * 1024
    )


def smem():
    return pl.BlockSpec(memory_space=pltpu.SMEM)


class Chunk:
    def __init__(self, meta, index):
        in_trunk = index < TRUNK_CHUNKS
        beyond = jnp.maximum(index - TRUNK_CHUNKS, 0)
        self.in_trunk = in_trunk
        self.segment = jnp.where(in_trunk, 0, 1 + beyond // 2)
        self.first = jnp.where(in_trunk, index * CHUNK, (beyond % 2) * CHUNK)
        length = meta[self.segment]
        trunk_length = meta[0]
        self.trunk_length = trunk_length
        self.length = length
        self.is_leaf = self.segment >= 5
        self.parent = meta[13 + jnp.clip(self.segment - 5, 0, 7)]
        parent_length = meta[1 + self.parent]
        self.start = jnp.where(
            in_trunk,
            self.first,
            trunk_length + self.first + jnp.where(self.is_leaf, parent_length, 0),
        )
        self.count = jnp.clip(length - self.first, 0, CHUNK)
        self.end = self.start + self.count
        self.continues = jnp.where(in_trunk, index + 1 < TRUNK_CHUNKS, beyond % 2 == 0)


def trunk_reference(meta, place, rows):
    return jnp.minimum(meta[0], jnp.minimum(rows * (place + 1), TRUNK))


def slot_branch(slot):
    return (slot - 4 + 2) % 4


def power(rate, exponent, width):
    return jnp.exp(jnp.full((1, width), exponent.astype(F32), F32) * rate)


def column_power(rate, exponents):
    return jnp.exp(exponents.astype(F32) * rate)


def token_column(width=1):
    return lax.broadcasted_iota(jnp.int32, (CHUNK, width), 0)


def decay_matrix(rate, count):
    t = lax.broadcasted_iota(jnp.int32, (CHUNK, CHUNK), 0)
    u = lax.broadcasted_iota(jnp.int32, (CHUNK, CHUNK), 1)
    seen = (u <= t) & (u < count)
    return jnp.where(seen, jnp.exp((t - u).astype(F32) * rate) * SCALE, 0.0)


def key_decay(rate, count):
    j = token_column()
    return jnp.where(j < count, column_power(rate, jnp.maximum(count - j, 0)), 0.0)


def export_terms(meta, chunk, local, chunks, place, slot, rows):
    if slot == 0:
        is_shift = ((place == 4) | (place == 6)) & (local == chunks - 1)
        exponent = jnp.where(
            chunk.in_trunk,
            jnp.maximum(trunk_reference(meta, place, rows) - chunk.end, 0),
            0,
        )
        return chunk.in_trunk | is_shift, exponent
    wanted = (place == 3) | (place == 4)
    mine = (chunk.segment % 2 == 1) if slot == 1 else (chunk.segment % 2 == 0)
    is_branch = (chunk.segment >= 1) & (chunk.segment < 5)
    exponent = jnp.where(is_branch, jnp.maximum(chunk.length - chunk.first - chunk.count, 0), 0)
    return wanted & mine & is_branch, exponent


def import_terms(meta, chunk, place, slot, rows):
    if slot < 4:
        sees = jnp.logical_not(chunk.in_trunk) | (place > slot)
        return sees, jnp.maximum(chunk.start - trunk_reference(meta, jnp.int32(slot), rows), 0)
    sees = chunk.is_leaf & (chunk.parent == slot_branch(slot))
    return sees, chunk.first


def shift_in(meta, place, chunks):
    previous = Chunk(meta, jnp.maximum(place * chunks - 1, 0))
    return (place == 5) | (place == 7), CHUNK - previous.count


def states_kernel(rows, chunks, meta, rates, key, value, out, acc):
    local = pl.program_id(1)
    rate = rates[pl.program_id(0)]
    place = meta[21]
    chunk = Chunk(meta, place * chunks + local)
    weighted = (key[...].astype(F32) * key_decay(rate, chunk.count)).astype(BF16)
    state = mm_tn(weighted, value[...])

    @pl.when(local == 0)
    def _():
        acc[...] = jnp.zeros_like(acc)

    for slot in range(3):
        on, exponent = export_terms(meta, chunk, local, chunks, place, slot, rows)

        @pl.when(on)
        def _():
            acc[slot] += state * power(rate, exponent, HV)

    @pl.when(local == chunks - 1)
    def _():
        out[:, 0] = acc[...].astype(BF16)


def make_states(meta, rates, key, value):
    rows = key.shape[0]
    heads = key.shape[1] // QK
    chunks = rows // CHUNK
    return pl.pallas_call(
        functools.partial(states_kernel, rows, chunks),
        grid=(heads, chunks),
        in_specs=[
            smem(),
            smem(),
            pl.BlockSpec((CHUNK, QK), lambda h, c: (c, h)),
            pl.BlockSpec((CHUNK, HV), lambda h, c: (c, h)),
        ],
        out_specs=pl.BlockSpec((3, 1, QK, HV), lambda h, c: (0, h, 0, 0)),
        out_shape=jax.ShapeDtypeStruct((3, heads, QK, HV), BF16),
        scratch_shapes=[pltpu.VMEM((3, QK, HV), F32)],
        compiler_params=params(("arbitrary", "arbitrary")),
        name="chunk_states",
        cost_estimate=pl.CostEstimate(
            flops=2 * rows * heads * QK * HV, bytes_accessed=rows * heads * 1536, transcendentals=0
        ),
    )(meta, rates, key, value)


def retain_kernel(
    rows, chunks, meta, rates, query, key, value, gate, shared, shifted, gain, bias,
    gated_out, normal_out, inverse_out, state_out, running,
):
    local = pl.program_id(1)
    rate = rates[pl.program_id(0)]
    place = meta[21]
    chunk = Chunk(meta, place * chunks + local)

    @pl.when(local == 0)
    def _():
        running[...] = jnp.zeros_like(running)
        on, exponent = shift_in(meta, place, chunks)

        @pl.when(on)
        def _():
            running[...] = shifted[0].astype(F32) * power(rate, exponent, HV)

    incoming = running[...]
    state_ref = state_out.at[0, 0]
    running_total = incoming
    for slot in range(SLOTS):
        on, exponent = import_terms(meta, chunk, place, slot, rows)
        scale = jnp.where(on, power(rate, exponent, HV), 0.0)
        running_total = running_total + shared[slot, 0].astype(F32) * scale
    state = running_total.astype(BF16)
    state_ref[...] = state

    q, k, v = query[...], key[...], value[...]
    scores = (mm_nt(q, k) * decay_matrix(rate, chunk.count)).astype(BF16)
    own = token_column()
    reach = column_power(rate, own) * SCALE
    retained = mm(scores, v) + mm(q, state) * reach

    j = token_column()
    ahead = jnp.where(j < chunk.count, column_power(rate, CHUNK - j), 0.0)
    fresh = mm_tn((k.astype(F32) * ahead).astype(BF16), v)
    keep = jnp.where(chunk.continues, 1.0, 0.0)
    running[...] = (incoming * power(rate, jnp.int32(CHUNK), HV) + fresh) * keep

    average = jnp.mean(retained, axis=1, keepdims=True)
    centred = retained - average
    inverse = lax.rsqrt(jnp.mean(centred * centred, axis=1, keepdims=True) + EPSILON)
    normal = centred * inverse
    gate_value = gate[...].astype(F32)
    gated = (normal * gain[...] + bias[...]) * (gate_value / (1.0 + jnp.exp(-gate_value)))
    gated_out[...] = gated.astype(BF16)
    normal_out[...] = normal.astype(BF16)
    inverse_out[0] = jnp.broadcast_to(inverse, (CHUNK, 128))


def retain(meta, rates, query, key, value, gate, shared, shifted, gain, bias):
    rows = key.shape[0]
    heads = key.shape[1] // QK
    chunks = rows // CHUNK
    wide = pl.BlockSpec((CHUNK, HV), lambda h, c: (c, h))
    narrow = pl.BlockSpec((CHUNK, QK), lambda h, c: (c, h))
    vector = pl.BlockSpec((1, HV), lambda h, c: (0, h))
    return pl.pallas_call(
        functools.partial(retain_kernel, rows, chunks),
        grid=(heads, chunks),
        in_specs=[
            smem(), smem(), narrow, narrow, wide, wide,
            pl.BlockSpec((SLOTS, 1, QK, HV), lambda h, c: (0, h, 0, 0)),
            pl.BlockSpec((1, QK, HV), lambda h, c: (h, 0, 0)),
            vector, vector,
        ],
        out_specs=[
            wide, wide,
            pl.BlockSpec((1, CHUNK, 128), lambda h, c: (h, c, 0)),
            pl.BlockSpec((1, 1, QK, HV), lambda h, c: (h, c, 0, 0)),
        ],
        out_shape=[
            jax.ShapeDtypeStruct((rows, heads * HV), BF16),
            jax.ShapeDtypeStruct((rows, heads * HV), BF16),
            jax.ShapeDtypeStruct((heads, rows, 128), F32),
            jax.ShapeDtypeStruct((heads, chunks, QK, HV), BF16),
        ],
        scratch_shapes=[pltpu.VMEM((QK, HV), F32)],
        compiler_params=params(("arbitrary", "arbitrary")),
        name="retention_forward",
        cost_estimate=pl.CostEstimate(
            flops=2 * rows * heads * (CHUNK * 768 + 2 * QK * HV),
            bytes_accessed=rows * heads * 8192,
            transcendentals=rows * heads * 768,
        ),
    )(meta, rates, query, key, value, gate, shared, shifted, gain[None, :], bias[None, :])


def gate_back_kernel(
    rows, chunks, meta, rates, wide, weight, gate, normal_in, inverse_in, query, gain, bias,
    gate_out, retained_out, gain_out, bias_out, exports, first_out, acc,
):
    local = pl.program_id(1)
    rate = rates[pl.program_id(0)]
    place = meta[21]
    chunk = Chunk(meta, place * chunks + local)
    grad_gated = mm(wide[...], weight[...])
    gate_value = gate[...].astype(F32)
    normal = normal_in[...].astype(F32)
    sigmoid = 1.0 / (1.0 + jnp.exp(-gate_value))
    normed = normal * gain[...] + bias[...]
    grad_gate = grad_gated * normed * (sigmoid * (1.0 + gate_value * (1.0 - sigmoid)))
    gate_out[...] = grad_gate.astype(BF16)
    grad_normed = grad_gated * (gate_value * sigmoid)

    @pl.when(local == 0)
    def _():
        gain_out[...] = jnp.zeros_like(gain_out)
        bias_out[...] = jnp.zeros_like(bias_out)
        acc[...] = jnp.zeros_like(acc)

    gain_out[...] += jnp.sum(grad_normed * normal, axis=0, keepdims=True)
    bias_out[...] += jnp.sum(grad_normed, axis=0, keepdims=True)
    scaled = grad_normed * gain[...]
    grad = inverse_in[0][:, :1] * (
        scaled
        - jnp.mean(scaled, axis=1, keepdims=True)
        - normal * jnp.mean(scaled * normal, axis=1, keepdims=True)
    )
    grad = grad.astype(BF16)
    retained_out[...] = grad
    reach = column_power(rate, token_column()) * SCALE
    state = mm_tn((query[...].astype(F32) * reach).astype(BF16), grad)
    for slot in range(SLOTS):
        on, exponent = import_terms(meta, chunk, place, slot, rows)

        @pl.when(on)
        def _():
            acc[slot] += state * power(rate, exponent, HV)

    @pl.when(local == 0)
    def _():
        on, exponent = shift_in(meta, place, chunks)
        scale = jnp.where(on, power(rate, exponent, HV), 0.0)
        first_out[0] = (state * scale).astype(BF16)

    @pl.when(local == chunks - 1)
    def _():
        exports[:, 0] = acc[...].astype(BF16)


def gate_back(meta, rates, wide, weight, gate, normal, inverse, query, gain, bias):
    rows = query.shape[0]
    heads = query.shape[1] // QK
    chunks = rows // CHUNK
    block = pl.BlockSpec((CHUNK, HV), lambda h, c: (c, h))
    vector = pl.BlockSpec((1, HV), lambda h, c: (0, h))
    return pl.pallas_call(
        functools.partial(gate_back_kernel, rows, chunks),
        grid=(heads, chunks),
        in_specs=[
            smem(), smem(),
            pl.BlockSpec((CHUNK, D), lambda h, c: (c, 0)),
            pl.BlockSpec((D, HV), lambda h, c: (0, h)),
            block, block,
            pl.BlockSpec((1, CHUNK, 128), lambda h, c: (h, c, 0)),
            pl.BlockSpec((CHUNK, QK), lambda h, c: (c, h)),
            vector, vector,
        ],
        out_specs=[
            block, block, vector, vector,
            pl.BlockSpec((SLOTS, 1, QK, HV), lambda h, c: (0, h, 0, 0)),
            pl.BlockSpec((1, QK, HV), lambda h, c: (h, 0, 0)),
        ],
        out_shape=[
            jax.ShapeDtypeStruct((rows, heads * HV), BF16),
            jax.ShapeDtypeStruct((rows, heads * HV), BF16),
            jax.ShapeDtypeStruct((1, heads * HV), F32),
            jax.ShapeDtypeStruct((1, heads * HV), F32),
            jax.ShapeDtypeStruct((SLOTS, heads, QK, HV), BF16),
            jax.ShapeDtypeStruct((heads, QK, HV), BF16),
        ],
        scratch_shapes=[pltpu.VMEM((SLOTS, QK, HV), F32)],
        compiler_params=params(("arbitrary", "arbitrary")),
        name="gate_backward",
        cost_estimate=pl.CostEstimate(
            flops=2 * rows * heads * HV * (D + QK),
            bytes_accessed=rows * heads * 12288,
            transcendentals=rows * heads * HV,
        ),
    )(meta, rates, wide, weight, gate, normal, inverse, query, gain[None, :], bias[None, :])


def retain_back_kernel(
    rows, chunks, meta, rates, query, key, value, grad, state_in, cosine, sine, own0, own1, own2,
    query_out, key_out, value_out, running,
):
    step = pl.program_id(1)
    local = chunks - 1 - step
    rate = rates[pl.program_id(0)]
    place = meta[21]
    chunk = Chunk(meta, place * chunks + local)
    before = Chunk(meta, jnp.maximum(place * chunks + local - 1, 0))

    @pl.when(step == 0)
    def _():
        running[...] = jnp.zeros_like(running)

    later = running[...]
    total = later
    for slot, ref in ((0, own0), (1, own1), (2, own2)):
        on, exponent = export_terms(meta, chunk, local, chunks, place, slot, rows)
        total = total + ref[0].astype(F32) * jnp.where(on, power(rate, exponent, HV), 0.0)
    total = total.astype(BF16)

    q, k, v, g = query[...], key[...], value[...], grad[...]
    decay = decay_matrix(rate, chunk.count)
    scores = (mm_nt(q, k) * decay).astype(BF16)
    slopes = (mm_nt(g, v) * decay).astype(BF16)
    reach = column_power(rate, token_column()) * SCALE
    toward = key_decay(rate, chunk.count)
    grad_query = mm(slopes, k) + mm_nt(g, state_in[0, 0]) * reach
    grad_key = mm_tn(slopes, q) + mm_nt(v, total) * toward
    grad_value = mm_tn(scores, g) + mm(k, total) * toward
    value_out[...] = grad_value.astype(BF16)
    cos, sin = cosine[...], sine[...]
    half = QK // 2
    for out, val in ((query_out, grad_query), (key_out, grad_key)):
        a, b = val[:, :half], val[:, half:]
        out[:, :half] = (a * cos + b * sin).astype(BF16)
        out[:, half:] = (b * cos - a * sin).astype(BF16)

    fresh = mm_tn((q.astype(F32) * reach).astype(BF16), g)
    carried = fresh + later * power(rate, chunk.count, HV)
    keep = jnp.where((local > 0) & before.continues, 1.0, 0.0)
    running[...] = carried * power(rate, CHUNK - before.count, HV) * keep


def retain_back(meta, rates, query, key, value, grad, states, cosine, sine, own):
    rows = query.shape[0]
    heads = query.shape[1] // QK
    chunks = rows // CHUNK
    last = chunks - 1
    wide = pl.BlockSpec((CHUNK, HV), lambda h, s: (last - s, h))
    narrow = pl.BlockSpec((CHUNK, QK), lambda h, s: (last - s, h))
    table = pl.BlockSpec((CHUNK, QK // 2), lambda h, s: (last - s, 0))
    state = pl.BlockSpec((1, QK, HV), lambda h, s: (h, 0, 0))
    return pl.pallas_call(
        functools.partial(retain_back_kernel, rows, chunks),
        grid=(heads, chunks),
        in_specs=[
            smem(), smem(), narrow, narrow, wide, wide,
            pl.BlockSpec((1, 1, QK, HV), lambda h, s: (h, last - s, 0, 0)),
            table, table, state, state, state,
        ],
        out_specs=[narrow, narrow, wide],
        out_shape=[
            jax.ShapeDtypeStruct((rows, heads * QK), BF16),
            jax.ShapeDtypeStruct((rows, heads * QK), BF16),
            jax.ShapeDtypeStruct((rows, heads * HV), BF16),
        ],
        scratch_shapes=[pltpu.VMEM((QK, HV), F32)],
        compiler_params=params(("arbitrary", "arbitrary")),
        name="retention_backward",
        cost_estimate=pl.CostEstimate(
            flops=2 * rows * heads * (CHUNK * 1792 + 4 * QK * HV),
            bytes_accessed=rows * heads * 6144,
            transcendentals=rows * heads * 256,
        ),
    )(meta, rates, query, key, value, grad, states, cosine, sine, *own)


def norm_kernel(values, gain, bias, out, average_out, inverse_out):
    x = values[...].astype(F32)
    average = jnp.mean(x, axis=1, keepdims=True)
    inverse = lax.rsqrt(jnp.mean(x * x, axis=1, keepdims=True) - average * average + EPSILON)
    out[...] = ((x - average) * inverse * gain[...] + bias[...]).astype(BF16)
    average_out[...] = jnp.broadcast_to(average, average_out.shape)
    inverse_out[...] = jnp.broadcast_to(inverse, inverse_out.shape)


def norm_wide(values, gain, bias):
    rows = values.shape[0]
    block = pl.BlockSpec((CHUNK, D), lambda i: (i, 0))
    vector = pl.BlockSpec((1, D), lambda i: (0, 0))
    stat = pl.BlockSpec((CHUNK, 128), lambda i: (i, 0))
    return pl.pallas_call(
        norm_kernel,
        grid=(rows // CHUNK,),
        in_specs=[block, vector, vector],
        out_specs=[block, stat, stat],
        out_shape=[
            jax.ShapeDtypeStruct((rows, D), BF16),
            jax.ShapeDtypeStruct((rows, 128), F32),
            jax.ShapeDtypeStruct((rows, 128), F32),
        ],
        compiler_params=params(("arbitrary",)),
        name="layer_norm",
        cost_estimate=pl.CostEstimate(
            flops=8 * rows * D, bytes_accessed=4 * rows * D, transcendentals=rows
        ),
    )(values, gain[None, :], bias[None, :])


def rotate_kernel(heads, values, weight, cosine, sine, out):
    raw = mm(values[...], weight[...])
    cos, sin = cosine[...], sine[...]
    half = QK // 2
    for head in range(heads):
        a = raw[:, head * QK : head * QK + half]
        b = raw[:, head * QK + half : (head + 1) * QK]
        out[:, head * QK : head * QK + half] = (a * cos - b * sin).astype(BF16)
        out[:, head * QK + half : (head + 1) * QK] = (b * cos + a * sin).astype(BF16)


def project_rotated(values, weight, cosine, sine):
    rows, width = values.shape[0], weight.shape[1]
    table = pl.BlockSpec((CHUNK, QK // 2), lambda i: (i, 0))
    return pl.pallas_call(
        functools.partial(rotate_kernel, width // QK),
        grid=(rows // CHUNK,),
        in_specs=[
            pl.BlockSpec((CHUNK, D), lambda i: (i, 0)),
            pl.BlockSpec((D, width), lambda i: (0, 0)),
            table, table,
        ],
        out_specs=pl.BlockSpec((CHUNK, width), lambda i: (i, 0)),
        out_shape=jax.ShapeDtypeStruct((rows, width), BF16),
        compiler_params=params(("arbitrary",)),
        name="project_rotated",
        cost_estimate=pl.CostEstimate(
            flops=2 * rows * D * width, bytes_accessed=2 * (rows + width) * D, transcendentals=0
        ),
    )(values, weight, cosine, sine)


def up_kernel(values, weight, bias, grad_hidden, hidden_out, grad_out, bias_out):
    before = mm(values[...], weight[...]) + bias[...]
    phi = 0.5 * (1.0 + lax.erf(before * (0.5**0.5)))
    hidden_out[...] = (before * phi).astype(BF16)
    density = jnp.exp(-0.5 * before * before) * 0.3989422804014327
    grad = (grad_hidden[...].astype(F32) * (phi + before * density)).astype(BF16)
    grad_out[...] = grad

    @pl.when(pl.program_id(0) == 0)
    def _():
        bias_out[...] = jnp.zeros_like(bias_out)

    bias_out[...] += jnp.sum(grad.astype(F32), axis=0, keepdims=True)


def feed_up(values, weight, bias, grad_hidden):
    rows, width = values.shape[0], weight.shape[1]
    block = pl.BlockSpec((CHUNK, width), lambda i: (i, 0))
    vector = pl.BlockSpec((1, width), lambda i: (0, 0))
    return pl.pallas_call(
        up_kernel,
        grid=(rows // CHUNK,),
        in_specs=[
            pl.BlockSpec((CHUNK, D), lambda i: (i, 0)),
            pl.BlockSpec((D, width), lambda i: (0, 0)),
            vector, block,
        ],
        out_specs=[block, block, vector],
        out_shape=[
            jax.ShapeDtypeStruct((rows, width), BF16),
            jax.ShapeDtypeStruct((rows, width), BF16),
            jax.ShapeDtypeStruct((1, width), F32),
        ],
        compiler_params=params(("arbitrary",)),
        name="feed_up",
        cost_estimate=pl.CostEstimate(
            flops=2 * rows * D * width,
            bytes_accessed=2 * (rows + width) * D + 8 * rows * width,
            transcendentals=2 * rows * width,
        ),
    )(values, weight, bias[None, :], grad_hidden)


PARTIAL_FLIP = (1, 3, 2, 3, 2, 1, 0, 0)
PARTIAL_HALF = (0, 0, 1, 1, 0, 1, 0, 1)


def table_lookup(table, step):
    result = jnp.int32(table[0])
    for index in range(1, len(table)):
        result = jnp.where(step == index, table[index], result)
    return result


def partial_kernel(count, row, *refs):
    values, weights = refs[:count], refs[count : 2 * count]
    outs = refs[2 * count :]
    step = pl.program_id(0)
    total = mm_nt(values[0][...], weights[0][...])
    for x, w in zip(values[1:], weights[1:]):
        total = total + mm_nt(x[...], w[...])
    for index, out in enumerate(outs):

        @pl.when(step // 2 == index)
        def _():
            out[0] = total.astype(out.dtype)


def partial_blocks(values, weights, row):
    rows = values[0].shape[0]
    half, block = rows // 2, D // 4
    count = len(values)

    def value_spec(x):
        return pl.BlockSpec((half, x.shape[1]), lambda s, r: (table_lookup(PARTIAL_HALF, s), 0))

    def weight_spec(w):
        return pl.BlockSpec(
            (block, w.shape[1]), lambda s, r: (r[0] ^ table_lookup(PARTIAL_FLIP, s), 0)
        )

    def out_spec(index):
        return pl.BlockSpec(
            (1, half, block), lambda s, r: (jnp.clip(s - 2 * index, 0, 1), 0, 0)
        )

    depth = sum(x.shape[1] for x in values)
    return pl.pallas_call(
        functools.partial(partial_kernel, count),
        grid_spec=pltpu.PrefetchScalarGridSpec(
            num_scalar_prefetch=1,
            grid=(8,),
            in_specs=[value_spec(x) for x in values] + [weight_spec(w) for w in weights],
            out_specs=[out_spec(index) for index in range(4)],
        ),
        out_shape=[
            jax.ShapeDtypeStruct((2, half, block), BF16 if index < 3 else F32) for index in range(4)
        ],
        compiler_params=params(("arbitrary",)),
        name="partial_blocks",
        cost_estimate=pl.CostEstimate(
            flops=2 * rows * D * depth,
            bytes_accessed=2 * (2 * rows + 2 * D) * depth + 4 * rows * D,
            transcendentals=0,
        ),
    )(row, *values, *weights)


def permute_row(value, pairs):
    return lax.ppermute(value, "row", pairs)


def reduce_row(values, weights, row):
    if lax.axis_size("row") != 4:
        total = sum(mm_nt(x, w) for x, w in zip(values, weights)).astype(BF16)
        return lax.psum_scatter(total, "row", scatter_dimension=1, tiled=True).astype(F32)
    send_x, send_y, keep, own = partial_blocks(values, weights, row)
    from_x = permute_row(send_x, X_PAIRS)
    from_y = permute_row(send_y, Y_PAIRS)
    next_y = (keep[0].astype(F32) + from_x[1].astype(F32)).astype(BF16)
    next_x = (keep[1].astype(F32) + from_y[1].astype(F32)).astype(BF16)
    last_y = permute_row(next_y, Y_PAIRS)
    last_x = permute_row(next_x, X_PAIRS)
    first_half = own[0] + from_x[0].astype(F32) + last_y.astype(F32)
    second_half = own[1] + from_y[0].astype(F32) + last_x.astype(F32)
    return jnp.concatenate([first_half, second_half], axis=0)


def gather_row(value):
    if lax.axis_size("row") != 4:
        return lax.all_gather(value, "row", axis=1, tiled=True)
    row = lax.axis_index("row")
    rows, block = value.shape
    half = rows // 2
    from_x = permute_row(value, X_PAIRS)
    from_y = permute_row(value, Y_PAIRS)
    far_a = permute_row(from_x[:half], Y_PAIRS)
    far_b = permute_row(from_y[half:], X_PAIRS)
    out = jnp.zeros((rows, 4 * block), value.dtype)
    zero = jnp.int32(0)
    out = lax.dynamic_update_slice(out, value, (zero, row * block))
    out = lax.dynamic_update_slice(out, from_x, (zero, (row ^ 1) * block))
    out = lax.dynamic_update_slice(out, from_y, (zero, (row ^ 2) * block))
    out = lax.dynamic_update_slice(out, far_a, (zero, (row ^ 3) * block))
    return lax.dynamic_update_slice(out, far_b, (jnp.int32(half), (row ^ 3) * block))


def gather_row_small(value):
    if lax.axis_size("row") != 4:
        return lax.all_gather(value, "row", axis=1, tiled=True)
    row = lax.axis_index("row")
    pieces = jnp.stack(
        [value] + [permute_row(value, pairs) for pairs in (X_PAIRS, Y_PAIRS, D_PAIRS)]
    )
    ordered = [
        lax.dynamic_index_in_dim(pieces, row ^ place, 0, keepdims=False) for place in range(4)
    ]
    return jnp.concatenate(ordered, axis=1)


def sum_row_small(value):
    if lax.axis_size("row") != 4:
        return lax.psum(value, "row")
    first = value + permute_row(value, X_PAIRS)
    return first + permute_row(first, Y_PAIRS)


def norm_backward(grad_out, normal, inverse, gain_vector):
    scaled = grad_out * gain_vector
    sums = sum_row_small(jnp.stack([jnp.sum(scaled, axis=1), jnp.sum(scaled * normal, axis=1)]))
    means = sums / D
    grad_in = inverse * (scaled - means[0][:, None] - normal * means[1][:, None])
    return (grad_in, jnp.sum(grad_out * normal, axis=0), jnp.sum(grad_out, axis=0))


def gather_col(weight):
    return lax.all_gather(weight, "col", axis=0, tiled=True)


def scatter_col(grad):
    return lax.psum_scatter(grad, "col", scatter_dimension=0, tiled=True).astype(F32)


def permute_col(value, pairs, place_count):
    size = lax.axis_size("col")
    all_pairs = [
        (base + a, base + b) for base in range(0, size, place_count) for a, b in pairs
    ]
    return lax.ppermute(value, "col", all_pairs)


def share_states(exports, place, tree):
    from_b0 = permute_col(exports[1], [(3, 6)], SLOTS)
    from_b = permute_col(exports[2], [(3, 7), (4, 5)], SLOTS)
    shifted = permute_col(exports[0], [(4, 5), (6, 7)], SLOTS)
    mine = jnp.where(
        place < 4,
        exports[0],
        jnp.where(place == 4, exports[1], jnp.where(place == 6, from_b0, from_b)),
    )
    shared = lax.all_gather(mine, "col", axis=0)
    if shared.shape[0] != SLOTS:
        shared = lax.dynamic_slice_in_dim(shared, tree * SLOTS, SLOTS, 0)
    return shared, shifted


def return_states(exports, first_state, place, tree):
    size = lax.axis_size("col")
    if size != SLOTS:
        full = jnp.zeros((size,) + exports.shape[1:], exports.dtype)
        zero = jnp.int32(0)
        exports = lax.dynamic_update_slice(full, exports, (tree * SLOTS, zero, zero, zero))
    mine = lax.psum_scatter(exports, "col", scatter_dimension=0, tiled=True)[0]
    to_b0 = permute_col(mine, [(6, 3)], SLOTS)
    to_b = permute_col(mine, [(7, 3), (5, 4)], SLOTS)
    shifted = permute_col(first_state, [(5, 4), (7, 6)], SLOTS)
    own0 = jnp.where(place < 4, mine, shifted)
    own1 = jnp.where(place == 4, mine, to_b0)
    return own0, own1, to_b


def sum_col_vectors(vectors, extra=None):
    col = lax.axis_index("col")
    size = lax.axis_size("col")
    parts = list(vectors) + ([extra] if extra is not None else [])
    total = jnp.sum(lax.all_gather(jnp.concatenate(parts), "col", axis=0), axis=0)
    results, first = [], 0
    for vector in vectors:
        width = vector.shape[0] // size
        results.append(lax.dynamic_slice_in_dim(total, first + col * width, width, 0))
        first += vector.shape[0]
    return results, total[first:]


def token_tables(place, rows, lengths, parents):
    index = place * rows + jnp.arange(rows, dtype=jnp.int32)
    in_trunk = index < TRUNK
    beyond = jnp.maximum(index - TRUNK, 0)
    segment = jnp.where(in_trunk, 0, 1 + beyond // SEG)
    position = jnp.where(in_trunk, index, beyond % SEG)

    def lookup(table, spots):
        hits = spots[:, None] == jnp.arange(table.shape[0], dtype=jnp.int32)
        return jnp.sum(jnp.where(hits, table, 0), axis=1)

    branch = 1 + lookup(parents, jnp.clip(segment - 5, 0, 7))
    parent_length = lookup(lengths, branch)
    depth = position + jnp.where(segment >= 1, lengths[0], 0)
    depth = depth + jnp.where(segment >= 5, parent_length, 0)
    valid = (position < lookup(lengths, segment)).astype(F32)
    half = QK // 2
    frequency = 10000.0 ** (-jnp.arange(half, dtype=F32) / (half - 1))
    angles = depth.astype(F32)[:, None] * frequency[None, :]
    return valid, jnp.cos(angles), jnp.sin(angles)


def body(
    tokens,
    cotangent,
    query_weight,
    key_weight,
    value_weight,
    gate_weight,
    out_weight,
    up_weight,
    down_weight,
    first_gain,
    first_bias,
    group_gain,
    group_bias,
    second_gain,
    second_bias,
    up_bias,
    down_bias,
    segment_lengths,
    leaf_parents,
):
    rows = tokens.shape[0]
    col = lax.axis_index("col")
    row = lax.axis_index("row")
    row_ref = row.astype(jnp.int32)[None]
    place = (col % SLOTS).astype(jnp.int32)
    tree = (col // SLOTS).astype(jnp.int32)
    lengths = lax.dynamic_index_in_dim(segment_lengths, tree, 0, keepdims=False)
    parents = lax.dynamic_index_in_dim(leaf_parents, tree, 0, keepdims=False)
    meta = jnp.concatenate([lengths, parents, place[None]]).astype(jnp.int32)
    heads = query_weight.shape[1] // QK
    head_numbers = (row * heads + jnp.arange(heads, dtype=jnp.int32)).astype(F32)
    rates = jnp.log(1.0 - 2.0 ** (-5.0 - head_numbers))

    query_full = gather_col(query_weight)
    key_full = gather_col(key_weight)
    value_full = gather_col(value_weight)
    gate_full = gather_col(gate_weight)
    out_full = gather_col(out_weight.T)
    up_full = gather_col(up_weight)
    down_full = gather_col(down_weight.T)

    valid, cosine, sine = token_tables(place, rows, lengths, parents)
    column = valid[:, None]
    gains = gather_row_small(jnp.stack([first_gain, first_bias, second_gain, second_bias]))
    token_wide = gather_row(tokens)
    fed_low = (cotangent.astype(F32) * column).astype(BF16)
    fed_wide = gather_row(fed_low)

    first_wide, first_average, first_inverse = norm_wide(token_wide, gains[0], gains[1])
    query_rot = project_rotated(first_wide, query_full, cosine, sine)
    key_rot = project_rotated(first_wide, key_full, cosine, sine)
    value_low = mm(first_wide, value_full).astype(BF16)
    exports = make_states(meta, rates, key_rot, value_low)
    shared, shifted = share_states(exports, place, tree)
    gate_raw = mm(first_wide, gate_full)
    gated, normal, inverse, states = retain(
        meta, rates, query_rot, key_rot, value_low, gate_raw, shared, shifted, group_gain, group_bias
    )

    attended = reduce_row([gated], [out_full], row_ref)
    middle = tokens.astype(F32) + attended
    middle_wide = gather_row(middle.astype(BF16))
    second_wide, second_average, second_inverse = norm_wide(middle_wide, gains[2], gains[3])
    grad_hidden = mm(fed_wide, down_full).astype(BF16)
    hidden, grad_before, up_bias_grad = feed_up(second_wide, up_full, up_bias, grad_hidden)
    second_back = reduce_row([grad_before], [up_full], row_ref)
    fed_out = reduce_row([hidden], [down_full], row_ref) + down_bias
    layer_out = middle + fed_out
    grad_fed = fed_low.astype(F32)
    down_grad = scatter_col(mm_tn(fed_wide, hidden).astype(BF16))
    up_grad = scatter_col(mm_tn(second_wide, grad_before).astype(BF16))
    down_bias_grad = jnp.sum(grad_fed, axis=0)

    second_normal = (middle - second_average[:, :1]) * second_inverse[:, :1]
    grad_middle_norm, second_gain_grad, second_bias_grad = norm_backward(
        second_back, second_normal, second_inverse[:, :1], second_gain
    )
    grad_middle = grad_fed + grad_middle_norm
    grad_wide = gather_row(grad_middle.astype(BF16))
    grad_gate, grad_retained, group_gain_grad, group_bias_grad, returns, first_state = gate_back(
        meta, rates, grad_wide, out_full, gate_raw, normal, inverse, query_rot, group_gain, group_bias
    )
    out_grad = scatter_col(mm_tn(grad_wide, gated).astype(BF16))
    own = return_states(returns, first_state, place, tree)
    gate_grad = scatter_col(mm_tn(first_wide, grad_gate).astype(BF16))
    grad_query, grad_key, grad_value = retain_back(
        meta, rates, query_rot, key_rot, value_low, grad_retained, states, cosine, sine, own
    )
    first_back = reduce_row(
        [grad_query, grad_key, grad_value, grad_gate],
        [query_full, key_full, value_full, gate_full],
        row_ref,
    )
    value_grad = scatter_col(mm_tn(first_wide, grad_value).astype(BF16))
    query_grad = scatter_col(mm_tn(first_wide, grad_query).astype(BF16))
    key_grad = scatter_col(mm_tn(first_wide, grad_key).astype(BF16))

    first_normal = (tokens.astype(F32) - first_average[:, :1]) * first_inverse[:, :1]
    grad_first, first_gain_grad, first_bias_grad = norm_backward(
        first_back, first_normal, first_inverse[:, :1], first_gain
    )
    tokens_grad = grad_middle + grad_first

    squares = jnp.stack(
        [
            jnp.sum(column * layer_out * layer_out),
            jnp.sum(column * attended * attended),
            jnp.sum(column * fed_out * fed_out),
        ]
    )
    vectors, col_squares = sum_col_vectors(
        (
            group_gain_grad[0],
            group_bias_grad[0],
            second_gain_grad,
            second_bias_grad,
            up_bias_grad[0],
            down_bias_grad,
        ),
        jnp.concatenate([squares, jnp.zeros((125,), F32)]),
    )
    totals = sum_row_small(col_squares[None, :])[0, :3]
    last, _ = sum_col_vectors((first_gain_grad, first_bias_grad))
    valid_count = jnp.sum(segment_lengths).astype(F32) * D
    norm_values = jnp.sqrt(totals / valid_count)
    return (
        layer_out.astype(BF16),
        tokens_grad,
        query_grad,
        key_grad,
        value_grad,
        gate_grad,
        out_grad.T,
        up_grad,
        down_grad.T,
        last[0],
        last[1],
        vectors[0],
        vectors[1],
        vectors[2],
        vectors[3],
        vectors[4],
        vectors[5],
        norm_values,
    )


def solution(mesh):
    matrix, turned, vector = P("col", "row"), P("row", "col"), P("row")
    in_specs = (matrix,) * 6 + (turned, matrix, turned) + (vector,) * 8 + (P(), P())
    split = P(("row", "col"))
    out_specs = (matrix,) * 6 + (turned, matrix, turned) + (split,) * 8 + (P(),)
    return jax.shard_map(body, mesh=mesh, in_specs=in_specs, out_specs=out_specs, check_vma=False)
```

time: 2910 us -> 1040 us (0.36)
  waiting for transfers between devices: 1720 us -> 535 us
  matrix products: 474 us -> 94 us
  other arithmetic: 319 us -> 56 us
  Pallas kernels: 0 us -> 175 us
  local copies, waits for them, and re-layouts: 198 us -> 59.7 us
  blocking collectives: 130 us -> 45.9 us
  starting transfers between devices: 0.97 us -> 54 us
  loops' own time: 34 us -> 0 us
    reduce_scatter x11 -> x8, waiting for transfers between devices: 925 us -> 173 us  [the longest x7 171 us: scatter_col(): lax.psum_scatter(grad, 'col', scatter_dimension=0, tiled=True).astype(F32)]
    all_gather x13 -> x8, waiting for transfers between devices: 791 us -> 127 us  [the longest x7 89.6 us: gather_col(): return lax.all_gather(weight, 'col', axis=0, tiled=True)]
    dot_general x39 -> x10, matrix products: 474 us -> 94 us  [the longest x7 64.1 us: mm_tn(): lax.dot_general(a, b, (((0,), (0,)), ((), ())), preferred_element_type=F32)]
    ppermute x0 -> x47, waiting for transfers between devices: none -> 231 us  [the longest x41 231 us: permute_row(): return lax.ppermute(value, 'row', pairs)]
    pallas_call x0 -> x13, Pallas kernels: none -> 175 us  [the longest x4 68.5 us: partial_blocks(): pl.pallas_call(functools.partial(partial_kernel, count), grid_spec=pltpu....]
    reduce_or x24 -> x0, other arithmetic: 109 us -> none  [coefficients(): return (jnp.where(visible[None, :, :], decayed, 0.0), jnp.any(visible))]
    psum x5 -> x0, blocking collectives: 101 us -> none  [the longest x4 63.5 us: row_sums(): return lax.psum((first_terms, second_terms), 'row')]
    convert_element_type x56 -> x11, other arithmetic: 104 us -> 18.6 us  [the longest x5 9.98 us: scatter_col(): lax.psum_scatter(grad, 'col', scatter_dimension=0, tiled=True).astype(F32)]
  transfers between devices with their start and end apart: 24 -> 63, of which waited for: 21 -> 36; matrix products, arithmetic and copies ran while one was open for 15% -> 17% of each run, Pallas kernels for 0% -> 12%
where the time goes in v1:
time: 1040 us; the launch traced here: 1030 us
  waiting for transfers between devices  535 us (51%)
  Pallas kernels  175 us (17%)
  matrix products  94 us (9%)
  local copies, waits for them, and re-layouts  59.7 us (6%)
  other arithmetic  56 us (5%)
  starting transfers between devices  54 us (5%)
  blocking collectives  45.9 us (4%)
  between operations  15.8 us (2%)
    ppermute x41, waiting for transfers between devices, permute_row(): return lax.ppermute(value, 'row', pairs)  231 us
    reduce_scatter x7, waiting for transfers between devices, scatter_col(): lax.psum_scatter(grad, 'col', scatter_dimension=0, tiled=True).astype(F32)  171 us
    all_gather x7, waiting for transfers between devices, gather_col(): return lax.all_gather(weight, 'col', axis=0, tiled=True)  89.6 us
    pallas_call x4, Pallas kernels, partial_blocks(): pl.pallas_call(functools.partial(partial_kernel, count), grid_spec=pltpu....  68.5 us
    dot_general x7, matrix products, mm_tn(): lax.dot_general(a, b, (((0,), (0,)), ((), ())), preferred_element_type=F32)  64.1 us
    ppermute x41, starting transfers between devices, permute_row(): return lax.ppermute(value, 'row', pairs)  47.3 us
    all_gather x2, blocking collectives, sum_col_vectors(): lax.all_gather(jnp.concatenate(parts), 'col', axis=0)  45.9 us
    all_gather x1, waiting for transfers between devices, share_states(): shared = lax.all_gather(mine, 'col', axis=0)  37.7 us
  transfers between devices with their start and end apart: 63, of which 36 were waited for; matrix products, arithmetic and copies ran while one was open for 17% of the time, Pallas kernels for 12%

profile of v1, /device:TPU:0, one launch (start us, length us, event | category | flops | bytes accessed | tf_op | source)
XLA Modules:
  0.0 1034.8 jit_solution(10483471220807773890)
XLA Ops:
  29.9 15.8 %collective-permute-done = bf16[1280,512]{1,0:T(8,128)(2,1)S(1)} collective-permute-done((bf16[1280,512]{1,0:T(8,128)(2,1)}, bf16[1280,512]{1,0:T(8,128)(2,1)S(1)}, u32[]{:S(2)}, u32[]{:S(2)}) %collective-permute-start) | collective-permute-done | bytes 1310752 | tf_op jit(solution)/shard_map/ppermute | solution.py:621
  52.0 8.9 collective-permute-done.2
  63.6 8.1 layer_norm.2
  71.8 7.8 project_rotated.3.key
  79.6 10.1 all-gather.17.cloned.1.call-done.refs_6_
  89.8 9.8 convolution_convert_fusion.1.value
  99.6 9.3 chunk_states.1
  119.6 7.8 project_rotated.2.query
  128.2 48.6 %all-gather.19.cloned.1.call-done.refs_7_ = bf16[2048,1024]{1,0:T(8,128)(2,1)} async-done(((bf16[256,1024]{1,0:T(8,128)(2,1)}), bf16[2048,1024]{1,0:T(8,128)(2,1)}) %all-gather.19.cloned.1.call-update) | async-done | bytes 4194320 | tf_op jit(solution)/shard_map/all_gather | solution.py:688
  176.8 10.2 fusion.39.gate
  187.0 37.7 %all-gather.27.cloned.1.call-done = bf16[16,256,512]{2,1,0:T(8,128)(2,1)} async-done(((bf16[2,256,512]{2,1,0:T(8,128)(2,1)}), bf16[16,256,512]{2,1,0:T(8,128)(2,1)}) %all-gather.27.cloned.1.call-update) | async-done | bytes 4194320 | tf_op jit(solution)/shard_map/all_gather | solution.py:712
  224.7 17.0 %retention_forward.1 = (bf16[1280,1024]{1,0:T(8,128)(2,1)}, bf16[1280,1024]{1,0:T(8,128)(2,1)}, f32[2,1280,128]{2,1,0:T(8,128)}, bf16[2,5,256,512]{3,2,1,0:T(8,128)(2,1)}) custom-call(s32[22]{0:T(128)} %pad_add_fusion.meta, f32[2]{0:T(128)} %subtract_log_fusion.rates, bf16[1280,512]{1,0:T(8,128)(2,1)} %project_rotated.2.query, ...), custom_call_target="tpu_custom_call" | custom-call | flops 2348810240 | bytes 20971520 | tf_op jit(solution)/shard_map/retention_forward/pallas_call | solution.py:243
  241.8 30.9 %all-gather.21.cloned.1.call-done.refs_1_.weight = bf16[2048,1024]{1,0:T(8,128)(2,1)} async-done(((bf16[256,1024]{1,0:T(8,128)(2,1)}), bf16[2048,1024]{1,0:T(8,128)(2,1)}) %all-gather.21.cloned.1.call-update) | async-done | bytes 4194320 | tf_op jit(solution)/shard_map/all_gather | solution.py:688
  272.6 14.1 %partial_blocks.4 = (bf16[2,640,512]{2,1,0:T(8,128)(2,1)}, bf16[2,640,512]{2,1,0:T(8,128)(2,1)}, bf16[2,640,512]{2,1,0:T(8,128)(2,1)}, f32[2,640,512]{2,1,0:T(8,128)}) custom-call(s32[1]{0:T(128)} %bitcast.row, bf16[1280,1024]{1,0:T(8,128)(2,1)} %get-tuple-element.57.refs_0_, bf16[2048,1024]{1,0:T(8,128)(2,1)} %all-gather.21.cloned.1.call-done.refs_1_.weight), custom_call_target="tpu_custom_call" | custom-call | flops 5368709120 | bytes 24117248 | tf_op jit(solution)/shard_map/partial_blocks/pallas_call | solution.py:599
  289.8 28.1 %collective-permute-done.10 = bf16[2,640,512]{2,1,0:T(8,128)(2,1)S(1)} collective-permute-done((bf16[2,640,512]{2,1,0:T(8,128)(2,1)}, bf16[2,640,512]{2,1,0:T(8,128)(2,1)S(1)}, u32[]{:S(2)}, u32[]{:S(2)}) %collective-permute-start.10) | collective-permute-done | bytes 1310752 | tf_op jit(solution)/shard_map/ppermute | solution.py:621
  326.1 12.6 %collective-permute-done.11 = bf16[640,512]{1,0:T(8,128)(2,1)S(1)} collective-permute-done((bf16[640,512]{1,0:T(8,128)(2,1)S(1)}, bf16[640,512]{1,0:T(8,128)(2,1)S(1)}, u32[]{:S(2)}, u32[]{:S(2)}) %collective-permute-start.11) | collective-permute-done | bytes 655392 | tf_op jit(solution)/shard_map/ppermute | solution.py:621
  345.4 22.9 %collective-permute-done.18 = bf16[1280,512]{1,0:T(8,128)(2,1)S(1)} collective-permute-done((bf16[1280,512]{1,0:T(8,128)(2,1)S(1)}, bf16[1280,512]{1,0:T(8,128)(2,1)S(1)}, u32[]{:S(2)}, u32[]{:S(2)}) %collective-permute-start.18) | collective-permute-done | bytes 1310752 | tf_op jit(solution)/shard_map/ppermute | solution.py:621
  376.2 6.0 collective-permute-done.20
  383.7 24.7 %collective-permute-done.21 = bf16[640,512]{1,0:T(8,128)(2,1)S(1)} collective-permute-done((bf16[640,512]{1,0:T(8,128)(2,1)S(1)}, bf16[640,512]{1,0:T(8,128)(2,1)S(1)}, u32[]{:S(2)}, u32[]{:S(2)}) %collective-permute-start.21) | collective-permute-done | bytes 655392 | tf_op jit(solution)/shard_map/ppermute | solution.py:621
  411.8 9.9 convolution_convert_fusion.grad_hidden
  428.3 9.1 collective-permute-done.17
  438.3 8.1 layer_norm.3
  446.5 13.2 %feed_up.1 = (bf16[1280,1024]{1,0:T(8,128)(2,1)}, bf16[1280,1024]{1,0:T(8,128)(2,1)}, f32[1,1024]{1,0:T(1,128)}) custom-call(bf16[1280,2048]{1,0:T(8,128)(2,1)} %get-tuple-element.62.values, bf16[2048,1024]{1,0:T(8,128)(2,1)} %all-gather.23.cloned.1.call-done.weight.refs_1_, f32[1,1024]{1,0:T(1,128)} %bitcast.138, ...), custom_call_target="tpu_custom_call" | custom-call | flops 5368709120 | bytes 19922944 | tf_op jit(solution)/shard_map/feed_up/pallas_call | solution.py:531
  459.7 13.9 %partial_blocks.6 = (bf16[2,640,512]{2,1,0:T(8,128)(2,1)}, bf16[2,640,512]{2,1,0:T(8,128)(2,1)}, bf16[2,640,512]{2,1,0:T(8,128)(2,1)}, f32[2,640,512]{2,1,0:T(8,128)}) custom-call(s32[1]{0:T(128)} %bitcast.row, bf16[1280,1024]{1,0:T(8,128)(2,1)} %get-tuple-element.69.refs_0_, bf16[2048,1024]{1,0:T(8,128)(2,1)} %all-gather.23.cloned.1.call-done.weight.refs_1_), custom_call_target="tpu_custom_call" | custom-call | flops 5368709120 | bytes 24117248 | tf_op jit(solution)/shard_map/partial_blocks/pallas_call | solution.py:599
  475.7 13.8 %partial_blocks.5 = (bf16[2,640,512]{2,1,0:T(8,128)(2,1)}, bf16[2,640,512]{2,1,0:T(8,128)(2,1)}, bf16[2,640,512]{2,1,0:T(8,128)(2,1)}, f32[2,640,512]{2,1,0:T(8,128)}) custom-call(s32[1]{0:T(128)} %bitcast.row, bf16[1280,1024]{1,0:T(8,128)(2,1)} %get-tuple-element.63.refs_0_, bf16[2048,1024]{1,0:T(8,128)(2,1)} %all-gather.25.cloned.1.call-done.refs_1_), custom_call_target="tpu_custom_call" | custom-call | flops 5368709120 | bytes 24117248 | tf_op jit(solution)/shard_map/partial_blocks/pallas_call | solution.py:599
  491.5 14.1 %collective-permute-done.26 = bf16[2,640,512]{2,1,0:T(8,128)(2,1)} collective-permute-done((bf16[2,640,512]{2,1,0:T(8,128)(2,1)}, bf16[2,640,512]{2,1,0:T(8,128)(2,1)}, u32[]{:S(2)}, u32[]{:S(2)}) %collective-permute-start.26) | collective-permute-done | bytes 1310752 | tf_op jit(solution)/shard_map/ppermute | solution.py:621
  511.3 22.3 %collective-permute-done.22 = bf16[2,640,512]{2,1,0:T(8,128)(2,1)S(1)} collective-permute-done((bf16[2,640,512]{2,1,0:T(8,128)(2,1)}, bf16[2,640,512]{2,1,0:T(8,128)(2,1)S(1)}, u32[]{:S(2)}, u32[]{:S(2)}) %collective-permute-start.22) | collective-permute-done | bytes 1310752 | tf_op jit(solution)/shard_map/ppermute | solution.py:621
  538.1 10.3 collective-permute-done.27
  550.6 7.6 collective-permute-done.23
  559.9 5.2 fusion.11
  581.1 25.5 %collective-permute-done.32 = bf16[1280,512]{1,0:T(8,128)(2,1)S(1)} collective-permute-done((bf16[1280,512]{1,0:T(8,128)(2,1)S(1)}, bf16[1280,512]{1,0:T(8,128)(2,1)S(1)}, u32[]{:S(2)}, u32[]{:S(2)}) %collective-permute-start.32) | collective-permute-done | bytes 1310752 | tf_op jit(solution)/shard_map/ppermute | solution.py:621
  612.5 5.1 collective-permute-done.34
  620.5 21.2 %gate_backward.1 = (bf16[1280,1024]{1,0:T(8,128)(2,1)}, bf16[1280,1024]{1,0:T(8,128)(2,1)}, f32[1,1024]{1,0:T(1,128)}, f32[1,1024]{1,0:T(1,128)}, bf16[8,2,256,5...) custom-call(s32[22]{0:T(128)} %pad_add_fusion.meta, f32[2]{0:T(128)} %subtract_log_fusion.rates, ...), custom_call_target="tpu_custom_call" | custom-call | flops 6039797760 | bytes 31457280 | tf_op jit(solution)/shard_map/gate_backward/pallas_call | solution.py:333
  643.5 9.7 convolution_convert_fusion.2
  655.0 9.8 convolution_convert_fusion.3
  666.6 9.8 convolution_convert_fusion.4
  678.2 10.0 convolution_convert_fusion.5
  696.6 13.5 %retention_backward.1 = (bf16[1280,512]{1,0:T(8,128)(2,1)}, bf16[1280,512]{1,0:T(8,128)(2,1)}, bf16[1280,1024]{1,0:T(8,128)(2,1)}) custom-call(s32[22]{0:T(128)} %pad_add_fusion.meta, f32[2]{0:T(128)} %subtract_log_fusion.rates, bf16[1280,512]{1,0:T(8,128)(2,1)} %project_rotated.2.query, bf16[1280,512]{1,0:T(8,128)(2,1)} %project_rotated.3.key, ...), custom_call_target="tpu_custom_call" | custom-call | flops 5033164800 | bytes 15728640 | tf_op jit(solution)/shard_map/retention_backward/pallas_call | solution.py:423
  710.1 7.1 convolution_convert_fusion.7
  717.3 7.4 convolution_convert_fusion.8
  724.8 10.1 convolution_convert_fusion.6
  735.0 26.6 %partial_blocks.7 = (bf16[2,640,512]{2,1,0:T(8,128)(2,1)}, bf16[2,640,512]{2,1,0:T(8,128)(2,1)}, bf16[2,640,512]{2,1,0:T(8,128)(2,1)}, f32[2,640,512]{2,1,0:T(8,128)}) custom-call(s32[1]{0:T(128)} %bitcast.row, bf16[1280,512]{1,0:T(8,128)(2,1)} %get-tuple-element.82.refs_0_, bf16[1280,512]{1,0:T(8,128)(2,1)} %get-tuple-element.83.refs_1_, ...), custom_call_target="tpu_custom_call" | custom-call | flops 16106127360 | bytes 51380224 | tf_op jit(solution)/shard_map/partial_blocks/pallas_call | solution.py:599
  768.0 31.8 %all-gather.3 = f32[8,1,4736]{2,1,0:T(1,128)S(1)} all-gather(f32[1,1,4736]{2,1,0:T(1,128)S(1)} %reshape.153), channel_id=4, replica_groups=mesh['row'=4,'col'=8] {'col'}, dimensions={0}, use_global_device_ids=true | all-gather | bytes 170496 | tf_op jit(solution)/shard_map/all_gather | solution.py:737
  817.6 33.9 %reduce-scatter.19.cloned.1.call-done = bf16[256,1024]{1,0:T(8,128)(2,1)} async-done(((bf16[2048,1024]{1,0:T(8,128)(2,1)}), bf16[256,1024]{1,0:T(8,128)(2,1)}) %reduce-scatter.19.cloned.1.call-update) | async-done | bytes 524304 | tf_op jit(solution)/shard_map/reduce_scatter | solution.py:692
  854.0 48.0 %reduce-scatter.17.cloned.1.call-done = bf16[256,1024]{1,0:T(8,128)(2,1)} async-done(((bf16[2048,1024]{1,0:T(8,128)(2,1)}), bf16[256,1024]{1,0:T(8,128)(2,1)}) %reduce-scatter.17.cloned.1.call-update) | async-done | bytes 524304 | tf_op jit(solution)/shard_map/reduce_scatter | solution.py:692
  911.5 14.1 %all-gather.1 = f32[8192]{0:T(1024)S(1)} all-gather(f32[1024]{0:T(1024)S(1)} %pad_maximum_fusion.8), channel_id=3, replica_groups=mesh['row'=4,'col'=8] {'col'}, dimensions={0}, use_global_device_ids=true | all-gather | bytes 36864 | tf_op jit(solution)/shard_map/all_gather | solution.py:737
  939.9 34.8 %reduce-scatter.11.cloned.1.call-done = bf16[256,512]{1,0:T(8,128)(2,1)} async-done(((bf16[2048,512]{1,0:T(8,128)(2,1)}), bf16[256,512]{1,0:T(8,128)(2,1)}) %reduce-scatter.11.cloned.1.call-update) | async-done | bytes 262160 | tf_op jit(solution)/shard_map/reduce_scatter | solution.py:692
  976.5 49.1 %reduce-scatter.15.cloned.1.call-done = bf16[256,1024]{1,0:T(8,128)(2,1)} async-done(((bf16[2048,1024]{1,0:T(8,128)(2,1)}), bf16[256,1024]{1,0:T(8,128)(2,1)}) %reduce-scatter.15.cloned.1.call-update) | async-done | bytes 524304 | tf_op jit(solution)/shard_map/reduce_scatter | solution.py:692
  (313 shorter events, 193.0 us)
Async XLA Ops:
  7.2 64.6 %all-gather.15.cloned.1.call-start = ((), (), s32[]{:S(2)}) async-start(), calls=%async_computation.9 | async-start | bytes 2359296 | tf_op jit(solution)/shard_map/all_gather | solution.py:688
  7.9 81.8 %all-gather.17.cloned.1.call-start = ((), (), s32[]{:S(2)}) async-start(), calls=%async_computation.10 | async-start | bytes 4718592 | tf_op jit(solution)/shard_map/all_gather | solution.py:688
  8.7 110.9 %all-gather.13.cloned.1.call-start = ((), (), s32[]{:S(2)}) async-start(), calls=%async_computation.8 | async-start | bytes 2359296 | tf_op jit(solution)/shard_map/all_gather | solution.py:688
  9.4 167.4 %all-gather.19.cloned.1.call-start = ((), (), s32[]{:S(2)}) async-start(), calls=%async_computation.11 | async-start | bytes 4718592 | tf_op jit(solution)/shard_map/all_gather | solution.py:688
  10.0 214.7 %all-gather.27.cloned.1.call-start = ((), (), s32[]{:S(2)}) async-start(), calls=%async_computation.23 | async-start | bytes 4718592 | tf_op jit(solution)/shard_map/all_gather | solution.py:712
  10.8 19.0 %collective-permute-start.5 = (f32[4,512]{1,0:T(4,128)S(1)}, f32[4,512]{1,0:T(4,128)S(1)}, u32[]{:S(2)}, u32[]{:S(2)}) collective-permute-start(f32[4,512]{1,0:T(4,128)S(1)} %get-tuple-element.240), channel_id=1, source_target_pairs={{0,16},{16,0},{8,24},{24,8},{1,17},{17,1},{9,25},{25,9},{2,18},{18... | collective-permute-start | bytes 24584 | tf_op jit(solution)/shard_map/ppermute | solution.py:621
  13.8 16.0 %collective-permute-start.6 = (f32[4,512]{1,0:T(4,128)S(1)}, f32[4,512]{1,0:T(4,128)S(1)}, u32[]{:S(2)}, u32[]{:S(2)}) collective-permute-start(f32[4,512]{1,0:T(4,128)S(1)} %get-tuple-element.240), channel_id=1, source_target_pairs={{0,24},{24,0},{8,16},{16,8},{1,25},{25,1},{9,17},{17,9},{2,26},{26... | collective-permute-start | bytes 24584 | tf_op jit(solution)/shard_map/ppermute | solution.py:621
  15.4 30.3 %collective-permute-start = (bf16[1280,512]{1,0:T(8,128)(2,1)}, bf16[1280,512]{1,0:T(8,128)(2,1)S(1)}, u32[]{:S(2)}, u32[]{:S(2)}) collective-permute-start(bf16[1280,512]{1,0:T(8,128)(2,1)} %param.19), channel_id=1, source_target_pairs={{0,8},{8,0},{16,24},{24,16},{1,9},{9,1},{17,25},{25,17},{2,10},{10... | collective-permute-start | bytes 3932168 | tf_op jit(solution)/shard_map/ppermute | solution.py:621
  17.3 30.8 %collective-permute-start.1 = (bf16[1280,512]{1,0:T(8,128)(2,1)}, bf16[1280,512]{1,0:T(8,128)(2,1)S(1)}, u32[]{:S(2)}, u32[]{:S(2)}) collective-permute-start(bf16[1280,512]{1,0:T(8,128)(2,1)} %param.19), channel_id=1, source_target_pairs={{0,16},{16,0},{8,24},{24,8},{1,17},{17,1},{9,25},{25,9},{2,18},{18... | collective-permute-start | bytes 3932168 | tf_op jit(solution)/shard_map/ppermute | solution.py:621
  45.7 15.3 %collective-permute-start.2 = (bf16[640,512]{1,0:T(8,128)(2,1)S(1)}, bf16[640,512]{1,0:T(8,128)(2,1)S(1)}, u32[]{:S(2)}, u32[]{:S(2)}) collective-permute-start(bf16[640,512]{1,0:T(8,128)(2,1)S(1)} %slice.237), channel_id=1, source_target_pairs={{0,16},{16,0},{8,24},{24,8},{1,17},{17,1},{9,25},{25,9},{2,18},{18... | collective-permute-start | bytes 1966088 | tf_op jit(solution)/shard_map/ppermute | solution.py:621
  48.1 14.6 %collective-permute-start.3 = (bf16[640,512]{1,0:T(8,128)(2,1)S(1)}, bf16[640,512]{1,0:T(8,128)(2,1)S(1)}, u32[]{:S(2)}, u32[]{:S(2)}) collective-permute-start(bf16[640,512]{1,0:T(8,128)(2,1)S(1)} %slice.238), channel_id=1, source_target_pairs={{0,8},{8,0},{16,24},{24,16},{1,9},{9,1},{17,25},{25,17},{2,10},{10... | collective-permute-start | bytes 1966088 | tf_op jit(solution)/shard_map/ppermute | solution.py:621
  116.6 156.1 %all-gather.21.cloned.1.call-start = ((), (), s32[]{:S(2)}) async-start(), calls=%async_computation.12 | async-start | bytes 4718592 | tf_op jit(solution)/shard_map/all_gather | solution.py:688
  117.7 294.2 %all-gather.25.cloned.1.call-start = ((), (), s32[]{:S(2)}) async-start(), calls=%async_computation.14 | async-start | bytes 4718592 | tf_op jit(solution)/shard_map/all_gather | solution.py:688
  118.7 327.7 %all-gather.23.cloned.1.call-start = ((), (), s32[]{:S(2)}) async-start(), calls=%async_computation.13 | async-start | bytes 4718592 | tf_op jit(solution)/shard_map/all_gather | solution.py:688
  119.5 572.8 %reduce-scatter.9.cloned.1.call-start = ((), (), s32[]{:S(2)}) async-start(), calls=%async_computation.15 | async-start | bytes 4718592 | tf_op jit(solution)/shard_map/reduce_scatter | solution.py:724
  127.3 59.7 %collective-permute-start.9 = (bf16[2,256,512]{2,1,0:T(8,128)(2,1)S(1)}, bf16[2,256,512]{2,1,0:T(8,128)(2,1)S(1)}, u32[]{:S(2)}, u32[]{:S(2)}) collective-permute-start(bf16[2,256,512]{2,1,0:T(8,128)(2,1)S(1)} %get-tuple-element.209), channel_id=1, source_target_pairs={{4,5},{6,7},{12,13},{14,15},{20,21},{22,23},{28,29},{30,31}} | collective-permute-start | bytes 1572872 | tf_op jit(solution)/shard_map/ppermute | solution.py:700
  286.7 31.2 %collective-permute-start.10 = (bf16[2,640,512]{2,1,0:T(8,128)(2,1)}, bf16[2,640,512]{2,1,0:T(8,128)(2,1)S(1)}, u32[]{:S(2)}, u32[]{:S(2)}) collective-permute-start(bf16[2,640,512]{2,1,0:T(8,128)(2,1)} %get-tuple-element.59), channel_id=1, source_target_pairs={{0,8},{8,0},{16,24},{24,16},{1,9},{9,1},{17,25},{25,17},{2,10},{10... | collective-permute-start | bytes 3932168 | tf_op jit(solution)/shard_map/ppermute | solution.py:621
  288.4 30.8 %collective-permute-start.12 = (bf16[2,640,512]{2,1,0:T(8,128)(2,1)}, bf16[2,640,512]{2,1,0:T(8,128)(2,1)S(1)}, u32[]{:S(2)}, u32[]{:S(2)}) collective-permute-start(bf16[2,640,512]{2,1,0:T(8,128)(2,1)} %get-tuple-element.61), channel_id=1, source_target_pairs={{0,16},{16,0},{8,24},{24,8},{1,17},{17,1},{9,25},{25,9},{2,18},{18... | collective-permute-start | bytes 3932168 | tf_op jit(solution)/shard_map/ppermute | solution.py:621
  321.0 17.7 %collective-permute-start.11 = (bf16[640,512]{1,0:T(8,128)(2,1)S(1)}, bf16[640,512]{1,0:T(8,128)(2,1)S(1)}, u32[]{:S(2)}, u32[]{:S(2)}) collective-permute-start(bf16[640,512]{1,0:T(8,128)(2,1)S(1)} %get-tuple-element.218), channel_id=1, source_target_pairs={{0,16},{16,0},{8,24},{24,8},{1,17},{17,1},{9,25},{25,9},{2,18},{18... | collective-permute-start | bytes 1966088 | tf_op jit(solution)/shard_map/ppermute | solution.py:621
  322.6 17.7 %collective-permute-start.13 = (bf16[640,512]{1,0:T(8,128)(2,1)S(1)}, bf16[640,512]{1,0:T(8,128)(2,1)S(1)}, u32[]{:S(2)}, u32[]{:S(2)}) collective-permute-start(bf16[640,512]{1,0:T(8,128)(2,1)S(1)} %get-tuple-element.219), channel_id=1, source_target_pairs={{0,8},{8,0},{16,24},{24,16},{1,9},{9,1},{17,25},{25,17},{2,10},{10... | collective-permute-start | bytes 1966088 | tf_op jit(solution)/shard_map/ppermute | solution.py:621
  324.1 44.2 %collective-permute-start.18 = (bf16[1280,512]{1,0:T(8,128)(2,1)S(1)}, bf16[1280,512]{1,0:T(8,128)(2,1)S(1)}, u32[]{:S(2)}, u32[]{:S(2)}) collective-permute-start(bf16[1280,512]{1,0:T(8,128)(2,1)S(1)} %get-tuple-element.185), channel_id=1, source_target_pairs={{0,8},{8,0},{16,24},{24,16},{1,9},{9,1},{17,25},{25,17},{2,10},{10... | collective-permute-start | bytes 3932168 | tf_op jit(solution)/shard_map/ppermute | solution.py:621
  325.6 47.7 %collective-permute-start.19 = (bf16[1280,512]{1,0:T(8,128)(2,1)S(1)}, bf16[1280,512]{1,0:T(8,128)(2,1)S(1)}, u32[]{:S(2)}, u32[]{:S(2)}) collective-permute-start(bf16[1280,512]{1,0:T(8,128)(2,1)S(1)} %get-tuple-element.185), channel_id=1, source_target_pairs={{0,16},{16,0},{8,24},{24,8},{1,17},{17,1},{9,25},{25,9},{2,18},{18... | collective-permute-start | bytes 3932168 | tf_op jit(solution)/shard_map/ppermute | solution.py:621
  344.8 64.4 %collective-permute-start.14 = (bf16[1280,512]{1,0:T(8,128)(2,1)}, bf16[1280,512]{1,0:T(8,128)(2,1)S(1)}, u32[]{:S(2)}, u32[]{:S(2)}) collective-permute-start(bf16[1280,512]{1,0:T(8,128)(2,1)} %get-tuple-element.198), channel_id=1, source_target_pairs={{0,8},{8,0},{16,24},{24,16},{1,9},{9,1},{17,25},{25,17},{2,10},{10... | collective-permute-start | bytes 3932168 | tf_op jit(solution)/shard_map/ppermute | solution.py:621
  373.3 35.1 %collective-permute-start.21 = (bf16[640,512]{1,0:T(8,128)(2,1)S(1)}, bf16[640,512]{1,0:T(8,128)(2,1)S(1)}, u32[]{:S(2)}, u32[]{:S(2)}) collective-permute-start(bf16[640,512]{1,0:T(8,128)(2,1)S(1)} %slice.253), channel_id=1, source_target_pairs={{0,8},{8,0},{16,24},{24,16},{1,9},{9,1},{17,25},{25,17},{2,10},{10... | collective-permute-start | bytes 1966088 | tf_op jit(solution)/shard_map/ppermute | solution.py:621
  383.1 38.6 %collective-permute-start.15 = (bf16[1280,512]{1,0:T(8,128)(2,1)}, bf16[1280,512]{1,0:T(8,128)(2,1)}, u32[]{:S(2)}, u32[]{:S(2)}) collective-permute-start(bf16[1280,512]{1,0:T(8,128)(2,1)} %get-tuple-element.198), channel_id=1, source_target_pairs={{0,16},{16,0},{8,24},{24,8},{1,17},{17,1},{9,25},{25,9},{2,18},{18... | collective-permute-start | bytes 3932168 | tf_op jit(solution)/shard_map/ppermute | solution.py:621
  411.3 16.1 %collective-permute-start.16 = (bf16[640,512]{1,0:T(8,128)(2,1)}, bf16[640,512]{1,0:T(8,128)(2,1)S(1)}, u32[]{:S(2)}, u32[]{:S(2)}) collective-permute-start(bf16[640,512]{1,0:T(8,128)(2,1)} %slice.248), channel_id=1, source_target_pairs={{0,16},{16,0},{8,24},{24,8},{1,17},{17,1},{9,25},{25,9},{2,18},{18... | collective-permute-start | bytes 1966088 | tf_op jit(solution)/shard_map/ppermute | solution.py:621
  473.6 32.0 %collective-permute-start.26 = (bf16[2,640,512]{2,1,0:T(8,128)(2,1)}, bf16[2,640,512]{2,1,0:T(8,128)(2,1)}, u32[]{:S(2)}, u32[]{:S(2)}) collective-permute-start(bf16[2,640,512]{2,1,0:T(8,128)(2,1)} %get-tuple-element.71), channel_id=1, source_target_pairs={{0,8},{8,0},{16,24},{24,16},{1,9},{9,1},{17,25},{25,17},{2,10},{10... | collective-permute-start | bytes 3932168 | tf_op jit(solution)/shard_map/ppermute | solution.py:621
  474.4 32.0 %collective-permute-start.28 = (bf16[2,640,512]{2,1,0:T(8,128)(2,1)}, bf16[2,640,512]{2,1,0:T(8,128)(2,1)}, u32[]{:S(2)}, u32[]{:S(2)}) collective-permute-start(bf16[2,640,512]{2,1,0:T(8,128)(2,1)} %get-tuple-element.73), channel_id=1, source_target_pairs={{0,16},{16,0},{8,24},{24,8},{1,17},{17,1},{9,25},{25,9},{2,18},{18... | collective-permute-start | bytes 3932168 | tf_op jit(solution)/shard_map/ppermute | solution.py:621
  489.5 44.1 %collective-permute-start.22 = (bf16[2,640,512]{2,1,0:T(8,128)(2,1)}, bf16[2,640,512]{2,1,0:T(8,128)(2,1)S(1)}, u32[]{:S(2)}, u32[]{:S(2)}) collective-permute-start(bf16[2,640,512]{2,1,0:T(8,128)(2,1)} %get-tuple-element.65), channel_id=1, source_target_pairs={{0,8},{8,0},{16,24},{24,16},{1,9},{9,1},{17,25},{25,17},{2,10},{10... | collective-permute-start | bytes 3932168 | tf_op jit(solution)/shard_map/ppermute | solution.py:621
  491.0 43.4 %collective-permute-start.24 = (bf16[2,640,512]{2,1,0:T(8,128)(2,1)}, bf16[2,640,512]{2,1,0:T(8,128)(2,1)S(1)}, u32[]{:S(2)}, u32[]{:S(2)}) collective-permute-start(bf16[2,640,512]{2,1,0:T(8,128)(2,1)} %get-tuple-element.67), channel_id=1, source_target_pairs={{0,16},{16,0},{8,24},{24,8},{1,17},{17,1},{9,25},{25,9},{2,18},{18... | collective-permute-start | bytes 3932168 | tf_op jit(solution)/shard_map/ppermute | solution.py:621
  508.5 40.0 %collective-permute-start.27 = (bf16[640,512]{1,0:T(8,128)(2,1)S(1)}, bf16[640,512]{1,0:T(8,128)(2,1)S(1)}, u32[]{:S(2)}, u32[]{:S(2)}) collective-permute-start(bf16[640,512]{1,0:T(8,128)(2,1)S(1)} %get-tuple-element.214), channel_id=1, source_target_pairs={{0,16},{16,0},{8,24},{24,8},{1,17},{17,1},{9,25},{25,9},{2,18},{18... | collective-permute-start | bytes 1966088 | tf_op jit(solution)/shard_map/ppermute | solution.py:621
  509.9 38.6 %collective-permute-start.29 = (bf16[640,512]{1,0:T(8,128)(2,1)S(1)}, bf16[640,512]{1,0:T(8,128)(2,1)S(1)}, u32[]{:S(2)}, u32[]{:S(2)}) collective-permute-start(bf16[640,512]{1,0:T(8,128)(2,1)S(1)} %get-tuple-element.215), channel_id=1, source_target_pairs={{0,8},{8,0},{16,24},{24,16},{1,9},{9,1},{17,25},{25,17},{2,10},{10... | collective-permute-start | bytes 1966088 | tf_op jit(solution)/shard_map/ppermute | solution.py:621
  534.8 23.4 %collective-permute-start.23 = (bf16[640,512]{1,0:T(8,128)(2,1)S(1)}, bf16[640,512]{1,0:T(8,128)(2,1)S(1)}, u32[]{:S(2)}, u32[]{:S(2)}) collective-permute-start(bf16[640,512]{1,0:T(8,128)(2,1)S(1)} %get-tuple-element.216), channel_id=1, source_target_pairs={{0,16},{16,0},{8,24},{24,8},{1,17},{17,1},{9,25},{25,9},{2,18},{18... | collective-permute-start | bytes 1966088 | tf_op jit(solution)/shard_map/ppermute | solution.py:621
  536.2 22.0 %collective-permute-start.25 = (bf16[640,512]{1,0:T(8,128)(2,1)S(1)}, bf16[640,512]{1,0:T(8,128)(2,1)S(1)}, u32[]{:S(2)}, u32[]{:S(2)}) collective-permute-start(bf16[640,512]{1,0:T(8,128)(2,1)S(1)} %get-tuple-element.217), channel_id=1, source_target_pairs={{0,8},{8,0},{16,24},{24,16},{1,9},{9,1},{17,25},{25,17},{2,10},{10... | collective-permute-start | bytes 1966088 | tf_op jit(solution)/shard_map/ppermute | solution.py:621
  578.6 28.1 %collective-permute-start.32 = (bf16[1280,512]{1,0:T(8,128)(2,1)S(1)}, bf16[1280,512]{1,0:T(8,128)(2,1)S(1)}, u32[]{:S(2)}, u32[]{:S(2)}) collective-permute-start(bf16[1280,512]{1,0:T(8,128)(2,1)S(1)} %get-tuple-element.195), channel_id=1, source_target_pairs={{0,8},{8,0},{16,24},{24,16},{1,9},{9,1},{17,25},{25,17},{2,10},{10... | collective-permute-start | bytes 3932168 | tf_op jit(solution)/shard_map/ppermute | solution.py:621
  579.7 29.2 %collective-permute-start.33 = (bf16[1280,512]{1,0:T(8,128)(2,1)S(1)}, bf16[1280,512]{1,0:T(8,128)(2,1)S(1)}, u32[]{:S(2)}, u32[]{:S(2)}) collective-permute-start(bf16[1280,512]{1,0:T(8,128)(2,1)S(1)} %get-tuple-element.195), channel_id=1, source_target_pairs={{0,16},{16,0},{8,24},{24,8},{1,17},{17,1},{9,25},{25,9},{2,18},{18... | collective-permute-start | bytes 3932168 | tf_op jit(solution)/shard_map/ppermute | solution.py:621
  641.8 171.2 %reduce-scatter.23.cloned.1.call-start = ((), (), s32[]{:S(2)}) async-start(), calls=%async_computation.22 | async-start | bytes 4718592 | tf_op jit(solution)/shard_map/reduce_scatter | solution.py:692
  653.3 162.2 %reduce-scatter.21.cloned.1.call-start = ((), (), s32[]{:S(2)}) async-start(), calls=%async_computation.21 | async-start | bytes 4718592 | tf_op jit(solution)/shard_map/reduce_scatter | solution.py:692
  664.8 186.7 %reduce-scatter.19.cloned.1.call-start = ((), (), s32[]{:S(2)}) async-start(), calls=%async_computation.20 | async-start | bytes 4718592 | tf_op jit(solution)/shard_map/reduce_scatter | solution.py:692
  676.4 225.5 %reduce-scatter.17.cloned.1.call-start = ((), (), s32[]{:S(2)}) async-start(), calls=%async_computation.19 | async-start | bytes 4718592 | tf_op jit(solution)/shard_map/reduce_scatter | solution.py:692
  688.2 249.8 %reduce-scatter.13.cloned.1.call-start = ((), (), s32[]{:S(2)}) async-start(), calls=%async_computation.17 | async-start | bytes 2359296 | tf_op jit(solution)/shard_map/reduce_scatter | solution.py:692
  717.2 257.5 %reduce-scatter.11.cloned.1.call-start = ((), (), s32[]{:S(2)}) async-start(), calls=%async_computation.16 | async-start | bytes 2359296 | tf_op jit(solution)/shard_map/reduce_scatter | solution.py:692
  724.7 300.9 %reduce-scatter.15.cloned.1.call-start = ((), (), s32[]{:S(2)}) async-start(), calls=%async_computation.18 | async-start | bytes 4718592 | tf_op jit(solution)/shard_map/reduce_scatter | solution.py:692
  761.6 46.0 %collective-permute-start.39 = (bf16[2,640,512]{2,1,0:T(8,128)(2,1)}, bf16[2,640,512]{2,1,0:T(8,128)(2,1)S(1)}, u32[]{:S(2)}, u32[]{:S(2)}) collective-permute-start(bf16[2,640,512]{2,1,0:T(8,128)(2,1)} %get-tuple-element.87), channel_id=1, source_target_pairs={{0,8},{8,0},{16,24},{24,16},{1,9},{9,1},{17,25},{25,17},{2,10},{10... | collective-permute-start | bytes 3932168 | tf_op jit(solution)/shard_map/ppermute | solution.py:621
  763.2 44.4 %collective-permute-start.41 = (bf16[2,640,512]{2,1,0:T(8,128)(2,1)}, bf16[2,640,512]{2,1,0:T(8,128)(2,1)S(1)}, u32[]{:S(2)}, u32[]{:S(2)}) collective-permute-start(bf16[2,640,512]{2,1,0:T(8,128)(2,1)} %get-tuple-element.89), channel_id=1, source_target_pairs={{0,16},{16,0},{8,24},{24,8},{1,17},{17,1},{9,25},{25,9},{2,18},{18... | collective-permute-start | bytes 3932168 | tf_op jit(solution)/shard_map/ppermute | solution.py:621
  811.3 92.8 %collective-permute-start.40 = (bf16[640,512]{1,0:T(8,128)(2,1)}, bf16[640,512]{1,0:T(8,128)(2,1)S(1)}, u32[]{:S(2)}, u32[]{:S(2)}) collective-permute-start(bf16[640,512]{1,0:T(8,128)(2,1)} %get-tuple-element.212), channel_id=1, source_target_pairs={{0,16},{16,0},{8,24},{24,8},{1,17},{17,1},{9,25},{25,9},{2,18},{18... | collective-permute-start | bytes 1966088 | tf_op jit(solution)/shard_map/ppermute | solution.py:621
  811.9 92.2 %collective-permute-start.42 = (bf16[640,512]{1,0:T(8,128)(2,1)}, bf16[640,512]{1,0:T(8,128)(2,1)}, u32[]{:S(2)}, u32[]{:S(2)}) collective-permute-start(bf16[640,512]{1,0:T(8,128)(2,1)} %get-tuple-element.213), channel_id=1, source_target_pairs={{0,8},{8,0},{16,24},{24,16},{1,9},{9,1},{17,25},{25,17},{2,10},{10... | collective-permute-start | bytes 1966088 | tf_op jit(solution)/shard_map/ppermute | solution.py:621
  909.9 15.7 %collective-permute-start.43 = (f32[2,1280]{1,0:T(2,128)S(1)}, f32[2,1280]{1,0:T(2,128)S(1)}, u32[]{:S(2)}, u32[]{:S(2)}) collective-permute-start(f32[2,1280]{1,0:T(2,128)S(1)} %pad_maximum_fusion.6), channel_id=1, source_target_pairs={{0,8},{8,0},{16,24},{24,16},{1,9},{9,1},{17,25},{25,17},{2,10},{10... | collective-permute-start | bytes 30728 | tf_op jit(solution)/shard_map/ppermute | solution.py:621
  (60 other events, 735.8 us)
Sparse Core Ops, SparseCore 0:
  9.6 31.7 all-gather.14
  43.1 46.6 all-gather.16
  91.4 27.8 all-gather.12
  120.7 56.0 all-gather.18
  178.8 45.8 all-gather.26
  226.7 45.8 all-gather.20
  274.2 45.8 all-gather.24
  321.7 45.8 all-gather.22
  641.9 50.3 reduce-scatter.8
  694.4 54.8 reduce-scatter.22
  751.6 49.3 reduce-scatter.20
  803.2 48.2 reduce-scatter.18
  853.8 48.1 reduce-scatter.16
  904.1 33.9 reduce-scatter.12
  940.2 34.4 reduce-scatter.10
  976.9 48.7 reduce-scatter.14

commit v2 on v1

--- a/solution.py
+++ b/solution.py
@@ -77,10 +77,6 @@
     return jnp.minimum(meta[0], jnp.minimum(rows * (place + 1), TRUNK))
 
 
-def slot_branch(slot):
-    return (slot - 4 + 2) % 4
-
-
 def power(rate, exponent, width):
     return jnp.exp(jnp.full((1, width), exponent.astype(F32), F32) * rate)
 
@@ -124,8 +120,10 @@
 def import_terms(meta, chunk, place, slot, rows):
     if slot < 4:
         sees = jnp.logical_not(chunk.in_trunk) | (place > slot)
+        if slot < 3:
+            sees = sees & (place < 4)
         return sees, jnp.maximum(chunk.start - trunk_reference(meta, jnp.int32(slot), rows), 0)
-    sees = chunk.is_leaf & (chunk.parent == slot_branch(slot))
+    sees = chunk.is_leaf & (chunk.parent == slot - 4)
     return sees, chunk.first
 
 
@@ -184,7 +182,7 @@
 
 def retain_kernel(
     rows, chunks, meta, rates, query, key, value, gate, shared, shifted, gain, bias,
-    gated_out, normal_out, inverse_out, state_out, running,
+    gated_out, normal_out, inverse_out, state_out, running, total,
 ):
     local = pl.program_id(1)
     rate = rates[pl.program_id(0)]
@@ -201,14 +199,16 @@
             running[...] = shifted[0].astype(F32) * power(rate, exponent, HV)
 
     incoming = running[...]
-    state_ref = state_out.at[0, 0]
-    running_total = incoming
+    total[...] = incoming
     for slot in range(SLOTS):
         on, exponent = import_terms(meta, chunk, place, slot, rows)
-        scale = jnp.where(on, power(rate, exponent, HV), 0.0)
-        running_total = running_total + shared[slot, 0].astype(F32) * scale
-    state = running_total.astype(BF16)
-    state_ref[...] = state
+
+        @pl.when(on)
+        def _():
+            total[...] += shared[slot, 0].astype(F32) * power(rate, exponent, HV)
+
+    state = total[...].astype(BF16)
+    state_out[0, 0] = state
 
     q, k, v = query[...], key[...], value[...]
     scores = (mm_nt(q, k) * decay_matrix(rate, chunk.count)).astype(BF16)
@@ -260,7 +260,7 @@
             jax.ShapeDtypeStruct((heads, rows, 128), F32),
             jax.ShapeDtypeStruct((heads, chunks, QK, HV), BF16),
         ],
-        scratch_shapes=[pltpu.VMEM((QK, HV), F32)],
+        scratch_shapes=[pltpu.VMEM((QK, HV), F32), pltpu.VMEM((QK, HV), F32)],
         compiler_params=params(("arbitrary", "arbitrary")),
         name="retention_forward",
         cost_estimate=pl.CostEstimate(
@@ -325,6 +325,8 @@
 
 
 def gate_back(meta, rates, wide, weight, gate, normal, inverse, query, gain, bias):
+    array, width, number = weight
+    first = number * (width // HV)
     rows = query.shape[0]
     heads = query.shape[1] // QK
     chunks = rows // CHUNK
@@ -336,7 +338,7 @@
         in_specs=[
             smem(), smem(),
             pl.BlockSpec((CHUNK, D), lambda h, c: (c, 0)),
-            pl.BlockSpec((D, HV), lambda h, c: (0, h)),
+            pl.BlockSpec((D, HV), lambda h, c: (0, first + h)),
             block, block,
             pl.BlockSpec((1, CHUNK, 128), lambda h, c: (h, c, 0)),
             pl.BlockSpec((CHUNK, QK), lambda h, c: (c, h)),
@@ -363,12 +365,12 @@
             bytes_accessed=rows * heads * 12288,
             transcendentals=rows * heads * HV,
         ),
-    )(meta, rates, wide, weight, gate, normal, inverse, query, gain[None, :], bias[None, :])
+    )(meta, rates, wide, array, gate, normal, inverse, query, gain[None, :], bias[None, :])
 
 
 def retain_back_kernel(
     rows, chunks, meta, rates, query, key, value, grad, state_in, cosine, sine, own0, own1, own2,
-    query_out, key_out, value_out, running,
+    query_out, key_out, value_out, running, total_ref,
 ):
     step = pl.program_id(1)
     local = chunks - 1 - step
@@ -382,11 +384,15 @@
         running[...] = jnp.zeros_like(running)
 
     later = running[...]
-    total = later
+    total_ref[...] = later
     for slot, ref in ((0, own0), (1, own1), (2, own2)):
         on, exponent = export_terms(meta, chunk, local, chunks, place, slot, rows)
-        total = total + ref[0].astype(F32) * jnp.where(on, power(rate, exponent, HV), 0.0)
-    total = total.astype(BF16)
+
+        @pl.when(on)
+        def _():
+            total_ref[...] += ref[0].astype(F32) * power(rate, exponent, HV)
+
+    total = total_ref[...].astype(BF16)
 
     q, k, v, g = query[...], key[...], value[...], grad[...]
     decay = decay_matrix(rate, chunk.count)
@@ -434,7 +440,7 @@
             jax.ShapeDtypeStruct((rows, heads * QK), BF16),
             jax.ShapeDtypeStruct((rows, heads * HV), BF16),
         ],
-        scratch_shapes=[pltpu.VMEM((QK, HV), F32)],
+        scratch_shapes=[pltpu.VMEM((QK, HV), F32), pltpu.VMEM((QK, HV), F32)],
         compiler_params=params(("arbitrary", "arbitrary")),
         name="retention_backward",
         cost_estimate=pl.CostEstimate(
@@ -477,36 +483,168 @@
     )(values, gain[None, :], bias[None, :])
 
 
-def rotate_kernel(heads, values, weight, cosine, sine, out):
+def join_kernel(row, own, from_x, from_y, far_a, far_b, *refs, norm):
+    block = own.shape[1]
+    second = pl.program_id(0) >= pl.num_programs(0) // 2
+    spots = [
+        pl.ds(pl.multiple_of((row[0] ^ flip) * block, 128), block) for flip in range(4)
+    ]
+    pieces = [own[...], from_x[...], from_y[...], jnp.where(second, far_b[...], far_a[...])]
+    if not norm:
+        for spot, piece in zip(spots, pieces):
+            refs[0][:, spot] = piece
+        return
+    gain, bias, out, average_out, inverse_out = refs
+    pieces = [piece.astype(F32) for piece in pieces]
+    average = sum(jnp.sum(piece, axis=1, keepdims=True) for piece in pieces) / D
+    squares = sum(jnp.sum(piece * piece, axis=1, keepdims=True) for piece in pieces) / D
+    inverse = lax.rsqrt(squares - average * average + EPSILON)
+    for spot, piece in zip(spots, pieces):
+        out[:, spot] = ((piece - average) * inverse * gain[:, spot] + bias[:, spot]).astype(BF16)
+    average_out[...] = jnp.broadcast_to(average, average_out.shape)
+    inverse_out[...] = jnp.broadcast_to(inverse, inverse_out.shape)
+
+
+def join(pieces, row, gain=None, bias=None):
+    norm = gain is not None
+    if not isinstance(pieces, tuple):
+        return norm_wide(pieces, gain, bias) if norm else pieces
+    rows, block = pieces[0].shape
+    steps = 4
+    tile = rows // steps
+    piece = pl.BlockSpec((tile, block), lambda i, r: (i, 0))
+    far_a = pl.BlockSpec((tile, block), lambda i, r: (jnp.minimum(i, steps // 2 - 1), 0))
+    far_b = pl.BlockSpec((tile, block), lambda i, r: (jnp.maximum(i - steps // 2, 0), 0))
+    vector = pl.BlockSpec((1, D), lambda i, r: (0, 0))
+    wide = pl.BlockSpec((tile, D), lambda i, r: (i, 0))
+    stat = pl.BlockSpec((tile, 128), lambda i, r: (i, 0))
+    wide_shape = jax.ShapeDtypeStruct((rows, D), BF16)
+    stat_shape = jax.ShapeDtypeStruct((rows, 128), F32)
+    return pl.pallas_call(
+        functools.partial(join_kernel, norm=norm),
+        grid_spec=pltpu.PrefetchScalarGridSpec(
+            num_scalar_prefetch=1,
+            grid=(steps,),
+            in_specs=[piece] * 3 + [far_a, far_b] + ([vector] * 2 if norm else []),
+            out_specs=[wide, stat, stat] if norm else wide,
+        ),
+        out_shape=[wide_shape, stat_shape, stat_shape] if norm else wide_shape,
+        compiler_params=params(("arbitrary",)),
+        name="join_norm" if norm else "join",
+        cost_estimate=pl.CostEstimate(
+            flops=8 * rows * D, bytes_accessed=4 * rows * D, transcendentals=0
+        ),
+    )(row, *pieces, *((gain[None, :], bias[None, :]) if norm else ()))
+
+
+def project_kernel(heads, values, weight, cosine, sine, query_out, key_out, value_out):
     raw = mm(values[...], weight[...])
     cos, sin = cosine[...], sine[...]
     half = QK // 2
-    for head in range(heads):
-        a = raw[:, head * QK : head * QK + half]
-        b = raw[:, head * QK + half : (head + 1) * QK]
-        out[:, head * QK : head * QK + half] = (a * cos - b * sin).astype(BF16)
-        out[:, head * QK + half : (head + 1) * QK] = (b * cos + a * sin).astype(BF16)
-
-
-def project_rotated(values, weight, cosine, sine):
+    for part, out in ((0, query_out), (1, key_out)):
+        for head in range(heads):
+            first = (part * heads + head) * QK
+            a, b = raw[:, first : first + half], raw[:, first + half : first + QK]
+            out[:, head * QK : head * QK + half] = (a * cos - b * sin).astype(BF16)
+            out[:, head * QK + half : (head + 1) * QK] = (b * cos + a * sin).astype(BF16)
+    value_out[...] = raw[:, 2 * heads * QK :].astype(BF16)
+
+
+def project(values, weight, cosine, sine):
     rows, width = values.shape[0], weight.shape[1]
+    heads = width // (2 * QK + HV)
     table = pl.BlockSpec((CHUNK, QK // 2), lambda i: (i, 0))
+    widths = (heads * QK, heads * QK, heads * HV)
     return pl.pallas_call(
-        functools.partial(rotate_kernel, width // QK),
+        functools.partial(project_kernel, heads),
         grid=(rows // CHUNK,),
         in_specs=[
             pl.BlockSpec((CHUNK, D), lambda i: (i, 0)),
             pl.BlockSpec((D, width), lambda i: (0, 0)),
             table, table,
         ],
-        out_specs=pl.BlockSpec((CHUNK, width), lambda i: (i, 0)),
-        out_shape=jax.ShapeDtypeStruct((rows, width), BF16),
+        out_specs=[pl.BlockSpec((CHUNK, w), lambda i: (i, 0)) for w in widths],
+        out_shape=[jax.ShapeDtypeStruct((rows, w), BF16) for w in widths],
         compiler_params=params(("arbitrary",)),
-        name="project_rotated",
+        name="project",
         cost_estimate=pl.CostEstimate(
             flops=2 * rows * D * width, bytes_accessed=2 * (rows + width) * D, transcendentals=0
         ),
     )(values, weight, cosine, sine)
+
+
+def matmul_kernel(values, weight, out):
+    out[...] = mm(values[...], weight[...]).astype(out.dtype)
+
+
+def matmul(values, weight, kind):
+    array, width, number = weight
+    rows = values.shape[0]
+    return pl.pallas_call(
+        matmul_kernel,
+        grid=(rows // CHUNK,),
+        in_specs=[
+            pl.BlockSpec((CHUNK, D), lambda i: (i, 0)),
+            pl.BlockSpec((D, width), lambda i: (0, number)),
+        ],
+        out_specs=pl.BlockSpec((CHUNK, width), lambda i: (i, 0)),
+        out_shape=jax.ShapeDtypeStruct((rows, width), kind),
+        compiler_params=params(("arbitrary",)),
+        name="matmul",
+        cost_estimate=pl.CostEstimate(
+            flops=2 * rows * D * width, bytes_accessed=2 * (rows + width) * D, transcendentals=0
+        ),
+    )(values, array)
+
+
+def weight_grad_kernel(spans, *refs):
+    count = len(spans)
+    lefts, rights, out = refs[:count], refs[count : 2 * count], refs[2 * count]
+    tile = pl.program_id(0)
+    for left, right, (first, last) in zip(lefts, rights, spans):
+
+        @pl.when((tile >= first) & (tile < last))
+        def _():
+            out[...] = mm_tn(left[...], right[...]).astype(BF16)
+
+
+def weight_grads(pairs):
+    rows = pairs[0][0].shape[0]
+    wide = min(right.shape[1] for _, right in pairs)
+    tall = 1024
+    steps = D // tall
+    spans, first = [], 0
+    for _, right in pairs:
+        spans.append((first, first + right.shape[1] // wide))
+        first = spans[-1][1]
+
+    def left_spec(span):
+        return pl.BlockSpec(
+            (rows, tall),
+            lambda n, m: (
+                0, jnp.where(n < span[0], 0, jnp.where(n < span[1], m, steps - 1)),
+            ),
+        )
+
+    def right_spec(span):
+        return pl.BlockSpec(
+            (rows, wide), lambda n, m: (0, jnp.clip(n - span[0], 0, span[1] - span[0] - 1))
+        )
+
+    return pl.pallas_call(
+        functools.partial(weight_grad_kernel, tuple(spans)),
+        grid=(first, steps),
+        in_specs=[left_spec(span) for span in spans] + [right_spec(span) for span in spans],
+        out_specs=pl.BlockSpec((tall, wide), lambda n, m: (m, n)),
+        out_shape=jax.ShapeDtypeStruct((D, first * wide), BF16),
+        compiler_params=params(("arbitrary", "arbitrary")),
+        name="weight_grads",
+        cost_estimate=pl.CostEstimate(
+            flops=2 * rows * D * first * wide,
+            bytes_accessed=2 * D * first * wide + 4 * rows * D,
+            transcendentals=0,
+        ),
+    )(*[left for left, _ in pairs], *[right for _, right in pairs])
 
 
 def up_kernel(values, weight, bias, grad_hidden, hidden_out, grad_out, bias_out):
@@ -525,7 +663,8 @@
 
 
 def feed_up(values, weight, bias, grad_hidden):
-    rows, width = values.shape[0], weight.shape[1]
+    array, width, number = weight
+    rows = values.shape[0]
     block = pl.BlockSpec((CHUNK, width), lambda i: (i, 0))
     vector = pl.BlockSpec((1, width), lambda i: (0, 0))
     return pl.pallas_call(
@@ -533,7 +672,7 @@
         grid=(rows // CHUNK,),
         in_specs=[
             pl.BlockSpec((CHUNK, D), lambda i: (i, 0)),
-            pl.BlockSpec((D, width), lambda i: (0, 0)),
+            pl.BlockSpec((D, width), lambda i: (0, number)),
             vector, block,
         ],
         out_specs=[block, block, vector],
@@ -549,7 +688,7 @@
             bytes_accessed=2 * (rows + width) * D + 8 * rows * width,
             transcendentals=2 * rows * width,
         ),
-    )(values, weight, bias[None, :], grad_hidden)
+    )(values, array, bias[None, :], grad_hidden)
 
 
 PARTIAL_FLIP = (1, 3, 2, 3, 2, 1, 0, 0)
@@ -577,83 +716,91 @@
             out[0] = total.astype(out.dtype)
 
 
-def partial_blocks(values, weights, row):
+def partial_blocks(values, weights, row, first, kinds):
     rows = values[0].shape[0]
     half, block = rows // 2, D // 4
     count = len(values)
+    flips = PARTIAL_FLIP[2 * first : 2 * (first + len(kinds))]
+    halves = PARTIAL_HALF[2 * first : 2 * (first + len(kinds))]
 
     def value_spec(x):
-        return pl.BlockSpec((half, x.shape[1]), lambda s, r: (table_lookup(PARTIAL_HALF, s), 0))
+        return pl.BlockSpec((half, x.shape[1]), lambda s, r: (table_lookup(halves, s), 0))
 
     def weight_spec(w):
-        return pl.BlockSpec(
-            (block, w.shape[1]), lambda s, r: (r[0] ^ table_lookup(PARTIAL_FLIP, s), 0)
-        )
+        return pl.BlockSpec((block, w[1]), lambda s, r: (r[0] ^ table_lookup(flips, s), w[2]))
 
     def out_spec(index):
-        return pl.BlockSpec(
-            (1, half, block), lambda s, r: (jnp.clip(s - 2 * index, 0, 1), 0, 0)
-        )
+        return pl.BlockSpec((1, half, block), lambda s, r: (jnp.clip(s - 2 * index, 0, 1), 0, 0))
 
     depth = sum(x.shape[1] for x in values)
     return pl.pallas_call(
         functools.partial(partial_kernel, count),
         grid_spec=pltpu.PrefetchScalarGridSpec(
             num_scalar_prefetch=1,
-            grid=(8,),
+            grid=(2 * len(kinds),),
             in_specs=[value_spec(x) for x in values] + [weight_spec(w) for w in weights],
-            out_specs=[out_spec(index) for index in range(4)],
-        ),
-        out_shape=[
-            jax.ShapeDtypeStruct((2, half, block), BF16 if index < 3 else F32) for index in range(4)
-        ],
+            out_specs=[out_spec(index) for index in range(len(kinds))],
+        ),
+        out_shape=[jax.ShapeDtypeStruct((2, half, block), kind) for kind in kinds],
         compiler_params=params(("arbitrary",)),
         name="partial_blocks",
         cost_estimate=pl.CostEstimate(
-            flops=2 * rows * D * depth,
-            bytes_accessed=2 * (2 * rows + 2 * D) * depth + 4 * rows * D,
+            flops=rows * block * depth * 2 * len(kinds),
+            bytes_accessed=(rows + D) * depth * 2 + 4 * rows * block * len(kinds),
             transcendentals=0,
         ),
-    )(row, *values, *weights)
+    )(row, *values, *[w[0] for w in weights])
 
 
 def permute_row(value, pairs):
     return lax.ppermute(value, "row", pairs)
 
 
-def reduce_row(values, weights, row):
+def in_order(*values):
+    return lax.optimization_barrier(values)
+
+
+def reduce_row_start(values, weights, row):
     if lax.axis_size("row") != 4:
-        total = sum(mm_nt(x, w) for x, w in zip(values, weights)).astype(BF16)
-        return lax.psum_scatter(total, "row", scatter_dimension=1, tiled=True).astype(F32)
-    send_x, send_y, keep, own = partial_blocks(values, weights, row)
-    from_x = permute_row(send_x, X_PAIRS)
-    from_y = permute_row(send_y, Y_PAIRS)
+        columns = [array[:, n * width : (n + 1) * width] for array, width, n in weights]
+        return sum(mm_nt(x, w) for x, w in zip(values, columns)).astype(BF16)
+    return tuple(partial_blocks(values, weights, row, 0, (BF16, BF16)))
+
+
+def reduce_row_finish(sends, values, weights, row, between=None):
+    if lax.axis_size("row") != 4:
+        total = lax.psum_scatter(sends, "row", scatter_dimension=1, tiled=True).astype(F32)
+        return total, between() if between else None
+    from_x = permute_row(sends[0], X_PAIRS)
+    from_y = permute_row(sends[1], Y_PAIRS)
+    extra = None
+    if between is not None:
+        extra = between()
+        from_x, from_y, extra = in_order(from_x, from_y, extra)
+    keep, own = partial_blocks(values, weights, row, 2, (BF16, F32))
     next_y = (keep[0].astype(F32) + from_x[1].astype(F32)).astype(BF16)
     next_x = (keep[1].astype(F32) + from_y[1].astype(F32)).astype(BF16)
     last_y = permute_row(next_y, Y_PAIRS)
     last_x = permute_row(next_x, X_PAIRS)
     first_half = own[0] + from_x[0].astype(F32) + last_y.astype(F32)
     second_half = own[1] + from_y[0].astype(F32) + last_x.astype(F32)
-    return jnp.concatenate([first_half, second_half], axis=0)
-
-
-def gather_row(value):
+    return jnp.concatenate([first_half, second_half], axis=0), extra
+
+
+def gather_row(value, between=None):
     if lax.axis_size("row") != 4:
-        return lax.all_gather(value, "row", axis=1, tiled=True)
-    row = lax.axis_index("row")
-    rows, block = value.shape
-    half = rows // 2
+        gathered = lax.all_gather(value, "row", axis=1, tiled=True)
+        return gathered, between() if between else None
+    half = value.shape[0] // 2
     from_x = permute_row(value, X_PAIRS)
     from_y = permute_row(value, Y_PAIRS)
+    extra = None
+    if between is not None:
+        extra = between()
+        from_x, from_y, extra = in_order(from_x, from_y, extra)
     far_a = permute_row(from_x[:half], Y_PAIRS)
     far_b = permute_row(from_y[half:], X_PAIRS)
-    out = jnp.zeros((rows, 4 * block), value.dtype)
-    zero = jnp.int32(0)
-    out = lax.dynamic_update_slice(out, value, (zero, row * block))
-    out = lax.dynamic_update_slice(out, from_x, (zero, (row ^ 1) * block))
-    out = lax.dynamic_update_slice(out, from_y, (zero, (row ^ 2) * block))
-    out = lax.dynamic_update_slice(out, far_a, (zero, (row ^ 3) * block))
-    return lax.dynamic_update_slice(out, far_b, (jnp.int32(half), (row ^ 3) * block))
+    return (value, from_x, from_y, far_a, far_b), extra
 
 
 def gather_row_small(value):
@@ -692,49 +839,272 @@
     return lax.psum_scatter(grad, "col", scatter_dimension=0, tiled=True).astype(F32)
 
 
-def permute_col(value, pairs, place_count):
-    size = lax.axis_size("col")
-    all_pairs = [
-        (base + a, base + b) for base in range(0, size, place_count) for a, b in pairs
+class Exchange:
+    def __init__(self, messages, send_sem, recv_sem):
+        col = lax.axis_index("col")
+        self.base = (col // SLOTS) * SLOTS
+        self.place = col % SLOTS
+        self.messages, self.send_sem, self.recv_sem = messages, send_sem, recv_sem
+
+    def copy(self, index):
+        _, target, source, destination = self.messages[index]
+        return pltpu.make_async_remote_copy(
+            src_ref=source,
+            dst_ref=destination,
+            send_sem=self.send_sem.at[index],
+            recv_sem=self.recv_sem.at[index],
+            device_id={"col": self.base + target},
+            device_id_type=pl.DeviceIdType.MESH,
+        )
+
+    def greet(self):
+        barrier = pltpu.get_barrier_semaphore()
+        for step in range(1, SLOTS):
+            other = self.base + (self.place + step) % SLOTS
+            pl.semaphore_signal(
+                barrier, inc=1, device_id={"col": other}, device_id_type=pl.DeviceIdType.MESH
+            )
+        pl.semaphore_wait(barrier, SLOTS - 1)
+
+    def run(self, programs):
+        for place, program in enumerate(programs):
+
+            @pl.when(self.place == place)
+            def _():
+                sent = []
+                for action in program:
+                    if callable(action):
+                        action()
+                    elif action >= 0:
+                        self.copy(action).start()
+                        sent.append(action)
+                    else:
+                        self.copy(~action).wait_recv()
+                for index in sent:
+                    self.copy(index).wait_send()
+
+
+def scaled_add(meta, rates, target, terms, rows):
+    heads = target.shape[0]
+    for head in range(heads):
+        total = None
+        for term in terms:
+            if isinstance(term, tuple):
+                ref, slot = term
+                exponent = jnp.maximum(
+                    trunk_reference(meta, jnp.int32(3), rows)
+                    - trunk_reference(meta, jnp.int32(slot), rows),
+                    0,
+                )
+                value = ref[head].astype(F32) * power(rates[head], exponent, HV)
+            else:
+                value = term[head].astype(F32)
+            total = value if total is None else total + value
+        target[head] = total.astype(BF16)
+
+
+def share_kernel(rows, meta, rates, ex, sh, shift, tot, send_sem, recv_sem):
+    messages = [
+        (0, 2, ex.at[0], sh.at[0]),
+        (0, 1, ex.at[0], sh.at[0]),
+        (1, 3, ex.at[0], sh.at[1]),
+        (2, 3, ex.at[0], sh.at[2]),
+        (2, 3, sh.at[0], sh.at[0]),
+        (3, 2, sh.at[1], sh.at[1]),
+        (3, 4, ex.at[1], sh.at[4]),
+        (3, 5, ex.at[2], sh.at[5]),
+        (3, 4, tot, sh.at[3]),
+        (4, 5, ex.at[1], sh.at[6]),
+        (4, 6, ex.at[1], sh.at[6]),
+        (4, 5, ex.at[2], sh.at[7]),
+        (5, 7, sh.at[7], sh.at[7]),
+        (4, 5, sh.at[4], sh.at[4]),
+        (4, 6, sh.at[4], sh.at[4]),
+        (5, 4, sh.at[5], sh.at[5]),
+        (5, 7, sh.at[5], sh.at[5]),
+        (4, 5, sh.at[3], sh.at[3]),
+        (4, 6, sh.at[3], sh.at[3]),
+        (6, 7, sh.at[6], sh.at[6]),
+        (6, 7, sh.at[4], sh.at[4]),
+        (6, 7, sh.at[3], sh.at[3]),
+        (7, 6, sh.at[7], sh.at[7]),
+        (7, 6, sh.at[5], sh.at[5]),
+        (4, 5, ex.at[0], shift),
+        (6, 7, ex.at[0], shift),
     ]
-    return lax.ppermute(value, "col", all_pairs)
-
-
-def share_states(exports, place, tree):
-    from_b0 = permute_col(exports[1], [(3, 6)], SLOTS)
-    from_b = permute_col(exports[2], [(3, 7), (4, 5)], SLOTS)
-    shifted = permute_col(exports[0], [(4, 5), (6, 7)], SLOTS)
-    mine = jnp.where(
-        place < 4,
-        exports[0],
-        jnp.where(place == 4, exports[1], jnp.where(place == 6, from_b0, from_b)),
-    )
-    shared = lax.all_gather(mine, "col", axis=0)
-    if shared.shape[0] != SLOTS:
-        shared = lax.dynamic_slice_in_dim(shared, tree * SLOTS, SLOTS, 0)
-    return shared, shifted
-
-
-def return_states(exports, first_state, place, tree):
+    exchange = Exchange(messages, send_sem, recv_sem)
+
+    def keep_trunk():
+        sh[3] = ex[0]
+
+    def total_trunk():
+        terms = [(sh.at[slot], slot) for slot in range(3)] + [ex.at[0]]
+        scaled_add(meta, rates, tot, terms, rows)
+
+    def keep_branches():
+        sh[6] = ex[1]
+        sh[7] = ex[2]
+
+    exchange.greet()
+    exchange.run(
+        [
+            [0, 1],
+            [2, ~1],
+            [3, ~0, 4, ~5],
+            [6, 7, keep_trunk, ~2, 5, ~4, ~3, total_trunk, 8],
+            [10, 11, 9, 24, keep_branches, ~6, 14, 13, ~15, ~8, 18, 17],
+            [~11, 12, ~7, 16, 15, ~9, ~24, ~13, ~17],
+            [25, ~10, 19, ~14, 20, ~22, ~23, ~18, 21],
+            [~12, 22, ~16, 23, ~19, ~20, ~25, ~21],
+        ]
+    )
+
+
+def vmem():
+    return pl.BlockSpec(memory_space=pltpu.VMEM)
+
+
+def share_states(meta, rates, exports, rows):
+    heads = exports.shape[1]
+    state = (heads, QK, HV)
+    return pl.pallas_call(
+        functools.partial(share_kernel, rows),
+        in_specs=[smem(), smem(), vmem()],
+        out_specs=[vmem(), vmem()],
+        out_shape=[
+            jax.ShapeDtypeStruct((SLOTS,) + state, BF16),
+            jax.ShapeDtypeStruct(state, BF16),
+        ],
+        scratch_shapes=[
+            pltpu.VMEM(state, BF16),
+            pltpu.SemaphoreType.DMA((26,)),
+            pltpu.SemaphoreType.DMA((26,)),
+        ],
+        compiler_params=pltpu.CompilerParams(
+            collective_id=1, has_side_effects=True, vmem_limit_bytes=40 * 1024 * 1024
+        ),
+        name="share_states",
+        cost_estimate=pl.CostEstimate(
+            flops=0, bytes_accessed=100 * 1024 * 1024, transcendentals=0
+        ),
+    )(meta, rates, exports)
+
+
+def return_kernel(rows, meta, rates, y, first, own0, own1, own2, rx, tx, send_sem, recv_sem):
+    messages = [
+        (7, 6, y.at[3], rx.at[0]),
+        (7, 6, y.at[4], rx.at[1]),
+        (7, 6, y.at[5], rx.at[2]),
+        (6, 7, y.at[6], rx.at[0]),
+        (6, 7, y.at[7], rx.at[1]),
+        (7, 5, tx.at[0], rx.at[0]),
+        (7, 5, tx.at[1], rx.at[1]),
+        (6, 4, tx.at[0], rx.at[0]),
+        (6, 4, tx.at[1], rx.at[1]),
+        (6, 4, tx.at[2], rx.at[2]),
+        (5, 4, y.at[3], rx.at[3]),
+        (5, 4, y.at[4], rx.at[4]),
+        (5, 4, y.at[5], rx.at[5]),
+        (5, 4, tx.at[0], rx.at[6]),
+        (5, 4, tx.at[1], rx.at[7]),
+        (4, 3, tx.at[0], rx.at[0]),
+        (4, 3, tx.at[1], own1),
+        (4, 3, tx.at[2], own2),
+        (2, 3, y.at[0], rx.at[1]),
+        (2, 3, y.at[1], rx.at[2]),
+        (3, 2, tx.at[2], own0),
+        (3, 1, tx.at[1], own0),
+        (3, 0, tx.at[0], rx.at[0]),
+        (1, 0, y.at[0], rx.at[1]),
+        (5, 4, first, own0),
+        (7, 6, first, own0),
+    ]
+    exchange = Exchange(messages, send_sem, recv_sem)
+
+    def add(target, *terms):
+        return lambda: scaled_add(meta, rates, target, terms, rows)
+
+    exchange.greet()
+    exchange.run(
+        [
+            [~23, ~22, add(own0, rx.at[0], rx.at[1])],
+            [23, ~21],
+            [18, 19, ~20],
+            [
+                ~18, ~19, ~15,
+                add(tx.at[0], y.at[0], rx.at[1], (rx.at[0], 0)), 22,
+                add(tx.at[1], y.at[1], rx.at[2], (rx.at[0], 1)), 21,
+                add(tx.at[2], y.at[2], (rx.at[0], 2)), 20,
+                add(own0, rx.at[0], y.at[3]),
+                ~16, ~17,
+            ],
+            [
+                ~10, ~7, add(tx.at[0], y.at[3], rx.at[0], rx.at[3]), 15,
+                ~11, ~8, add(tx.at[1], y.at[4], rx.at[1], rx.at[4]), 16,
+                ~12, ~9, add(tx.at[2], y.at[5], rx.at[2], rx.at[5]), 17,
+                ~13, add(own1, y.at[6], rx.at[6]),
+                ~14, add(own2, y.at[7], rx.at[7]),
+                ~24,
+            ],
+            [
+                10, 11, 12, 24,
+                ~5, add(tx.at[0], y.at[6], rx.at[0]), 13,
+                ~6, add(tx.at[1], y.at[7], rx.at[1]), 14,
+            ],
+            [
+                3, 4,
+                ~0, add(tx.at[0], y.at[3], rx.at[0]), 7,
+                ~1, add(tx.at[1], y.at[4], rx.at[1]), 8,
+                ~2, add(tx.at[2], y.at[5], rx.at[2]), 9,
+                ~25,
+            ],
+            [
+                0, 1, 2, 25,
+                ~3, add(tx.at[0], y.at[6], rx.at[0]), 5,
+                ~4, add(tx.at[1], y.at[7], rx.at[1]), 6,
+            ],
+        ]
+    )
+
+
+def return_states(meta, rates, exports, first_state, rows):
+    heads = exports.shape[1]
+    state = (heads, QK, HV)
+    return pl.pallas_call(
+        functools.partial(return_kernel, rows),
+        in_specs=[smem(), smem(), vmem(), vmem()],
+        out_specs=[vmem()] * 3,
+        out_shape=[jax.ShapeDtypeStruct(state, BF16)] * 3,
+        scratch_shapes=[
+            pltpu.VMEM((8,) + state, BF16),
+            pltpu.VMEM((3,) + state, BF16),
+            pltpu.SemaphoreType.DMA((26,)),
+            pltpu.SemaphoreType.DMA((26,)),
+        ],
+        compiler_params=pltpu.CompilerParams(
+            collective_id=2, has_side_effects=True, vmem_limit_bytes=40 * 1024 * 1024
+        ),
+        name="return_states",
+        cost_estimate=pl.CostEstimate(
+            flops=0, bytes_accessed=100 * 1024 * 1024, transcendentals=0
+        ),
+    )(meta, rates, exports, first_state)
+
+
+def sum_col(value):
     size = lax.axis_size("col")
     if size != SLOTS:
-        full = jnp.zeros((size,) + exports.shape[1:], exports.dtype)
-        zero = jnp.int32(0)
-        exports = lax.dynamic_update_slice(full, exports, (tree * SLOTS, zero, zero, zero))
-    mine = lax.psum_scatter(exports, "col", scatter_dimension=0, tiled=True)[0]
-    to_b0 = permute_col(mine, [(6, 3)], SLOTS)
-    to_b = permute_col(mine, [(7, 3), (5, 4)], SLOTS)
-    shifted = permute_col(first_state, [(5, 4), (7, 6)], SLOTS)
-    own0 = jnp.where(place < 4, mine, shifted)
-    own1 = jnp.where(place == 4, mine, to_b0)
-    return own0, own1, to_b
+        return lax.psum(value, "col")
+    for flip in (1, 2, 4):
+        value = value + lax.ppermute(value, "col", [(a, a ^ flip) for a in range(size)])
+    return value
 
 
 def sum_col_vectors(vectors, extra=None):
     col = lax.axis_index("col")
     size = lax.axis_size("col")
     parts = list(vectors) + ([extra] if extra is not None else [])
-    total = jnp.sum(lax.all_gather(jnp.concatenate(parts), "col", axis=0), axis=0)
+    total = sum_col(jnp.concatenate(parts).reshape(-1, 128)).reshape(-1)
     results, first = [], 0
     for vector in vectors:
         width = vector.shape[0] // size
@@ -799,44 +1169,60 @@
     head_numbers = (row * heads + jnp.arange(heads, dtype=jnp.int32)).astype(F32)
     rates = jnp.log(1.0 - 2.0 ** (-5.0 - head_numbers))
 
-    query_full = gather_col(query_weight)
-    key_full = gather_col(key_weight)
-    value_full = gather_col(value_weight)
-    gate_full = gather_col(gate_weight)
-    out_full = gather_col(out_weight.T)
-    up_full = gather_col(up_weight)
-    down_full = gather_col(down_weight.T)
+    wide = heads * HV
+    narrow = heads * QK
+    project_full = gather_col(jnp.concatenate([query_weight, key_weight, value_weight], axis=1))
+    mix_full = gather_col(jnp.concatenate([gate_weight, out_weight.T], axis=1))
+    feed_full = gather_col(jnp.concatenate([down_weight.T, up_weight], axis=1))
+    query_part, key_part = (project_full, narrow, 0), (project_full, narrow, 1)
+    value_part = (project_full, wide, 1)
+    gate_part, out_part = (mix_full, wide, 0), (mix_full, wide, 1)
+    down_part, up_part = (feed_full, wide, 0), (feed_full, wide, 1)
 
     valid, cosine, sine = token_tables(place, rows, lengths, parents)
     column = valid[:, None]
     gains = gather_row_small(jnp.stack([first_gain, first_bias, second_gain, second_bias]))
-    token_wide = gather_row(tokens)
+    token_pieces, _ = gather_row(tokens)
+    first_wide, first_average, first_inverse = join(token_pieces, row_ref, gains[0], gains[1])
     fed_low = (cotangent.astype(F32) * column).astype(BF16)
-    fed_wide = gather_row(fed_low)
-
-    first_wide, first_average, first_inverse = norm_wide(token_wide, gains[0], gains[1])
-    query_rot = project_rotated(first_wide, query_full, cosine, sine)
-    key_rot = project_rotated(first_wide, key_full, cosine, sine)
-    value_low = mm(first_wide, value_full).astype(BF16)
+    fed_low, first_average = lax.optimization_barrier((fed_low, first_average))
+
+    fed_pieces, projected = gather_row(
+        fed_low, lambda: project(first_wide, project_full, cosine, sine)
+    )
+    query_rot, key_rot, value_low = projected
     exports = make_states(meta, rates, key_rot, value_low)
-    shared, shifted = share_states(exports, place, tree)
-    gate_raw = mm(first_wide, gate_full)
+    shared, shifted = share_states(meta, rates, exports, rows)
+    mix_full, shared = in_order(mix_full, shared)
+    gate_part, out_part = (mix_full, wide, 0), (mix_full, wide, 1)
+    gate_raw = matmul(first_wide, gate_part, F32)
+    gate_raw, fed_pieces = in_order(gate_raw, fed_pieces)
     gated, normal, inverse, states = retain(
         meta, rates, query_rot, key_rot, value_low, gate_raw, shared, shifted, group_gain, group_bias
     )
 
-    attended = reduce_row([gated], [out_full], row_ref)
+    sends = reduce_row_start([gated], [out_part], row_ref)
+    attended, _ = reduce_row_finish(sends, [gated], [out_part], row_ref)
     middle = tokens.astype(F32) + attended
-    middle_wide = gather_row(middle.astype(BF16))
-    second_wide, second_average, second_inverse = norm_wide(middle_wide, gains[2], gains[3])
-    grad_hidden = mm(fed_wide, down_full).astype(BF16)
-    hidden, grad_before, up_bias_grad = feed_up(second_wide, up_full, up_bias, grad_hidden)
-    second_back = reduce_row([grad_before], [up_full], row_ref)
-    fed_out = reduce_row([hidden], [down_full], row_ref) + down_bias
-    layer_out = middle + fed_out
+
+    def feed_gradient():
+        joined = join(fed_pieces, row_ref)
+        return joined, matmul(joined, down_part, BF16)
+
+    middle_pieces, (fed_wide, grad_hidden) = gather_row(middle.astype(BF16), feed_gradient)
+    second_wide, second_average, second_inverse = join(middle_pieces, row_ref, gains[2], gains[3])
+    hidden, grad_before, up_bias_grad = feed_up(second_wide, up_part, up_bias, grad_hidden)
+    sends = reduce_row_start([grad_before], [up_part], row_ref)
+    sends, hidden = in_order(sends, hidden)
+    second_back, feed_partial = reduce_row_finish(
+        sends,
+        [grad_before],
+        [up_part],
+        row_ref,
+        lambda: weight_grads([(fed_wide, hidden), (second_wide, grad_before)]),
+    )
+    feed_grad = scatter_col(feed_partial)
     grad_fed = fed_low.astype(F32)
-    down_grad = scatter_col(mm_tn(fed_wide, hidden).astype(BF16))
-    up_grad = scatter_col(mm_tn(second_wide, grad_before).astype(BF16))
     down_bias_grad = jnp.sum(grad_fed, axis=0)
 
     second_normal = (middle - second_average[:, :1]) * second_inverse[:, :1]
@@ -844,24 +1230,50 @@
         second_back, second_normal, second_inverse[:, :1], second_gain
     )
     grad_middle = grad_fed + grad_middle_norm
-    grad_wide = gather_row(grad_middle.astype(BF16))
-    grad_gate, grad_retained, group_gain_grad, group_bias_grad, returns, first_state = gate_back(
-        meta, rates, grad_wide, out_full, gate_raw, normal, inverse, query_rot, group_gain, group_bias
-    )
-    out_grad = scatter_col(mm_tn(grad_wide, gated).astype(BF16))
-    own = return_states(returns, first_state, place, tree)
-    gate_grad = scatter_col(mm_tn(first_wide, grad_gate).astype(BF16))
+    grad_pieces, fed_sends = gather_row(
+        grad_middle.astype(BF16), lambda: reduce_row_start([hidden], [down_part], row_ref)
+    )
+    grad_wide = join(grad_pieces, row_ref)
+    out_partial = weight_grads([(grad_wide, gated)])
+    out_partial, grad_wide, feed_grad, fed_sends = in_order(
+        out_partial, grad_wide, feed_grad, fed_sends
+    )
+    out_grad = scatter_col(out_partial)
+    fed_out, gate_results = reduce_row_finish(
+        fed_sends,
+        [hidden],
+        [down_part],
+        row_ref,
+        lambda: gate_back(
+            meta, rates, grad_wide, out_part, gate_raw, normal, inverse, query_rot, group_gain, group_bias
+        ),
+    )
+    fed_out = fed_out + down_bias
+    layer_out = middle + fed_out
+    grad_gate, grad_retained, group_gain_grad, group_bias_grad, returns, first_state = gate_results
+    own = return_states(meta, rates, returns, first_state, rows)
+    grad_gate, own = in_order(grad_gate, own)
+    gate_partial = weight_grads([(first_wide, grad_gate)])
+    gate_partial, own, out_grad = in_order(gate_partial, own, out_grad)
+    gate_grad = scatter_col(gate_partial)
     grad_query, grad_key, grad_value = retain_back(
         meta, rates, query_rot, key_rot, value_low, grad_retained, states, cosine, sine, own
     )
-    first_back = reduce_row(
-        [grad_query, grad_key, grad_value, grad_gate],
-        [query_full, key_full, value_full, gate_full],
+    back_values = [grad_query, grad_key, grad_value, grad_gate]
+    back_weights = [query_part, key_part, value_part, gate_part]
+    sends = reduce_row_start(back_values, back_weights, row_ref)
+    sends, grad_value = in_order(sends, grad_value)
+    first_back, project_partial = reduce_row_finish(
+        sends,
+        back_values,
+        back_weights,
         row_ref,
-    )
-    value_grad = scatter_col(mm_tn(first_wide, grad_value).astype(BF16))
-    query_grad = scatter_col(mm_tn(first_wide, grad_query).astype(BF16))
-    key_grad = scatter_col(mm_tn(first_wide, grad_key).astype(BF16))
+        lambda: weight_grads(
+            [(first_wide, grad_query), (first_wide, grad_key), (first_wide, grad_value)]
+        ),
+    )
+    project_partial, gate_grad = in_order(project_partial, gate_grad)
+    project_grad = scatter_col(project_partial)
 
     first_normal = (tokens.astype(F32) - first_average[:, :1]) * first_inverse[:, :1]
     grad_first, first_gain_grad, first_bias_grad = norm_backward(
@@ -869,14 +1281,7 @@
     )
     tokens_grad = grad_middle + grad_first
 
-    squares = jnp.stack(
-        [
-            jnp.sum(column * layer_out * layer_out),
-            jnp.sum(column * attended * attended),
-            jnp.sum(column * fed_out * fed_out),
-        ]
-    )
-    vectors, col_squares = sum_col_vectors(
+    vectors, _ = sum_col_vectors(
         (
             group_gain_grad[0],
             group_bias_grad[0],
@@ -884,23 +1289,31 @@
             second_bias_grad,
             up_bias_grad[0],
             down_bias_grad,
-        ),
-        jnp.concatenate([squares, jnp.zeros((125,), F32)]),
+        )
+    )
+    squares = jnp.stack(
+        [
+            jnp.sum(column * layer_out * layer_out),
+            jnp.sum(column * attended * attended),
+            jnp.sum(column * fed_out * fed_out),
+        ]
+    )
+    last, col_squares = sum_col_vectors(
+        (first_gain_grad, first_bias_grad), jnp.concatenate([squares, jnp.zeros((125,), F32)])
     )
     totals = sum_row_small(col_squares[None, :])[0, :3]
-    last, _ = sum_col_vectors((first_gain_grad, first_bias_grad))
     valid_count = jnp.sum(segment_lengths).astype(F32) * D
     norm_values = jnp.sqrt(totals / valid_count)
     return (
         layer_out.astype(BF16),
         tokens_grad,
-        query_grad,
-        key_grad,
-        value_grad,
+        project_grad[:, :narrow],
+        project_grad[:, narrow : 2 * narrow],
+        project_grad[:, 2 * narrow :],
         gate_grad,
         out_grad.T,
-        up_grad,
-        down_grad.T,
+        feed_grad[:, wide:],
+        feed_grad[:, :wide].T,
         last[0],
         last[1],
         vectors[0],

time: 1040 us -> 755 us (0.73)
  waiting for transfers between devices: 535 us -> 237 us
  Pallas kernels: 175 us -> 343 us
  matrix products: 94 us -> 0 us
  blocking collectives: 45.9 us -> 0 us
  local copies, waits for them, and re-layouts: 59.7 us -> 40.9 us
    pallas_call x4 -> x13, Pallas kernels: 31.8 us -> 192 us  [the longest x4 57.2 us: weight_grads(): pl.pallas_call(functools.partial(weight_grad_kernel, tuple(spans)), grid=...]
    reduce_scatter x7 -> x4, waiting for transfers between devices: 171 us -> 23.8 us  [scatter_col(): lax.psum_scatter(grad, 'col', scatter_dimension=0, tiled=True).astype(F32)]
    dot_general x10 -> x0, matrix products: 94 us -> none  [the longest x7 64.1 us: mm_tn(): lax.dot_general(a, b, (((0,), (0,)), ((), ())), preferred_element_type=F32)]
    ppermute x41, waiting for transfers between devices: 231 us -> 171 us  [permute_row(): return lax.ppermute(value, 'row', pairs)]
    all_gather x7 -> x3, waiting for transfers between devices: 89.6 us -> 39.9 us  [gather_col(): return lax.all_gather(weight, 'col', axis=0, tiled=True)]
    all_gather x2 -> x0, blocking collectives: 45.9 us -> none  [sum_col_vectors(): lax.all_gather(jnp.concatenate(parts), 'col', axis=0)]
    all_gather x1 -> x0, waiting for transfers between devices: 37.7 us -> none  [share_states(): shared = lax.all_gather(mine, 'col', axis=0)]
    dynamic_update_slice x18 -> x0, local copies, waits for them, and re-layouts: 19.8 us -> none  [the longest x4 6.15 us: gather_row(): out = lax.dynamic_update_slice(out, from_y, (zero, (row ^ 2) * block))]
  transfers between devices with their start and end apart: 63 -> 54, of which waited for: 36 -> 36; matrix products, arithmetic and copies ran while one was open for 17% -> 9% of each run, Pallas kernels for 12% -> 42%
where the time goes in v2:
time: 755 us; the launch traced here: 747 us
  Pallas kernels  343 us (45%)
  waiting for transfers between devices  237 us (31%)
  starting transfers between devices  58.8 us (8%)
  other arithmetic  52.1 us (7%)
  local copies, waits for them, and re-layouts  40.9 us (5%)
  between operations  15.8 us (2%)
    ppermute x41, waiting for transfers between devices, permute_row(): return lax.ppermute(value, 'row', pairs)  171 us
    pallas_call x8, Pallas kernels, partial_blocks(): pl.pallas_call(functools.partial(partial_kernel, count), grid_spec=pltpu....  75.4 us
    pallas_call x4, Pallas kernels, weight_grads(): pl.pallas_call(functools.partial(weight_grad_kernel, tuple(spans)), grid=...  57.2 us
    ppermute x41, starting transfers between devices, permute_row(): return lax.ppermute(value, 'row', pairs)  51.3 us
    pallas_call x1, Pallas kernels, return_states(): pl.pallas_call(functools.partial(return_kernel, rows), in_specs=[smem(),...  46.4 us
    all_gather x3, waiting for transfers between devices, gather_col(): return lax.all_gather(weight, 'col', axis=0, tiled=True)  39.9 us
    pallas_call x1, Pallas kernels, share_states(): pl.pallas_call(functools.partial(share_kernel, rows), in_specs=[smem(), s...  26 us
    pallas_call x4, Pallas kernels, join(): pl.pallas_call(functools.partial(join_kernel, norm=norm), grid_spec=pltpu...  25.5 us
  transfers between devices with their start and end apart: 54, of which 36 were waited for; matrix products, arithmetic and copies ran while one was open for 9% of the time, Pallas kernels for 42%

profile of v2, /device:TPU:0, one launch (start us, length us, event | category | flops | bytes accessed | tf_op | source)
XLA Modules:
  0.0 746.8 jit_solution(9006829723603191088)
XLA Ops:
  24.2 24.6 %collective-permute-done.from_x = bf16[1280,512]{1,0:T(8,128)(2,1)} collective-permute-done((bf16[1280,512]{1,0:T(8,128)(2,1)S(1)}, bf16[1280,512]{1,0:T(8,128)(2,1)}, u32[]{:S(2)}, u32[]{:S(2)}) %collective-permute-start) | collective-permute-done | bytes 1310752 | tf_op jit(solution)/shard_map/ppermute | solution.py:756
  54.9 10.1 %collective-permute-done.2.far_a = bf16[640,512]{1,0:T(8,128)(2,1)S(1)} collective-permute-done((bf16[640,512]{1,0:T(8,128)(2,1)S(1)}, bf16[640,512]{1,0:T(8,128)(2,1)S(1)}, u32[]{:S(2)}, u32[]{:S(2)}) %collective-permute-start.2) | collective-permute-done | bytes 655392 | tf_op jit(solution)/shard_map/ppermute | solution.py:756
  68.1 7.4 join_norm.2
  77.8 3.7 multiply_sine_fusion
  82.0 13.0 %all-gather.4.cloned.1.call-done.weight.refs_4_.refs_5_.refs_6_ = bf16[2048,2048]{1,0:T(8,128)(2,1)} async-done(((bf16[256,2048]{1,0:T(8,128)(2,1)}), bf16[2048,2048]{1,0:T(8,128)(2,1)}) %all-gather.4.cloned.1.call-update) | async-done | bytes 8388624 | tf_op jit(solution)/shard_map/all_gather | solution.py:835
  95.0 16.9 %project.1 = (bf16[1280,512]{1,0:T(8,128)(2,1)}, bf16[1280,512]{1,0:T(8,128)(2,1)}, bf16[1280,1024]{1,0:T(8,128)(2,1)}) custom-call(bf16[1280,2048]{1,0:T(8,128)(2,1)} %get-tuple-element.125.values.refs_0_.refs_1_.refs_2_, bf16[2048,2048]{1,0:T(8,128)(2,1)} %all-gather.4.cloned.1.call-done.weight.refs_4_.refs_5_.refs_6_, ...), custom_call_target="tpu_custom_call" | custom-call | flops 10737418240 | bytes 13631488 | tf_op jit(solution)/shard_map/project/pallas_call | solution.py:558
  117.2 9.4 %chunk_states.1.ex = bf16[3,2,256,512]{3,2,1,0:T(8,128)(2,1)} custom-call(s32[22]{0:T(128)} %pad_add_fusion.meta, f32[2]{0:T(128)} %subtract_log_fusion.rates, bf16[1280,512]{1,0:T(8,128)(2,1)} %get-tuple-element.130.key, bf16[1280,1024]{1,0:T(8,128)(2,1)} %get-tuple-element.131.value), custom_call_target="tpu_custom_call" | custom-call | flops 671088640 | bytes 3932160 | tf_op jit(solution)/shard_map/chunk_states/pallas_call | solution.py:163
  128.0 26.0 %share_states.1 = (bf16[8,2,256,512]{3,2,1,0:T(8,128)(2,1)S(1)}, bf16[2,256,512]{2,1,0:T(8,128)(2,1)S(1)}) custom-call(s32[22]{0:T(128)S(1)} %copy-done.5, f32[2]{0:T(128)S(1)} %copy-done.7, bf16[3,2,256,512]{3,2,1,0:T(8,128)(2,1)S(1)} %copy-done), custom_call_target="tpu_custom_call" | custom-call | bytes 104857600 | tf_op jit(solution)/shard_map/share_states/pallas_call | solution.py:970
  156.9 26.9 %all-gather.6.cloned.1.call-done.weight.refs_1_.refs_7_ = bf16[2048,2048]{1,0:T(8,128)(2,1)} async-done(((bf16[256,2048]{1,0:T(8,128)(2,1)}), bf16[2048,2048]{1,0:T(8,128)(2,1)}) %all-gather.6.cloned.1.call-update) | async-done | bytes 8388624 | tf_op jit(solution)/shard_map/all_gather | solution.py:835
  183.8 10.5 %matmul.2.gate = f32[1280,1024]{1,0:T(8,128)} custom-call(bf16[1280,2048]{1,0:T(8,128)(2,1)} %get-tuple-element.125.values.refs_0_.refs_1_.refs_2_, bf16[2048,2048]{1,0:T(8,128)(2,1)} %all-gather.6.cloned.1.call-done.weight.refs_1_.refs_7_), custom_call_target="tpu_custom_call" | custom-call | flops 5368709120 | bytes 9437184 | tf_op jit(solution)/shard_map/matmul/pallas_call | solution.py:583
  194.3 16.7 %retention_forward.1 = (bf16[1280,1024]{1,0:T(8,128)(2,1)}, bf16[1280,1024]{1,0:T(8,128)(2,1)}, f32[2,1280,128]{2,1,0:T(8,128)}, bf16[2,5,256,512]{3,2,1,0:T(8,128)(2,1)}) custom-call(s32[22]{0:T(128)} %pad_add_fusion.meta, f32[2]{0:T(128)} %subtract_log_fusion.rates, bf16[1280,512]{1,0:T(8,128)(2,1)} %get-tuple-element.129.query, ...), custom_call_target="tpu_custom_call" | custom-call | flops 2348810240 | bytes 20971520 | tf_op jit(solution)/shard_map/retention_forward/pallas_call | solution.py:243
  211.1 7.5 %partial_blocks.9 = (bf16[2,640,512]{2,1,0:T(8,128)(2,1)}, bf16[2,640,512]{2,1,0:T(8,128)(2,1)}) custom-call(s32[1]{0:T(128)} %bitcast.row, bf16[1280,1024]{1,0:T(8,128)(2,1)} %get-tuple-element.139.refs_0_.refs_1_, bf16[2048,2048]{1,0:T(8,128)(2,1)} %all-gather.6.cloned.1.call-done.weight.refs_1_.refs_7_), custom_call_target="tpu_custom_call" | custom-call | flops 2684354560 | bytes 12058624 | tf_op jit(solution)/shard_map/partial_blocks/pallas_call | solution.py:736
  221.6 7.8 %partial_blocks.8 = (bf16[2,640,512]{2,1,0:T(8,128)(2,1)}, f32[2,640,512]{2,1,0:T(8,128)}) custom-call(s32[1]{0:T(128)} %bitcast.row, bf16[1280,1024]{1,0:T(8,128)(2,1)} %get-tuple-element.139.refs_0_.refs_1_, bf16[2048,2048]{1,0:T(8,128)(2,1)} %all-gather.6.cloned.1.call-done.weight.refs_1_.refs_7_), custom_call_target="tpu_custom_call" | custom-call | flops 2684354560 | bytes 12058624 | tf_op jit(solution)/shard_map/partial_blocks/pallas_call | solution.py:736
  229.4 20.2 %collective-permute-done.11 = bf16[2,640,512]{2,1,0:T(8,128)(2,1)S(1)} collective-permute-done((bf16[2,640,512]{2,1,0:T(8,128)(2,1)}, bf16[2,640,512]{2,1,0:T(8,128)(2,1)S(1)}, u32[]{:S(2)}, u32[]{:S(2)}) %collective-permute-start.11) | collective-permute-done | bytes 1310752 | tf_op jit(solution)/shard_map/ppermute | solution.py:756
  255.0 13.7 %collective-permute-done.12 = bf16[640,512]{1,0:T(8,128)(2,1)S(1)} collective-permute-done((bf16[640,512]{1,0:T(8,128)(2,1)S(1)}, bf16[640,512]{1,0:T(8,128)(2,1)S(1)}, u32[]{:S(2)}, u32[]{:S(2)}) %collective-permute-start.12) | collective-permute-done | bytes 655392 | tf_op jit(solution)/shard_map/ppermute | solution.py:756
  273.9 5.3 join.2.values.refs_0_
  279.1 9.9 %matmul.3.grad_hidden = bf16[1280,1024]{1,0:T(8,128)(2,1)} custom-call(bf16[1280,2048]{1,0:T(8,128)(2,1)} %join.2.values.refs_0_, bf16[2048,2048]{1,0:T(8,128)(2,1)} %all-gather.8.cloned.1.call-done.weight.refs_1_), custom_call_target="tpu_custom_call" | custom-call | flops 5368709120 | bytes 9437184 | tf_op jit(solution)/shard_map/matmul/pallas_call | solution.py:583
  289.1 12.2 %collective-permute-done.16.from_y = bf16[1280,512]{1,0:T(8,128)(2,1)} collective-permute-done((bf16[1280,512]{1,0:T(8,128)(2,1)}, bf16[1280,512]{1,0:T(8,128)(2,1)}, u32[]{:S(2)}, u32[]{:S(2)}) %collective-permute-start.16) | collective-permute-done | bytes 1310752 | tf_op jit(solution)/shard_map/ppermute | solution.py:756
  306.3 11.5 %collective-permute-done.18.far_b = bf16[640,512]{1,0:T(8,128)(2,1)S(1)} collective-permute-done((bf16[640,512]{1,0:T(8,128)(2,1)S(1)}, bf16[640,512]{1,0:T(8,128)(2,1)S(1)}, u32[]{:S(2)}, u32[]{:S(2)}) %collective-permute-start.18) | collective-permute-done | bytes 655392 | tf_op jit(solution)/shard_map/ppermute | solution.py:756
  319.2 7.5 %join_norm.3 = (bf16[1280,2048]{1,0:T(8,128)(2,1)}, f32[1280,128]{1,0:T(8,128)}, f32[1280,128]{1,0:T(8,128)}) custom-call(s32[1]{0:T(128)} %bitcast.row, bf16[1280,512]{1,0:T(8,128)(2,1)} %get-tuple-element.307.own, bf16[1280,512]{1,0:T(8,128)(2,1)} %collective-permute-done.15.from_x, bf16[1280,512]{1,0:T(8,128)(2,1)} %collective-permute-done.16.from_y, ...), custom_call_target="tpu_custom_call" | custom-call | flops 20971520 | bytes 10485760 | tf_op jit(solution)/shard_map/join_norm/pallas_call | solution.py:523
  326.8 12.8 %feed_up.1 = (bf16[1280,1024]{1,0:T(8,128)(2,1)}, bf16[1280,1024]{1,0:T(8,128)(2,1)}, f32[1,1024]{1,0:T(1,128)}) custom-call(bf16[1280,2048]{1,0:T(8,128)(2,1)} %get-tuple-element.151.values.refs_1_, bf16[2048,2048]{1,0:T(8,128)(2,1)} %all-gather.8.cloned.1.call-done.weight.refs_1_, f32[1,1024]{1,0:T(1,128)} %bitcast.111, bf16[1280,1024]{1,0:T(8,128)(2,1)} %matmul.3.grad_hidden), custom_call_target="tpu_custom_call" | custom-call | flops 5368709120 | bytes 19922944 | tf_op jit(solution)/shard_map/feed_up/pallas_call | solution.py:670
  339.6 7.5 %partial_blocks.10 = (bf16[2,640,512]{2,1,0:T(8,128)(2,1)}, bf16[2,640,512]{2,1,0:T(8,128)(2,1)}) custom-call(s32[1]{0:T(128)} %bitcast.row, bf16[1280,1024]{1,0:T(8,128)(2,1)} %get-tuple-element.153.refs_0_.refs_3_, bf16[2048,2048]{1,0:T(8,128)(2,1)} %all-gather.8.cloned.1.call-done.weight.refs_1_), custom_call_target="tpu_custom_call" | custom-call | flops 2684354560 | bytes 12058624 | tf_op jit(solution)/shard_map/partial_blocks/pallas_call | solution.py:736
  349.2 17.4 %weight_grads.4 = bf16[2048,2048]{1,0:T(8,128)(2,1)} custom-call(bf16[1280,2048]{1,0:T(8,128)(2,1)} %join.2.values.refs_0_, bf16[1280,2048]{1,0:T(8,128)(2,1)} %get-tuple-element.151.values.refs_1_, bf16[1280,1024]{1,0:T(8,128)(2,1)} %get-tuple-element.157.refs_0_.refs_2_, bf16[1280,1024]{1,0:T(8,128)(2,1)} %get-tuple-element.153.refs_0_.refs_3_), custom_call_target="tpu_custom_call" | custom-call | flops 10737418240 | bytes 18874368 | tf_op jit(solution)/shard_map/weight_grads/pallas_call | solution.py:634
  366.6 7.2 collective-permute-done.19
  374.7 7.7 %partial_blocks.12 = (bf16[2,640,512]{2,1,0:T(8,128)(2,1)}, f32[2,640,512]{2,1,0:T(8,128)}) custom-call(s32[1]{0:T(128)} %bitcast.row, bf16[1280,1024]{1,0:T(8,128)(2,1)} %get-tuple-element.153.refs_0_.refs_3_, bf16[2048,2048]{1,0:T(8,128)(2,1)} %all-gather.8.cloned.1.call-done.weight.refs_1_), custom_call_target="tpu_custom_call" | custom-call | flops 2684354560 | bytes 12058624 | tf_op jit(solution)/shard_map/partial_blocks/pallas_call | solution.py:736
  387.0 8.7 %collective-permute-done.21 = bf16[640,512]{1,0:T(8,128)(2,1)S(1)} collective-permute-done((bf16[640,512]{1,0:T(8,128)(2,1)S(1)}, bf16[640,512]{1,0:T(8,128)(2,1)S(1)}, u32[]{:S(2)}, u32[]{:S(2)}) %collective-permute-start.21) | collective-permute-done | bytes 655392 | tf_op jit(solution)/shard_map/ppermute | solution.py:756
  413.1 7.5 %partial_blocks.13 = (bf16[2,640,512]{2,1,0:T(8,128)(2,1)}, bf16[2,640,512]{2,1,0:T(8,128)(2,1)}) custom-call(s32[1]{0:T(128)} %bitcast.row, bf16[1280,1024]{1,0:T(8,128)(2,1)} %get-tuple-element.157.refs_0_.refs_2_, bf16[2048,2048]{1,0:T(8,128)(2,1)} %all-gather.8.cloned.1.call-done.weight.refs_1_), custom_call_target="tpu_custom_call" | custom-call | flops 2684354560 | bytes 12058624 | tf_op jit(solution)/shard_map/partial_blocks/pallas_call | solution.py:736
  420.6 15.0 %collective-permute-done.26.from_y = bf16[1280,512]{1,0:T(8,128)(2,1)} collective-permute-done((bf16[1280,512]{1,0:T(8,128)(2,1)}, bf16[1280,512]{1,0:T(8,128)(2,1)}, u32[]{:S(2)}, u32[]{:S(2)}) %collective-permute-start.26) | collective-permute-done | bytes 1310752 | tf_op jit(solution)/shard_map/ppermute | solution.py:756
  442.6 9.1 %collective-permute-done.28.far_b = bf16[640,512]{1,0:T(8,128)(2,1)S(1)} collective-permute-done((bf16[640,512]{1,0:T(8,128)(2,1)S(1)}, bf16[640,512]{1,0:T(8,128)(2,1)S(1)}, u32[]{:S(2)}, u32[]{:S(2)}) %collective-permute-start.28) | collective-permute-done | bytes 655392 | tf_op jit(solution)/shard_map/ppermute | solution.py:756
  453.0 5.3 join.3.refs_0_.wide
  458.3 9.9 %weight_grads.5 = bf16[2048,1024]{1,0:T(8,128)(2,1)} custom-call(bf16[1280,2048]{1,0:T(8,128)(2,1)} %join.3.refs_0_.wide, bf16[1280,1024]{1,0:T(8,128)(2,1)} %get-tuple-element.139.refs_0_.refs_1_), custom_call_target="tpu_custom_call" | custom-call | flops 5368709120 | bytes 14680064 | tf_op jit(solution)/shard_map/weight_grads/pallas_call | solution.py:634
  468.1 19.5 %reduce-scatter.5.cloned.1.call-done = bf16[256,2048]{1,0:T(8,128)(2,1)} async-done(((bf16[2048,2048]{1,0:T(8,128)(2,1)}), bf16[256,2048]{1,0:T(8,128)(2,1)}) %reduce-scatter.5.cloned.1.call-update) | async-done | bytes 1048592 | tf_op jit(solution)/shard_map/reduce_scatter | solution.py:839
  493.6 21.7 %gate_backward.1 = (bf16[1280,1024]{1,0:T(8,128)(2,1)}, bf16[1280,1024]{1,0:T(8,128)(2,1)}, f32[1,1024]{1,0:T(1,128)}, f32[1,1024]{1,0:T(1,128)}, bf16[8,2,256,5...) custom-call(s32[22]{0:T(128)} %pad_add_fusion.meta, f32[2]{0:T(128)} %subtract_log_fusion.rates, ...), custom_call_target="tpu_custom_call" | custom-call | flops 6039797760 | bytes 31457280 | tf_op jit(solution)/shard_map/gate_backward/pallas_call | solution.py:335
  515.3 4.0 collective-permute-done.29
  523.8 46.4 %return_states.1 = (bf16[2,256,512]{2,1,0:T(8,128)(2,1)S(1)}, bf16[2,256,512]{2,1,0:T(8,128)(2,1)S(1)}, bf16[2,256,512]{2,1,0:T(8,128)(2,1)S(1)}) custom-call(s32[22]{0:T(128)S(1)} %copy-done.6, f32[2]{0:T(128)S(1)} %copy-done.8, bf16[8,2,256,512]{3,2,1,0:T(8,128)(2,1)S(1)} %copy-done.2, bf16[2,256,512]{2,1,0:T(8,128)(2,1)S(1)} %copy-done.3), custom_call_target="tpu_custom_call" | custom-call | bytes 104857600 | tf_op jit(solution)/shard_map/return_states/pallas_call | solution.py:1073
  572.6 9.7 %weight_grads.6 = bf16[2048,1024]{1,0:T(8,128)(2,1)} custom-call(bf16[1280,2048]{1,0:T(8,128)(2,1)} %get-tuple-element.125.values.refs_0_.refs_1_.refs_2_, bf16[1280,1024]{1,0:T(8,128)(2,1)} %get-tuple-element.198.refs_1_.refs_3_), custom_call_target="tpu_custom_call" | custom-call | flops 5368709120 | bytes 14680064 | tf_op jit(solution)/shard_map/weight_grads/pallas_call | solution.py:634
  584.5 14.2 %retention_backward.1 = (bf16[1280,512]{1,0:T(8,128)(2,1)}, bf16[1280,512]{1,0:T(8,128)(2,1)}, bf16[1280,1024]{1,0:T(8,128)(2,1)}) custom-call(s32[22]{0:T(128)} %pad_add_fusion.meta, f32[2]{0:T(128)} %subtract_log_fusion.rates, bf16[1280,512]{1,0:T(8,128)(2,1)} %get-tuple-element.129.query, bf16[1280,512]{1,0:T(8,128)(2,1)} %get-tuple-element.130.key, ...), custom_call_target="tpu_custom_call" | custom-call | flops 5033164800 | bytes 15728640 | tf_op jit(solution)/shard_map/retention_backward/pallas_call | solution.py:429
  598.7 14.5 %partial_blocks.15 = (bf16[2,640,512]{2,1,0:T(8,128)(2,1)}, bf16[2,640,512]{2,1,0:T(8,128)(2,1)}) custom-call(s32[1]{0:T(128)} %bitcast.row, bf16[1280,512]{1,0:T(8,128)(2,1)} %get-tuple-element.206.refs_0_.refs_3_, bf16[1280,512]{1,0:T(8,128)(2,1)} %get-tuple-element.207.refs_1_.refs_4_, bf16[1280,1024]{1,0:T(8,128)(2,1)} %get-tuple-element.214.refs_2_.refs_5_, ...), custom_call_target="tpu_custom_call" | custom-call | flops 8053063680 | bytes 25690112 | tf_op jit(solution)/shard_map/partial_blocks/pallas_call | solution.py:736
  615.5 20.2 %weight_grads.7 = bf16[2048,2048]{1,0:T(8,128)(2,1)} custom-call(bf16[1280,2048]{1,0:T(8,128)(2,1)} %get-tuple-element.125.values.refs_0_.refs_1_.refs_2_, bf16[1280,2048]{1,0:T(8,128)(2,1)} %get-tuple-element.125.values.refs_0_.refs_1_.refs_2_, bf16[1280,2048]{1,0:T(8,128)(2,1)} %get-tuple-element.125.values.refs_0_.refs_1_.refs_2_, ...), custom_call_target="tpu_custom_call" | custom-call | flops 10737418240 | bytes 18874368 | tf_op jit(solution)/shard_map/weight_grads/pallas_call | solution.py:634
  635.7 4.9 collective-permute-done.33
  647.4 3.6 collective-permute-start.42
  651.0 8.1 %partial_blocks.11 = (bf16[2,640,512]{2,1,0:T(8,128)(2,1)}, f32[2,640,512]{2,1,0:T(8,128)}) custom-call(s32[1]{0:T(128)} %bitcast.row, bf16[1280,1024]{1,0:T(8,128)(2,1)} %get-tuple-element.157.refs_0_.refs_2_, bf16[2048,2048]{1,0:T(8,128)(2,1)} %all-gather.8.cloned.1.call-done.weight.refs_1_), custom_call_target="tpu_custom_call" | custom-call | flops 2684354560 | bytes 12058624 | tf_op jit(solution)/shard_map/partial_blocks/pallas_call | solution.py:736
  665.3 3.1 fusion.17
  671.0 14.8 %partial_blocks.14 = (bf16[2,640,512]{2,1,0:T(8,128)(2,1)}, f32[2,640,512]{2,1,0:T(8,128)}) custom-call(s32[1]{0:T(128)} %bitcast.row, bf16[1280,512]{1,0:T(8,128)(2,1)} %get-tuple-element.206.refs_0_.refs_3_, bf16[1280,512]{1,0:T(8,128)(2,1)} %get-tuple-element.207.refs_1_.refs_4_, bf16[1280,1024]{1,0:T(8,128)(2,1)} %get-tuple-element.214.refs_2_.refs_5_, ...), custom_call_target="tpu_custom_call" | custom-call | flops 8053063680 | bytes 25690112 | tf_op jit(solution)/shard_map/partial_blocks/pallas_call | solution.py:736
  693.0 4.2 fusion.11
  697.2 6.8 collective-permute-done.35
  728.9 3.9 fusion.7
  732.7 3.8 reduce-scatter.11.cloned.1.call-done
  (293 shorter events, 158.4 us)
Async XLA Ops:
  7.2 87.8 %all-gather.4.cloned.1.call-start = ((), (), s32[]{:S(2)}) async-start(), calls=%async_computation.4 | async-start | bytes 9437184 | tf_op jit(solution)/shard_map/all_gather | solution.py:835
  9.6 174.2 %all-gather.6.cloned.1.call-start = ((), (), s32[]{:S(2)}) async-start(), calls=%async_computation.5 | async-start | bytes 9437184 | tf_op jit(solution)/shard_map/all_gather | solution.py:835
  11.7 267.4 %all-gather.8.cloned.1.call-start = ((), (), s32[]{:S(2)}) async-start(), calls=%async_computation.6 | async-start | bytes 9437184 | tf_op jit(solution)/shard_map/all_gather | solution.py:835
  13.9 473.8 %reduce-scatter.5.cloned.1.call-start = ((), (), s32[]{:S(2)}) async-start(), calls=%async_computation.7 | async-start | bytes 9437184 | tf_op jit(solution)/shard_map/reduce_scatter | solution.py:839
  14.0 10.2 %collective-permute-start.5 = (f32[4,512]{1,0:T(4,128)S(1)}, f32[4,512]{1,0:T(4,128)S(1)}, u32[]{:S(2)}, u32[]{:S(2)}) collective-permute-start(f32[4,512]{1,0:T(4,128)S(1)} %get-tuple-element.350), channel_id=1, source_target_pairs={{0,16},{16,0},{8,24},{24,8},{1,17},{17,1},{9,25},{25,9},{2,18},{18... | collective-permute-start | bytes 24584 | tf_op jit(solution)/shard_map/ppermute | solution.py:756
  17.0 7.2 collective-permute-start.4
  18.5 5.7 collective-permute-start.6
  18.6 30.2 %collective-permute-start = (bf16[1280,512]{1,0:T(8,128)(2,1)S(1)}, bf16[1280,512]{1,0:T(8,128)(2,1)}, u32[]{:S(2)}, u32[]{:S(2)}) collective-permute-start(bf16[1280,512]{1,0:T(8,128)(2,1)S(1)} %copy-done.12), channel_id=1, source_target_pairs={{0,8},{8,0},{16,24},{24,16},{1,9},{9,1},{17,25},{25,17},{2,10},{10... | collective-permute-start | bytes 3932168 | tf_op jit(solution)/shard_map/ppermute | solution.py:756
  20.5 31.2 %collective-permute-start.1 = (bf16[1280,512]{1,0:T(8,128)(2,1)S(1)}, bf16[1280,512]{1,0:T(8,128)(2,1)}, u32[]{:S(2)}, u32[]{:S(2)}) collective-permute-start(bf16[1280,512]{1,0:T(8,128)(2,1)S(1)} %copy-done.12), channel_id=1, source_target_pairs={{0,16},{16,0},{8,24},{24,8},{1,17},{17,1},{9,25},{25,9},{2,18},{18... | collective-permute-start | bytes 3932168 | tf_op jit(solution)/shard_map/ppermute | solution.py:756
  50.0 15.1 %collective-permute-start.2 = (bf16[640,512]{1,0:T(8,128)(2,1)S(1)}, bf16[640,512]{1,0:T(8,128)(2,1)S(1)}, u32[]{:S(2)}, u32[]{:S(2)}) collective-permute-start(bf16[640,512]{1,0:T(8,128)(2,1)S(1)} %slice.244), channel_id=1, source_target_pairs={{0,16},{16,0},{8,24},{24,8},{1,17},{17,1},{9,25},{25,9},{2,18},{18... | collective-permute-start | bytes 1966088 | tf_op jit(solution)/shard_map/ppermute | solution.py:756
  52.8 14.5 %collective-permute-start.3 = (bf16[640,512]{1,0:T(8,128)(2,1)S(1)}, bf16[640,512]{1,0:T(8,128)(2,1)S(1)}, u32[]{:S(2)}, u32[]{:S(2)}) collective-permute-start(bf16[640,512]{1,0:T(8,128)(2,1)S(1)} %slice.245), channel_id=1, source_target_pairs={{0,8},{8,0},{16,24},{24,16},{1,9},{9,1},{17,25},{25,17},{2,10},{10... | collective-permute-start | bytes 1966088 | tf_op jit(solution)/shard_map/ppermute | solution.py:756
  75.6 36.3 %collective-permute-start.8 = (bf16[1280,512]{1,0:T(8,128)(2,1)S(1)}, bf16[1280,512]{1,0:T(8,128)(2,1)S(1)}, u32[]{:S(2)}, u32[]{:S(2)}) collective-permute-start(bf16[1280,512]{1,0:T(8,128)(2,1)S(1)} %multiply_convert_fusion.own), channel_id=1, source_target_pairs={{0,16},{16,0},{8,24},{24,8},{1,17},{17,1},{9,25},{25,9},{2,18},{18... | collective-permute-start | bytes 3932168 | tf_op jit(solution)/shard_map/ppermute | solution.py:756
  76.4 35.5 %collective-permute-start.7 = (bf16[1280,512]{1,0:T(8,128)(2,1)S(1)}, bf16[1280,512]{1,0:T(8,128)(2,1)}, u32[]{:S(2)}, u32[]{:S(2)}) collective-permute-start(bf16[1280,512]{1,0:T(8,128)(2,1)S(1)} %multiply_convert_fusion.own), channel_id=1, source_target_pairs={{0,8},{8,0},{16,24},{24,16},{1,9},{9,1},{17,25},{25,17},{2,10},{10... | collective-permute-start | bytes 3932168 | tf_op jit(solution)/shard_map/ppermute | solution.py:756
  113.6 80.7 %collective-permute-start.10 = (bf16[640,512]{1,0:T(8,128)(2,1)S(1)}, bf16[640,512]{1,0:T(8,128)(2,1)S(1)}, u32[]{:S(2)}, u32[]{:S(2)}) collective-permute-start(bf16[640,512]{1,0:T(8,128)(2,1)S(1)} %slice.190), channel_id=1, source_target_pairs={{0,8},{8,0},{16,24},{24,16},{1,9},{9,1},{17,25},{25,17},{2,10},{10... | collective-permute-start | bytes 1966088 | tf_op jit(solution)/shard_map/ppermute | solution.py:756
  115.2 79.1 %collective-permute-start.9 = (bf16[640,512]{1,0:T(8,128)(2,1)S(1)}, bf16[640,512]{1,0:T(8,128)(2,1)S(1)}, u32[]{:S(2)}, u32[]{:S(2)}) collective-permute-start(bf16[640,512]{1,0:T(8,128)(2,1)S(1)} %slice.189), channel_id=1, source_target_pairs={{0,16},{16,0},{8,24},{24,8},{1,17},{17,1},{9,25},{25,9},{2,18},{18... | collective-permute-start | bytes 1966088 | tf_op jit(solution)/shard_map/ppermute | solution.py:756
  218.6 31.1 %collective-permute-start.11 = (bf16[2,640,512]{2,1,0:T(8,128)(2,1)}, bf16[2,640,512]{2,1,0:T(8,128)(2,1)S(1)}, u32[]{:S(2)}, u32[]{:S(2)}) collective-permute-start(bf16[2,640,512]{2,1,0:T(8,128)(2,1)} %get-tuple-element.141), channel_id=1, source_target_pairs={{0,8},{8,0},{16,24},{24,16},{1,9},{9,1},{17,25},{25,17},{2,10},{10... | collective-permute-start | bytes 3932168 | tf_op jit(solution)/shard_map/ppermute | solution.py:756
  220.2 30.8 %collective-permute-start.13 = (bf16[2,640,512]{2,1,0:T(8,128)(2,1)}, bf16[2,640,512]{2,1,0:T(8,128)(2,1)S(1)}, u32[]{:S(2)}, u32[]{:S(2)}) collective-permute-start(bf16[2,640,512]{2,1,0:T(8,128)(2,1)} %get-tuple-element.143), channel_id=1, source_target_pairs={{0,16},{16,0},{8,24},{24,8},{1,17},{17,1},{9,25},{25,9},{2,18},{18... | collective-permute-start | bytes 3932168 | tf_op jit(solution)/shard_map/ppermute | solution.py:756
  252.8 15.8 %collective-permute-start.12 = (bf16[640,512]{1,0:T(8,128)(2,1)S(1)}, bf16[640,512]{1,0:T(8,128)(2,1)S(1)}, u32[]{:S(2)}, u32[]{:S(2)}) collective-permute-start(bf16[640,512]{1,0:T(8,128)(2,1)S(1)} %get-tuple-element.327), channel_id=1, source_target_pairs={{0,16},{16,0},{8,24},{24,8},{1,17},{17,1},{9,25},{25,9},{2,18},{18... | collective-permute-start | bytes 1966088 | tf_op jit(solution)/shard_map/ppermute | solution.py:756
  254.1 15.4 %collective-permute-start.14 = (bf16[640,512]{1,0:T(8,128)(2,1)S(1)}, bf16[640,512]{1,0:T(8,128)(2,1)S(1)}, u32[]{:S(2)}, u32[]{:S(2)}) collective-permute-start(bf16[640,512]{1,0:T(8,128)(2,1)S(1)} %get-tuple-element.328), channel_id=1, source_target_pairs={{0,8},{8,0},{16,24},{24,16},{1,9},{9,1},{17,25},{25,17},{2,10},{10... | collective-permute-start | bytes 1966088 | tf_op jit(solution)/shard_map/ppermute | solution.py:756
  272.4 28.9 %collective-permute-start.16 = (bf16[1280,512]{1,0:T(8,128)(2,1)}, bf16[1280,512]{1,0:T(8,128)(2,1)}, u32[]{:S(2)}, u32[]{:S(2)}) collective-permute-start(bf16[1280,512]{1,0:T(8,128)(2,1)} %get-tuple-element.307.own), channel_id=1, source_target_pairs={{0,16},{16,0},{8,24},{24,8},{1,17},{17,1},{9,25},{25,9},{2,18},{18... | collective-permute-start | bytes 3932168 | tf_op jit(solution)/shard_map/ppermute | solution.py:756
  273.3 28.7 %collective-permute-start.15 = (bf16[1280,512]{1,0:T(8,128)(2,1)}, bf16[1280,512]{1,0:T(8,128)(2,1)}, u32[]{:S(2)}, u32[]{:S(2)}) collective-permute-start(bf16[1280,512]{1,0:T(8,128)(2,1)} %get-tuple-element.307.own), channel_id=1, source_target_pairs={{0,8},{8,0},{16,24},{24,16},{1,9},{9,1},{17,25},{25,17},{2,10},{10... | collective-permute-start | bytes 3932168 | tf_op jit(solution)/shard_map/ppermute | solution.py:756
  304.3 13.5 %collective-permute-start.18 = (bf16[640,512]{1,0:T(8,128)(2,1)S(1)}, bf16[640,512]{1,0:T(8,128)(2,1)S(1)}, u32[]{:S(2)}, u32[]{:S(2)}) collective-permute-start(bf16[640,512]{1,0:T(8,128)(2,1)S(1)} %slice.200), channel_id=1, source_target_pairs={{0,8},{8,0},{16,24},{24,16},{1,9},{9,1},{17,25},{25,17},{2,10},{10... | collective-permute-start | bytes 1966088 | tf_op jit(solution)/shard_map/ppermute | solution.py:756
  305.1 13.3 %collective-permute-start.17 = (bf16[640,512]{1,0:T(8,128)(2,1)S(1)}, bf16[640,512]{1,0:T(8,128)(2,1)S(1)}, u32[]{:S(2)}, u32[]{:S(2)}) collective-permute-start(bf16[640,512]{1,0:T(8,128)(2,1)S(1)} %slice.199), channel_id=1, source_target_pairs={{0,16},{16,0},{8,24},{24,8},{1,17},{17,1},{9,25},{25,9},{2,18},{18... | collective-permute-start | bytes 1966088 | tf_op jit(solution)/shard_map/ppermute | solution.py:756
  347.1 26.7 %collective-permute-start.19 = (bf16[2,640,512]{2,1,0:T(8,128)(2,1)}, bf16[2,640,512]{2,1,0:T(8,128)(2,1)}, u32[]{:S(2)}, u32[]{:S(2)}) collective-permute-start(bf16[2,640,512]{2,1,0:T(8,128)(2,1)} %get-tuple-element.161), channel_id=1, source_target_pairs={{0,8},{8,0},{16,24},{24,16},{1,9},{9,1},{17,25},{25,17},{2,10},{10... | collective-permute-start | bytes 3932168 | tf_op jit(solution)/shard_map/ppermute | solution.py:756
  348.2 26.3 %collective-permute-start.20 = (bf16[2,640,512]{2,1,0:T(8,128)(2,1)}, bf16[2,640,512]{2,1,0:T(8,128)(2,1)}, u32[]{:S(2)}, u32[]{:S(2)}) collective-permute-start(bf16[2,640,512]{2,1,0:T(8,128)(2,1)} %get-tuple-element.162), channel_id=1, source_target_pairs={{0,16},{16,0},{8,24},{24,8},{1,17},{17,1},{9,25},{25,9},{2,18},{18... | collective-permute-start | bytes 3932168 | tf_op jit(solution)/shard_map/ppermute | solution.py:756
  374.6 207.7 %reduce-scatter.7.cloned.1.call-start = ((), (), s32[]{:S(2)}) async-start(), calls=%async_computation.8 | async-start | bytes 4718592 | tf_op jit(solution)/shard_map/reduce_scatter | solution.py:839
  384.6 11.1 %collective-permute-start.21 = (bf16[640,512]{1,0:T(8,128)(2,1)S(1)}, bf16[640,512]{1,0:T(8,128)(2,1)S(1)}, u32[]{:S(2)}, u32[]{:S(2)}) collective-permute-start(bf16[640,512]{1,0:T(8,128)(2,1)S(1)} %get-tuple-element.325), channel_id=1, source_target_pairs={{0,16},{16,0},{8,24},{24,8},{1,17},{17,1},{9,25},{25,9},{2,18},{18... | collective-permute-start | bytes 1966088 | tf_op jit(solution)/shard_map/ppermute | solution.py:756
  385.5 10.8 %collective-permute-start.22 = (bf16[640,512]{1,0:T(8,128)(2,1)S(1)}, bf16[640,512]{1,0:T(8,128)(2,1)S(1)}, u32[]{:S(2)}, u32[]{:S(2)}) collective-permute-start(bf16[640,512]{1,0:T(8,128)(2,1)S(1)} %get-tuple-element.326), channel_id=1, source_target_pairs={{0,8},{8,0},{16,24},{24,16},{1,9},{9,1},{17,25},{25,17},{2,10},{10... | collective-permute-start | bytes 1966088 | tf_op jit(solution)/shard_map/ppermute | solution.py:756
  410.7 25.0 %collective-permute-start.26 = (bf16[1280,512]{1,0:T(8,128)(2,1)}, bf16[1280,512]{1,0:T(8,128)(2,1)}, u32[]{:S(2)}, u32[]{:S(2)}) collective-permute-start(bf16[1280,512]{1,0:T(8,128)(2,1)} %get-tuple-element.305.own), channel_id=1, source_target_pairs={{0,16},{16,0},{8,24},{24,8},{1,17},{17,1},{9,25},{25,9},{2,18},{18... | collective-permute-start | bytes 3932168 | tf_op jit(solution)/shard_map/ppermute | solution.py:756
  412.0 26.8 %collective-permute-start.25 = (bf16[1280,512]{1,0:T(8,128)(2,1)}, bf16[1280,512]{1,0:T(8,128)(2,1)}, u32[]{:S(2)}, u32[]{:S(2)}) collective-permute-start(bf16[1280,512]{1,0:T(8,128)(2,1)} %get-tuple-element.305.own), channel_id=1, source_target_pairs={{0,8},{8,0},{16,24},{24,16},{1,9},{9,1},{17,25},{25,17},{2,10},{10... | collective-permute-start | bytes 3932168 | tf_op jit(solution)/shard_map/ppermute | solution.py:756
  441.1 10.7 %collective-permute-start.28 = (bf16[640,512]{1,0:T(8,128)(2,1)S(1)}, bf16[640,512]{1,0:T(8,128)(2,1)S(1)}, u32[]{:S(2)}, u32[]{:S(2)}) collective-permute-start(bf16[640,512]{1,0:T(8,128)(2,1)S(1)} %slice.217), channel_id=1, source_target_pairs={{0,8},{8,0},{16,24},{24,16},{1,9},{9,1},{17,25},{25,17},{2,10},{10... | collective-permute-start | bytes 1966088 | tf_op jit(solution)/shard_map/ppermute | solution.py:756
  442.3 10.7 %collective-permute-start.27 = (bf16[640,512]{1,0:T(8,128)(2,1)S(1)}, bf16[640,512]{1,0:T(8,128)(2,1)}, u32[]{:S(2)}, u32[]{:S(2)}) collective-permute-start(bf16[640,512]{1,0:T(8,128)(2,1)S(1)} %slice.216), channel_id=1, source_target_pairs={{0,16},{16,0},{8,24},{24,8},{1,17},{17,1},{9,25},{25,9},{2,18},{18... | collective-permute-start | bytes 1966088 | tf_op jit(solution)/shard_map/ppermute | solution.py:756
  490.5 151.8 %reduce-scatter.9.cloned.1.call-start = ((), (), s32[]{:S(2)}) async-start(), calls=%async_computation.9 | async-start | bytes 4718592 | tf_op jit(solution)/shard_map/reduce_scatter | solution.py:839
  490.6 28.7 %collective-permute-start.29 = (bf16[2,640,512]{2,1,0:T(8,128)(2,1)}, bf16[2,640,512]{2,1,0:T(8,128)(2,1)}, u32[]{:S(2)}, u32[]{:S(2)}) collective-permute-start(bf16[2,640,512]{2,1,0:T(8,128)(2,1)} %get-tuple-element.175), channel_id=1, source_target_pairs={{0,8},{8,0},{16,24},{24,16},{1,9},{9,1},{17,25},{25,17},{2,10},{10... | collective-permute-start | bytes 3932168 | tf_op jit(solution)/shard_map/ppermute | solution.py:756
  492.1 28.4 %collective-permute-start.30 = (bf16[2,640,512]{2,1,0:T(8,128)(2,1)}, bf16[2,640,512]{2,1,0:T(8,128)(2,1)}, u32[]{:S(2)}, u32[]{:S(2)}) collective-permute-start(bf16[2,640,512]{2,1,0:T(8,128)(2,1)} %get-tuple-element.176), channel_id=1, source_target_pairs={{0,16},{16,0},{8,24},{24,8},{1,17},{17,1},{9,25},{25,9},{2,18},{18... | collective-permute-start | bytes 3932168 | tf_op jit(solution)/shard_map/ppermute | solution.py:756
  584.4 152.0 %reduce-scatter.11.cloned.1.call-start = ((), (), s32[]{:S(2)}) async-start(), calls=%async_computation.10 | async-start | bytes 9437184 | tf_op jit(solution)/shard_map/reduce_scatter | solution.py:839
  613.2 27.5 %collective-permute-start.33 = (bf16[2,640,512]{2,1,0:T(8,128)(2,1)}, bf16[2,640,512]{2,1,0:T(8,128)(2,1)}, u32[]{:S(2)}, u32[]{:S(2)}) collective-permute-start(bf16[2,640,512]{2,1,0:T(8,128)(2,1)} %get-tuple-element.212), channel_id=1, source_target_pairs={{0,8},{8,0},{16,24},{24,16},{1,9},{9,1},{17,25},{25,17},{2,10},{10... | collective-permute-start | bytes 3932168 | tf_op jit(solution)/shard_map/ppermute | solution.py:756
  614.0 27.8 %collective-permute-start.34 = (bf16[2,640,512]{2,1,0:T(8,128)(2,1)}, bf16[2,640,512]{2,1,0:T(8,128)(2,1)}, u32[]{:S(2)}, u32[]{:S(2)}) collective-permute-start(bf16[2,640,512]{2,1,0:T(8,128)(2,1)} %get-tuple-element.213), channel_id=1, source_target_pairs={{0,16},{16,0},{8,24},{24,8},{1,17},{17,1},{9,25},{25,9},{2,18},{18... | collective-permute-start | bytes 3932168 | tf_op jit(solution)/shard_map/ppermute | solution.py:756
  647.4 11.7 %collective-permute-start.42 = (f32[36,128]{1,0:T(8,128)S(1)}, f32[36,128]{1,0:T(8,128)S(1)}, u32[]{:S(2)}, u32[]{:S(2)}) collective-permute-start(f32[36,128]{1,0:T(8,128)S(1)} %bitcast.89), channel_id=1, source_target_pairs={{0,1},{1,0},{2,3},{3,2},{4,5},{5,4},{6,7},{7,6},{8,9},{9,8},{10,11... | collective-permute-start | bytes 55304 | tf_op jit(solution)/shard_map/ppermute | solution.py:1099
  659.1 6.0 collective-permute-start.43
  665.2 5.8 collective-permute-start.44
  668.4 22.1 %collective-permute-start.31 = (bf16[640,512]{1,0:T(8,128)(2,1)}, bf16[640,512]{1,0:T(8,128)(2,1)S(1)}, u32[]{:S(2)}, u32[]{:S(2)}) collective-permute-start(bf16[640,512]{1,0:T(8,128)(2,1)} %get-tuple-element.323), channel_id=1, source_target_pairs={{0,16},{16,0},{8,24},{24,8},{1,17},{17,1},{9,25},{25,9},{2,18},{18... | collective-permute-start | bytes 1966088 | tf_op jit(solution)/shard_map/ppermute | solution.py:756
  669.8 20.7 %collective-permute-start.32 = (bf16[640,512]{1,0:T(8,128)(2,1)}, bf16[640,512]{1,0:T(8,128)(2,1)}, u32[]{:S(2)}, u32[]{:S(2)}) collective-permute-start(bf16[640,512]{1,0:T(8,128)(2,1)} %get-tuple-element.324), channel_id=1, source_target_pairs={{0,8},{8,0},{16,24},{24,16},{1,9},{9,1},{17,25},{25,17},{2,10},{10... | collective-permute-start | bytes 1966088 | tf_op jit(solution)/shard_map/ppermute | solution.py:756
  688.0 16.1 %collective-permute-start.35 = (bf16[640,512]{1,0:T(8,128)(2,1)S(1)}, bf16[640,512]{1,0:T(8,128)(2,1)S(1)}, u32[]{:S(2)}, u32[]{:S(2)}) collective-permute-start(bf16[640,512]{1,0:T(8,128)(2,1)S(1)} %get-tuple-element.321), channel_id=1, source_target_pairs={{0,16},{16,0},{8,24},{24,8},{1,17},{17,1},{9,25},{25,9},{2,18},{18... | collective-permute-start | bytes 1966088 | tf_op jit(solution)/shard_map/ppermute | solution.py:756
  689.3 15.6 %collective-permute-start.36 = (bf16[640,512]{1,0:T(8,128)(2,1)S(1)}, bf16[640,512]{1,0:T(8,128)(2,1)S(1)}, u32[]{:S(2)}, u32[]{:S(2)}) collective-permute-start(bf16[640,512]{1,0:T(8,128)(2,1)S(1)} %get-tuple-element.322), channel_id=1, source_target_pairs={{0,8},{8,0},{16,24},{24,16},{1,9},{9,1},{17,25},{25,17},{2,10},{10... | collective-permute-start | bytes 1966088 | tf_op jit(solution)/shard_map/ppermute | solution.py:756
  713.2 9.1 %collective-permute-start.37 = (f32[2,1280]{1,0:T(2,128)S(1)}, f32[2,1280]{1,0:T(2,128)S(1)}, u32[]{:S(2)}, u32[]{:S(2)}) collective-permute-start(f32[2,1280]{1,0:T(2,128)S(1)} %pad_maximum_fusion.9), channel_id=1, source_target_pairs={{0,8},{8,0},{16,24},{24,16},{1,9},{9,1},{17,25},{25,17},{2,10},{10... | collective-permute-start | bytes 30728 | tf_op jit(solution)/shard_map/ppermute | solution.py:756
  716.1 5.0 collective-permute-start.41
  722.3 6.5 collective-permute-start.38
  (61 other events, 335.6 us)
Sparse Core Ops, SparseCore 0:
  10.2 84.7 all-gather.3
  97.2 86.5 all-gather.5
  186.0 92.1 all-gather.7
  374.7 112.9 reduce-scatter.4
  490.6 65.5 reduce-scatter.6
  584.6 57.6 reduce-scatter.8
  644.6 91.8 reduce-scatter.10

commit v3 on v2

--- a/solution.py
+++ b/solution.py
@@ -89,11 +89,15 @@
     return lax.broadcasted_iota(jnp.int32, (CHUNK, width), 0)
 
 
-def decay_matrix(rate, count):
+def decay_matrix(rate):
     t = lax.broadcasted_iota(jnp.int32, (CHUNK, CHUNK), 0)
     u = lax.broadcasted_iota(jnp.int32, (CHUNK, CHUNK), 1)
-    seen = (u <= t) & (u < count)
-    return jnp.where(seen, jnp.exp((t - u).astype(F32) * rate) * SCALE, 0.0)
+    return jnp.where(u <= t, jnp.exp((t - u).astype(F32) * rate) * SCALE, 0.0)
+
+
+def valid_decay(decay, count):
+    u = lax.broadcasted_iota(jnp.int32, (1, CHUNK), 1)
+    return decay[...] * jnp.where(u < count, 1.0, 0.0)
 
 
 def key_decay(rate, count):
@@ -132,57 +136,9 @@
     return (place == 5) | (place == 7), CHUNK - previous.count
 
 
-def states_kernel(rows, chunks, meta, rates, key, value, out, acc):
-    local = pl.program_id(1)
-    rate = rates[pl.program_id(0)]
-    place = meta[21]
-    chunk = Chunk(meta, place * chunks + local)
-    weighted = (key[...].astype(F32) * key_decay(rate, chunk.count)).astype(BF16)
-    state = mm_tn(weighted, value[...])
-
-    @pl.when(local == 0)
-    def _():
-        acc[...] = jnp.zeros_like(acc)
-
-    for slot in range(3):
-        on, exponent = export_terms(meta, chunk, local, chunks, place, slot, rows)
-
-        @pl.when(on)
-        def _():
-            acc[slot] += state * power(rate, exponent, HV)
-
-    @pl.when(local == chunks - 1)
-    def _():
-        out[:, 0] = acc[...].astype(BF16)
-
-
-def make_states(meta, rates, key, value):
-    rows = key.shape[0]
-    heads = key.shape[1] // QK
-    chunks = rows // CHUNK
-    return pl.pallas_call(
-        functools.partial(states_kernel, rows, chunks),
-        grid=(heads, chunks),
-        in_specs=[
-            smem(),
-            smem(),
-            pl.BlockSpec((CHUNK, QK), lambda h, c: (c, h)),
-            pl.BlockSpec((CHUNK, HV), lambda h, c: (c, h)),
-        ],
-        out_specs=pl.BlockSpec((3, 1, QK, HV), lambda h, c: (0, h, 0, 0)),
-        out_shape=jax.ShapeDtypeStruct((3, heads, QK, HV), BF16),
-        scratch_shapes=[pltpu.VMEM((3, QK, HV), F32)],
-        compiler_params=params(("arbitrary", "arbitrary")),
-        name="chunk_states",
-        cost_estimate=pl.CostEstimate(
-            flops=2 * rows * heads * QK * HV, bytes_accessed=rows * heads * 1536, transcendentals=0
-        ),
-    )(meta, rates, key, value)
-
-
 def retain_kernel(
-    rows, chunks, meta, rates, query, key, value, gate, shared, shifted, gain, bias,
-    gated_out, normal_out, inverse_out, state_out, running, total,
+    rows, chunks, meta, rates, query, key, value, wide, weight, shared, shifted, gain, bias,
+    gate_out, gated_out, normal_out, inverse_out, state_out, running, total, decay,
 ):
     local = pl.program_id(1)
     rate = rates[pl.program_id(0)]
@@ -191,6 +147,7 @@
 
     @pl.when(local == 0)
     def _():
+        decay[...] = decay_matrix(rate)
         running[...] = jnp.zeros_like(running)
         on, exponent = shift_in(meta, place, chunks)
 
@@ -211,7 +168,7 @@
     state_out[0, 0] = state
 
     q, k, v = query[...], key[...], value[...]
-    scores = (mm_nt(q, k) * decay_matrix(rate, chunk.count)).astype(BF16)
+    scores = (mm_nt(q, k) * valid_decay(decay, chunk.count)).astype(BF16)
     own = token_column()
     reach = column_power(rate, own) * SCALE
     retained = mm(scores, v) + mm(q, state) * reach
@@ -226,14 +183,16 @@
     centred = retained - average
     inverse = lax.rsqrt(jnp.mean(centred * centred, axis=1, keepdims=True) + EPSILON)
     normal = centred * inverse
-    gate_value = gate[...].astype(F32)
+    gate_value = mm(wide[...], weight[...])
+    gate_out[...] = gate_value
     gated = (normal * gain[...] + bias[...]) * (gate_value / (1.0 + jnp.exp(-gate_value)))
     gated_out[...] = gated.astype(BF16)
     normal_out[...] = normal.astype(BF16)
     inverse_out[0] = jnp.broadcast_to(inverse, (CHUNK, 128))
 
 
-def retain(meta, rates, query, key, value, gate, shared, shifted, gain, bias):
+def retain(meta, rates, query, key, value, inputs, weight, shared, shifted, gain, bias):
+    array, _, number = weight
     rows = key.shape[0]
     heads = key.shape[1] // QK
     chunks = rows // CHUNK
@@ -244,31 +203,36 @@
         functools.partial(retain_kernel, rows, chunks),
         grid=(heads, chunks),
         in_specs=[
-            smem(), smem(), narrow, narrow, wide, wide,
+            smem(), smem(), narrow, narrow, wide,
+            pl.BlockSpec((CHUNK, D), lambda h, c: (c, 0)),
+            pl.BlockSpec((D, HV), lambda h, c: (0, number * heads + h)),
             pl.BlockSpec((SLOTS, 1, QK, HV), lambda h, c: (0, h, 0, 0)),
             pl.BlockSpec((1, QK, HV), lambda h, c: (h, 0, 0)),
             vector, vector,
         ],
         out_specs=[
-            wide, wide,
+            wide, wide, wide,
             pl.BlockSpec((1, CHUNK, 128), lambda h, c: (h, c, 0)),
             pl.BlockSpec((1, 1, QK, HV), lambda h, c: (h, c, 0, 0)),
         ],
         out_shape=[
+            jax.ShapeDtypeStruct((rows, heads * HV), F32),
             jax.ShapeDtypeStruct((rows, heads * HV), BF16),
             jax.ShapeDtypeStruct((rows, heads * HV), BF16),
             jax.ShapeDtypeStruct((heads, rows, 128), F32),
             jax.ShapeDtypeStruct((heads, chunks, QK, HV), BF16),
         ],
-        scratch_shapes=[pltpu.VMEM((QK, HV), F32), pltpu.VMEM((QK, HV), F32)],
+        scratch_shapes=[
+            pltpu.VMEM((QK, HV), F32), pltpu.VMEM((QK, HV), F32), pltpu.VMEM((CHUNK, CHUNK), F32)
+        ],
         compiler_params=params(("arbitrary", "arbitrary")),
         name="retention_forward",
         cost_estimate=pl.CostEstimate(
-            flops=2 * rows * heads * (CHUNK * 768 + 2 * QK * HV),
+            flops=2 * rows * heads * (CHUNK * 768 + 2 * QK * HV + D * HV),
             bytes_accessed=rows * heads * 8192,
             transcendentals=rows * heads * 768,
         ),
-    )(meta, rates, query, key, value, gate, shared, shifted, gain[None, :], bias[None, :])
+    )(meta, rates, query, key, value, inputs, array, shared, shifted, gain[None, :], bias[None, :])
 
 
 def gate_back_kernel(
@@ -370,7 +334,7 @@
 
 def retain_back_kernel(
     rows, chunks, meta, rates, query, key, value, grad, state_in, cosine, sine, own0, own1, own2,
-    query_out, key_out, value_out, running, total_ref,
+    query_out, key_out, value_out, running, total_ref, decay_ref,
 ):
     step = pl.program_id(1)
     local = chunks - 1 - step
@@ -381,6 +345,7 @@
 
     @pl.when(step == 0)
     def _():
+        decay_ref[...] = decay_matrix(rate)
         running[...] = jnp.zeros_like(running)
 
     later = running[...]
@@ -395,7 +360,7 @@
     total = total_ref[...].astype(BF16)
 
     q, k, v, g = query[...], key[...], value[...], grad[...]
-    decay = decay_matrix(rate, chunk.count)
+    decay = valid_decay(decay_ref, chunk.count)
     scores = (mm_nt(q, k) * decay).astype(BF16)
     slopes = (mm_nt(g, v) * decay).astype(BF16)
     reach = column_power(rate, token_column()) * SCALE
@@ -440,7 +405,9 @@
             jax.ShapeDtypeStruct((rows, heads * QK), BF16),
             jax.ShapeDtypeStruct((rows, heads * HV), BF16),
         ],
-        scratch_shapes=[pltpu.VMEM((QK, HV), F32), pltpu.VMEM((QK, HV), F32)],
+        scratch_shapes=[
+            pltpu.VMEM((QK, HV), F32), pltpu.VMEM((QK, HV), F32), pltpu.VMEM((CHUNK, CHUNK), F32)
+        ],
         compiler_params=params(("arbitrary", "arbitrary")),
         name="retention_backward",
         cost_estimate=pl.CostEstimate(
@@ -537,7 +504,13 @@
     )(row, *pieces, *((gain[None, :], bias[None, :]) if norm else ()))
 
 
-def project_kernel(heads, values, weight, cosine, sine, query_out, key_out, value_out):
+def project_kernel(
+    heads, rows, chunks, meta, rates, values, weight, cosine, sine,
+    query_out, key_out, value_out, exports, acc,
+):
+    local = pl.program_id(0)
+    place = meta[21]
+    chunk = Chunk(meta, place * chunks + local)
     raw = mm(values[...], weight[...])
     cos, sin = cosine[...], sine[...]
     half = QK // 2
@@ -549,28 +522,54 @@
             out[:, head * QK + half : (head + 1) * QK] = (b * cos + a * sin).astype(BF16)
     value_out[...] = raw[:, 2 * heads * QK :].astype(BF16)
 
-
-def project(values, weight, cosine, sine):
+    @pl.when(local == 0)
+    def _():
+        acc[...] = jnp.zeros_like(acc)
+
+    for head in range(heads):
+        rate = rates[head]
+        key = key_out[:, head * QK : (head + 1) * QK].astype(F32)
+        weighted = (key * key_decay(rate, chunk.count)).astype(BF16)
+        state = mm_tn(weighted, value_out[:, head * HV : (head + 1) * HV])
+        for slot in range(3):
+            on, exponent = export_terms(meta, chunk, local, chunks, place, slot, rows)
+
+            @pl.when(on)
+            def _():
+                acc[slot, head] += state * power(rate, exponent, HV)
+
+    @pl.when(local == chunks - 1)
+    def _():
+        exports[...] = acc[...].astype(BF16)
+
+
+def project(meta, rates, values, weight, cosine, sine):
     rows, width = values.shape[0], weight.shape[1]
     heads = width // (2 * QK + HV)
+    chunks = rows // CHUNK
     table = pl.BlockSpec((CHUNK, QK // 2), lambda i: (i, 0))
     widths = (heads * QK, heads * QK, heads * HV)
+    states = (3, heads, QK, HV)
     return pl.pallas_call(
-        functools.partial(project_kernel, heads),
-        grid=(rows // CHUNK,),
+        functools.partial(project_kernel, heads, rows, chunks),
+        grid=(chunks,),
         in_specs=[
+            smem(), smem(),
             pl.BlockSpec((CHUNK, D), lambda i: (i, 0)),
             pl.BlockSpec((D, width), lambda i: (0, 0)),
             table, table,
         ],
-        out_specs=[pl.BlockSpec((CHUNK, w), lambda i: (i, 0)) for w in widths],
-        out_shape=[jax.ShapeDtypeStruct((rows, w), BF16) for w in widths],
+        out_specs=[pl.BlockSpec((CHUNK, w), lambda i: (i, 0)) for w in widths]
+        + [pl.BlockSpec(states, lambda i: (0, 0, 0, 0))],
+        out_shape=[jax.ShapeDtypeStruct((rows, w), BF16) for w in widths]
+        + [jax.ShapeDtypeStruct(states, BF16)],
+        scratch_shapes=[pltpu.VMEM(states, F32)],
         compiler_params=params(("arbitrary",)),
         name="project",
         cost_estimate=pl.CostEstimate(
             flops=2 * rows * D * width, bytes_accessed=2 * (rows + width) * D, transcendentals=0
         ),
-    )(values, weight, cosine, sine)
+    )(meta, rates, values, weight, cosine, sine)
 
 
 def matmul_kernel(values, weight, out):
@@ -647,7 +646,139 @@
     )(*[left for left, _ in pairs], *[right for _, right in pairs])
 
 
-def up_kernel(values, weight, bias, grad_hidden, hidden_out, grad_out, bias_out):
+def paired_grad_kernel(spans, tiles, steps, *refs):
+    count = len(spans)
+    lefts, rights, out = refs[:count], refs[count : 2 * count], refs[2 * count]
+    made, received, send_sem, recv_sem = refs[2 * count + 1 :]
+    step = pl.program_id(0)
+    core = lax.axis_index("col") % 2
+    partner = lax.axis_index("col") + 1 - 2 * core
+
+    def copy(index):
+        return pltpu.make_async_remote_copy(
+            src_ref=made.at[index, :, 1 - core],
+            dst_ref=received.at[index],
+            send_sem=send_sem.at[index],
+            recv_sem=recv_sem.at[index],
+            device_id={"col": partner},
+            device_id_type=pl.DeviceIdType.MESH,
+        )
+
+    @pl.when(step == 0)
+    def _():
+        barrier = pltpu.get_barrier_semaphore()
+        pl.semaphore_signal(
+            barrier, inc=1, device_id={"col": partner}, device_id_type=pl.DeviceIdType.MESH
+        )
+        pl.semaphore_wait(barrier, 1)
+
+    for left, right, (first, last) in zip(lefts, rights, spans):
+
+        @pl.when((step >= first * steps) & (step < last * steps))
+        def _():
+            total = mm_tn(left[...], right[...]).astype(BF16)
+            made[step] = total.reshape(made.shape[1:])
+
+    @pl.when(step < tiles)
+    def _():
+        copy(step).start()
+
+    @pl.when(step > 0)
+    def _():
+        index = step - 1
+        copy(index).wait()
+        out[...] = (made[index, :, core].astype(F32) + received[index].astype(F32)).astype(BF16)
+
+
+def paired_grads(pairs, number):
+    rows = pairs[0][0].shape[0]
+    wide = min(right.shape[1] for _, right in pairs)
+    wide = min(wide, 512)
+    tall = 1024
+    steps = D // tall
+    block = D // SLOTS
+    depth = tall // block // 2
+    spans, first = [], 0
+    for _, right in pairs:
+        spans.append((first, first + right.shape[1] // wide))
+        first = spans[-1][1]
+    tiles = first * steps
+
+    def left_spec(span):
+        def index(s):
+            n, m = s // steps, s % steps
+            return 0, jnp.where(n < span[0], 0, jnp.where(n < span[1], m, steps - 1))
+
+        return pl.BlockSpec((rows, tall), index)
+
+    def right_spec(span):
+        def index(s):
+            return 0, jnp.clip(s // steps - span[0], 0, span[1] - span[0] - 1)
+
+        return pl.BlockSpec((rows, wide), index)
+
+    def out_index(s):
+        done = jnp.maximum(s - 1, 0)
+        return done % steps, 0, done // steps
+
+    result = pl.pallas_call(
+        functools.partial(paired_grad_kernel, tuple(spans), tiles, steps),
+        grid=(tiles + 1,),
+        in_specs=[left_spec(span) for span in spans] + [right_spec(span) for span in spans],
+        out_specs=pl.BlockSpec((depth, block, wide), out_index),
+        out_shape=jax.ShapeDtypeStruct((SLOTS // 2, block, first * wide), BF16),
+        scratch_shapes=[
+            pltpu.VMEM((tiles, depth, 2, block, wide), BF16),
+            pltpu.VMEM((tiles, depth, block, wide), BF16),
+            pltpu.SemaphoreType.DMA((tiles,)),
+            pltpu.SemaphoreType.DMA((tiles,)),
+        ],
+        compiler_params=pltpu.CompilerParams(
+            dimension_semantics=("arbitrary",),
+            collective_id=number,
+            has_side_effects=True,
+            vmem_limit_bytes=60 * 1024 * 1024,
+        ),
+        name="paired_grads",
+        cost_estimate=pl.CostEstimate(
+            flops=2 * rows * D * first * wide,
+            bytes_accessed=2 * D * first * wide + 4 * rows * D,
+            transcendentals=0,
+        ),
+    )(*[left for left, _ in pairs], *[right for _, right in pairs])
+    return result
+
+
+def column_grads(pairs, number):
+    if lax.axis_size("col") != SLOTS:
+        return weight_grads(pairs)
+    return paired_grads(pairs, number)
+
+
+def norm_pieces(row, own, from_x, from_y, far_a, far_b, gain, bias, out, average_out, inverse_out):
+    block = own.shape[1]
+    second = pl.program_id(0) >= pl.num_programs(0) // 2
+    far = jnp.where(second, far_b[...], far_a[...])
+    pieces = [piece.astype(F32) for piece in (own[...], from_x[...], from_y[...], far)]
+    average = sum(jnp.sum(piece, axis=1, keepdims=True) for piece in pieces) / D
+    squares = sum(jnp.sum(piece * piece, axis=1, keepdims=True) for piece in pieces) / D
+    inverse = lax.rsqrt(squares - average * average + EPSILON)
+    for flip, piece in enumerate(pieces):
+        spot = pl.ds(pl.multiple_of((row[0] ^ flip) * block, 128), block)
+        out[:, spot] = ((piece - average) * inverse * gain[:, spot] + bias[:, spot]).astype(BF16)
+    average_out[...] = jnp.broadcast_to(average, average_out.shape)
+    inverse_out[...] = jnp.broadcast_to(inverse, inverse_out.shape)
+
+
+def up_kernel(row, *refs, joined):
+    if joined:
+        pieces, gain, norm_bias = refs[:5], refs[5], refs[6]
+        weight, bias, grad_hidden, second_out, average_out, inverse_out = refs[7:13]
+        hidden_out, grad_out, bias_out = refs[13:]
+        norm_pieces(row, *pieces, gain, norm_bias, second_out, average_out, inverse_out)
+        values = second_out
+    else:
+        values, weight, bias, grad_hidden, hidden_out, grad_out, bias_out = refs
     before = mm(values[...], weight[...]) + bias[...]
     phi = 0.5 * (1.0 + lax.erf(before * (0.5**0.5)))
     hidden_out[...] = (before * phi).astype(BF16)
@@ -662,21 +793,48 @@
     bias_out[...] += jnp.sum(grad.astype(F32), axis=0, keepdims=True)
 
 
-def feed_up(values, weight, bias, grad_hidden):
+def feed_up(pieces, row, gain, norm_bias, weight, bias, grad_hidden):
     array, width, number = weight
-    rows = values.shape[0]
-    block = pl.BlockSpec((CHUNK, width), lambda i: (i, 0))
-    vector = pl.BlockSpec((1, width), lambda i: (0, 0))
-    return pl.pallas_call(
-        up_kernel,
-        grid=(rows // CHUNK,),
-        in_specs=[
-            pl.BlockSpec((CHUNK, D), lambda i: (i, 0)),
-            pl.BlockSpec((D, width), lambda i: (0, number)),
-            vector, block,
-        ],
-        out_specs=[block, block, vector],
-        out_shape=[
+    joined = isinstance(pieces, tuple)
+    rows = grad_hidden.shape[0]
+    steps = 4
+    tile = rows // steps
+    block = pl.BlockSpec((tile, width), lambda i, r: (i, 0))
+    vector = pl.BlockSpec((1, width), lambda i, r: (0, 0))
+    wide = pl.BlockSpec((tile, D), lambda i, r: (i, 0))
+    stat = pl.BlockSpec((tile, 128), lambda i, r: (i, 0))
+    gains = pl.BlockSpec((1, D), lambda i, r: (0, 0))
+    if joined:
+        piece = pl.BlockSpec((tile, pieces[0].shape[1]), lambda i, r: (i, 0))
+        far_a = pl.BlockSpec(
+            (tile, pieces[0].shape[1]), lambda i, r: (jnp.minimum(i, steps // 2 - 1), 0)
+        )
+        far_b = pl.BlockSpec(
+            (tile, pieces[0].shape[1]), lambda i, r: (jnp.maximum(i - steps // 2, 0), 0)
+        )
+        inputs = list(pieces) + [gain[None, :], norm_bias[None, :]]
+        in_specs = [piece] * 3 + [far_a, far_b, gains, gains]
+        early_specs = [wide, stat, stat]
+        early_shapes = [
+            jax.ShapeDtypeStruct((rows, D), BF16),
+            jax.ShapeDtypeStruct((rows, 128), F32),
+            jax.ShapeDtypeStruct((rows, 128), F32),
+        ]
+        normed = []
+    else:
+        normed = list(norm_wide(pieces, gain, norm_bias))
+        inputs, in_specs, early_specs, early_shapes = [normed[0]], [wide], [], []
+    outs = pl.pallas_call(
+        functools.partial(up_kernel, joined=joined),
+        grid_spec=pltpu.PrefetchScalarGridSpec(
+            num_scalar_prefetch=1,
+            grid=(steps,),
+            in_specs=in_specs
+            + [pl.BlockSpec((D, width), lambda i, r: (0, number)), vector, block],
+            out_specs=early_specs + [block, block, vector],
+        ),
+        out_shape=early_shapes
+        + [
             jax.ShapeDtypeStruct((rows, width), BF16),
             jax.ShapeDtypeStruct((rows, width), BF16),
             jax.ShapeDtypeStruct((1, width), F32),
@@ -685,10 +843,11 @@
         name="feed_up",
         cost_estimate=pl.CostEstimate(
             flops=2 * rows * D * width,
-            bytes_accessed=2 * (rows + width) * D + 8 * rows * width,
+            bytes_accessed=2 * (2 * rows + width) * D + 8 * rows * width,
             transcendentals=2 * rows * width,
         ),
-    )(values, array, bias[None, :], grad_hidden)
+    )(row, *inputs, array, bias[None, :], grad_hidden)
+    return normed + list(outs)
 
 
 PARTIAL_FLIP = (1, 3, 2, 3, 2, 1, 0, 0)
@@ -787,9 +946,11 @@
     return jnp.concatenate([first_half, second_half], axis=0), extra
 
 
-def gather_row(value, between=None):
+def gather_row(value, between=None, later=None):
     if lax.axis_size("row") != 4:
         gathered = lax.all_gather(value, "row", axis=1, tiled=True)
+        if later is not None:
+            return gathered, later[0](later[1])
         return gathered, between() if between else None
     half = value.shape[0] // 2
     from_x = permute_row(value, X_PAIRS)
@@ -798,8 +959,13 @@
     if between is not None:
         extra = between()
         from_x, from_y, extra = in_order(from_x, from_y, extra)
+    if later is not None:
+        from_x, from_y, argument = in_order(from_x, from_y, later[1])
     far_a = permute_row(from_x[:half], Y_PAIRS)
     far_b = permute_row(from_y[half:], X_PAIRS)
+    if later is not None:
+        extra = later[0](argument)
+        far_a, far_b, extra = in_order(far_a, far_b, extra)
     return (value, from_x, from_y, far_a, far_b), extra
 
 
@@ -836,7 +1002,11 @@
 
 
 def scatter_col(grad):
-    return lax.psum_scatter(grad, "col", scatter_dimension=0, tiled=True).astype(F32)
+    if grad.ndim == 2:
+        return lax.psum_scatter(grad, "col", scatter_dimension=0, tiled=True).astype(F32)
+    groups = [list(range(core, SLOTS, 2)) for core in range(2)]
+    total = lax.psum_scatter(grad, "col", scatter_dimension=0, axis_index_groups=groups)
+    return total.astype(F32)
 
 
 class Exchange:
@@ -1172,11 +1342,12 @@
     wide = heads * HV
     narrow = heads * QK
     project_full = gather_col(jnp.concatenate([query_weight, key_weight, value_weight], axis=1))
-    mix_full = gather_col(jnp.concatenate([gate_weight, out_weight.T], axis=1))
+    gate_full = gather_col(gate_weight)
+    out_full = gather_col(out_weight.T)
     feed_full = gather_col(jnp.concatenate([down_weight.T, up_weight], axis=1))
     query_part, key_part = (project_full, narrow, 0), (project_full, narrow, 1)
     value_part = (project_full, wide, 1)
-    gate_part, out_part = (mix_full, wide, 0), (mix_full, wide, 1)
+    out_part = (out_full, wide, 0)
     down_part, up_part = (feed_full, wide, 0), (feed_full, wide, 1)
 
     valid, cosine, sine = token_tables(place, rows, lengths, parents)
@@ -1188,30 +1359,33 @@
     fed_low, first_average = lax.optimization_barrier((fed_low, first_average))
 
     fed_pieces, projected = gather_row(
-        fed_low, lambda: project(first_wide, project_full, cosine, sine)
-    )
-    query_rot, key_rot, value_low = projected
-    exports = make_states(meta, rates, key_rot, value_low)
+        fed_low, lambda: project(meta, rates, first_wide, project_full, cosine, sine)
+    )
+    query_rot, key_rot, value_low, exports = projected
     shared, shifted = share_states(meta, rates, exports, rows)
-    mix_full, shared = in_order(mix_full, shared)
-    gate_part, out_part = (mix_full, wide, 0), (mix_full, wide, 1)
-    gate_raw = matmul(first_wide, gate_part, F32)
-    gate_raw, fed_pieces = in_order(gate_raw, fed_pieces)
-    gated, normal, inverse, states = retain(
-        meta, rates, query_rot, key_rot, value_low, gate_raw, shared, shifted, group_gain, group_bias
+    gate_full, shared = in_order(gate_full, shared)
+    gate_part = (gate_full, wide, 0)
+    gate_full, fed_pieces = in_order(gate_full, fed_pieces)
+    gate_part = (gate_full, wide, 0)
+    gate_raw, gated, normal, inverse, states = retain(
+        meta, rates, query_rot, key_rot, value_low, first_wide, gate_part, shared, shifted,
+        group_gain, group_bias,
     )
 
     sends = reduce_row_start([gated], [out_part], row_ref)
     attended, _ = reduce_row_finish(sends, [gated], [out_part], row_ref)
     middle = tokens.astype(F32) + attended
 
-    def feed_gradient():
-        joined = join(fed_pieces, row_ref)
+    def feed_gradient(pieces):
+        joined = join(pieces, row_ref)
         return joined, matmul(joined, down_part, BF16)
 
-    middle_pieces, (fed_wide, grad_hidden) = gather_row(middle.astype(BF16), feed_gradient)
-    second_wide, second_average, second_inverse = join(middle_pieces, row_ref, gains[2], gains[3])
-    hidden, grad_before, up_bias_grad = feed_up(second_wide, up_part, up_bias, grad_hidden)
+    middle_pieces, (fed_wide, grad_hidden) = gather_row(
+        middle.astype(BF16), later=(feed_gradient, fed_pieces)
+    )
+    second_wide, second_average, second_inverse, hidden, grad_before, up_bias_grad = feed_up(
+        middle_pieces, row_ref, gains[2], gains[3], up_part, up_bias, grad_hidden
+    )
     sends = reduce_row_start([grad_before], [up_part], row_ref)
     sends, hidden = in_order(sends, hidden)
     second_back, feed_partial = reduce_row_finish(
@@ -1219,7 +1393,7 @@
         [grad_before],
         [up_part],
         row_ref,
-        lambda: weight_grads([(fed_wide, hidden), (second_wide, grad_before)]),
+        lambda: column_grads([(fed_wide, hidden), (second_wide, grad_before)], 3),
     )
     feed_grad = scatter_col(feed_partial)
     grad_fed = fed_low.astype(F32)
@@ -1234,7 +1408,7 @@
         grad_middle.astype(BF16), lambda: reduce_row_start([hidden], [down_part], row_ref)
     )
     grad_wide = join(grad_pieces, row_ref)
-    out_partial = weight_grads([(grad_wide, gated)])
+    out_partial = column_grads([(grad_wide, gated)], 4)
     out_partial, grad_wide, feed_grad, fed_sends = in_order(
         out_partial, grad_wide, feed_grad, fed_sends
     )
@@ -1253,12 +1427,14 @@
     grad_gate, grad_retained, group_gain_grad, group_bias_grad, returns, first_state = gate_results
     own = return_states(meta, rates, returns, first_state, rows)
     grad_gate, own = in_order(grad_gate, own)
-    gate_partial = weight_grads([(first_wide, grad_gate)])
+    gate_partial = column_grads([(first_wide, grad_gate)], 5)
     gate_partial, own, out_grad = in_order(gate_partial, own, out_grad)
     gate_grad = scatter_col(gate_partial)
     grad_query, grad_key, grad_value = retain_back(
         meta, rates, query_rot, key_rot, value_low, grad_retained, states, cosine, sine, own
     )
+    back_values = [grad_query, grad_key, grad_value, grad_gate]
+    back_weights = [query_part, key_part, value_part, gate_part]
     back_values = [grad_query, grad_key, grad_value, grad_gate]
     back_weights = [query_part, key_part, value_part, gate_part]
     sends = reduce_row_start(back_values, back_weights, row_ref)
@@ -1268,11 +1444,13 @@
         back_values,
         back_weights,
         row_ref,
-        lambda: weight_grads(
-            [(first_wide, grad_query), (first_wide, grad_key), (first_wide, grad_value)]
-        ),
-    )
-    project_partial, gate_grad = in_order(project_partial, gate_grad)
+        lambda: column_grads(
+            [(first_wide, grad_query), (first_wide, grad_key), (first_wide, grad_value)], 6
+        ),
+    )
+    project_partial, gate_grad, group_gain_grad = in_order(
+        project_partial, gate_grad, group_gain_grad
+    )
     project_grad = scatter_col(project_partial)
 
     first_normal = (tokens.astype(F32) - first_average[:, :1]) * first_inverse[:, :1]

time: 755 us -> 742 us (0.983)
  waiting for transfers between devices: 237 us -> 220 us
    reduce_scatter x4, waiting for transfers between devices: 23.8 us -> 0.05 us  [scatter_col(): lax.psum_scatter(grad, 'col', scatter_dimension=0, axis_index_groups=groups)]
    pallas_call x7 -> x6, Pallas kernels: 96.3 us -> 111 us  [the longest x4 72.4 us: paired_grads(): pl.pallas_call(functools.partial(paired_grad_kernel, tuple(spans), tiles,...]
    pallas_call x2 -> x1, Pallas kernels: 20.4 us -> 9.91 us  [matmul(): pl.pallas_call(matmul_kernel, grid=(rows // CHUNK,), in_specs=[pl.BlockSp...]
    pallas_call x4 -> x3, Pallas kernels: 25.5 us -> 18.1 us  [join(): pl.pallas_call(functools.partial(join_kernel, norm=norm), grid_spec=pltpu...]
    unnamed x118 -> x114, local copies, waits for them, and re-layouts: 19.5 us -> 17.6 us
    all_gather x3 -> x4, waiting for transfers between devices: 39.9 us -> 40.5 us  [gather_col(): return lax.all_gather(weight, 'col', axis=0, tiled=True)]
  transfers between devices with their start and end apart: 54 -> 55, of which waited for: 36 -> 32; matrix products, arithmetic and copies ran while one was open for 9% -> 9% of each run, Pallas kernels for 42% -> 44%
where the time goes in v3:
time: 742 us; the launch traced here: 733 us
  Pallas kernels  349 us (47%)
  waiting for transfers between devices  220 us (30%)
  starting transfers between devices  60.2 us (8%)
  other arithmetic  51.3 us (7%)
  local copies, waits for them, and re-layouts  36.8 us (5%)
  between operations  16 us (2%)
    ppermute x41, waiting for transfers between devices, permute_row(): return lax.ppermute(value, 'row', pairs)  175 us
    pallas_call x8, Pallas kernels, partial_blocks(): pl.pallas_call(functools.partial(partial_kernel, count), grid_spec=pltpu....  75.1 us
    pallas_call x4, Pallas kernels, paired_grads(): pl.pallas_call(functools.partial(paired_grad_kernel, tuple(spans), tiles,...  72.4 us
    pallas_call x1, Pallas kernels, return_states(): pl.pallas_call(functools.partial(return_kernel, rows), in_specs=[smem(),...  52.2 us
    ppermute x41, starting transfers between devices, permute_row(): return lax.ppermute(value, 'row', pairs)  50 us
    all_gather x4, waiting for transfers between devices, gather_col(): return lax.all_gather(weight, 'col', axis=0, tiled=True)  40.5 us
    pallas_call x1, Pallas kernels, share_states(): pl.pallas_call(functools.partial(share_kernel, rows), in_specs=[smem(), s...  25.5 us
    pallas_call x1, Pallas kernels, gate_back(): pl.pallas_call(functools.partial(gate_back_kernel, rows, chunks), grid=(h...  21.5 us
  transfers between devices with their start and end apart: 55, of which 32 were waited for; matrix products, arithmetic and copies ran while one was open for 9% of the time, Pallas kernels for 44%

profile of v3, /device:TPU:0, one launch (start us, length us, event | category | flops | bytes accessed | tf_op | source)
XLA Modules:
  0.0 733.1 jit_solution(13722376733181609586)
XLA Ops:
  13.1 3.0 collective-permute-start.5
  23.5 24.5 %collective-permute-done.from_x = bf16[1280,512]{1,0:T(8,128)(2,1)} collective-permute-done((bf16[1280,512]{1,0:T(8,128)(2,1)S(1)}, bf16[1280,512]{1,0:T(8,128)(2,1)}, u32[]{:S(2)}, u32[]{:S(2)}) %collective-permute-start) | collective-permute-done | bytes 1310752 | tf_op jit(solution)/shard_map/ppermute | solution.py:915
  54.1 10.2 %collective-permute-done.2.far_a = bf16[640,512]{1,0:T(8,128)(2,1)S(1)} collective-permute-done((bf16[640,512]{1,0:T(8,128)(2,1)S(1)}, bf16[640,512]{1,0:T(8,128)(2,1)S(1)}, u32[]{:S(2)}, u32[]{:S(2)}) %collective-permute-start.2) | collective-permute-done | bytes 655392 | tf_op jit(solution)/shard_map/ppermute | solution.py:915
  67.3 7.6 %join_norm.1 = (bf16[1280,2048]{1,0:T(8,128)(2,1)}, f32[1280,128]{1,0:T(8,128)}, f32[1280,128]{1,0:T(8,128)}) custom-call(s32[1]{0:T(128)} %bitcast.row, bf16[1280,512]{1,0:T(8,128)(2,1)} %own.1, bf16[1280,512]{1,0:T(8,128)(2,1)} %collective-permute-done.from_x, bf16[1280,512]{1,0:T(8,128)(2,1)} %collective-permute-done.1.from_y, ...), custom_call_target="tpu_custom_call" | custom-call | flops 20971520 | bytes 10485760 | tf_op jit(solution)/shard_map/join_norm/pallas_call | solution.py:490
  77.1 3.7 multiply_sine_fusion
  81.9 13.1 %all-gather.5.cloned.1.call-done.weight.refs_4_.refs_5_.refs_6_ = bf16[2048,2048]{1,0:T(8,128)(2,1)} async-done(((bf16[256,2048]{1,0:T(8,128)(2,1)}), bf16[2048,2048]{1,0:T(8,128)(2,1)}) %all-gather.5.cloned.1.call-update) | async-done | bytes 8388624 | tf_op jit(solution)/shard_map/all_gather | solution.py:1001
  95.0 21.4 %project.1 = (bf16[1280,512]{1,0:T(8,128)(2,1)}, bf16[1280,512]{1,0:T(8,128)(2,1)}, bf16[1280,1024]{1,0:T(8,128)(2,1)}, bf16[3,2,256,512]{3,2,1,0:T(8,128)(2,1)}) custom-call(s32[22]{0:T(128)} %pad_add_fusion.meta, f32[2]{0:T(128)} %subtract_log_fusion.rates, bf16[1280,2048]{1,0:T(8,128)(2,1)} %get-tuple-element.136.values.wide.refs_0_.refs_1_.refs_2_, ...), custom_call_target="tpu_custom_call" | custom-call | flops 10737418240 | bytes 13631488 | tf_op jit(solution)/shard_map/project/pallas_call | solution.py:553
  121.2 25.5 %share_states.1 = (bf16[8,2,256,512]{3,2,1,0:T(8,128)(2,1)S(1)}, bf16[2,256,512]{2,1,0:T(8,128)(2,1)S(1)}) custom-call(s32[22]{0:T(128)S(1)} %copy-done.3, f32[2]{0:T(128)S(1)} %copy-done.5, bf16[3,2,256,512]{3,2,1,0:T(8,128)(2,1)S(1)} %copy-done.1), custom_call_target="tpu_custom_call" | custom-call | bytes 104857600 | tf_op jit(solution)/shard_map/share_states/pallas_call | solution.py:1140
  149.5 21.3 %retention_forward.1 = (f32[1280,1024]{1,0:T(8,128)}, bf16[1280,1024]{1,0:T(8,128)(2,1)}, bf16[1280,1024]{1,0:T(8,128)(2,1)}, f32[2,1280,128]{2,1,0:T(8,128)}, bf16[2,5,256,512]{3,2,1,0:T(8,128)(2,1)}) custom-call(s32[22]{0:T(128)} %pad_add_fusion.meta, f32[2]{0:T(128)} %subtract_log_fusion.rates, bf16[1280,512]{1,0:T(8,128)(2,1)} %get-tuple-element.141.query, ...), custom_call_target="tpu_custom_call" | custom-call | flops 7717519360 | bytes 20971520 | tf_op jit(solution)/shard_map/retention_forward/pallas_call | solution.py:202
  170.9 27.4 %all-gather.9.cloned.1.call-done.refs_1_.weight = bf16[2048,1024]{1,0:T(8,128)(2,1)} async-done(((bf16[256,1024]{1,0:T(8,128)(2,1)}), bf16[2048,1024]{1,0:T(8,128)(2,1)}) %all-gather.9.cloned.1.call-update) | async-done | bytes 4194320 | tf_op jit(solution)/shard_map/all_gather | solution.py:1001
  198.2 7.4 %partial_blocks.9 = (bf16[2,640,512]{2,1,0:T(8,128)(2,1)}, bf16[2,640,512]{2,1,0:T(8,128)(2,1)}) custom-call(s32[1]{0:T(128)} %bitcast.row, bf16[1280,1024]{1,0:T(8,128)(2,1)} %get-tuple-element.152.refs_0_.refs_1_, bf16[2048,1024]{1,0:T(8,128)(2,1)} %all-gather.9.cloned.1.call-done.refs_1_.weight), custom_call_target="tpu_custom_call" | custom-call | flops 2684354560 | bytes 12058624 | tf_op jit(solution)/shard_map/partial_blocks/pallas_call | solution.py:895
  208.6 8.0 %partial_blocks.8 = (bf16[2,640,512]{2,1,0:T(8,128)(2,1)}, f32[2,640,512]{2,1,0:T(8,128)}) custom-call(s32[1]{0:T(128)} %bitcast.row, bf16[1280,1024]{1,0:T(8,128)(2,1)} %get-tuple-element.152.refs_0_.refs_1_, bf16[2048,1024]{1,0:T(8,128)(2,1)} %all-gather.9.cloned.1.call-done.refs_1_.weight), custom_call_target="tpu_custom_call" | custom-call | flops 2684354560 | bytes 12058624 | tf_op jit(solution)/shard_map/partial_blocks/pallas_call | solution.py:895
  216.6 20.2 %collective-permute-done.11 = bf16[2,640,512]{2,1,0:T(8,128)(2,1)S(1)} collective-permute-done((bf16[2,640,512]{2,1,0:T(8,128)(2,1)}, bf16[2,640,512]{2,1,0:T(8,128)(2,1)S(1)}, u32[]{:S(2)}, u32[]{:S(2)}) %collective-permute-start.11) | collective-permute-done | bytes 1310752 | tf_op jit(solution)/shard_map/ppermute | solution.py:915
  241.9 13.8 %collective-permute-done.12 = bf16[640,512]{1,0:T(8,128)(2,1)S(1)} collective-permute-done((bf16[640,512]{1,0:T(8,128)(2,1)S(1)}, bf16[640,512]{1,0:T(8,128)(2,1)S(1)}, u32[]{:S(2)}, u32[]{:S(2)}) %collective-permute-start.12) | collective-permute-done | bytes 655392 | tf_op jit(solution)/shard_map/ppermute | solution.py:915
  260.4 27.6 %collective-permute-done.16.refs_2_ = bf16[1280,512]{1,0:T(8,128)(2,1)S(1)} collective-permute-done((bf16[1280,512]{1,0:T(8,128)(2,1)S(1)}, bf16[1280,512]{1,0:T(8,128)(2,1)S(1)}, u32[]{:S(2)}, u32[]{:S(2)}) %collective-permute-start.16) | collective-permute-done | bytes 1310752 | tf_op jit(solution)/shard_map/ppermute | solution.py:915
  291.4 5.3 join.2.values.refs_0_
  296.7 9.9 %matmul.1.refs_9_ = bf16[1280,1024]{1,0:T(8,128)(2,1)} custom-call(bf16[1280,2048]{1,0:T(8,128)(2,1)} %join.2.values.refs_0_, bf16[2048,2048]{1,0:T(8,128)(2,1)} %all-gather.11.cloned.1.call-done.weight.refs_7_.refs_1_), custom_call_target="tpu_custom_call" | custom-call | flops 5368709120 | bytes 9437184 | tf_op jit(solution)/shard_map/matmul/pallas_call | solution.py:582
  306.6 17.7 %feed_up.1 = (bf16[1280,2048]{1,0:T(8,128)(2,1)}, f32[1280,128]{1,0:T(8,128)}, f32[1280,128]{1,0:T(8,128)}, bf16[1280,1024]{1,0:T(8,128)(2,1)}, bf16[1280,1024]{1,0:T(8,128)(2,1)}, /*index=5*/f32[1,1024]{1,0:T(1,128)}) custom-call(s32[1]{0:T(128)} %bitcast.row, bf16[1280,512]{1,0:T(8,128)(2,1)} %copy-done.27, bf16[1280,512]{1,0:T(8,128)(2,1)} %copy-done.40, ...), custom_call_target="tpu_custom_call" | custom-call | flops 5368709120 | bytes 25165824 | tf_op jit(solution)/shard_map/feed_up/pallas_call | solution.py:827
  324.2 7.5 %partial_blocks.10 = (bf16[2,640,512]{2,1,0:T(8,128)(2,1)}, bf16[2,640,512]{2,1,0:T(8,128)(2,1)}) custom-call(s32[1]{0:T(128)} %bitcast.row, bf16[1280,1024]{1,0:T(8,128)(2,1)} %get-tuple-element.172.refs_0_.refs_3_, bf16[2048,2048]{1,0:T(8,128)(2,1)} %all-gather.11.cloned.1.call-done.weight.refs_7_.refs_1_), custom_call_target="tpu_custom_call" | custom-call | flops 2684354560 | bytes 12058624 | tf_op jit(solution)/shard_map/partial_blocks/pallas_call | solution.py:895
  333.8 21.2 %paired_grads.4 = bf16[4,256,2048]{2,1,0:T(8,128)(2,1)} custom-call(bf16[1280,2048]{1,0:T(8,128)(2,1)} %join.2.values.refs_0_, bf16[1280,2048]{1,0:T(8,128)(2,1)} %get-tuple-element.183.refs_1_, bf16[1280,1024]{1,0:T(8,128)(2,1)} %get-tuple-element.176.refs_0_.refs_2_, bf16[1280,1024]{1,0:T(8,128)(2,1)} %get-tuple-element.172.refs_0_.refs_3_), custom_call_target="tpu_custom_call" | custom-call | flops 10737418240 | bytes 18874368 | tf_op jit(solution)/shard_map/paired_grads/pallas_call | solution.py:724
  355.0 4.1 collective-permute-done.19
  360.4 7.7 %partial_blocks.12 = (bf16[2,640,512]{2,1,0:T(8,128)(2,1)}, f32[2,640,512]{2,1,0:T(8,128)}) custom-call(s32[1]{0:T(128)} %bitcast.row, bf16[1280,1024]{1,0:T(8,128)(2,1)} %get-tuple-element.172.refs_0_.refs_3_, bf16[2048,2048]{1,0:T(8,128)(2,1)} %all-gather.11.cloned.1.call-done.weight.refs_7_.refs_1_), custom_call_target="tpu_custom_call" | custom-call | flops 2684354560 | bytes 12058624 | tf_op jit(solution)/shard_map/partial_blocks/pallas_call | solution.py:895
  372.4 9.9 %collective-permute-done.21 = bf16[640,512]{1,0:T(8,128)(2,1)S(1)} collective-permute-done((bf16[640,512]{1,0:T(8,128)(2,1)S(1)}, bf16[640,512]{1,0:T(8,128)(2,1)S(1)}, u32[]{:S(2)}, u32[]{:S(2)}) %collective-permute-start.21) | collective-permute-done | bytes 655392 | tf_op jit(solution)/shard_map/ppermute | solution.py:915
  388.0 2.7 collective-permute-done.23
  394.7 2.8 fusion.35
  399.0 7.5 %partial_blocks.13 = (bf16[2,640,512]{2,1,0:T(8,128)(2,1)}, bf16[2,640,512]{2,1,0:T(8,128)(2,1)}) custom-call(s32[1]{0:T(128)} %bitcast.row, bf16[1280,1024]{1,0:T(8,128)(2,1)} %get-tuple-element.176.refs_0_.refs_2_, bf16[2048,2048]{1,0:T(8,128)(2,1)} %all-gather.11.cloned.1.call-done.weight.refs_7_.refs_1_), custom_call_target="tpu_custom_call" | custom-call | flops 2684354560 | bytes 12058624 | tf_op jit(solution)/shard_map/partial_blocks/pallas_call | solution.py:895
  406.4 17.5 %collective-permute-done.26.from_y = bf16[1280,512]{1,0:T(8,128)(2,1)} collective-permute-done((bf16[1280,512]{1,0:T(8,128)(2,1)}, bf16[1280,512]{1,0:T(8,128)(2,1)}, u32[]{:S(2)}, u32[]{:S(2)}) %collective-permute-start.26) | collective-permute-done | bytes 1310752 | tf_op jit(solution)/shard_map/ppermute | solution.py:915
  429.6 8.5 %collective-permute-done.28.far_b = bf16[640,512]{1,0:T(8,128)(2,1)S(1)} collective-permute-done((bf16[640,512]{1,0:T(8,128)(2,1)S(1)}, bf16[640,512]{1,0:T(8,128)(2,1)S(1)}, u32[]{:S(2)}, u32[]{:S(2)}) %collective-permute-start.28) | collective-permute-done | bytes 655392 | tf_op jit(solution)/shard_map/ppermute | solution.py:915
  439.0 5.3 join.3.refs_0_.wide
  444.3 12.1 %paired_grads.5 = bf16[4,256,1024]{2,1,0:T(8,128)(2,1)} custom-call(bf16[1280,2048]{1,0:T(8,128)(2,1)} %join.3.refs_0_.wide, bf16[1280,1024]{1,0:T(8,128)(2,1)} %get-tuple-element.152.refs_0_.refs_1_), custom_call_target="tpu_custom_call" | custom-call | flops 5368709120 | bytes 14680064 | tf_op jit(solution)/shard_map/paired_grads/pallas_call | solution.py:724
  456.4 2.8 bitcast_convert_fusion
  461.7 21.5 %gate_backward.1 = (bf16[1280,1024]{1,0:T(8,128)(2,1)}, bf16[1280,1024]{1,0:T(8,128)(2,1)}, f32[1,1024]{1,0:T(1,128)}, f32[1,1024]{1,0:T(1,128)}, bf16[8,2,256,5...) custom-call(s32[22]{0:T(128)} %pad_add_fusion.meta, f32[2]{0:T(128)} %subtract_log_fusion.rates, ...), custom_call_target="tpu_custom_call" | custom-call | flops 6039797760 | bytes 31457280 | tf_op jit(solution)/shard_map/gate_backward/pallas_call | solution.py:299
  483.2 7.3 collective-permute-done.29
  494.8 52.2 %return_states.1 = (bf16[2,256,512]{2,1,0:T(8,128)(2,1)S(1)}, bf16[2,256,512]{2,1,0:T(8,128)(2,1)S(1)}, bf16[2,256,512]{2,1,0:T(8,128)(2,1)S(1)}) custom-call(s32[22]{0:T(128)S(1)} %copy-done.4, f32[2]{0:T(128)S(1)} %copy-done.6, bf16[8,2,256,512]{3,2,1,0:T(8,128)(2,1)S(1)} %copy-done, bf16[2,256,512]{2,1,0:T(8,128)(2,1)S(1)} %copy-done.2), custom_call_target="tpu_custom_call" | custom-call | bytes 104857600 | tf_op jit(solution)/shard_map/return_states/pallas_call | solution.py:1243
  549.4 17.0 %paired_grads.6 = bf16[4,256,1024]{2,1,0:T(8,128)(2,1)} custom-call(bf16[1280,2048]{1,0:T(8,128)(2,1)} %get-tuple-element.136.values.wide.refs_0_.refs_1_.refs_2_, bf16[1280,1024]{1,0:T(8,128)(2,1)} %get-tuple-element.219.refs_1_.refs_3_), custom_call_target="tpu_custom_call" | custom-call | flops 5368709120 | bytes 14680064 | tf_op jit(solution)/shard_map/paired_grads/pallas_call | solution.py:724
  568.6 14.1 %retention_backward.1 = (bf16[1280,512]{1,0:T(8,128)(2,1)}, bf16[1280,512]{1,0:T(8,128)(2,1)}, bf16[1280,1024]{1,0:T(8,128)(2,1)}) custom-call(s32[22]{0:T(128)} %pad_add_fusion.meta, f32[2]{0:T(128)} %subtract_log_fusion.rates, bf16[1280,512]{1,0:T(8,128)(2,1)} %get-tuple-element.141.query, bf16[1280,512]{1,0:T(8,128)(2,1)} %get-tuple-element.142.key, ...), custom_call_target="tpu_custom_call" | custom-call | flops 5033164800 | bytes 15728640 | tf_op jit(solution)/shard_map/retention_backward/pallas_call | solution.py:394
  582.7 14.5 %partial_blocks.15 = (bf16[2,640,512]{2,1,0:T(8,128)(2,1)}, bf16[2,640,512]{2,1,0:T(8,128)(2,1)}) custom-call(s32[1]{0:T(128)} %bitcast.row, bf16[1280,512]{1,0:T(8,128)(2,1)} %get-tuple-element.227.refs_0_.refs_3_, bf16[1280,512]{1,0:T(8,128)(2,1)} %get-tuple-element.228.refs_1_.refs_4_, bf16[1280,1024]{1,0:T(8,128)(2,1)} %get-tuple-element.235.refs_2_.refs_5_, ...), custom_call_target="tpu_custom_call" | custom-call | flops 8053063680 | bytes 25690112 | tf_op jit(solution)/shard_map/partial_blocks/pallas_call | solution.py:895
  600.2 22.1 %paired_grads.7 = bf16[4,256,2048]{2,1,0:T(8,128)(2,1)} custom-call(bf16[1280,2048]{1,0:T(8,128)(2,1)} %get-tuple-element.136.values.wide.refs_0_.refs_1_.refs_2_, bf16[1280,2048]{1,0:T(8,128)(2,1)} %get-tuple-element.136.values.wide.refs_0_.refs_1_.refs_2_, bf16[1280,2048]{1,0:T(8,128)(2,1)} %get-tuple-element.136.values.wide.refs_0_.refs_1_.refs_2_, ...), custom_call_target="tpu_custom_call" | custom-call | flops 10737418240 | bytes 18874368 | tf_op jit(solution)/shard_map/paired_grads/pallas_call | solution.py:724
  622.3 6.3 collective-permute-done.33
  633.6 7.7 %partial_blocks.11 = (bf16[2,640,512]{2,1,0:T(8,128)(2,1)}, f32[2,640,512]{2,1,0:T(8,128)}) custom-call(s32[1]{0:T(128)} %bitcast.row, bf16[1280,1024]{1,0:T(8,128)(2,1)} %get-tuple-element.176.refs_0_.refs_2_, bf16[2048,2048]{1,0:T(8,128)(2,1)} %all-gather.11.cloned.1.call-done.weight.refs_7_.refs_1_), custom_call_target="tpu_custom_call" | custom-call | flops 2684354560 | bytes 12058624 | tf_op jit(solution)/shard_map/partial_blocks/pallas_call | solution.py:895
  641.3 3.1 fusion.17
  646.4 14.8 %partial_blocks.14 = (bf16[2,640,512]{2,1,0:T(8,128)(2,1)}, f32[2,640,512]{2,1,0:T(8,128)}) custom-call(s32[1]{0:T(128)} %bitcast.row, bf16[1280,512]{1,0:T(8,128)(2,1)} %get-tuple-element.227.refs_0_.refs_3_, bf16[1280,512]{1,0:T(8,128)(2,1)} %get-tuple-element.228.refs_1_.refs_4_, bf16[1280,1024]{1,0:T(8,128)(2,1)} %get-tuple-element.235.refs_2_.refs_5_, ...), custom_call_target="tpu_custom_call" | custom-call | flops 8053063680 | bytes 25690112 | tf_op jit(solution)/shard_map/partial_blocks/pallas_call | solution.py:895
  667.8 4.0 fusion.11
  671.8 7.4 %collective-permute-done.35 = bf16[640,512]{1,0:T(8,128)(2,1)S(1)} collective-permute-done((bf16[640,512]{1,0:T(8,128)(2,1)S(1)}, bf16[640,512]{1,0:T(8,128)(2,1)S(1)}, u32[]{:S(2)}, u32[]{:S(2)}) %collective-permute-start.35) | collective-permute-done | bytes 655392 | tf_op jit(solution)/shard_map/ppermute | solution.py:915
  686.7 4.9 collective-permute-start.40
  693.8 3.1 slice_bitcast_fusion
  714.8 2.7 collective-permute-start.44
  717.5 3.8 fusion.7
  (289 shorter events, 133.5 us)
Async XLA Ops:
  7.2 87.8 %all-gather.5.cloned.1.call-start = ((), (), s32[]{:S(2)}) async-start(), calls=%async_computation.4 | async-start | bytes 9437184 | tf_op jit(solution)/shard_map/all_gather | solution.py:1001
  9.5 139.9 %all-gather.7.cloned.1.call-start = ((), (), s32[]{:S(2)}) async-start(), calls=%async_computation.5 | async-start | bytes 4718592 | tf_op jit(solution)/shard_map/all_gather | solution.py:1001
  10.3 187.9 %all-gather.9.cloned.1.call-start = ((), (), s32[]{:S(2)}) async-start(), calls=%async_computation.6 | async-start | bytes 4718592 | tf_op jit(solution)/shard_map/all_gather | solution.py:1001
  11.6 285.1 %all-gather.11.cloned.1.call-start = ((), (), s32[]{:S(2)}) async-start(), calls=%async_computation.7 | async-start | bytes 9437184 | tf_op jit(solution)/shard_map/all_gather | solution.py:1001
  13.0 443.4 %reduce-scatter.5.cloned.1.call-start = ((), (), s32[]{:S(2)}) async-start(), calls=%async_computation.8 | async-start | bytes 5242880 | tf_op jit(solution)/shard_map/reduce_scatter | solution.py:1008
  13.1 10.3 %collective-permute-start.5 = (f32[4,512]{1,0:T(4,128)S(1)}, f32[4,512]{1,0:T(4,128)S(1)}, u32[]{:S(2)}, u32[]{:S(2)}) collective-permute-start(f32[4,512]{1,0:T(4,128)S(1)} %get-tuple-element.372), channel_id=1, source_target_pairs={{0,16},{16,0},{8,24},{24,8},{1,17},{17,1},{9,25},{25,9},{2,18},{18... | collective-permute-start | bytes 24584 | tf_op jit(solution)/shard_map/ppermute | solution.py:915
  16.2 7.3 collective-permute-start.4
  17.7 5.8 collective-permute-start.6
  17.7 30.2 %collective-permute-start = (bf16[1280,512]{1,0:T(8,128)(2,1)S(1)}, bf16[1280,512]{1,0:T(8,128)(2,1)}, u32[]{:S(2)}, u32[]{:S(2)}) collective-permute-start(bf16[1280,512]{1,0:T(8,128)(2,1)S(1)} %copy-done.12), channel_id=1, source_target_pairs={{0,8},{8,0},{16,24},{24,16},{1,9},{9,1},{17,25},{25,17},{2,10},{10... | collective-permute-start | bytes 3932168 | tf_op jit(solution)/shard_map/ppermute | solution.py:915
  19.6 31.1 %collective-permute-start.1 = (bf16[1280,512]{1,0:T(8,128)(2,1)S(1)}, bf16[1280,512]{1,0:T(8,128)(2,1)}, u32[]{:S(2)}, u32[]{:S(2)}) collective-permute-start(bf16[1280,512]{1,0:T(8,128)(2,1)S(1)} %copy-done.12), channel_id=1, source_target_pairs={{0,16},{16,0},{8,24},{24,8},{1,17},{17,1},{9,25},{25,9},{2,18},{18... | collective-permute-start | bytes 3932168 | tf_op jit(solution)/shard_map/ppermute | solution.py:915
  49.1 15.2 %collective-permute-start.2 = (bf16[640,512]{1,0:T(8,128)(2,1)S(1)}, bf16[640,512]{1,0:T(8,128)(2,1)S(1)}, u32[]{:S(2)}, u32[]{:S(2)}) collective-permute-start(bf16[640,512]{1,0:T(8,128)(2,1)S(1)} %slice.244), channel_id=1, source_target_pairs={{0,16},{16,0},{8,24},{24,8},{1,17},{17,1},{9,25},{25,9},{2,18},{18... | collective-permute-start | bytes 1966088 | tf_op jit(solution)/shard_map/ppermute | solution.py:915
  51.9 14.6 %collective-permute-start.3 = (bf16[640,512]{1,0:T(8,128)(2,1)S(1)}, bf16[640,512]{1,0:T(8,128)(2,1)S(1)}, u32[]{:S(2)}, u32[]{:S(2)}) collective-permute-start(bf16[640,512]{1,0:T(8,128)(2,1)S(1)} %slice.245), channel_id=1, source_target_pairs={{0,8},{8,0},{16,24},{24,16},{1,9},{9,1},{17,25},{25,17},{2,10},{10... | collective-permute-start | bytes 1966088 | tf_op jit(solution)/shard_map/ppermute | solution.py:915
  74.9 41.5 %collective-permute-start.8 = (bf16[1280,512]{1,0:T(8,128)(2,1)S(1)}, bf16[1280,512]{1,0:T(8,128)(2,1)S(1)}, u32[]{:S(2)}, u32[]{:S(2)}) collective-permute-start(bf16[1280,512]{1,0:T(8,128)(2,1)S(1)} %multiply_convert_fusion.own), channel_id=1, source_target_pairs={{0,16},{16,0},{8,24},{24,8},{1,17},{17,1},{9,25},{25,9},{2,18},{18... | collective-permute-start | bytes 3932168 | tf_op jit(solution)/shard_map/ppermute | solution.py:915
  75.6 40.7 %collective-permute-start.7 = (bf16[1280,512]{1,0:T(8,128)(2,1)S(1)}, bf16[1280,512]{1,0:T(8,128)(2,1)}, u32[]{:S(2)}, u32[]{:S(2)}) collective-permute-start(bf16[1280,512]{1,0:T(8,128)(2,1)S(1)} %multiply_convert_fusion.own), channel_id=1, source_target_pairs={{0,8},{8,0},{16,24},{24,16},{1,9},{9,1},{17,25},{25,17},{2,10},{10... | collective-permute-start | bytes 3932168 | tf_op jit(solution)/shard_map/ppermute | solution.py:915
  118.1 31.4 %collective-permute-start.10 = (bf16[640,512]{1,0:T(8,128)(2,1)S(1)}, bf16[640,512]{1,0:T(8,128)(2,1)S(1)}, u32[]{:S(2)}, u32[]{:S(2)}) collective-permute-start(bf16[640,512]{1,0:T(8,128)(2,1)S(1)} %slice.190), channel_id=1, source_target_pairs={{0,8},{8,0},{16,24},{24,16},{1,9},{9,1},{17,25},{25,17},{2,10},{10... | collective-permute-start | bytes 1966088 | tf_op jit(solution)/shard_map/ppermute | solution.py:915
  119.7 29.8 %collective-permute-start.9 = (bf16[640,512]{1,0:T(8,128)(2,1)S(1)}, bf16[640,512]{1,0:T(8,128)(2,1)S(1)}, u32[]{:S(2)}, u32[]{:S(2)}) collective-permute-start(bf16[640,512]{1,0:T(8,128)(2,1)S(1)} %slice.189), channel_id=1, source_target_pairs={{0,16},{16,0},{8,24},{24,8},{1,17},{17,1},{9,25},{25,9},{2,18},{18... | collective-permute-start | bytes 1966088 | tf_op jit(solution)/shard_map/ppermute | solution.py:915
  205.7 31.1 %collective-permute-start.11 = (bf16[2,640,512]{2,1,0:T(8,128)(2,1)}, bf16[2,640,512]{2,1,0:T(8,128)(2,1)S(1)}, u32[]{:S(2)}, u32[]{:S(2)}) collective-permute-start(bf16[2,640,512]{2,1,0:T(8,128)(2,1)} %get-tuple-element.154), channel_id=1, source_target_pairs={{0,8},{8,0},{16,24},{24,16},{1,9},{9,1},{17,25},{25,17},{2,10},{10... | collective-permute-start | bytes 3932168 | tf_op jit(solution)/shard_map/ppermute | solution.py:915
  207.2 30.9 %collective-permute-start.13 = (bf16[2,640,512]{2,1,0:T(8,128)(2,1)}, bf16[2,640,512]{2,1,0:T(8,128)(2,1)S(1)}, u32[]{:S(2)}, u32[]{:S(2)}) collective-permute-start(bf16[2,640,512]{2,1,0:T(8,128)(2,1)} %get-tuple-element.156), channel_id=1, source_target_pairs={{0,16},{16,0},{8,24},{24,8},{1,17},{17,1},{9,25},{25,9},{2,18},{18... | collective-permute-start | bytes 3932168 | tf_op jit(solution)/shard_map/ppermute | solution.py:915
  239.8 15.9 %collective-permute-start.12 = (bf16[640,512]{1,0:T(8,128)(2,1)S(1)}, bf16[640,512]{1,0:T(8,128)(2,1)S(1)}, u32[]{:S(2)}, u32[]{:S(2)}) collective-permute-start(bf16[640,512]{1,0:T(8,128)(2,1)S(1)} %get-tuple-element.351), channel_id=1, source_target_pairs={{0,16},{16,0},{8,24},{24,8},{1,17},{17,1},{9,25},{25,9},{2,18},{18... | collective-permute-start | bytes 1966088 | tf_op jit(solution)/shard_map/ppermute | solution.py:915
  241.4 15.6 %collective-permute-start.14 = (bf16[640,512]{1,0:T(8,128)(2,1)S(1)}, bf16[640,512]{1,0:T(8,128)(2,1)S(1)}, u32[]{:S(2)}, u32[]{:S(2)}) collective-permute-start(bf16[640,512]{1,0:T(8,128)(2,1)S(1)} %get-tuple-element.352), channel_id=1, source_target_pairs={{0,8},{8,0},{16,24},{24,16},{1,9},{9,1},{17,25},{25,17},{2,10},{10... | collective-permute-start | bytes 1966088 | tf_op jit(solution)/shard_map/ppermute | solution.py:915
  259.2 28.8 %collective-permute-start.16 = (bf16[1280,512]{1,0:T(8,128)(2,1)S(1)}, bf16[1280,512]{1,0:T(8,128)(2,1)S(1)}, u32[]{:S(2)}, u32[]{:S(2)}) collective-permute-start(bf16[1280,512]{1,0:T(8,128)(2,1)S(1)} %get-tuple-element.329.refs_0_), channel_id=1, source_target_pairs={{0,16},{16,0},{8,24},{24,8},{1,17},{17,1},{9,25},{25,9},{2,18},{18... | collective-permute-start | bytes 3932168 | tf_op jit(solution)/shard_map/ppermute | solution.py:915
  259.7 28.5 %collective-permute-start.15 = (bf16[1280,512]{1,0:T(8,128)(2,1)S(1)}, bf16[1280,512]{1,0:T(8,128)(2,1)S(1)}, u32[]{:S(2)}, u32[]{:S(2)}) collective-permute-start(bf16[1280,512]{1,0:T(8,128)(2,1)S(1)} %get-tuple-element.329.refs_0_), channel_id=1, source_target_pairs={{0,8},{8,0},{16,24},{24,16},{1,9},{9,1},{17,25},{25,17},{2,10},{10... | collective-permute-start | bytes 3932168 | tf_op jit(solution)/shard_map/ppermute | solution.py:915
  289.4 17.1 %collective-permute-start.18 = (bf16[640,512]{1,0:T(8,128)(2,1)}, bf16[640,512]{1,0:T(8,128)(2,1)}, u32[]{:S(2)}, u32[]{:S(2)}) collective-permute-start(bf16[640,512]{1,0:T(8,128)(2,1)} %slice.200), channel_id=1, source_target_pairs={{0,8},{8,0},{16,24},{24,16},{1,9},{9,1},{17,25},{25,17},{2,10},{10... | collective-permute-start | bytes 1966088 | tf_op jit(solution)/shard_map/ppermute | solution.py:915
  290.1 16.5 %collective-permute-start.17 = (bf16[640,512]{1,0:T(8,128)(2,1)S(1)}, bf16[640,512]{1,0:T(8,128)(2,1)}, u32[]{:S(2)}, u32[]{:S(2)}) collective-permute-start(bf16[640,512]{1,0:T(8,128)(2,1)S(1)} %slice.199), channel_id=1, source_target_pairs={{0,16},{16,0},{8,24},{24,8},{1,17},{17,1},{9,25},{25,9},{2,18},{18... | collective-permute-start | bytes 1966088 | tf_op jit(solution)/shard_map/ppermute | solution.py:915
  331.7 27.4 %collective-permute-start.19 = (bf16[2,640,512]{2,1,0:T(8,128)(2,1)}, bf16[2,640,512]{2,1,0:T(8,128)(2,1)}, u32[]{:S(2)}, u32[]{:S(2)}) collective-permute-start(bf16[2,640,512]{2,1,0:T(8,128)(2,1)} %get-tuple-element.180), channel_id=1, source_target_pairs={{0,8},{8,0},{16,24},{24,16},{1,9},{9,1},{17,25},{25,17},{2,10},{10... | collective-permute-start | bytes 3932168 | tf_op jit(solution)/shard_map/ppermute | solution.py:915
  333.1 27.2 %collective-permute-start.20 = (bf16[2,640,512]{2,1,0:T(8,128)(2,1)}, bf16[2,640,512]{2,1,0:T(8,128)(2,1)}, u32[]{:S(2)}, u32[]{:S(2)}) collective-permute-start(bf16[2,640,512]{2,1,0:T(8,128)(2,1)} %get-tuple-element.181), channel_id=1, source_target_pairs={{0,16},{16,0},{8,24},{24,8},{1,17},{17,1},{9,25},{25,9},{2,18},{18... | collective-permute-start | bytes 3932168 | tf_op jit(solution)/shard_map/ppermute | solution.py:915
  360.3 206.1 %reduce-scatter.7.cloned.1.call-start = ((), (), s32[]{:S(2)}) async-start(), calls=%async_computation.9 | async-start | bytes 2621440 | tf_op jit(solution)/shard_map/reduce_scatter | solution.py:1008
  370.3 12.0 %collective-permute-start.21 = (bf16[640,512]{1,0:T(8,128)(2,1)S(1)}, bf16[640,512]{1,0:T(8,128)(2,1)S(1)}, u32[]{:S(2)}, u32[]{:S(2)}) collective-permute-start(bf16[640,512]{1,0:T(8,128)(2,1)S(1)} %get-tuple-element.349), channel_id=1, source_target_pairs={{0,16},{16,0},{8,24},{24,8},{1,17},{17,1},{9,25},{25,9},{2,18},{18... | collective-permute-start | bytes 1966088 | tf_op jit(solution)/shard_map/ppermute | solution.py:915
  371.2 11.8 %collective-permute-start.22 = (bf16[640,512]{1,0:T(8,128)(2,1)S(1)}, bf16[640,512]{1,0:T(8,128)(2,1)S(1)}, u32[]{:S(2)}, u32[]{:S(2)}) collective-permute-start(bf16[640,512]{1,0:T(8,128)(2,1)S(1)} %get-tuple-element.350), channel_id=1, source_target_pairs={{0,8},{8,0},{16,24},{24,16},{1,9},{9,1},{17,25},{25,17},{2,10},{10... | collective-permute-start | bytes 1966088 | tf_op jit(solution)/shard_map/ppermute | solution.py:915
  397.5 26.4 %collective-permute-start.26 = (bf16[1280,512]{1,0:T(8,128)(2,1)}, bf16[1280,512]{1,0:T(8,128)(2,1)}, u32[]{:S(2)}, u32[]{:S(2)}) collective-permute-start(bf16[1280,512]{1,0:T(8,128)(2,1)} %get-tuple-element.327.own), channel_id=1, source_target_pairs={{0,16},{16,0},{8,24},{24,8},{1,17},{17,1},{9,25},{25,9},{2,18},{18... | collective-permute-start | bytes 3932168 | tf_op jit(solution)/shard_map/ppermute | solution.py:915
  398.8 26.5 %collective-permute-start.25 = (bf16[1280,512]{1,0:T(8,128)(2,1)}, bf16[1280,512]{1,0:T(8,128)(2,1)}, u32[]{:S(2)}, u32[]{:S(2)}) collective-permute-start(bf16[1280,512]{1,0:T(8,128)(2,1)} %get-tuple-element.327.own), channel_id=1, source_target_pairs={{0,8},{8,0},{16,24},{24,16},{1,9},{9,1},{17,25},{25,17},{2,10},{10... | collective-permute-start | bytes 3932168 | tf_op jit(solution)/shard_map/ppermute | solution.py:915
  427.5 10.7 %collective-permute-start.28 = (bf16[640,512]{1,0:T(8,128)(2,1)S(1)}, bf16[640,512]{1,0:T(8,128)(2,1)S(1)}, u32[]{:S(2)}, u32[]{:S(2)}) collective-permute-start(bf16[640,512]{1,0:T(8,128)(2,1)S(1)} %slice.217), channel_id=1, source_target_pairs={{0,8},{8,0},{16,24},{24,16},{1,9},{9,1},{17,25},{25,17},{2,10},{10... | collective-permute-start | bytes 1966088 | tf_op jit(solution)/shard_map/ppermute | solution.py:915
  427.6 10.8 %collective-permute-start.27 = (bf16[640,512]{1,0:T(8,128)(2,1)S(1)}, bf16[640,512]{1,0:T(8,128)(2,1)}, u32[]{:S(2)}, u32[]{:S(2)}) collective-permute-start(bf16[640,512]{1,0:T(8,128)(2,1)S(1)} %slice.216), channel_id=1, source_target_pairs={{0,16},{16,0},{8,24},{24,8},{1,17},{17,1},{9,25},{25,9},{2,18},{18... | collective-permute-start | bytes 1966088 | tf_op jit(solution)/shard_map/ppermute | solution.py:915
  459.2 170.5 %reduce-scatter.9.cloned.1.call-start = ((), (), s32[]{:S(2)}) async-start(), calls=%async_computation.10 | async-start | bytes 2621440 | tf_op jit(solution)/shard_map/reduce_scatter | solution.py:1008
  459.3 31.2 %collective-permute-start.29 = (bf16[2,640,512]{2,1,0:T(8,128)(2,1)}, bf16[2,640,512]{2,1,0:T(8,128)(2,1)}, u32[]{:S(2)}, u32[]{:S(2)}) collective-permute-start(bf16[2,640,512]{2,1,0:T(8,128)(2,1)} %get-tuple-element.195), channel_id=1, source_target_pairs={{0,8},{8,0},{16,24},{24,16},{1,9},{9,1},{17,25},{25,17},{2,10},{10... | collective-permute-start | bytes 3932168 | tf_op jit(solution)/shard_map/ppermute | solution.py:915
  460.6 30.9 %collective-permute-start.30 = (bf16[2,640,512]{2,1,0:T(8,128)(2,1)}, bf16[2,640,512]{2,1,0:T(8,128)(2,1)}, u32[]{:S(2)}, u32[]{:S(2)}) collective-permute-start(bf16[2,640,512]{2,1,0:T(8,128)(2,1)} %get-tuple-element.196), channel_id=1, source_target_pairs={{0,16},{16,0},{8,24},{24,8},{1,17},{17,1},{9,25},{25,9},{2,18},{18... | collective-permute-start | bytes 3932168 | tf_op jit(solution)/shard_map/ppermute | solution.py:915
  568.5 154.0 %reduce-scatter.11.cloned.1.call-start = ((), (), s32[]{:S(2)}) async-start(), calls=%async_computation.11 | async-start | bytes 5242880 | tf_op jit(solution)/shard_map/reduce_scatter | solution.py:1008
  597.2 31.3 %collective-permute-start.33 = (bf16[2,640,512]{2,1,0:T(8,128)(2,1)}, bf16[2,640,512]{2,1,0:T(8,128)(2,1)}, u32[]{:S(2)}, u32[]{:S(2)}) collective-permute-start(bf16[2,640,512]{2,1,0:T(8,128)(2,1)} %get-tuple-element.233), channel_id=1, source_target_pairs={{0,8},{8,0},{16,24},{24,16},{1,9},{9,1},{17,25},{25,17},{2,10},{10... | collective-permute-start | bytes 3932168 | tf_op jit(solution)/shard_map/ppermute | solution.py:915
  598.8 31.0 %collective-permute-start.34 = (bf16[2,640,512]{2,1,0:T(8,128)(2,1)}, bf16[2,640,512]{2,1,0:T(8,128)(2,1)}, u32[]{:S(2)}, u32[]{:S(2)}) collective-permute-start(bf16[2,640,512]{2,1,0:T(8,128)(2,1)} %get-tuple-element.234), channel_id=1, source_target_pairs={{0,16},{16,0},{8,24},{24,8},{1,17},{17,1},{9,25},{25,9},{2,18},{18... | collective-permute-start | bytes 3932168 | tf_op jit(solution)/shard_map/ppermute | solution.py:915
  644.4 21.0 %collective-permute-start.31 = (bf16[640,512]{1,0:T(8,128)(2,1)}, bf16[640,512]{1,0:T(8,128)(2,1)S(1)}, u32[]{:S(2)}, u32[]{:S(2)}) collective-permute-start(bf16[640,512]{1,0:T(8,128)(2,1)} %get-tuple-element.347), channel_id=1, source_target_pairs={{0,16},{16,0},{8,24},{24,8},{1,17},{17,1},{9,25},{25,9},{2,18},{18... | collective-permute-start | bytes 1966088 | tf_op jit(solution)/shard_map/ppermute | solution.py:915
  645.8 19.6 %collective-permute-start.32 = (bf16[640,512]{1,0:T(8,128)(2,1)}, bf16[640,512]{1,0:T(8,128)(2,1)}, u32[]{:S(2)}, u32[]{:S(2)}) collective-permute-start(bf16[640,512]{1,0:T(8,128)(2,1)} %get-tuple-element.348), channel_id=1, source_target_pairs={{0,8},{8,0},{16,24},{24,16},{1,9},{9,1},{17,25},{25,17},{2,10},{10... | collective-permute-start | bytes 1966088 | tf_op jit(solution)/shard_map/ppermute | solution.py:915
  663.4 15.7 %collective-permute-start.35 = (bf16[640,512]{1,0:T(8,128)(2,1)S(1)}, bf16[640,512]{1,0:T(8,128)(2,1)S(1)}, u32[]{:S(2)}, u32[]{:S(2)}) collective-permute-start(bf16[640,512]{1,0:T(8,128)(2,1)S(1)} %get-tuple-element.345), channel_id=1, source_target_pairs={{0,16},{16,0},{8,24},{24,8},{1,17},{17,1},{9,25},{25,9},{2,18},{18... | collective-permute-start | bytes 1966088 | tf_op jit(solution)/shard_map/ppermute | solution.py:915
  663.9 15.5 %collective-permute-start.36 = (bf16[640,512]{1,0:T(8,128)(2,1)S(1)}, bf16[640,512]{1,0:T(8,128)(2,1)S(1)}, u32[]{:S(2)}, u32[]{:S(2)}) collective-permute-start(bf16[640,512]{1,0:T(8,128)(2,1)S(1)} %get-tuple-element.346), channel_id=1, source_target_pairs={{0,8},{8,0},{16,24},{24,16},{1,9},{9,1},{17,25},{25,17},{2,10},{10... | collective-permute-start | bytes 1966088 | tf_op jit(solution)/shard_map/ppermute | solution.py:915
  686.7 6.8 collective-permute-start.40
  691.6 11.9 %collective-permute-start.37 = (f32[2,1280]{1,0:T(2,128)S(1)}, f32[2,1280]{1,0:T(2,128)S(1)}, u32[]{:S(2)}, u32[]{:S(2)}) collective-permute-start(f32[2,1280]{1,0:T(2,128)S(1)} %pad_maximum_fusion.8), channel_id=1, source_target_pairs={{0,8},{8,0},{16,24},{24,16},{1,9},{9,1},{17,25},{25,17},{2,10},{10... | collective-permute-start | bytes 30728 | tf_op jit(solution)/shard_map/ppermute | solution.py:915
  693.4 8.6 %collective-permute-start.41 = (f32[9,128]{1,0:T(8,128)S(1)}, f32[9,128]{1,0:T(8,128)S(1)}, u32[]{:S(2)}, u32[]{:S(2)}) collective-permute-start(f32[9,128]{1,0:T(8,128)S(1)} %fusion.43), channel_id=1, source_target_pairs={{0,4},{1,5},{2,6},{3,7},{4,0},{5,1},{6,2},{7,3},{8,12},{9,13},{10,... | collective-permute-start | bytes 13832 | tf_op jit(solution)/shard_map/ppermute | solution.py:1269
  703.5 6.3 collective-permute-start.38
  714.8 6.5 collective-permute-start.44
  (60 other events, 391.6 us)
Sparse Core Ops, SparseCore 0:
  10.2 84.7 all-gather.4
  96.6 52.0 all-gather.6
  150.9 47.3 all-gather.8
  200.3 86.4 all-gather.10
  360.4 93.1 reduce-scatter.4
  459.4 61.5 reduce-scatter.6
  568.7 46.0 reduce-scatter.8
  632.1 78.4 reduce-scatter.10

commit v4 on v3

--- a/solution.py
+++ b/solution.py
@@ -16,6 +16,7 @@
 CHUNK = 256
 TRUNK_CHUNKS = TRUNK // CHUNK
 SLOTS = 8
+GRAD_TILE = 256
 
 EPSILON = 1e-05
 SCALE = QK**-0.5
@@ -604,7 +605,14 @@
 
         @pl.when((tile >= first) & (tile < last))
         def _():
-            out[...] = mm_tn(left[...], right[...]).astype(BF16)
+            height = 2 * GRAD_TILE
+
+            def part(index, _):
+                spot = pl.ds(pl.multiple_of(index * height, height), height)
+                out[spot, :] = mm_tn(left[:, spot], right[...]).astype(BF16)
+                return 0
+
+            lax.fori_loop(0, left.shape[1] // height, part, 0)
 
 
 def weight_grads(pairs):
@@ -648,8 +656,8 @@
 
 def paired_grad_kernel(spans, tiles, steps, *refs):
     count = len(spans)
-    lefts, rights, out = refs[:count], refs[count : 2 * count], refs[2 * count]
-    made, received, send_sem, recv_sem = refs[2 * count + 1 :]
+    lefts, rights = refs[:count], refs[count : 2 * count]
+    out, made, received, send_sem, recv_sem = refs[2 * count :]
     step = pl.program_id(0)
     core = lax.axis_index("col") % 2
     partner = lax.axis_index("col") + 1 - 2 * core
@@ -773,12 +781,13 @@
 def up_kernel(row, *refs, joined):
     if joined:
         pieces, gain, norm_bias = refs[:5], refs[5], refs[6]
-        weight, bias, grad_hidden, second_out, average_out, inverse_out = refs[7:13]
-        hidden_out, grad_out, bias_out = refs[13:]
+        weight, bias, grad_hidden, scales, second_out, average_out, inverse_out = refs[7:14]
+        hidden_out, grad_out, bias_out, sums_out, moved = refs[14:]
         norm_pieces(row, *pieces, gain, norm_bias, second_out, average_out, inverse_out)
         values = second_out
     else:
-        values, weight, bias, grad_hidden, hidden_out, grad_out, bias_out = refs
+        values, weight, bias, grad_hidden, scales = refs[:5]
+        hidden_out, grad_out, bias_out, sums_out, moved = refs[5:]
     before = mm(values[...], weight[...]) + bias[...]
     phi = 0.5 * (1.0 + lax.erf(before * (0.5**0.5)))
     hidden_out[...] = (before * phi).astype(BF16)
@@ -789,8 +798,16 @@
     @pl.when(pl.program_id(0) == 0)
     def _():
         bias_out[...] = jnp.zeros_like(bias_out)
-
-    bias_out[...] += jnp.sum(grad.astype(F32), axis=0, keepdims=True)
+        parts = mm(scales[...], weight[...])
+        moved[0:1] = parts[0:1] + parts[1:2]
+        moved[1:2] = parts[2:3] + parts[3:4]
+
+    wide_grad = grad.astype(F32)
+    bias_out[...] += jnp.sum(wide_grad, axis=0, keepdims=True)
+    plain = jnp.sum(wide_grad * moved[0:1], axis=1, keepdims=True)
+    crossed = jnp.sum(wide_grad * (before - bias[...] - moved[1:2]), axis=1, keepdims=True)
+    lane = lax.broadcasted_iota(jnp.int32, sums_out.shape, 1)
+    sums_out[...] = jnp.where(lane == 0, plain, crossed)
 
 
 def feed_up(pieces, row, gain, norm_bias, weight, bias, grad_hidden):
@@ -824,20 +841,30 @@
     else:
         normed = list(norm_wide(pieces, gain, norm_bias))
         inputs, in_specs, early_specs, early_shapes = [normed[0]], [wide], [], []
+    scales = jnp.stack([gain, norm_bias])
+    high = lax.reduce_precision(scales, 8, 7)
+    low = scales - high
+    rest = jnp.zeros((4, D), F32)
+    scales = jnp.concatenate([high[:1], low[:1], high[1:], low[1:], rest], axis=0).astype(BF16)
     outs = pl.pallas_call(
         functools.partial(up_kernel, joined=joined),
         grid_spec=pltpu.PrefetchScalarGridSpec(
             num_scalar_prefetch=1,
             grid=(steps,),
             in_specs=in_specs
-            + [pl.BlockSpec((D, width), lambda i, r: (0, number)), vector, block],
-            out_specs=early_specs + [block, block, vector],
+            + [
+                pl.BlockSpec((D, width), lambda i, r: (0, number)), vector, block,
+                pl.BlockSpec((8, D), lambda i, r: (0, 0)),
+            ],
+            out_specs=early_specs + [block, block, vector, stat],
+            scratch_shapes=[pltpu.VMEM((8, width), F32)],
         ),
         out_shape=early_shapes
         + [
             jax.ShapeDtypeStruct((rows, width), BF16),
             jax.ShapeDtypeStruct((rows, width), BF16),
             jax.ShapeDtypeStruct((1, width), F32),
+            jax.ShapeDtypeStruct((rows, 128), F32),
         ],
         compiler_params=params(("arbitrary",)),
         name="feed_up",
@@ -846,7 +873,7 @@
             bytes_accessed=2 * (2 * rows + width) * D + 8 * rows * width,
             transcendentals=2 * rows * width,
         ),
-    )(row, *inputs, array, bias[None, :], grad_hidden)
+    )(row, *inputs, array, bias[None, :], grad_hidden, scales)
     return normed + list(outs)
 
 
@@ -865,14 +892,22 @@
     values, weights = refs[:count], refs[count : 2 * count]
     outs = refs[2 * count :]
     step = pl.program_id(0)
-    total = mm_nt(values[0][...], weights[0][...])
-    for x, w in zip(values[1:], weights[1:]):
-        total = total + mm_nt(x[...], w[...])
-    for index, out in enumerate(outs):
-
-        @pl.when(step // 2 == index)
-        def _():
-            out[0] = total.astype(out.dtype)
+    strip = values[0].shape[0] // 2
+
+    def part(number, _):
+        spot = pl.ds(pl.multiple_of(number * strip, strip), strip)
+        total = mm_nt(values[0][spot, :], weights[0][...])
+        for x, w in zip(values[1:], weights[1:]):
+            total = total + mm_nt(x[spot, :], w[...])
+        for index, out in enumerate(outs):
+
+            @pl.when(step // 2 == index)
+            def _():
+                out[0, spot, :] = total.astype(out.dtype)
+
+        return 0
+
+    lax.fori_loop(0, 2, part, 0)
 
 
 def partial_blocks(values, weights, row, first, kinds):
@@ -926,17 +961,19 @@
     return tuple(partial_blocks(values, weights, row, 0, (BF16, BF16)))
 
 
-def reduce_row_finish(sends, values, weights, row, between=None):
+def reduce_row_finish(sends, values, weights, row, between=None, tied=None):
     if lax.axis_size("row") != 4:
         total = lax.psum_scatter(sends, "row", scatter_dimension=1, tiled=True).astype(F32)
-        return total, between() if between else None
+        return total, between(tied) if between else None
     from_x = permute_row(sends[0], X_PAIRS)
     from_y = permute_row(sends[1], Y_PAIRS)
+    keep, own = partial_blocks(values, weights, row, 2, (BF16, F32))
     extra = None
     if between is not None:
-        extra = between()
+        if tied is not None:
+            keep, own, tied = in_order(keep, own, tied)
+        extra = between(tied)
         from_x, from_y, extra = in_order(from_x, from_y, extra)
-    keep, own = partial_blocks(values, weights, row, 2, (BF16, F32))
     next_y = (keep[0].astype(F32) + from_x[1].astype(F32)).astype(BF16)
     next_x = (keep[1].astype(F32) + from_y[1].astype(F32)).astype(BF16)
     last_y = permute_row(next_y, Y_PAIRS)
@@ -989,9 +1026,17 @@
     return first + permute_row(first, Y_PAIRS)
 
 
-def norm_backward(grad_out, normal, inverse, gain_vector):
+def sum_row_direct(value):
+    if lax.axis_size("row") != 4:
+        return lax.psum(value, "row")
+    others = [permute_row(value, pairs) for pairs in (X_PAIRS, Y_PAIRS, D_PAIRS)]
+    return value + others[0] + (others[1] + others[2])
+
+
+def norm_backward(grad_out, normal, inverse, gain_vector, sums=None):
     scaled = grad_out * gain_vector
-    sums = sum_row_small(jnp.stack([jnp.sum(scaled, axis=1), jnp.sum(scaled * normal, axis=1)]))
+    if sums is None:
+        sums = sum_row_small(jnp.stack([jnp.sum(scaled, axis=1), jnp.sum(scaled * normal, axis=1)]))
     means = sums / D
     grad_in = inverse * (scaled - means[0][:, None] - normal * means[1][:, None])
     return (grad_in, jnp.sum(grad_out * normal, axis=0), jnp.sum(grad_out, axis=0))
@@ -1036,41 +1081,59 @@
             )
         pl.semaphore_wait(barrier, SLOTS - 1)
 
-    def run(self, programs):
+    def run(self, programs, drain=True):
         for place, program in enumerate(programs):
+            if not program:
+                continue
 
             @pl.when(self.place == place)
             def _():
-                sent = []
                 for action in program:
                     if callable(action):
                         action()
                     elif action >= 0:
                         self.copy(action).start()
-                        sent.append(action)
                     else:
                         self.copy(~action).wait_recv()
-                for index in sent:
-                    self.copy(index).wait_send()
+
+        if drain:
+            self.drain()
+
+    def drain(self):
+        for place in range(SLOTS):
+            mine = [i for i, message in enumerate(self.messages) if message[0] == place]
+            if mine:
+
+                @pl.when(self.place == place)
+                def _():
+                    for index in mine:
+                        self.copy(index).wait_send()
 
 
 def scaled_add(meta, rates, target, terms, rows):
     heads = target.shape[0]
+    strip = 64
     for head in range(heads):
-        total = None
-        for term in terms:
-            if isinstance(term, tuple):
-                ref, slot = term
-                exponent = jnp.maximum(
-                    trunk_reference(meta, jnp.int32(3), rows)
-                    - trunk_reference(meta, jnp.int32(slot), rows),
-                    0,
-                )
-                value = ref[head].astype(F32) * power(rates[head], exponent, HV)
-            else:
-                value = term[head].astype(F32)
-            total = value if total is None else total + value
-        target[head] = total.astype(BF16)
+
+        def add(index, _):
+            spot = pl.ds(pl.multiple_of(index * strip, strip), strip)
+            total = None
+            for term in terms:
+                if isinstance(term, tuple):
+                    ref, slot = term
+                    exponent = jnp.maximum(
+                        trunk_reference(meta, jnp.int32(3), rows)
+                        - trunk_reference(meta, jnp.int32(slot), rows),
+                        0,
+                    )
+                    value = ref[head, spot, :].astype(F32) * power(rates[head], exponent, HV)
+                else:
+                    value = term[head, spot, :].astype(F32)
+                total = value if total is None else total + value
+            target[head, spot, :] = total.astype(BF16)
+            return 0
+
+        lax.fori_loop(0, QK // strip, add, 0)
 
 
 def share_kernel(rows, meta, rates, ex, sh, shift, tot, send_sem, recv_sem):
@@ -1160,7 +1223,9 @@
     )(meta, rates, exports)
 
 
-def return_kernel(rows, meta, rates, y, first, own0, own1, own2, rx, tx, send_sem, recv_sem):
+def return_kernel(
+    rows, meta, rates, y, first, left, right, own0, own1, own2, grads, rx, tx, send_sem, recv_sem
+):
     messages = [
         (7, 6, y.at[3], rx.at[0]),
         (7, 6, y.at[4], rx.at[1]),
@@ -1194,20 +1259,24 @@
     def add(target, *terms):
         return lambda: scaled_add(meta, rates, target, terms, rows)
 
+    def multiply(begin, end):
+        def tile(index, _):
+            spot = pl.ds(pl.multiple_of(index * GRAD_TILE, GRAD_TILE), GRAD_TILE)
+            grads[spot, :] = mm_tn(left[:, spot], right[...]).astype(BF16)
+            return 0
+
+        lax.fori_loop(begin, end, tile, 0)
+
+    tiles = D // GRAD_TILE
     exchange.greet()
+    exchange.run([[], [23], [18, 19], [], [], [10, 11, 12, 24], [3, 4], [0, 1, 2, 25]], False)
+    multiply(0, tiles // 2)
     exchange.run(
         [
-            [~23, ~22, add(own0, rx.at[0], rx.at[1])],
-            [23, ~21],
-            [18, 19, ~20],
-            [
-                ~18, ~19, ~15,
-                add(tx.at[0], y.at[0], rx.at[1], (rx.at[0], 0)), 22,
-                add(tx.at[1], y.at[1], rx.at[2], (rx.at[0], 1)), 21,
-                add(tx.at[2], y.at[2], (rx.at[0], 2)), 20,
-                add(own0, rx.at[0], y.at[3]),
-                ~16, ~17,
-            ],
+            [],
+            [],
+            [],
+            [],
             [
                 ~10, ~7, add(tx.at[0], y.at[3], rx.at[0], rx.at[3]), 15,
                 ~11, ~8, add(tx.at[1], y.at[4], rx.at[1], rx.at[4]), 16,
@@ -1217,34 +1286,55 @@
                 ~24,
             ],
             [
-                10, 11, 12, 24,
                 ~5, add(tx.at[0], y.at[6], rx.at[0]), 13,
                 ~6, add(tx.at[1], y.at[7], rx.at[1]), 14,
             ],
             [
-                3, 4,
                 ~0, add(tx.at[0], y.at[3], rx.at[0]), 7,
                 ~1, add(tx.at[1], y.at[4], rx.at[1]), 8,
                 ~2, add(tx.at[2], y.at[5], rx.at[2]), 9,
                 ~25,
             ],
             [
-                0, 1, 2, 25,
                 ~3, add(tx.at[0], y.at[6], rx.at[0]), 5,
                 ~4, add(tx.at[1], y.at[7], rx.at[1]), 6,
             ],
-        ]
-    )
-
-
-def return_states(meta, rates, exports, first_state, rows):
+        ],
+        False,
+    )
+    multiply(tiles // 2, tiles)
+    exchange.run(
+        [
+            [~23, ~22, add(own0, rx.at[0], rx.at[1])],
+            [~21],
+            [~20],
+            [
+                ~18, ~19, ~15,
+                add(tx.at[0], y.at[0], rx.at[1], (rx.at[0], 0)), 22,
+                add(tx.at[1], y.at[1], rx.at[2], (rx.at[0], 1)), 21,
+                add(tx.at[2], y.at[2], (rx.at[0], 2)), 20,
+                add(own0, rx.at[0], y.at[3]),
+                ~16, ~17,
+            ],
+            [],
+            [],
+            [],
+            [],
+        ],
+        False,
+    )
+    exchange.drain()
+
+
+def return_states(meta, rates, exports, first_state, left, right, rows):
     heads = exports.shape[1]
     state = (heads, QK, HV)
     return pl.pallas_call(
         functools.partial(return_kernel, rows),
-        in_specs=[smem(), smem(), vmem(), vmem()],
-        out_specs=[vmem()] * 3,
-        out_shape=[jax.ShapeDtypeStruct(state, BF16)] * 3,
+        in_specs=[smem(), smem(), vmem(), vmem(), vmem(), vmem()],
+        out_specs=[vmem()] * 4,
+        out_shape=[jax.ShapeDtypeStruct(state, BF16)] * 3
+        + [jax.ShapeDtypeStruct((D, right.shape[1]), BF16)],
         scratch_shapes=[
             pltpu.VMEM((8,) + state, BF16),
             pltpu.VMEM((3,) + state, BF16),
@@ -1258,7 +1348,7 @@
         cost_estimate=pl.CostEstimate(
             flops=0, bytes_accessed=100 * 1024 * 1024, transcendentals=0
         ),
-    )(meta, rates, exports, first_state)
+    )(meta, rates, exports, first_state, left, right)
 
 
 def sum_col(value):
@@ -1383,9 +1473,10 @@
     middle_pieces, (fed_wide, grad_hidden) = gather_row(
         middle.astype(BF16), later=(feed_gradient, fed_pieces)
     )
-    second_wide, second_average, second_inverse, hidden, grad_before, up_bias_grad = feed_up(
-        middle_pieces, row_ref, gains[2], gains[3], up_part, up_bias, grad_hidden
-    )
+    second_wide, second_average, second_inverse, hidden, grad_before, up_bias_grad, feed_sums = (
+        feed_up(middle_pieces, row_ref, gains[2], gains[3], up_part, up_bias, grad_hidden)
+    )
+    feed_sums = sum_row_direct(feed_sums[:, :2].T)
     sends = reduce_row_start([grad_before], [up_part], row_ref)
     sends, hidden = in_order(sends, hidden)
     second_back, feed_partial = reduce_row_finish(
@@ -1393,7 +1484,8 @@
         [grad_before],
         [up_part],
         row_ref,
-        lambda: column_grads([(fed_wide, hidden), (second_wide, grad_before)], 3),
+        lambda hidden: weight_grads([(fed_wide, hidden), (second_wide, grad_before)]),
+        hidden,
     )
     feed_grad = scatter_col(feed_partial)
     grad_fed = fed_low.astype(F32)
@@ -1401,40 +1493,33 @@
 
     second_normal = (middle - second_average[:, :1]) * second_inverse[:, :1]
     grad_middle_norm, second_gain_grad, second_bias_grad = norm_backward(
-        second_back, second_normal, second_inverse[:, :1], second_gain
+        second_back, second_normal, second_inverse[:, :1], second_gain, feed_sums
     )
     grad_middle = grad_fed + grad_middle_norm
     grad_pieces, fed_sends = gather_row(
         grad_middle.astype(BF16), lambda: reduce_row_start([hidden], [down_part], row_ref)
     )
     grad_wide = join(grad_pieces, row_ref)
-    out_partial = column_grads([(grad_wide, gated)], 4)
-    out_partial, grad_wide, feed_grad, fed_sends = in_order(
-        out_partial, grad_wide, feed_grad, fed_sends
-    )
-    out_grad = scatter_col(out_partial)
-    fed_out, gate_results = reduce_row_finish(
-        fed_sends,
-        [hidden],
-        [down_part],
-        row_ref,
-        lambda: gate_back(
-            meta, rates, grad_wide, out_part, gate_raw, normal, inverse, query_rot, group_gain, group_bias
-        ),
+    fed_sends, grad_wide = in_order(fed_sends, grad_wide)
+    fed_out, out_partial = reduce_row_finish(
+        fed_sends, [hidden], [down_part], row_ref, lambda _: column_grads([(grad_wide, gated)], 4)
     )
     fed_out = fed_out + down_bias
     layer_out = middle + fed_out
-    grad_gate, grad_retained, group_gain_grad, group_bias_grad, returns, first_state = gate_results
-    own = return_states(meta, rates, returns, first_state, rows)
-    grad_gate, own = in_order(grad_gate, own)
-    gate_partial = column_grads([(first_wide, grad_gate)], 5)
-    gate_partial, own, out_grad = in_order(gate_partial, own, out_grad)
+    out_partial, grad_wide, feed_grad = in_order(out_partial, grad_wide, feed_grad)
+    out_grad = scatter_col(out_partial)
+    grad_gate, grad_retained, group_gain_grad, group_bias_grad, returns, first_state = gate_back(
+        meta, rates, grad_wide, out_part, gate_raw, normal, inverse, query_rot, group_gain, group_bias
+    )
+    own0, own1, own2, gate_partial = return_states(
+        meta, rates, returns, first_state, first_wide, grad_gate, rows
+    )
+    gate_partial, own0, out_grad = in_order(gate_partial, own0, out_grad)
+    own = (own0, own1, own2)
     gate_grad = scatter_col(gate_partial)
     grad_query, grad_key, grad_value = retain_back(
         meta, rates, query_rot, key_rot, value_low, grad_retained, states, cosine, sine, own
     )
-    back_values = [grad_query, grad_key, grad_value, grad_gate]
-    back_weights = [query_part, key_part, value_part, gate_part]
     back_values = [grad_query, grad_key, grad_value, grad_gate]
     back_weights = [query_part, key_part, value_part, gate_part]
     sends = reduce_row_start(back_values, back_weights, row_ref)
@@ -1444,13 +1529,11 @@
         back_values,
         back_weights,
         row_ref,
-        lambda: column_grads(
+        lambda _: column_grads(
             [(first_wide, grad_query), (first_wide, grad_key), (first_wide, grad_value)], 6
         ),
     )
-    project_partial, gate_grad, group_gain_grad = in_order(
-        project_partial, gate_grad, group_gain_grad
-    )
+    project_partial, gate_grad = in_order(project_partial, gate_grad)
     project_grad = scatter_col(project_partial)
 
     first_normal = (tokens.astype(F32) - first_average[:, :1]) * first_inverse[:, :1]
@@ -1459,25 +1542,25 @@
     )
     tokens_grad = grad_middle + grad_first
 
-    vectors, _ = sum_col_vectors(
+    squares = jnp.stack(
+        [
+            jnp.sum(column * layer_out * layer_out),
+            jnp.sum(column * attended * attended),
+            jnp.sum(column * fed_out * fed_out),
+        ]
+    )
+    vectors, col_squares = sum_col_vectors(
         (
+            first_gain_grad,
+            first_bias_grad,
             group_gain_grad[0],
             group_bias_grad[0],
             second_gain_grad,
             second_bias_grad,
             up_bias_grad[0],
             down_bias_grad,
-        )
-    )
-    squares = jnp.stack(
-        [
-            jnp.sum(column * layer_out * layer_out),
-            jnp.sum(column * attended * attended),
-            jnp.sum(column * fed_out * fed_out),
-        ]
-    )
-    last, col_squares = sum_col_vectors(
-        (first_gain_grad, first_bias_grad), jnp.concatenate([squares, jnp.zeros((125,), F32)])
+        ),
+        jnp.concatenate([squares, jnp.zeros((125,), F32)]),
     )
     totals = sum_row_small(col_squares[None, :])[0, :3]
     valid_count = jnp.sum(segment_lengths).astype(F32) * D
@@ -1492,14 +1575,7 @@
         out_grad.T,
         feed_grad[:, wide:],
         feed_grad[:, :wide].T,
-        last[0],
-        last[1],
-        vectors[0],
-        vectors[1],
-        vectors[2],
-        vectors[3],
-        vectors[4],
-        vectors[5],
+        *vectors,
         norm_values,
     )
 

time: 742 us -> 734 us (0.989)
  waiting for transfers between devices: 220 us -> 209 us
    pallas_call x4 -> x2, Pallas kernels: 72.4 us -> 39 us  [paired_grads(): pl.pallas_call(functools.partial(paired_grad_kernel, tuple(spans), tiles,...]
    pallas_call x0 -> x1, Pallas kernels: none -> 18.6 us  [weight_grads(): pl.pallas_call(functools.partial(weight_grad_kernel, tuple(spans)), grid=...]
    ppermute x41 -> x42, waiting for transfers between devices: 175 us -> 160 us  [permute_row(): return lax.ppermute(value, 'row', pairs)]
    ppermute x41 -> x42, starting transfers between devices: 50 us -> 52.9 us  [permute_row(): return lax.ppermute(value, 'row', pairs)]
    unnamed x114 -> x138, local copies, waits for them, and re-layouts: 17.6 us -> 18.8 us
  transfers between devices with their start and end apart: 55 -> 53, of which waited for: 32 -> 28; matrix products, arithmetic and copies ran while one was open for 9% -> 10% of each run, Pallas kernels for 44% -> 44%
where the time goes in v4:
time: 734 us; the launch traced here: 725 us
  Pallas kernels  344 us (47%)
  waiting for transfers between devices  209 us (28%)
  starting transfers between devices  59.3 us (8%)
  other arithmetic  53.6 us (7%)
  local copies, waits for them, and re-layouts  43.5 us (6%)
  between operations  16.1 us (2%)
    ppermute x42, waiting for transfers between devices, permute_row(): return lax.ppermute(value, 'row', pairs)  160 us
    pallas_call x8, Pallas kernels, partial_blocks(): pl.pallas_call(functools.partial(partial_kernel, count), grid_spec=pltpu....  80 us
    pallas_call x1, Pallas kernels, return_states(): pl.pallas_call(functools.partial(return_kernel, rows), in_specs=[smem(),...  56.1 us
    ppermute x42, starting transfers between devices, permute_row(): return lax.ppermute(value, 'row', pairs)  52.9 us
    all_gather x4, waiting for transfers between devices, gather_col(): return lax.all_gather(weight, 'col', axis=0, tiled=True)  39.2 us
    pallas_call x2, Pallas kernels, paired_grads(): pl.pallas_call(functools.partial(paired_grad_kernel, tuple(spans), tiles,...  39 us
    pallas_call x1, Pallas kernels, share_states(): pl.pallas_call(functools.partial(share_kernel, rows), in_specs=[smem(), s...  25.3 us
    pallas_call x1, Pallas kernels, gate_back(): pl.pallas_call(functools.partial(gate_back_kernel, rows, chunks), grid=(h...  21.4 us
  transfers between devices with their start and end apart: 53, of which 28 were waited for; matrix products, arithmetic and copies ran while one was open for 10% of the time, Pallas kernels for 44%

profile of v4, /device:TPU:0, one launch (start us, length us, event | category | flops | bytes accessed | tf_op | source)
XLA Modules:
  0.0 725.4 jit_solution(17710240824014004523)
XLA Ops:
  7.2 2.3 pad_maximum_fusion.3
  13.1 3.0 collective-permute-start.5
  23.5 24.4 %collective-permute-done.from_x = bf16[1280,512]{1,0:T(8,128)(2,1)} collective-permute-done((bf16[1280,512]{1,0:T(8,128)(2,1)S(1)}, bf16[1280,512]{1,0:T(8,128)(2,1)}, u32[]{:S(2)}, u32[]{:S(2)}) %collective-permute-start) | collective-permute-done | bytes 1310752 | tf_op jit(solution)/shard_map/ppermute | solution.py:950
  54.1 10.2 %collective-permute-done.2.far_a = bf16[640,512]{1,0:T(8,128)(2,1)S(1)} collective-permute-done((bf16[640,512]{1,0:T(8,128)(2,1)S(1)}, bf16[640,512]{1,0:T(8,128)(2,1)S(1)}, u32[]{:S(2)}, u32[]{:S(2)}) %collective-permute-start.2) | collective-permute-done | bytes 655392 | tf_op jit(solution)/shard_map/ppermute | solution.py:950
  67.3 7.5 %join_norm.1 = (bf16[1280,2048]{1,0:T(8,128)(2,1)}, f32[1280,128]{1,0:T(8,128)}, f32[1280,128]{1,0:T(8,128)}) custom-call(s32[1]{0:T(128)} %bitcast.row, bf16[1280,512]{1,0:T(8,128)(2,1)} %own.1, bf16[1280,512]{1,0:T(8,128)(2,1)} %collective-permute-done.from_x, bf16[1280,512]{1,0:T(8,128)(2,1)} %collective-permute-done.1.from_y, ...), custom_call_target="tpu_custom_call" | custom-call | flops 20971520 | bytes 10485760 | tf_op jit(solution)/shard_map/join_norm/pallas_call | solution.py:491
  77.0 3.7 multiply_sine_fusion
  81.8 13.1 %all-gather.5.cloned.1.call-done.weight.refs_4_.refs_5_.refs_6_ = bf16[2048,2048]{1,0:T(8,128)(2,1)} async-done(((bf16[256,2048]{1,0:T(8,128)(2,1)}), bf16[2048,2048]{1,0:T(8,128)(2,1)}) %all-gather.5.cloned.1.call-update) | async-done | bytes 8388624 | tf_op jit(solution)/shard_map/all_gather | solution.py:1046
  95.0 21.3 %project.1 = (bf16[1280,512]{1,0:T(8,128)(2,1)}, bf16[1280,512]{1,0:T(8,128)(2,1)}, bf16[1280,1024]{1,0:T(8,128)(2,1)}, bf16[3,2,256,512]{3,2,1,0:T(8,128)(2,1)}) custom-call(s32[22]{0:T(128)} %pad_add_fusion.meta, f32[2]{0:T(128)} %subtract_log_fusion.rates, bf16[1280,2048]{1,0:T(8,128)(2,1)} %get-tuple-element.130.values.wide.left.refs_0_.refs_1_.refs_2_, ...), custom_call_target="tpu_custom_call" | custom-call | flops 10737418240 | bytes 13631488 | tf_op jit(solution)/shard_map/project/pallas_call | solution.py:554
  122.8 25.3 %share_states.1 = (bf16[8,2,256,512]{3,2,1,0:T(8,128)(2,1)S(1)}, bf16[2,256,512]{2,1,0:T(8,128)(2,1)S(1)}) custom-call(s32[22]{0:T(128)S(1)} %copy-done.5, f32[2]{0:T(128)S(1)} %copy-done.7, bf16[3,2,256,512]{3,2,1,0:T(8,128)(2,1)S(1)} %copy-done.3), custom_call_target="tpu_custom_call" | custom-call | bytes 104857600 | tf_op jit(solution)/shard_map/share_states/pallas_call | solution.py:1203
  150.9 21.3 %retention_forward.1 = (f32[1280,1024]{1,0:T(8,128)}, bf16[1280,1024]{1,0:T(8,128)(2,1)}, bf16[1280,1024]{1,0:T(8,128)(2,1)}, f32[2,1280,128]{2,1,0:T(8,128)}, bf16[2,5,256,512]{3,2,1,0:T(8,128)(2,1)}) custom-call(s32[22]{0:T(128)} %pad_add_fusion.meta, f32[2]{0:T(128)} %subtract_log_fusion.rates, bf16[1280,512]{1,0:T(8,128)(2,1)} %get-tuple-element.135.query, ...), custom_call_target="tpu_custom_call" | custom-call | flops 7717519360 | bytes 20971520 | tf_op jit(solution)/shard_map/retention_forward/pallas_call | solution.py:203
  172.2 26.0 %all-gather.9.cloned.1.call-done.refs_1_.weight = bf16[2048,1024]{1,0:T(8,128)(2,1)} async-done(((bf16[256,1024]{1,0:T(8,128)(2,1)}), bf16[2048,1024]{1,0:T(8,128)(2,1)}) %all-gather.9.cloned.1.call-update) | async-done | bytes 4194320 | tf_op jit(solution)/shard_map/all_gather | solution.py:1046
  198.2 8.0 %partial_blocks.9 = (bf16[2,640,512]{2,1,0:T(8,128)(2,1)}, bf16[2,640,512]{2,1,0:T(8,128)(2,1)}) custom-call(s32[1]{0:T(128)} %bitcast.row, bf16[1280,1024]{1,0:T(8,128)(2,1)} %get-tuple-element.146.refs_0_.refs_1_, bf16[2048,1024]{1,0:T(8,128)(2,1)} %all-gather.9.cloned.1.call-done.refs_1_.weight), custom_call_target="tpu_custom_call" | custom-call | flops 2684354560 | bytes 12058624 | tf_op jit(solution)/shard_map/partial_blocks/pallas_call | solution.py:930
  209.2 8.5 %partial_blocks.8 = (bf16[2,640,512]{2,1,0:T(8,128)(2,1)}, f32[2,640,512]{2,1,0:T(8,128)}) custom-call(s32[1]{0:T(128)} %bitcast.row, bf16[1280,1024]{1,0:T(8,128)(2,1)} %get-tuple-element.146.refs_0_.refs_1_, bf16[2048,1024]{1,0:T(8,128)(2,1)} %all-gather.9.cloned.1.call-done.refs_1_.weight), custom_call_target="tpu_custom_call" | custom-call | flops 2684354560 | bytes 12058624 | tf_op jit(solution)/shard_map/partial_blocks/pallas_call | solution.py:930
  217.7 19.7 %collective-permute-done.11 = bf16[2,640,512]{2,1,0:T(8,128)(2,1)S(1)} collective-permute-done((bf16[2,640,512]{2,1,0:T(8,128)(2,1)}, bf16[2,640,512]{2,1,0:T(8,128)(2,1)S(1)}, u32[]{:S(2)}, u32[]{:S(2)}) %collective-permute-start.11) | collective-permute-done | bytes 1310752 | tf_op jit(solution)/shard_map/ppermute | solution.py:950
  243.1 13.6 %collective-permute-done.12 = bf16[640,512]{1,0:T(8,128)(2,1)S(1)} collective-permute-done((bf16[640,512]{1,0:T(8,128)(2,1)S(1)}, bf16[640,512]{1,0:T(8,128)(2,1)S(1)}, u32[]{:S(2)}, u32[]{:S(2)}) %collective-permute-start.12) | collective-permute-done | bytes 655392 | tf_op jit(solution)/shard_map/ppermute | solution.py:950
  262.6 27.1 %collective-permute-done.16.refs_2_ = bf16[1280,512]{1,0:T(8,128)(2,1)S(1)} collective-permute-done((bf16[1280,512]{1,0:T(8,128)(2,1)S(1)}, bf16[1280,512]{1,0:T(8,128)(2,1)S(1)}, u32[]{:S(2)}, u32[]{:S(2)}) %collective-permute-start.16) | collective-permute-done | bytes 1310752 | tf_op jit(solution)/shard_map/ppermute | solution.py:950
  294.7 5.3 join.2.values.refs_0_
  300.0 9.9 %matmul.1.refs_9_ = bf16[1280,1024]{1,0:T(8,128)(2,1)} custom-call(bf16[1280,2048]{1,0:T(8,128)(2,1)} %join.2.values.refs_0_, bf16[2048,2048]{1,0:T(8,128)(2,1)} %all-gather.11.cloned.1.call-done.weight.refs_7_.refs_1_), custom_call_target="tpu_custom_call" | custom-call | flops 5368709120 | bytes 9437184 | tf_op jit(solution)/shard_map/matmul/pallas_call | solution.py:583
  309.9 19.3 %feed_up.1 = (bf16[1280,2048]{1,0:T(8,128)(2,1)}, f32[1280,128]{1,0:T(8,128)}, f32[1280,128]{1,0:T(8,128)}, bf16[1280,1024]{1,0:T(8,128)(2,1)}, bf16[1280,1024]{...) custom-call(s32[1]{0:T(128)} %bitcast.row, bf16[1280,512]{1,0:T(8,128)(2,1)} %copy-done.39, ...), custom_call_target="tpu_custom_call" | custom-call | flops 5368709120 | bytes 25165824 | tf_op jit(solution)/shard_map/feed_up/pallas_call | solution.py:849
  329.2 8.2 %partial_blocks.10 = (bf16[2,640,512]{2,1,0:T(8,128)(2,1)}, bf16[2,640,512]{2,1,0:T(8,128)(2,1)}) custom-call(s32[1]{0:T(128)} %bitcast.row, bf16[1280,1024]{1,0:T(8,128)(2,1)} %get-tuple-element.166.refs_0_.refs_3_, bf16[2048,2048]{1,0:T(8,128)(2,1)} %all-gather.11.cloned.1.call-done.weight.refs_7_.refs_1_), custom_call_target="tpu_custom_call" | custom-call | flops 2684354560 | bytes 12058624 | tf_op jit(solution)/shard_map/partial_blocks/pallas_call | solution.py:930
  338.8 8.3 %partial_blocks.12 = (bf16[2,640,512]{2,1,0:T(8,128)(2,1)}, f32[2,640,512]{2,1,0:T(8,128)}) custom-call(s32[1]{0:T(128)} %bitcast.row, bf16[1280,1024]{1,0:T(8,128)(2,1)} %get-tuple-element.166.refs_0_.refs_3_, bf16[2048,2048]{1,0:T(8,128)(2,1)} %all-gather.11.cloned.1.call-done.weight.refs_7_.refs_1_), custom_call_target="tpu_custom_call" | custom-call | flops 2684354560 | bytes 12058624 | tf_op jit(solution)/shard_map/partial_blocks/pallas_call | solution.py:930
  347.1 18.6 %weight_grads.1 = bf16[2048,2048]{1,0:T(8,128)(2,1)} custom-call(bf16[1280,2048]{1,0:T(8,128)(2,1)} %join.2.values.refs_0_, bf16[1280,2048]{1,0:T(8,128)(2,1)} %get-tuple-element.179.refs_1_, bf16[1280,1024]{1,0:T(8,128)(2,1)} %get-tuple-element.180.refs_0_.refs_2_, bf16[1280,1024]{1,0:T(8,128)(2,1)} %get-tuple-element.166.refs_0_.refs_3_), custom_call_target="tpu_custom_call" | custom-call | flops 10737418240 | bytes 18874368 | tf_op jit(solution)/shard_map/weight_grads/pallas_call | solution.py:641
  381.6 8.2 %collective-permute-done.21 = bf16[640,512]{1,0:T(8,128)(2,1)S(1)} collective-permute-done((bf16[640,512]{1,0:T(8,128)(2,1)S(1)}, bf16[640,512]{1,0:T(8,128)(2,1)S(1)}, u32[]{:S(2)}, u32[]{:S(2)}) %collective-permute-start.21) | collective-permute-done | bytes 655392 | tf_op jit(solution)/shard_map/ppermute | solution.py:950
  392.7 3.7 fusion.36
  398.9 8.1 %partial_blocks.13 = (bf16[2,640,512]{2,1,0:T(8,128)(2,1)}, bf16[2,640,512]{2,1,0:T(8,128)(2,1)}) custom-call(s32[1]{0:T(128)} %bitcast.row, bf16[1280,1024]{1,0:T(8,128)(2,1)} %get-tuple-element.180.refs_0_.refs_2_, bf16[2048,2048]{1,0:T(8,128)(2,1)} %all-gather.11.cloned.1.call-done.weight.refs_7_.refs_1_), custom_call_target="tpu_custom_call" | custom-call | flops 2684354560 | bytes 12058624 | tf_op jit(solution)/shard_map/partial_blocks/pallas_call | solution.py:930
  407.0 13.7 %collective-permute-done.27.from_y = bf16[1280,512]{1,0:T(8,128)(2,1)} collective-permute-done((bf16[1280,512]{1,0:T(8,128)(2,1)}, bf16[1280,512]{1,0:T(8,128)(2,1)}, u32[]{:S(2)}, u32[]{:S(2)}) %collective-permute-start.27) | collective-permute-done | bytes 1310752 | tf_op jit(solution)/shard_map/ppermute | solution.py:950
  420.7 3.3 collective-permute-done.26.from_x
  429.2 7.7 %collective-permute-done.29.far_b = bf16[640,512]{1,0:T(8,128)(2,1)S(1)} collective-permute-done((bf16[640,512]{1,0:T(8,128)(2,1)S(1)}, bf16[640,512]{1,0:T(8,128)(2,1)S(1)}, u32[]{:S(2)}, u32[]{:S(2)}) %collective-permute-start.29) | collective-permute-done | bytes 655392 | tf_op jit(solution)/shard_map/ppermute | solution.py:950
  438.8 5.3 join.3.refs_0_.wide
  445.9 12.2 %paired_grads.2 = bf16[4,256,1024]{2,1,0:T(8,128)(2,1)} custom-call(bf16[1280,2048]{1,0:T(8,128)(2,1)} %join.3.refs_0_.wide, bf16[1280,1024]{1,0:T(8,128)(2,1)} %get-tuple-element.146.refs_0_.refs_1_), custom_call_target="tpu_custom_call" | custom-call | flops 5368709120 | bytes 14680064 | tf_op jit(solution)/shard_map/paired_grads/pallas_call | solution.py:732
  458.1 8.0 %collective-permute-done.30 = bf16[2,640,512]{2,1,0:T(8,128)(2,1)} collective-permute-done((bf16[2,640,512]{2,1,0:T(8,128)(2,1)}, bf16[2,640,512]{2,1,0:T(8,128)(2,1)}, u32[]{:S(2)}, u32[]{:S(2)}) %collective-permute-start.30) | collective-permute-done | bytes 1310752 | tf_op jit(solution)/shard_map/ppermute | solution.py:950
  467.6 4.9 reduce-scatter.5.cloned.1.call-done
  472.6 2.8 convert_element_type.275
  475.5 21.4 %gate_backward.1 = (bf16[1280,1024]{1,0:T(8,128)(2,1)}, bf16[1280,1024]{1,0:T(8,128)(2,1)}, f32[1,1024]{1,0:T(1,128)}, f32[1,1024]{1,0:T(1,128)}, bf16[8,2,256,5...) custom-call(s32[22]{0:T(128)} %pad_add_fusion.meta, f32[2]{0:T(128)} %subtract_log_fusion.rates, ...), custom_call_target="tpu_custom_call" | custom-call | flops 6039797760 | bytes 31457280 | tf_op jit(solution)/shard_map/gate_backward/pallas_call | solution.py:300
  498.6 2.2 copy-done.1
  501.9 56.1 %return_states.1 = (bf16[2,256,512]{2,1,0:T(8,128)(2,1)S(1)}, bf16[2,256,512]{2,1,0:T(8,128)(2,1)S(1)}, bf16[2,256,512]{2,1,0:T(8,128)(2,1)S(1)}, bf16[2048,1024]{1,0:T(8,128)(2,1)S(1)}) custom-call(s32[22]{0:T(128)S(1)} %copy-done.6, f32[2]{0:T(128)S(1)} %copy-done.8, bf16[8,2,256,512]{3,2,1,0:T(8,128)(2,1)S(1)} %copy-done.1, ...), custom_call_target="tpu_custom_call" | custom-call | bytes 104857600 | tf_op jit(solution)/shard_map/return_states/pallas_call | solution.py:1332
  564.6 14.0 %retention_backward.1 = (bf16[1280,512]{1,0:T(8,128)(2,1)}, bf16[1280,512]{1,0:T(8,128)(2,1)}, bf16[1280,1024]{1,0:T(8,128)(2,1)}) custom-call(s32[22]{0:T(128)} %pad_add_fusion.meta, f32[2]{0:T(128)} %subtract_log_fusion.rates, bf16[1280,512]{1,0:T(8,128)(2,1)} %get-tuple-element.135.query, bf16[1280,512]{1,0:T(8,128)(2,1)} %get-tuple-element.136.key, ...), custom_call_target="tpu_custom_call" | custom-call | flops 5033164800 | bytes 15728640 | tf_op jit(solution)/shard_map/retention_backward/pallas_call | solution.py:395
  578.6 15.1 %partial_blocks.15 = (bf16[2,640,512]{2,1,0:T(8,128)(2,1)}, bf16[2,640,512]{2,1,0:T(8,128)(2,1)}) custom-call(s32[1]{0:T(128)} %bitcast.row, bf16[1280,512]{1,0:T(8,128)(2,1)} %get-tuple-element.216.refs_0_.refs_3_, bf16[1280,512]{1,0:T(8,128)(2,1)} %get-tuple-element.217.refs_1_.refs_4_, bf16[1280,1024]{1,0:T(8,128)(2,1)} %get-tuple-element.224.refs_2_.refs_5_, ...), custom_call_target="tpu_custom_call" | custom-call | flops 8053063680 | bytes 25690112 | tf_op jit(solution)/shard_map/partial_blocks/pallas_call | solution.py:930
  596.5 26.7 %paired_grads.3 = bf16[4,256,2048]{2,1,0:T(8,128)(2,1)} custom-call(bf16[1280,2048]{1,0:T(8,128)(2,1)} %get-tuple-element.130.values.wide.left.refs_0_.refs_1_.refs_2_, bf16[1280,2048]{1,0:T(8,128)(2,1)} %get-tuple-element.130.values.wide.left.refs_0_.refs_1_.refs_2_, bf16[1280,2048]{1,0:T(8,128)(2,1)} %get-tuple-element.130.values.wide.left.refs_0_.refs_1_.refs_2_, ...), custom_call_target="tpu_custom_call" | custom-call | flops 10737418240 | bytes 18874368 | tf_op jit(solution)/shard_map/paired_grads/pallas_call | solution.py:732
  626.8 8.3 %partial_blocks.11 = (bf16[2,640,512]{2,1,0:T(8,128)(2,1)}, f32[2,640,512]{2,1,0:T(8,128)}) custom-call(s32[1]{0:T(128)} %bitcast.row, bf16[1280,1024]{1,0:T(8,128)(2,1)} %get-tuple-element.180.refs_0_.refs_2_, bf16[2048,2048]{1,0:T(8,128)(2,1)} %all-gather.11.cloned.1.call-done.weight.refs_7_.refs_1_), custom_call_target="tpu_custom_call" | custom-call | flops 2684354560 | bytes 12058624 | tf_op jit(solution)/shard_map/partial_blocks/pallas_call | solution.py:930
  635.1 3.1 fusion.17
  639.9 15.4 %partial_blocks.14 = (bf16[2,640,512]{2,1,0:T(8,128)(2,1)}, f32[2,640,512]{2,1,0:T(8,128)}) custom-call(s32[1]{0:T(128)} %bitcast.row, bf16[1280,512]{1,0:T(8,128)(2,1)} %get-tuple-element.216.refs_0_.refs_3_, bf16[1280,512]{1,0:T(8,128)(2,1)} %get-tuple-element.217.refs_1_.refs_4_, bf16[1280,1024]{1,0:T(8,128)(2,1)} %get-tuple-element.224.refs_2_.refs_5_, ...), custom_call_target="tpu_custom_call" | custom-call | flops 8053063680 | bytes 25690112 | tf_op jit(solution)/shard_map/partial_blocks/pallas_call | solution.py:930
  660.5 2.4 bitcast_add_fusion.3
  662.9 9.6 %collective-permute-done.36 = bf16[640,512]{1,0:T(8,128)(2,1)S(1)} collective-permute-done((bf16[640,512]{1,0:T(8,128)(2,1)S(1)}, bf16[640,512]{1,0:T(8,128)(2,1)S(1)}, u32[]{:S(2)}, u32[]{:S(2)}) %collective-permute-start.36) | collective-permute-done | bytes 655392 | tf_op jit(solution)/shard_map/ppermute | solution.py:950
  679.7 5.5 fusion.9
  694.5 3.8 collective-permute-start.41
  698.9 3.5 collective-permute-done.41
  702.7 3.9 fusion.7
  (309 shorter events, 135.7 us)
Async XLA Ops:
  7.2 87.8 %all-gather.5.cloned.1.call-start = ((), (), s32[]{:S(2)}) async-start(), calls=%async_computation.4 | async-start | bytes 9437184 | tf_op jit(solution)/shard_map/all_gather | solution.py:1046
  9.5 141.4 %all-gather.7.cloned.1.call-start = ((), (), s32[]{:S(2)}) async-start(), calls=%async_computation.5 | async-start | bytes 4718592 | tf_op jit(solution)/shard_map/all_gather | solution.py:1046
  10.3 187.9 %all-gather.9.cloned.1.call-start = ((), (), s32[]{:S(2)}) async-start(), calls=%async_computation.6 | async-start | bytes 4718592 | tf_op jit(solution)/shard_map/all_gather | solution.py:1046
  11.6 288.4 %all-gather.11.cloned.1.call-start = ((), (), s32[]{:S(2)}) async-start(), calls=%async_computation.7 | async-start | bytes 9437184 | tf_op jit(solution)/shard_map/all_gather | solution.py:1046
  13.0 459.5 %reduce-scatter.5.cloned.1.call-start = ((), (), s32[]{:S(2)}) async-start(), calls=%async_computation.8 | async-start | bytes 9437184 | tf_op jit(solution)/shard_map/reduce_scatter | solution.py:1051
  13.1 10.3 %collective-permute-start.5 = (f32[4,512]{1,0:T(4,128)S(1)}, f32[4,512]{1,0:T(4,128)S(1)}, u32[]{:S(2)}, u32[]{:S(2)}) collective-permute-start(f32[4,512]{1,0:T(4,128)S(1)} %get-tuple-element.398), channel_id=1, source_target_pairs={{0,16},{16,0},{8,24},{24,8},{1,17},{17,1},{9,25},{25,9},{2,18},{18... | collective-permute-start | bytes 24584 | tf_op jit(solution)/shard_map/ppermute | solution.py:950
  16.2 7.3 %collective-permute-start.4 = (f32[4,512]{1,0:T(4,128)S(1)}, f32[4,512]{1,0:T(4,128)S(1)}, u32[]{:S(2)}, u32[]{:S(2)}) collective-permute-start(f32[4,512]{1,0:T(4,128)S(1)} %get-tuple-element.398), channel_id=1, source_target_pairs={{0,8},{8,0},{16,24},{24,16},{1,9},{9,1},{17,25},{25,17},{2,10},{10... | collective-permute-start | bytes 24584 | tf_op jit(solution)/shard_map/ppermute | solution.py:950
  17.7 5.8 collective-permute-start.6
  17.7 30.2 %collective-permute-start = (bf16[1280,512]{1,0:T(8,128)(2,1)S(1)}, bf16[1280,512]{1,0:T(8,128)(2,1)}, u32[]{:S(2)}, u32[]{:S(2)}) collective-permute-start(bf16[1280,512]{1,0:T(8,128)(2,1)S(1)} %copy-done.14), channel_id=1, source_target_pairs={{0,8},{8,0},{16,24},{24,16},{1,9},{9,1},{17,25},{25,17},{2,10},{10... | collective-permute-start | bytes 3932168 | tf_op jit(solution)/shard_map/ppermute | solution.py:950
  19.6 31.1 %collective-permute-start.1 = (bf16[1280,512]{1,0:T(8,128)(2,1)S(1)}, bf16[1280,512]{1,0:T(8,128)(2,1)}, u32[]{:S(2)}, u32[]{:S(2)}) collective-permute-start(bf16[1280,512]{1,0:T(8,128)(2,1)S(1)} %copy-done.14), channel_id=1, source_target_pairs={{0,16},{16,0},{8,24},{24,8},{1,17},{17,1},{9,25},{25,9},{2,18},{18... | collective-permute-start | bytes 3932168 | tf_op jit(solution)/shard_map/ppermute | solution.py:950
  49.1 15.2 %collective-permute-start.2 = (bf16[640,512]{1,0:T(8,128)(2,1)S(1)}, bf16[640,512]{1,0:T(8,128)(2,1)S(1)}, u32[]{:S(2)}, u32[]{:S(2)}) collective-permute-start(bf16[640,512]{1,0:T(8,128)(2,1)S(1)} %slice.269), channel_id=1, source_target_pairs={{0,16},{16,0},{8,24},{24,8},{1,17},{17,1},{9,25},{25,9},{2,18},{18... | collective-permute-start | bytes 1966088 | tf_op jit(solution)/shard_map/ppermute | solution.py:950
  51.9 14.6 %collective-permute-start.3 = (bf16[640,512]{1,0:T(8,128)(2,1)S(1)}, bf16[640,512]{1,0:T(8,128)(2,1)S(1)}, u32[]{:S(2)}, u32[]{:S(2)}) collective-permute-start(bf16[640,512]{1,0:T(8,128)(2,1)S(1)} %slice.270), channel_id=1, source_target_pairs={{0,8},{8,0},{16,24},{24,16},{1,9},{9,1},{17,25},{25,17},{2,10},{10... | collective-permute-start | bytes 1966088 | tf_op jit(solution)/shard_map/ppermute | solution.py:950
  74.8 41.5 %collective-permute-start.8 = (bf16[1280,512]{1,0:T(8,128)(2,1)S(1)}, bf16[1280,512]{1,0:T(8,128)(2,1)S(1)}, u32[]{:S(2)}, u32[]{:S(2)}) collective-permute-start(bf16[1280,512]{1,0:T(8,128)(2,1)S(1)} %multiply_convert_fusion.own), channel_id=1, source_target_pairs={{0,16},{16,0},{8,24},{24,8},{1,17},{17,1},{9,25},{25,9},{2,18},{18... | collective-permute-start | bytes 3932168 | tf_op jit(solution)/shard_map/ppermute | solution.py:950
  75.6 40.7 %collective-permute-start.7 = (bf16[1280,512]{1,0:T(8,128)(2,1)S(1)}, bf16[1280,512]{1,0:T(8,128)(2,1)}, u32[]{:S(2)}, u32[]{:S(2)}) collective-permute-start(bf16[1280,512]{1,0:T(8,128)(2,1)S(1)} %multiply_convert_fusion.own), channel_id=1, source_target_pairs={{0,8},{8,0},{16,24},{24,16},{1,9},{9,1},{17,25},{25,17},{2,10},{10... | collective-permute-start | bytes 3932168 | tf_op jit(solution)/shard_map/ppermute | solution.py:950
  119.8 31.1 %collective-permute-start.10 = (bf16[640,512]{1,0:T(8,128)(2,1)S(1)}, bf16[640,512]{1,0:T(8,128)(2,1)S(1)}, u32[]{:S(2)}, u32[]{:S(2)}) collective-permute-start(bf16[640,512]{1,0:T(8,128)(2,1)S(1)} %slice.210), channel_id=1, source_target_pairs={{0,8},{8,0},{16,24},{24,16},{1,9},{9,1},{17,25},{25,17},{2,10},{10... | collective-permute-start | bytes 1966088 | tf_op jit(solution)/shard_map/ppermute | solution.py:950
  121.4 29.6 %collective-permute-start.9 = (bf16[640,512]{1,0:T(8,128)(2,1)S(1)}, bf16[640,512]{1,0:T(8,128)(2,1)S(1)}, u32[]{:S(2)}, u32[]{:S(2)}) collective-permute-start(bf16[640,512]{1,0:T(8,128)(2,1)S(1)} %slice.209), channel_id=1, source_target_pairs={{0,16},{16,0},{8,24},{24,8},{1,17},{17,1},{9,25},{25,9},{2,18},{18... | collective-permute-start | bytes 1966088 | tf_op jit(solution)/shard_map/ppermute | solution.py:950
  206.3 31.1 %collective-permute-start.11 = (bf16[2,640,512]{2,1,0:T(8,128)(2,1)}, bf16[2,640,512]{2,1,0:T(8,128)(2,1)S(1)}, u32[]{:S(2)}, u32[]{:S(2)}) collective-permute-start(bf16[2,640,512]{2,1,0:T(8,128)(2,1)} %get-tuple-element.148), channel_id=1, source_target_pairs={{0,8},{8,0},{16,24},{24,16},{1,9},{9,1},{17,25},{25,17},{2,10},{10... | collective-permute-start | bytes 3932168 | tf_op jit(solution)/shard_map/ppermute | solution.py:950
  207.7 30.9 %collective-permute-start.13 = (bf16[2,640,512]{2,1,0:T(8,128)(2,1)}, bf16[2,640,512]{2,1,0:T(8,128)(2,1)S(1)}, u32[]{:S(2)}, u32[]{:S(2)}) collective-permute-start(bf16[2,640,512]{2,1,0:T(8,128)(2,1)} %get-tuple-element.150), channel_id=1, source_target_pairs={{0,16},{16,0},{8,24},{24,8},{1,17},{17,1},{9,25},{25,9},{2,18},{18... | collective-permute-start | bytes 3932168 | tf_op jit(solution)/shard_map/ppermute | solution.py:950
  240.8 15.9 %collective-permute-start.12 = (bf16[640,512]{1,0:T(8,128)(2,1)S(1)}, bf16[640,512]{1,0:T(8,128)(2,1)S(1)}, u32[]{:S(2)}, u32[]{:S(2)}) collective-permute-start(bf16[640,512]{1,0:T(8,128)(2,1)S(1)} %get-tuple-element.371), channel_id=1, source_target_pairs={{0,16},{16,0},{8,24},{24,8},{1,17},{17,1},{9,25},{25,9},{2,18},{18... | collective-permute-start | bytes 1966088 | tf_op jit(solution)/shard_map/ppermute | solution.py:950
  242.3 15.6 %collective-permute-start.14 = (bf16[640,512]{1,0:T(8,128)(2,1)S(1)}, bf16[640,512]{1,0:T(8,128)(2,1)S(1)}, u32[]{:S(2)}, u32[]{:S(2)}) collective-permute-start(bf16[640,512]{1,0:T(8,128)(2,1)S(1)} %get-tuple-element.372), channel_id=1, source_target_pairs={{0,8},{8,0},{16,24},{24,16},{1,9},{9,1},{17,25},{25,17},{2,10},{10... | collective-permute-start | bytes 1966088 | tf_op jit(solution)/shard_map/ppermute | solution.py:950
  261.0 28.8 %collective-permute-start.16 = (bf16[1280,512]{1,0:T(8,128)(2,1)S(1)}, bf16[1280,512]{1,0:T(8,128)(2,1)S(1)}, u32[]{:S(2)}, u32[]{:S(2)}) collective-permute-start(bf16[1280,512]{1,0:T(8,128)(2,1)S(1)} %fusion.31.refs_0_), channel_id=1, source_target_pairs={{0,16},{16,0},{8,24},{24,8},{1,17},{17,1},{9,25},{25,9},{2,18},{18... | collective-permute-start | bytes 3932168 | tf_op jit(solution)/shard_map/ppermute | solution.py:950
  261.5 28.5 %collective-permute-start.15 = (bf16[1280,512]{1,0:T(8,128)(2,1)S(1)}, bf16[1280,512]{1,0:T(8,128)(2,1)S(1)}, u32[]{:S(2)}, u32[]{:S(2)}) collective-permute-start(bf16[1280,512]{1,0:T(8,128)(2,1)S(1)} %fusion.31.refs_0_), channel_id=1, source_target_pairs={{0,8},{8,0},{16,24},{24,16},{1,9},{9,1},{17,25},{25,17},{2,10},{10... | collective-permute-start | bytes 3932168 | tf_op jit(solution)/shard_map/ppermute | solution.py:950
  291.3 18.6 %collective-permute-start.18 = (bf16[640,512]{1,0:T(8,128)(2,1)}, bf16[640,512]{1,0:T(8,128)(2,1)}, u32[]{:S(2)}, u32[]{:S(2)}) collective-permute-start(bf16[640,512]{1,0:T(8,128)(2,1)} %slice.220), channel_id=1, source_target_pairs={{0,8},{8,0},{16,24},{24,16},{1,9},{9,1},{17,25},{25,17},{2,10},{10... | collective-permute-start | bytes 1966088 | tf_op jit(solution)/shard_map/ppermute | solution.py:950
  292.7 17.2 %collective-permute-start.17 = (bf16[640,512]{1,0:T(8,128)(2,1)S(1)}, bf16[640,512]{1,0:T(8,128)(2,1)}, u32[]{:S(2)}, u32[]{:S(2)}) collective-permute-start(bf16[640,512]{1,0:T(8,128)(2,1)S(1)} %slice.219), channel_id=1, source_target_pairs={{0,16},{16,0},{8,24},{24,8},{1,17},{17,1},{9,25},{25,9},{2,18},{18... | collective-permute-start | bytes 1966088 | tf_op jit(solution)/shard_map/ppermute | solution.py:950
  337.4 28.3 %collective-permute-start.19 = (bf16[2,640,512]{2,1,0:T(8,128)(2,1)}, bf16[2,640,512]{2,1,0:T(8,128)(2,1)}, u32[]{:S(2)}, u32[]{:S(2)}) collective-permute-start(bf16[2,640,512]{2,1,0:T(8,128)(2,1)} %get-tuple-element.176), channel_id=1, source_target_pairs={{0,8},{8,0},{16,24},{24,16},{1,9},{9,1},{17,25},{25,17},{2,10},{10... | collective-permute-start | bytes 3932168 | tf_op jit(solution)/shard_map/ppermute | solution.py:950
  338.0 27.7 %collective-permute-start.20 = (bf16[2,640,512]{2,1,0:T(8,128)(2,1)}, bf16[2,640,512]{2,1,0:T(8,128)(2,1)}, u32[]{:S(2)}, u32[]{:S(2)}) collective-permute-start(bf16[2,640,512]{2,1,0:T(8,128)(2,1)} %get-tuple-element.177), channel_id=1, source_target_pairs={{0,16},{16,0},{8,24},{24,8},{1,17},{17,1},{9,25},{25,9},{2,18},{18... | collective-permute-start | bytes 3932168 | tf_op jit(solution)/shard_map/ppermute | solution.py:950
  365.7 196.6 %reduce-scatter.7.cloned.1.call-start = ((), (), s32[]{:S(2)}) async-start(), calls=%async_computation.9 | async-start | bytes 2621440 | tf_op jit(solution)/shard_map/reduce_scatter | solution.py:1053
  367.1 8.0 %collective-permute-start.25 = (f32[2,1280]{1,0:T(2,128)S(1)}, f32[2,1280]{1,0:T(2,128)S(1)}, u32[]{:S(2)}, u32[]{:S(2)}) collective-permute-start(f32[2,1280]{1,0:T(2,128)S(1)} %copy.77), channel_id=1, source_target_pairs={{0,24},{24,0},{8,16},{16,8},{1,25},{25,1},{9,17},{17,9},{2,26},{26... | collective-permute-start | bytes 30728 | tf_op jit(solution)/shard_map/ppermute | solution.py:950
  378.4 11.3 %collective-permute-start.21 = (bf16[640,512]{1,0:T(8,128)(2,1)S(1)}, bf16[640,512]{1,0:T(8,128)(2,1)S(1)}, u32[]{:S(2)}, u32[]{:S(2)}) collective-permute-start(bf16[640,512]{1,0:T(8,128)(2,1)S(1)} %get-tuple-element.369), channel_id=1, source_target_pairs={{0,16},{16,0},{8,24},{24,8},{1,17},{17,1},{9,25},{25,9},{2,18},{18... | collective-permute-start | bytes 1966088 | tf_op jit(solution)/shard_map/ppermute | solution.py:950
  379.7 10.9 %collective-permute-start.22 = (bf16[640,512]{1,0:T(8,128)(2,1)S(1)}, bf16[640,512]{1,0:T(8,128)(2,1)S(1)}, u32[]{:S(2)}, u32[]{:S(2)}) collective-permute-start(bf16[640,512]{1,0:T(8,128)(2,1)S(1)} %get-tuple-element.370), channel_id=1, source_target_pairs={{0,8},{8,0},{16,24},{24,16},{1,9},{9,1},{17,25},{25,17},{2,10},{10... | collective-permute-start | bytes 1966088 | tf_op jit(solution)/shard_map/ppermute | solution.py:950
  396.3 24.4 %collective-permute-start.27 = (bf16[1280,512]{1,0:T(8,128)(2,1)}, bf16[1280,512]{1,0:T(8,128)(2,1)}, u32[]{:S(2)}, u32[]{:S(2)}) collective-permute-start(bf16[1280,512]{1,0:T(8,128)(2,1)} %get-tuple-element.349.own), channel_id=1, source_target_pairs={{0,16},{16,0},{8,24},{24,8},{1,17},{17,1},{9,25},{25,9},{2,18},{18... | collective-permute-start | bytes 3932168 | tf_op jit(solution)/shard_map/ppermute | solution.py:950
  397.2 26.8 %collective-permute-start.26 = (bf16[1280,512]{1,0:T(8,128)(2,1)}, bf16[1280,512]{1,0:T(8,128)(2,1)}, u32[]{:S(2)}, u32[]{:S(2)}) collective-permute-start(bf16[1280,512]{1,0:T(8,128)(2,1)} %get-tuple-element.349.own), channel_id=1, source_target_pairs={{0,8},{8,0},{16,24},{24,16},{1,9},{9,1},{17,25},{25,17},{2,10},{10... | collective-permute-start | bytes 3932168 | tf_op jit(solution)/shard_map/ppermute | solution.py:950
  426.3 10.7 %collective-permute-start.29 = (bf16[640,512]{1,0:T(8,128)(2,1)S(1)}, bf16[640,512]{1,0:T(8,128)(2,1)S(1)}, u32[]{:S(2)}, u32[]{:S(2)}) collective-permute-start(bf16[640,512]{1,0:T(8,128)(2,1)S(1)} %slice.242), channel_id=1, source_target_pairs={{0,8},{8,0},{16,24},{24,16},{1,9},{9,1},{17,25},{25,17},{2,10},{10... | collective-permute-start | bytes 1966088 | tf_op jit(solution)/shard_map/ppermute | solution.py:950
  428.1 10.7 %collective-permute-start.28 = (bf16[640,512]{1,0:T(8,128)(2,1)S(1)}, bf16[640,512]{1,0:T(8,128)(2,1)}, u32[]{:S(2)}, u32[]{:S(2)}) collective-permute-start(bf16[640,512]{1,0:T(8,128)(2,1)S(1)} %slice.241), channel_id=1, source_target_pairs={{0,16},{16,0},{8,24},{24,8},{1,17},{17,1},{9,25},{25,9},{2,18},{18... | collective-permute-start | bytes 1966088 | tf_op jit(solution)/shard_map/ppermute | solution.py:950
  444.0 22.2 %collective-permute-start.30 = (bf16[2,640,512]{2,1,0:T(8,128)(2,1)}, bf16[2,640,512]{2,1,0:T(8,128)(2,1)}, u32[]{:S(2)}, u32[]{:S(2)}) collective-permute-start(bf16[2,640,512]{2,1,0:T(8,128)(2,1)} %get-tuple-element.192), channel_id=1, source_target_pairs={{0,8},{8,0},{16,24},{24,16},{1,9},{9,1},{17,25},{25,17},{2,10},{10... | collective-permute-start | bytes 3932168 | tf_op jit(solution)/shard_map/ppermute | solution.py:950
  444.8 22.8 %collective-permute-start.31 = (bf16[2,640,512]{2,1,0:T(8,128)(2,1)}, bf16[2,640,512]{2,1,0:T(8,128)(2,1)}, u32[]{:S(2)}, u32[]{:S(2)}) collective-permute-start(bf16[2,640,512]{2,1,0:T(8,128)(2,1)} %get-tuple-element.193), channel_id=1, source_target_pairs={{0,16},{16,0},{8,24},{24,8},{1,17},{17,1},{9,25},{25,9},{2,18},{18... | collective-permute-start | bytes 3932168 | tf_op jit(solution)/shard_map/ppermute | solution.py:950
  475.4 147.9 %reduce-scatter.9.cloned.1.call-start = ((), (), s32[]{:S(2)}) async-start(), calls=%async_computation.10 | async-start | bytes 4718592 | tf_op jit(solution)/shard_map/reduce_scatter | solution.py:1051
  564.5 150.3 %reduce-scatter.11.cloned.1.call-start = ((), (), s32[]{:S(2)}) async-start(), calls=%async_computation.11 | async-start | bytes 5242880 | tf_op jit(solution)/shard_map/reduce_scatter | solution.py:1053
  593.7 29.6 %collective-permute-start.34 = (bf16[2,640,512]{2,1,0:T(8,128)(2,1)}, bf16[2,640,512]{2,1,0:T(8,128)(2,1)}, u32[]{:S(2)}, u32[]{:S(2)}) collective-permute-start(bf16[2,640,512]{2,1,0:T(8,128)(2,1)} %get-tuple-element.222), channel_id=1, source_target_pairs={{0,8},{8,0},{16,24},{24,16},{1,9},{9,1},{17,25},{25,17},{2,10},{10... | collective-permute-start | bytes 3932168 | tf_op jit(solution)/shard_map/ppermute | solution.py:950
  595.2 28.1 %collective-permute-start.35 = (bf16[2,640,512]{2,1,0:T(8,128)(2,1)}, bf16[2,640,512]{2,1,0:T(8,128)(2,1)}, u32[]{:S(2)}, u32[]{:S(2)}) collective-permute-start(bf16[2,640,512]{2,1,0:T(8,128)(2,1)} %get-tuple-element.223), channel_id=1, source_target_pairs={{0,16},{16,0},{8,24},{24,8},{1,17},{17,1},{9,25},{25,9},{2,18},{18... | collective-permute-start | bytes 3932168 | tf_op jit(solution)/shard_map/ppermute | solution.py:950
  638.2 22.2 %collective-permute-start.32 = (bf16[640,512]{1,0:T(8,128)(2,1)}, bf16[640,512]{1,0:T(8,128)(2,1)S(1)}, u32[]{:S(2)}, u32[]{:S(2)}) collective-permute-start(bf16[640,512]{1,0:T(8,128)(2,1)} %get-tuple-element.367), channel_id=1, source_target_pairs={{0,16},{16,0},{8,24},{24,8},{1,17},{17,1},{9,25},{25,9},{2,18},{18... | collective-permute-start | bytes 1966088 | tf_op jit(solution)/shard_map/ppermute | solution.py:950
  639.2 21.2 %collective-permute-start.33 = (bf16[640,512]{1,0:T(8,128)(2,1)}, bf16[640,512]{1,0:T(8,128)(2,1)}, u32[]{:S(2)}, u32[]{:S(2)}) collective-permute-start(bf16[640,512]{1,0:T(8,128)(2,1)} %get-tuple-element.368), channel_id=1, source_target_pairs={{0,8},{8,0},{16,24},{24,16},{1,9},{9,1},{17,25},{25,17},{2,10},{10... | collective-permute-start | bytes 1966088 | tf_op jit(solution)/shard_map/ppermute | solution.py:950
  657.5 14.9 %collective-permute-start.36 = (bf16[640,512]{1,0:T(8,128)(2,1)S(1)}, bf16[640,512]{1,0:T(8,128)(2,1)S(1)}, u32[]{:S(2)}, u32[]{:S(2)}) collective-permute-start(bf16[640,512]{1,0:T(8,128)(2,1)S(1)} %get-tuple-element.365), channel_id=1, source_target_pairs={{0,16},{16,0},{8,24},{24,8},{1,17},{17,1},{9,25},{25,9},{2,18},{18... | collective-permute-start | bytes 1966088 | tf_op jit(solution)/shard_map/ppermute | solution.py:950
  658.6 15.5 %collective-permute-start.37 = (bf16[640,512]{1,0:T(8,128)(2,1)S(1)}, bf16[640,512]{1,0:T(8,128)(2,1)S(1)}, u32[]{:S(2)}, u32[]{:S(2)}) collective-permute-start(bf16[640,512]{1,0:T(8,128)(2,1)S(1)} %get-tuple-element.366), channel_id=1, source_target_pairs={{0,8},{8,0},{16,24},{24,16},{1,9},{9,1},{17,25},{25,17},{2,10},{10... | collective-permute-start | bytes 1966088 | tf_op jit(solution)/shard_map/ppermute | solution.py:950
  678.0 7.2 collective-permute-start.38
  685.2 8.6 %collective-permute-start.39 = (f32[2,1280]{1,0:T(2,128)S(1)}, f32[2,1280]{1,0:T(2,128)S(1)}, u32[]{:S(2)}, u32[]{:S(2)}) collective-permute-start(f32[2,1280]{1,0:T(2,128)S(1)} %fusion.30), channel_id=1, source_target_pairs={{0,16},{16,0},{8,24},{24,8},{1,17},{17,1},{9,25},{25,9},{2,18},{18... | collective-permute-start | bytes 30728 | tf_op jit(solution)/shard_map/ppermute | solution.py:950
  694.5 7.9 %collective-permute-start.41 = (f32[45,128]{1,0:T(8,128)S(1)}, f32[45,128]{1,0:T(8,128)S(1)}, u32[]{:S(2)}, u32[]{:S(2)}) collective-permute-start(f32[45,128]{1,0:T(8,128)S(1)} %bitcast_add_fusion.8), channel_id=1, source_target_pairs={{0,2},{1,3},{2,0},{3,1},{4,6},{5,7},{6,4},{7,5},{8,10},{9,11},{10,... | collective-permute-start | bytes 69128 | tf_op jit(solution)/shard_map/ppermute | solution.py:1359
  702.3 4.8 collective-permute-start.42
  (72 other events, 424.1 us)
Sparse Core Ops, SparseCore 0:
  10.2 84.7 all-gather.4
  96.6 52.1 all-gather.6
  150.9 47.2 all-gather.8
  200.3 86.4 all-gather.10
  365.8 106.6 reduce-scatter.4
  475.5 59.4 reduce-scatter.6
  564.6 56.9 reduce-scatter.8
  625.6 78.0 reduce-scatter.10

commit v5 on v4

--- a/solution.py
+++ b/solution.py
@@ -961,13 +961,19 @@
     return tuple(partial_blocks(values, weights, row, 0, (BF16, BF16)))
 
 
-def reduce_row_finish(sends, values, weights, row, between=None, tied=None):
+def reduce_row_rest(values, weights, row):
+    if lax.axis_size("row") != 4:
+        return ()
+    return tuple(partial_blocks(values, weights, row, 2, (BF16, F32)))
+
+
+def reduce_row_finish(sends, values, weights, row, between=None, tied=None, rest=None):
     if lax.axis_size("row") != 4:
         total = lax.psum_scatter(sends, "row", scatter_dimension=1, tiled=True).astype(F32)
         return total, between(tied) if between else None
     from_x = permute_row(sends[0], X_PAIRS)
     from_y = permute_row(sends[1], Y_PAIRS)
-    keep, own = partial_blocks(values, weights, row, 2, (BF16, F32))
+    keep, own = rest if rest is not None else reduce_row_rest(values, weights, row)
     extra = None
     if between is not None:
         if tied is not None:
@@ -1019,13 +1025,6 @@
     return jnp.concatenate(ordered, axis=1)
 
 
-def sum_row_small(value):
-    if lax.axis_size("row") != 4:
-        return lax.psum(value, "row")
-    first = value + permute_row(value, X_PAIRS)
-    return first + permute_row(first, Y_PAIRS)
-
-
 def sum_row_direct(value):
     if lax.axis_size("row") != 4:
         return lax.psum(value, "row")
@@ -1036,7 +1035,9 @@
 def norm_backward(grad_out, normal, inverse, gain_vector, sums=None):
     scaled = grad_out * gain_vector
     if sums is None:
-        sums = sum_row_small(jnp.stack([jnp.sum(scaled, axis=1), jnp.sum(scaled * normal, axis=1)]))
+        sums = sum_row_direct(
+            jnp.stack([jnp.sum(scaled, axis=1), jnp.sum(scaled * normal, axis=1)])
+        )
     means = sums / D
     grad_in = inverse * (scaled - means[0][:, None] - normal * means[1][:, None])
     return (grad_in, jnp.sum(grad_out * normal, axis=0), jnp.sum(grad_out, axis=0))
@@ -1496,21 +1497,34 @@
         second_back, second_normal, second_inverse[:, :1], second_gain, feed_sums
     )
     grad_middle = grad_fed + grad_middle_norm
-    grad_pieces, fed_sends = gather_row(
-        grad_middle.astype(BF16), lambda: reduce_row_start([hidden], [down_part], row_ref)
+    grad_pieces, (fed_sends, fed_rest) = gather_row(
+        grad_middle.astype(BF16),
+        lambda: (
+            reduce_row_start([hidden], [down_part], row_ref),
+            reduce_row_rest([hidden], [down_part], row_ref),
+        ),
     )
     grad_wide = join(grad_pieces, row_ref)
     fed_sends, grad_wide = in_order(fed_sends, grad_wide)
-    fed_out, out_partial = reduce_row_finish(
-        fed_sends, [hidden], [down_part], row_ref, lambda _: column_grads([(grad_wide, gated)], 4)
+    out_partial = column_grads([(grad_wide, gated)], 4)
+    out_partial, grad_wide = in_order(out_partial, grad_wide)
+    out_partial, feed_grad = in_order(out_partial, feed_grad)
+    out_grad = scatter_col(out_partial)
+    fed_out, gate_results = reduce_row_finish(
+        fed_sends,
+        [hidden],
+        [down_part],
+        row_ref,
+        lambda _: tuple(
+            gate_back(
+                meta, rates, grad_wide, out_part, gate_raw, normal, inverse, query_rot, group_gain, group_bias
+            )
+        ),
+        rest=fed_rest,
     )
     fed_out = fed_out + down_bias
     layer_out = middle + fed_out
-    out_partial, grad_wide, feed_grad = in_order(out_partial, grad_wide, feed_grad)
-    out_grad = scatter_col(out_partial)
-    grad_gate, grad_retained, group_gain_grad, group_bias_grad, returns, first_state = gate_back(
-        meta, rates, grad_wide, out_part, gate_raw, normal, inverse, query_rot, group_gain, group_bias
-    )
+    grad_gate, grad_retained, group_gain_grad, group_bias_grad, returns, first_state = gate_results
     own0, own1, own2, gate_partial = return_states(
         meta, rates, returns, first_state, first_wide, grad_gate, rows
     )
@@ -1562,7 +1576,7 @@
         ),
         jnp.concatenate([squares, jnp.zeros((125,), F32)]),
     )
-    totals = sum_row_small(col_squares[None, :])[0, :3]
+    totals = sum_row_direct(col_squares[None, :])[0, :3]
     valid_count = jnp.sum(segment_lengths).astype(F32) * D
     norm_values = jnp.sqrt(totals / valid_count)
     return (

time: 734 us -> 723 us (0.985)
  Pallas kernels: 344 us -> 329 us
    ppermute x42 -> x44, waiting for transfers between devices: 160 us -> 142 us  [permute_row(): return lax.ppermute(value, 'row', pairs)]
    pallas_call x1, Pallas kernels: 56.1 us -> 40.4 us  [return_states(): pl.pallas_call(functools.partial(return_kernel, rows), in_specs=[smem(),...]
    reduce_scatter x2, waiting for transfers between devices: 4.97 us -> 16.3 us  [scatter_col(): lax.psum_scatter(grad, 'col', scatter_dimension=0, tiled=True).astype(F32)]
    ppermute x42 -> x44, starting transfers between devices: 52.9 us -> 55.7 us  [permute_row(): return lax.ppermute(value, 'row', pairs)]
    unnamed x138 -> x128, local copies, waits for them, and re-layouts: 18.8 us -> 21.3 us
  transfers between devices with their start and end apart: 53 -> 55, of which waited for: 28 -> 27; matrix products, arithmetic and copies ran while one was open for 10% -> 11% of each run, Pallas kernels for 44% -> 42%
where the time goes in v5:
time: 723 us; the launch traced here: 714 us
  Pallas kernels  329 us (46%)
  waiting for transfers between devices  203 us (28%)
  starting transfers between devices  61.5 us (9%)
  other arithmetic  54.9 us (8%)
  local copies, waits for them, and re-layouts  49.8 us (7%)
  between operations  16 us (2%)
    ppermute x44, waiting for transfers between devices, permute_row(): return lax.ppermute(value, 'row', pairs)  142 us
    pallas_call x8, Pallas kernels, partial_blocks(): pl.pallas_call(functools.partial(partial_kernel, count), grid_spec=pltpu....  80 us
    ppermute x44, starting transfers between devices, permute_row(): return lax.ppermute(value, 'row', pairs)  55.7 us
    pallas_call x1, Pallas kernels, return_states(): pl.pallas_call(functools.partial(return_kernel, rows), in_specs=[smem(),...  40.4 us
    all_gather x4, waiting for transfers between devices, gather_col(): return lax.all_gather(weight, 'col', axis=0, tiled=True)  39.2 us
    pallas_call x2, Pallas kernels, paired_grads(): pl.pallas_call(functools.partial(paired_grad_kernel, tuple(spans), tiles,...  39.1 us
    pallas_call x1, Pallas kernels, share_states(): pl.pallas_call(functools.partial(share_kernel, rows), in_specs=[smem(), s...  25.3 us
    pallas_call x1, Pallas kernels, retain(): pl.pallas_call(functools.partial(retain_kernel, rows, chunks), grid=(head...  21.3 us
  transfers between devices with their start and end apart: 55, of which 27 were waited for; matrix products, arithmetic and copies ran while one was open for 11% of the time, Pallas kernels for 42%

profile of v5, /device:TPU:0, one launch (start us, length us, event | category | flops | bytes accessed | tf_op | source)
XLA Modules:
  0.0 714.2 jit_solution(9010195347558411652)
XLA Ops:
  7.2 2.3 pad_maximum_fusion.3
  13.1 3.0 collective-permute-start.5
  23.5 24.5 %collective-permute-done.from_x = bf16[1280,512]{1,0:T(8,128)(2,1)} collective-permute-done((bf16[1280,512]{1,0:T(8,128)(2,1)S(1)}, bf16[1280,512]{1,0:T(8,128)(2,1)}, u32[]{:S(2)}, u32[]{:S(2)}) %collective-permute-start) | collective-permute-done | bytes 1310752 | tf_op jit(solution)/shard_map/ppermute | solution.py:950
  54.1 10.2 %collective-permute-done.2.far_a = bf16[640,512]{1,0:T(8,128)(2,1)S(1)} collective-permute-done((bf16[640,512]{1,0:T(8,128)(2,1)S(1)}, bf16[640,512]{1,0:T(8,128)(2,1)S(1)}, u32[]{:S(2)}, u32[]{:S(2)}) %collective-permute-start.2) | collective-permute-done | bytes 655392 | tf_op jit(solution)/shard_map/ppermute | solution.py:950
  67.3 7.5 %join_norm.1 = (bf16[1280,2048]{1,0:T(8,128)(2,1)}, f32[1280,128]{1,0:T(8,128)}, f32[1280,128]{1,0:T(8,128)}) custom-call(s32[1]{0:T(128)} %bitcast.row, bf16[1280,512]{1,0:T(8,128)(2,1)} %own.1, bf16[1280,512]{1,0:T(8,128)(2,1)} %collective-permute-done.from_x, bf16[1280,512]{1,0:T(8,128)(2,1)} %collective-permute-done.1.from_y, ...), custom_call_target="tpu_custom_call" | custom-call | flops 20971520 | bytes 10485760 | tf_op jit(solution)/shard_map/join_norm/pallas_call | solution.py:491
  77.0 3.7 multiply_sine_fusion
  81.9 13.1 %all-gather.5.cloned.1.call-done.weight.refs_4_.refs_5_.refs_6_ = bf16[2048,2048]{1,0:T(8,128)(2,1)} async-done(((bf16[256,2048]{1,0:T(8,128)(2,1)}), bf16[2048,2048]{1,0:T(8,128)(2,1)}) %all-gather.5.cloned.1.call-update) | async-done | bytes 8388624 | tf_op jit(solution)/shard_map/all_gather | solution.py:1047
  95.0 21.3 %project.1 = (bf16[1280,512]{1,0:T(8,128)(2,1)}, bf16[1280,512]{1,0:T(8,128)(2,1)}, bf16[1280,1024]{1,0:T(8,128)(2,1)}, bf16[3,2,256,512]{3,2,1,0:T(8,128)(2,1)}) custom-call(s32[22]{0:T(128)} %pad_add_fusion.meta, f32[2]{0:T(128)} %subtract_log_fusion.rates, bf16[1280,2048]{1,0:T(8,128)(2,1)} %get-tuple-element.138.values.wide.left.refs_0_.refs_1_.refs_2_, ...), custom_call_target="tpu_custom_call" | custom-call | flops 10737418240 | bytes 13631488 | tf_op jit(solution)/shard_map/project/pallas_call | solution.py:554
  122.8 25.3 %share_states.1 = (bf16[8,2,256,512]{3,2,1,0:T(8,128)(2,1)S(1)}, bf16[2,256,512]{2,1,0:T(8,128)(2,1)S(1)}) custom-call(s32[22]{0:T(128)S(1)} %copy-done.5, f32[2]{0:T(128)S(1)} %copy-done.7, bf16[3,2,256,512]{3,2,1,0:T(8,128)(2,1)S(1)} %copy-done.3), custom_call_target="tpu_custom_call" | custom-call | bytes 104857600 | tf_op jit(solution)/shard_map/share_states/pallas_call | solution.py:1204
  150.9 21.3 %retention_forward.1 = (f32[1280,1024]{1,0:T(8,128)}, bf16[1280,1024]{1,0:T(8,128)(2,1)}, bf16[1280,1024]{1,0:T(8,128)(2,1)}, f32[2,1280,128]{2,1,0:T(8,128)}, bf16[2,5,256,512]{3,2,1,0:T(8,128)(2,1)}) custom-call(s32[22]{0:T(128)} %pad_add_fusion.meta, f32[2]{0:T(128)} %subtract_log_fusion.rates, bf16[1280,512]{1,0:T(8,128)(2,1)} %get-tuple-element.143.query, ...), custom_call_target="tpu_custom_call" | custom-call | flops 7717519360 | bytes 20971520 | tf_op jit(solution)/shard_map/retention_forward/pallas_call | solution.py:203
  172.2 26.0 %all-gather.9.cloned.1.call-done.refs_1_.weight = bf16[2048,1024]{1,0:T(8,128)(2,1)} async-done(((bf16[256,1024]{1,0:T(8,128)(2,1)}), bf16[2048,1024]{1,0:T(8,128)(2,1)}) %all-gather.9.cloned.1.call-update) | async-done | bytes 4194320 | tf_op jit(solution)/shard_map/all_gather | solution.py:1047
  198.3 8.1 %partial_blocks.9 = (bf16[2,640,512]{2,1,0:T(8,128)(2,1)}, bf16[2,640,512]{2,1,0:T(8,128)(2,1)}) custom-call(s32[1]{0:T(128)} %bitcast.row, bf16[1280,1024]{1,0:T(8,128)(2,1)} %get-tuple-element.154.refs_0_.refs_1_, bf16[2048,1024]{1,0:T(8,128)(2,1)} %all-gather.9.cloned.1.call-done.refs_1_.weight), custom_call_target="tpu_custom_call" | custom-call | flops 2684354560 | bytes 12058624 | tf_op jit(solution)/shard_map/partial_blocks/pallas_call | solution.py:930
  209.3 8.5 %partial_blocks.8 = (bf16[2,640,512]{2,1,0:T(8,128)(2,1)}, f32[2,640,512]{2,1,0:T(8,128)}) custom-call(s32[1]{0:T(128)} %bitcast.row, bf16[1280,1024]{1,0:T(8,128)(2,1)} %get-tuple-element.154.refs_0_.refs_1_, bf16[2048,1024]{1,0:T(8,128)(2,1)} %all-gather.9.cloned.1.call-done.refs_1_.weight), custom_call_target="tpu_custom_call" | custom-call | flops 2684354560 | bytes 12058624 | tf_op jit(solution)/shard_map/partial_blocks/pallas_call | solution.py:930
  217.8 19.7 %collective-permute-done.11 = bf16[2,640,512]{2,1,0:T(8,128)(2,1)S(1)} collective-permute-done((bf16[2,640,512]{2,1,0:T(8,128)(2,1)}, bf16[2,640,512]{2,1,0:T(8,128)(2,1)S(1)}, u32[]{:S(2)}, u32[]{:S(2)}) %collective-permute-start.11) | collective-permute-done | bytes 1310752 | tf_op jit(solution)/shard_map/ppermute | solution.py:950
  243.2 13.6 %collective-permute-done.12 = bf16[640,512]{1,0:T(8,128)(2,1)S(1)} collective-permute-done((bf16[640,512]{1,0:T(8,128)(2,1)S(1)}, bf16[640,512]{1,0:T(8,128)(2,1)S(1)}, u32[]{:S(2)}, u32[]{:S(2)}) %collective-permute-start.12) | collective-permute-done | bytes 655392 | tf_op jit(solution)/shard_map/ppermute | solution.py:950
  262.7 27.2 %collective-permute-done.16.refs_2_ = bf16[1280,512]{1,0:T(8,128)(2,1)S(1)} collective-permute-done((bf16[1280,512]{1,0:T(8,128)(2,1)S(1)}, bf16[1280,512]{1,0:T(8,128)(2,1)S(1)}, u32[]{:S(2)}, u32[]{:S(2)}) %collective-permute-start.16) | collective-permute-done | bytes 1310752 | tf_op jit(solution)/shard_map/ppermute | solution.py:950
  294.8 5.3 join.2.values.refs_0_
  300.1 9.9 %matmul.1.refs_9_ = bf16[1280,1024]{1,0:T(8,128)(2,1)} custom-call(bf16[1280,2048]{1,0:T(8,128)(2,1)} %join.2.values.refs_0_, bf16[2048,2048]{1,0:T(8,128)(2,1)} %all-gather.11.cloned.1.call-done.weight.refs_7_.refs_1_), custom_call_target="tpu_custom_call" | custom-call | flops 5368709120 | bytes 9437184 | tf_op jit(solution)/shard_map/matmul/pallas_call | solution.py:583
  310.0 19.3 %feed_up.1 = (bf16[1280,2048]{1,0:T(8,128)(2,1)}, f32[1280,128]{1,0:T(8,128)}, f32[1280,128]{1,0:T(8,128)}, bf16[1280,1024]{1,0:T(8,128)(2,1)}, bf16[1280,1024]{...) custom-call(s32[1]{0:T(128)} %bitcast.row, bf16[1280,512]{1,0:T(8,128)(2,1)} %copy-done.36, ...), custom_call_target="tpu_custom_call" | custom-call | flops 5368709120 | bytes 25165824 | tf_op jit(solution)/shard_map/feed_up/pallas_call | solution.py:849
  329.3 8.1 %partial_blocks.11 = (bf16[2,640,512]{2,1,0:T(8,128)(2,1)}, bf16[2,640,512]{2,1,0:T(8,128)(2,1)}) custom-call(s32[1]{0:T(128)} %bitcast.row, bf16[1280,1024]{1,0:T(8,128)(2,1)} %get-tuple-element.175.refs_0_.refs_3_, bf16[2048,2048]{1,0:T(8,128)(2,1)} %all-gather.11.cloned.1.call-done.weight.refs_7_.refs_1_), custom_call_target="tpu_custom_call" | custom-call | flops 2684354560 | bytes 12058624 | tf_op jit(solution)/shard_map/partial_blocks/pallas_call | solution.py:930
  338.7 8.3 %partial_blocks.10 = (bf16[2,640,512]{2,1,0:T(8,128)(2,1)}, f32[2,640,512]{2,1,0:T(8,128)}) custom-call(s32[1]{0:T(128)} %bitcast.row, bf16[1280,1024]{1,0:T(8,128)(2,1)} %get-tuple-element.175.refs_0_.refs_3_, bf16[2048,2048]{1,0:T(8,128)(2,1)} %all-gather.11.cloned.1.call-done.weight.refs_7_.refs_1_), custom_call_target="tpu_custom_call" | custom-call | flops 2684354560 | bytes 12058624 | tf_op jit(solution)/shard_map/partial_blocks/pallas_call | solution.py:930
  347.1 18.7 %weight_grads.1 = bf16[2048,2048]{1,0:T(8,128)(2,1)} custom-call(bf16[1280,2048]{1,0:T(8,128)(2,1)} %join.2.values.refs_0_, bf16[1280,2048]{1,0:T(8,128)(2,1)} %get-tuple-element.186.refs_1_, bf16[1280,1024]{1,0:T(8,128)(2,1)} %get-tuple-element.187.refs_2_.refs_0_, bf16[1280,1024]{1,0:T(8,128)(2,1)} %get-tuple-element.175.refs_0_.refs_3_), custom_call_target="tpu_custom_call" | custom-call | flops 10737418240 | bytes 18874368 | tf_op jit(solution)/shard_map/weight_grads/pallas_call | solution.py:641
  381.6 8.1 %collective-permute-done.21 = bf16[640,512]{1,0:T(8,128)(2,1)S(1)} collective-permute-done((bf16[640,512]{1,0:T(8,128)(2,1)S(1)}, bf16[640,512]{1,0:T(8,128)(2,1)S(1)}, u32[]{:S(2)}, u32[]{:S(2)}) %collective-permute-start.21) | collective-permute-done | bytes 655392 | tf_op jit(solution)/shard_map/ppermute | solution.py:950
  392.8 3.7 fusion.35
  399.0 8.1 %partial_blocks.12 = (bf16[2,640,512]{2,1,0:T(8,128)(2,1)}, bf16[2,640,512]{2,1,0:T(8,128)(2,1)}) custom-call(s32[1]{0:T(128)} %bitcast.row, bf16[1280,1024]{1,0:T(8,128)(2,1)} %get-tuple-element.187.refs_2_.refs_0_, bf16[2048,2048]{1,0:T(8,128)(2,1)} %all-gather.11.cloned.1.call-done.weight.refs_7_.refs_1_), custom_call_target="tpu_custom_call" | custom-call | flops 2684354560 | bytes 12058624 | tf_op jit(solution)/shard_map/partial_blocks/pallas_call | solution.py:930
  407.1 8.5 %partial_blocks.13 = (bf16[2,640,512]{2,1,0:T(8,128)(2,1)}, f32[2,640,512]{2,1,0:T(8,128)}) custom-call(s32[1]{0:T(128)} %bitcast.row, bf16[1280,1024]{1,0:T(8,128)(2,1)} %get-tuple-element.187.refs_2_.refs_0_, bf16[2048,2048]{1,0:T(8,128)(2,1)} %all-gather.11.cloned.1.call-done.weight.refs_7_.refs_1_), custom_call_target="tpu_custom_call" | custom-call | flops 2684354560 | bytes 12058624 | tf_op jit(solution)/shard_map/partial_blocks/pallas_call | solution.py:930
  415.6 5.3 collective-permute-done.27.from_y
  420.9 3.2 collective-permute-done.26.from_x
  429.3 7.7 %collective-permute-done.29.far_b = bf16[640,512]{1,0:T(8,128)(2,1)S(1)} collective-permute-done((bf16[640,512]{1,0:T(8,128)(2,1)S(1)}, bf16[640,512]{1,0:T(8,128)(2,1)S(1)}, u32[]{:S(2)}, u32[]{:S(2)}) %collective-permute-start.29) | collective-permute-done | bytes 655392 | tf_op jit(solution)/shard_map/ppermute | solution.py:950
  438.9 5.3 join.3.refs_0_.wide
  444.1 12.2 %paired_grads.2 = bf16[4,256,1024]{2,1,0:T(8,128)(2,1)} custom-call(bf16[1280,2048]{1,0:T(8,128)(2,1)} %join.3.refs_0_.wide, bf16[1280,1024]{1,0:T(8,128)(2,1)} %get-tuple-element.154.refs_0_.refs_1_), custom_call_target="tpu_custom_call" | custom-call | flops 5368709120 | bytes 14680064 | tf_op jit(solution)/shard_map/paired_grads/pallas_call | solution.py:732
  456.3 16.3 %reduce-scatter.5.cloned.1.call-done = bf16[256,2048]{1,0:T(8,128)(2,1)} async-done(((bf16[2048,2048]{1,0:T(8,128)(2,1)}), bf16[256,2048]{1,0:T(8,128)(2,1)}) %reduce-scatter.5.cloned.1.call-update) | async-done | bytes 1048592 | tf_op jit(solution)/shard_map/reduce_scatter | solution.py:1052
  472.6 2.9 convert_element_type.275
  478.6 21.1 %gate_backward.1 = (bf16[1280,1024]{1,0:T(8,128)(2,1)}, bf16[1280,1024]{1,0:T(8,128)(2,1)}, f32[1,1024]{1,0:T(1,128)}, f32[1,1024]{1,0:T(1,128)}, bf16[8,2,256,5...) custom-call(s32[22]{0:T(128)} %pad_add_fusion.meta, f32[2]{0:T(128)} %subtract_log_fusion.rates, ...), custom_call_target="tpu_custom_call" | custom-call | flops 6039797760 | bytes 31457280 | tf_op jit(solution)/shard_map/gate_backward/pallas_call | solution.py:300
  499.7 4.6 collective-permute-done.30
  510.5 40.4 %return_states.1 = (bf16[2,256,512]{2,1,0:T(8,128)(2,1)S(1)}, bf16[2,256,512]{2,1,0:T(8,128)(2,1)S(1)}, bf16[2,256,512]{2,1,0:T(8,128)(2,1)S(1)}, bf16[2048,1024]{1,0:T(8,128)(2,1)S(1)}) custom-call(s32[22]{0:T(128)S(1)} %copy-done.6, f32[2]{0:T(128)S(1)} %copy-done.8, bf16[8,2,256,512]{3,2,1,0:T(8,128)(2,1)S(1)} %copy-done.1, ...), custom_call_target="tpu_custom_call" | custom-call | bytes 104857600 | tf_op jit(solution)/shard_map/return_states/pallas_call | solution.py:1333
  557.4 14.4 %retention_backward.1 = (bf16[1280,512]{1,0:T(8,128)(2,1)}, bf16[1280,512]{1,0:T(8,128)(2,1)}, bf16[1280,1024]{1,0:T(8,128)(2,1)}) custom-call(s32[22]{0:T(128)} %pad_add_fusion.meta, f32[2]{0:T(128)} %subtract_log_fusion.rates, bf16[1280,512]{1,0:T(8,128)(2,1)} %get-tuple-element.143.query, bf16[1280,512]{1,0:T(8,128)(2,1)} %get-tuple-element.144.key, ...), custom_call_target="tpu_custom_call" | custom-call | flops 5033164800 | bytes 15728640 | tf_op jit(solution)/shard_map/retention_backward/pallas_call | solution.py:395
  571.8 15.1 %partial_blocks.15 = (bf16[2,640,512]{2,1,0:T(8,128)(2,1)}, bf16[2,640,512]{2,1,0:T(8,128)(2,1)}) custom-call(s32[1]{0:T(128)} %bitcast.row, bf16[1280,512]{1,0:T(8,128)(2,1)} %get-tuple-element.232.refs_0_.refs_3_, bf16[1280,512]{1,0:T(8,128)(2,1)} %get-tuple-element.233.refs_1_.refs_4_, bf16[1280,1024]{1,0:T(8,128)(2,1)} %get-tuple-element.240.refs_2_.refs_5_, ...), custom_call_target="tpu_custom_call" | custom-call | flops 8053063680 | bytes 25690112 | tf_op jit(solution)/shard_map/partial_blocks/pallas_call | solution.py:930
  589.0 26.9 %paired_grads.3 = bf16[4,256,2048]{2,1,0:T(8,128)(2,1)} custom-call(bf16[1280,2048]{1,0:T(8,128)(2,1)} %get-tuple-element.138.values.wide.left.refs_0_.refs_1_.refs_2_, bf16[1280,2048]{1,0:T(8,128)(2,1)} %get-tuple-element.138.values.wide.left.refs_0_.refs_1_.refs_2_, bf16[1280,2048]{1,0:T(8,128)(2,1)} %get-tuple-element.138.values.wide.left.refs_0_.refs_1_.refs_2_, ...), custom_call_target="tpu_custom_call" | custom-call | flops 10737418240 | bytes 18874368 | tf_op jit(solution)/shard_map/paired_grads/pallas_call | solution.py:732
  621.0 2.7 fusion.17
  625.9 15.3 %partial_blocks.14 = (bf16[2,640,512]{2,1,0:T(8,128)(2,1)}, f32[2,640,512]{2,1,0:T(8,128)}) custom-call(s32[1]{0:T(128)} %bitcast.row, bf16[1280,512]{1,0:T(8,128)(2,1)} %get-tuple-element.232.refs_0_.refs_3_, bf16[1280,512]{1,0:T(8,128)(2,1)} %get-tuple-element.233.refs_1_.refs_4_, bf16[1280,1024]{1,0:T(8,128)(2,1)} %get-tuple-element.240.refs_2_.refs_5_, ...), custom_call_target="tpu_custom_call" | custom-call | flops 8053063680 | bytes 25690112 | tf_op jit(solution)/shard_map/partial_blocks/pallas_call | solution.py:930
  648.3 5.3 fusion.9
  653.5 5.3 collective-permute-done.36
  669.6 2.5 copy.88
  672.1 2.5 copy.87
  683.0 3.2 collective-permute-start.42
  686.9 3.0 collective-permute-done.42
  690.9 3.8 fusion.7
  (305 shorter events, 145.9 us)
Async XLA Ops:
  7.2 87.8 %all-gather.5.cloned.1.call-start = ((), (), s32[]{:S(2)}) async-start(), calls=%async_computation.4 | async-start | bytes 9437184 | tf_op jit(solution)/shard_map/all_gather | solution.py:1047
  9.5 141.4 %all-gather.7.cloned.1.call-start = ((), (), s32[]{:S(2)}) async-start(), calls=%async_computation.5 | async-start | bytes 4718592 | tf_op jit(solution)/shard_map/all_gather | solution.py:1047
  10.3 187.9 %all-gather.9.cloned.1.call-start = ((), (), s32[]{:S(2)}) async-start(), calls=%async_computation.6 | async-start | bytes 4718592 | tf_op jit(solution)/shard_map/all_gather | solution.py:1047
  11.6 288.5 %all-gather.11.cloned.1.call-start = ((), (), s32[]{:S(2)}) async-start(), calls=%async_computation.7 | async-start | bytes 9437184 | tf_op jit(solution)/shard_map/all_gather | solution.py:1047
  13.0 459.6 %reduce-scatter.5.cloned.1.call-start = ((), (), s32[]{:S(2)}) async-start(), calls=%async_computation.8 | async-start | bytes 9437184 | tf_op jit(solution)/shard_map/reduce_scatter | solution.py:1052
  13.1 10.3 %collective-permute-start.5 = (f32[4,512]{1,0:T(4,128)S(1)}, f32[4,512]{1,0:T(4,128)S(1)}, u32[]{:S(2)}, u32[]{:S(2)}) collective-permute-start(f32[4,512]{1,0:T(4,128)S(1)} %get-tuple-element.414), channel_id=1, source_target_pairs={{0,16},{16,0},{8,24},{24,8},{1,17},{17,1},{9,25},{25,9},{2,18},{18... | collective-permute-start | bytes 24584 | tf_op jit(solution)/shard_map/ppermute | solution.py:950
  16.2 7.3 %collective-permute-start.4 = (f32[4,512]{1,0:T(4,128)S(1)}, f32[4,512]{1,0:T(4,128)S(1)}, u32[]{:S(2)}, u32[]{:S(2)}) collective-permute-start(f32[4,512]{1,0:T(4,128)S(1)} %get-tuple-element.414), channel_id=1, source_target_pairs={{0,8},{8,0},{16,24},{24,16},{1,9},{9,1},{17,25},{25,17},{2,10},{10... | collective-permute-start | bytes 24584 | tf_op jit(solution)/shard_map/ppermute | solution.py:950
  17.7 30.2 %collective-permute-start = (bf16[1280,512]{1,0:T(8,128)(2,1)S(1)}, bf16[1280,512]{1,0:T(8,128)(2,1)}, u32[]{:S(2)}, u32[]{:S(2)}) collective-permute-start(bf16[1280,512]{1,0:T(8,128)(2,1)S(1)} %copy-done.14), channel_id=1, source_target_pairs={{0,8},{8,0},{16,24},{24,16},{1,9},{9,1},{17,25},{25,17},{2,10},{10... | collective-permute-start | bytes 3932168 | tf_op jit(solution)/shard_map/ppermute | solution.py:950
  19.6 31.1 %collective-permute-start.1 = (bf16[1280,512]{1,0:T(8,128)(2,1)S(1)}, bf16[1280,512]{1,0:T(8,128)(2,1)}, u32[]{:S(2)}, u32[]{:S(2)}) collective-permute-start(bf16[1280,512]{1,0:T(8,128)(2,1)S(1)} %copy-done.14), channel_id=1, source_target_pairs={{0,16},{16,0},{8,24},{24,8},{1,17},{17,1},{9,25},{25,9},{2,18},{18... | collective-permute-start | bytes 3932168 | tf_op jit(solution)/shard_map/ppermute | solution.py:950
  49.1 15.2 %collective-permute-start.2 = (bf16[640,512]{1,0:T(8,128)(2,1)S(1)}, bf16[640,512]{1,0:T(8,128)(2,1)S(1)}, u32[]{:S(2)}, u32[]{:S(2)}) collective-permute-start(bf16[640,512]{1,0:T(8,128)(2,1)S(1)} %slice.269), channel_id=1, source_target_pairs={{0,16},{16,0},{8,24},{24,8},{1,17},{17,1},{9,25},{25,9},{2,18},{18... | collective-permute-start | bytes 1966088 | tf_op jit(solution)/shard_map/ppermute | solution.py:950
  51.9 14.6 %collective-permute-start.3 = (bf16[640,512]{1,0:T(8,128)(2,1)S(1)}, bf16[640,512]{1,0:T(8,128)(2,1)S(1)}, u32[]{:S(2)}, u32[]{:S(2)}) collective-permute-start(bf16[640,512]{1,0:T(8,128)(2,1)S(1)} %slice.270), channel_id=1, source_target_pairs={{0,8},{8,0},{16,24},{24,16},{1,9},{9,1},{17,25},{25,17},{2,10},{10... | collective-permute-start | bytes 1966088 | tf_op jit(solution)/shard_map/ppermute | solution.py:950
  74.8 41.4 %collective-permute-start.8 = (bf16[1280,512]{1,0:T(8,128)(2,1)S(1)}, bf16[1280,512]{1,0:T(8,128)(2,1)S(1)}, u32[]{:S(2)}, u32[]{:S(2)}) collective-permute-start(bf16[1280,512]{1,0:T(8,128)(2,1)S(1)} %multiply_convert_fusion.own), channel_id=1, source_target_pairs={{0,16},{16,0},{8,24},{24,8},{1,17},{17,1},{9,25},{25,9},{2,18},{18... | collective-permute-start | bytes 3932168 | tf_op jit(solution)/shard_map/ppermute | solution.py:950
  75.6 40.7 %collective-permute-start.7 = (bf16[1280,512]{1,0:T(8,128)(2,1)S(1)}, bf16[1280,512]{1,0:T(8,128)(2,1)}, u32[]{:S(2)}, u32[]{:S(2)}) collective-permute-start(bf16[1280,512]{1,0:T(8,128)(2,1)S(1)} %multiply_convert_fusion.own), channel_id=1, source_target_pairs={{0,8},{8,0},{16,24},{24,16},{1,9},{9,1},{17,25},{25,17},{2,10},{10... | collective-permute-start | bytes 3932168 | tf_op jit(solution)/shard_map/ppermute | solution.py:950
  119.7 31.2 %collective-permute-start.10 = (bf16[640,512]{1,0:T(8,128)(2,1)S(1)}, bf16[640,512]{1,0:T(8,128)(2,1)S(1)}, u32[]{:S(2)}, u32[]{:S(2)}) collective-permute-start(bf16[640,512]{1,0:T(8,128)(2,1)S(1)} %slice.210), channel_id=1, source_target_pairs={{0,8},{8,0},{16,24},{24,16},{1,9},{9,1},{17,25},{25,17},{2,10},{10... | collective-permute-start | bytes 1966088 | tf_op jit(solution)/shard_map/ppermute | solution.py:950
  121.3 29.6 %collective-permute-start.9 = (bf16[640,512]{1,0:T(8,128)(2,1)S(1)}, bf16[640,512]{1,0:T(8,128)(2,1)S(1)}, u32[]{:S(2)}, u32[]{:S(2)}) collective-permute-start(bf16[640,512]{1,0:T(8,128)(2,1)S(1)} %slice.209), channel_id=1, source_target_pairs={{0,16},{16,0},{8,24},{24,8},{1,17},{17,1},{9,25},{25,9},{2,18},{18... | collective-permute-start | bytes 1966088 | tf_op jit(solution)/shard_map/ppermute | solution.py:950
  206.4 31.1 %collective-permute-start.11 = (bf16[2,640,512]{2,1,0:T(8,128)(2,1)}, bf16[2,640,512]{2,1,0:T(8,128)(2,1)S(1)}, u32[]{:S(2)}, u32[]{:S(2)}) collective-permute-start(bf16[2,640,512]{2,1,0:T(8,128)(2,1)} %get-tuple-element.156), channel_id=1, source_target_pairs={{0,8},{8,0},{16,24},{24,16},{1,9},{9,1},{17,25},{25,17},{2,10},{10... | collective-permute-start | bytes 3932168 | tf_op jit(solution)/shard_map/ppermute | solution.py:950
  207.8 30.8 %collective-permute-start.13 = (bf16[2,640,512]{2,1,0:T(8,128)(2,1)}, bf16[2,640,512]{2,1,0:T(8,128)(2,1)S(1)}, u32[]{:S(2)}, u32[]{:S(2)}) collective-permute-start(bf16[2,640,512]{2,1,0:T(8,128)(2,1)} %get-tuple-element.158), channel_id=1, source_target_pairs={{0,16},{16,0},{8,24},{24,8},{1,17},{17,1},{9,25},{25,9},{2,18},{18... | collective-permute-start | bytes 3932168 | tf_op jit(solution)/shard_map/ppermute | solution.py:950
  240.9 15.9 %collective-permute-start.12 = (bf16[640,512]{1,0:T(8,128)(2,1)S(1)}, bf16[640,512]{1,0:T(8,128)(2,1)S(1)}, u32[]{:S(2)}, u32[]{:S(2)}) collective-permute-start(bf16[640,512]{1,0:T(8,128)(2,1)S(1)} %get-tuple-element.387), channel_id=1, source_target_pairs={{0,16},{16,0},{8,24},{24,8},{1,17},{17,1},{9,25},{25,9},{2,18},{18... | collective-permute-start | bytes 1966088 | tf_op jit(solution)/shard_map/ppermute | solution.py:950
  242.4 15.6 %collective-permute-start.14 = (bf16[640,512]{1,0:T(8,128)(2,1)S(1)}, bf16[640,512]{1,0:T(8,128)(2,1)S(1)}, u32[]{:S(2)}, u32[]{:S(2)}) collective-permute-start(bf16[640,512]{1,0:T(8,128)(2,1)S(1)} %get-tuple-element.388), channel_id=1, source_target_pairs={{0,8},{8,0},{16,24},{24,16},{1,9},{9,1},{17,25},{25,17},{2,10},{10... | collective-permute-start | bytes 1966088 | tf_op jit(solution)/shard_map/ppermute | solution.py:950
  261.1 28.8 %collective-permute-start.16 = (bf16[1280,512]{1,0:T(8,128)(2,1)S(1)}, bf16[1280,512]{1,0:T(8,128)(2,1)S(1)}, u32[]{:S(2)}, u32[]{:S(2)}) collective-permute-start(bf16[1280,512]{1,0:T(8,128)(2,1)S(1)} %fusion.30.refs_0_), channel_id=1, source_target_pairs={{0,16},{16,0},{8,24},{24,8},{1,17},{17,1},{9,25},{25,9},{2,18},{18... | collective-permute-start | bytes 3932168 | tf_op jit(solution)/shard_map/ppermute | solution.py:950
  261.6 28.5 %collective-permute-start.15 = (bf16[1280,512]{1,0:T(8,128)(2,1)S(1)}, bf16[1280,512]{1,0:T(8,128)(2,1)S(1)}, u32[]{:S(2)}, u32[]{:S(2)}) collective-permute-start(bf16[1280,512]{1,0:T(8,128)(2,1)S(1)} %fusion.30.refs_0_), channel_id=1, source_target_pairs={{0,8},{8,0},{16,24},{24,16},{1,9},{9,1},{17,25},{25,17},{2,10},{10... | collective-permute-start | bytes 3932168 | tf_op jit(solution)/shard_map/ppermute | solution.py:950
  291.3 18.7 %collective-permute-start.18 = (bf16[640,512]{1,0:T(8,128)(2,1)}, bf16[640,512]{1,0:T(8,128)(2,1)}, u32[]{:S(2)}, u32[]{:S(2)}) collective-permute-start(bf16[640,512]{1,0:T(8,128)(2,1)} %slice.220), channel_id=1, source_target_pairs={{0,8},{8,0},{16,24},{24,16},{1,9},{9,1},{17,25},{25,17},{2,10},{10... | collective-permute-start | bytes 1966088 | tf_op jit(solution)/shard_map/ppermute | solution.py:950
  292.7 17.3 %collective-permute-start.17 = (bf16[640,512]{1,0:T(8,128)(2,1)S(1)}, bf16[640,512]{1,0:T(8,128)(2,1)}, u32[]{:S(2)}, u32[]{:S(2)}) collective-permute-start(bf16[640,512]{1,0:T(8,128)(2,1)S(1)} %slice.219), channel_id=1, source_target_pairs={{0,16},{16,0},{8,24},{24,8},{1,17},{17,1},{9,25},{25,9},{2,18},{18... | collective-permute-start | bytes 1966088 | tf_op jit(solution)/shard_map/ppermute | solution.py:950
  337.4 28.3 %collective-permute-start.19 = (bf16[2,640,512]{2,1,0:T(8,128)(2,1)}, bf16[2,640,512]{2,1,0:T(8,128)(2,1)}, u32[]{:S(2)}, u32[]{:S(2)}) collective-permute-start(bf16[2,640,512]{2,1,0:T(8,128)(2,1)} %get-tuple-element.183), channel_id=1, source_target_pairs={{0,8},{8,0},{16,24},{24,16},{1,9},{9,1},{17,25},{25,17},{2,10},{10... | collective-permute-start | bytes 3932168 | tf_op jit(solution)/shard_map/ppermute | solution.py:950
  338.1 27.6 %collective-permute-start.20 = (bf16[2,640,512]{2,1,0:T(8,128)(2,1)}, bf16[2,640,512]{2,1,0:T(8,128)(2,1)}, u32[]{:S(2)}, u32[]{:S(2)}) collective-permute-start(bf16[2,640,512]{2,1,0:T(8,128)(2,1)} %get-tuple-element.184), channel_id=1, source_target_pairs={{0,16},{16,0},{8,24},{24,8},{1,17},{17,1},{9,25},{25,9},{2,18},{18... | collective-permute-start | bytes 3932168 | tf_op jit(solution)/shard_map/ppermute | solution.py:950
  365.7 189.5 %reduce-scatter.7.cloned.1.call-start = ((), (), s32[]{:S(2)}) async-start(), calls=%async_computation.9 | async-start | bytes 2621440 | tf_op jit(solution)/shard_map/reduce_scatter | solution.py:1054
  367.1 8.0 %collective-permute-start.25 = (f32[2,1280]{1,0:T(2,128)S(1)}, f32[2,1280]{1,0:T(2,128)S(1)}, u32[]{:S(2)}, u32[]{:S(2)}) collective-permute-start(f32[2,1280]{1,0:T(2,128)S(1)} %copy.77), channel_id=1, source_target_pairs={{0,24},{24,0},{8,16},{16,8},{1,25},{25,1},{9,17},{17,9},{2,26},{26... | collective-permute-start | bytes 30728 | tf_op jit(solution)/shard_map/ppermute | solution.py:950
  378.4 11.4 %collective-permute-start.21 = (bf16[640,512]{1,0:T(8,128)(2,1)S(1)}, bf16[640,512]{1,0:T(8,128)(2,1)S(1)}, u32[]{:S(2)}, u32[]{:S(2)}) collective-permute-start(bf16[640,512]{1,0:T(8,128)(2,1)S(1)} %get-tuple-element.385), channel_id=1, source_target_pairs={{0,16},{16,0},{8,24},{24,8},{1,17},{17,1},{9,25},{25,9},{2,18},{18... | collective-permute-start | bytes 1966088 | tf_op jit(solution)/shard_map/ppermute | solution.py:950
  379.8 10.9 %collective-permute-start.22 = (bf16[640,512]{1,0:T(8,128)(2,1)S(1)}, bf16[640,512]{1,0:T(8,128)(2,1)S(1)}, u32[]{:S(2)}, u32[]{:S(2)}) collective-permute-start(bf16[640,512]{1,0:T(8,128)(2,1)S(1)} %get-tuple-element.386), channel_id=1, source_target_pairs={{0,8},{8,0},{16,24},{24,16},{1,9},{9,1},{17,25},{25,17},{2,10},{10... | collective-permute-start | bytes 1966088 | tf_op jit(solution)/shard_map/ppermute | solution.py:950
  396.5 24.4 %collective-permute-start.27 = (bf16[1280,512]{1,0:T(8,128)(2,1)}, bf16[1280,512]{1,0:T(8,128)(2,1)}, u32[]{:S(2)}, u32[]{:S(2)}) collective-permute-start(bf16[1280,512]{1,0:T(8,128)(2,1)} %get-tuple-element.365.own), channel_id=1, source_target_pairs={{0,16},{16,0},{8,24},{24,8},{1,17},{17,1},{9,25},{25,9},{2,18},{18... | collective-permute-start | bytes 3932168 | tf_op jit(solution)/shard_map/ppermute | solution.py:950
  397.3 26.8 %collective-permute-start.26 = (bf16[1280,512]{1,0:T(8,128)(2,1)}, bf16[1280,512]{1,0:T(8,128)(2,1)}, u32[]{:S(2)}, u32[]{:S(2)}) collective-permute-start(bf16[1280,512]{1,0:T(8,128)(2,1)} %get-tuple-element.365.own), channel_id=1, source_target_pairs={{0,8},{8,0},{16,24},{24,16},{1,9},{9,1},{17,25},{25,17},{2,10},{10... | collective-permute-start | bytes 3932168 | tf_op jit(solution)/shard_map/ppermute | solution.py:950
  426.4 10.7 %collective-permute-start.29 = (bf16[640,512]{1,0:T(8,128)(2,1)S(1)}, bf16[640,512]{1,0:T(8,128)(2,1)S(1)}, u32[]{:S(2)}, u32[]{:S(2)}) collective-permute-start(bf16[640,512]{1,0:T(8,128)(2,1)S(1)} %slice.242), channel_id=1, source_target_pairs={{0,8},{8,0},{16,24},{24,16},{1,9},{9,1},{17,25},{25,17},{2,10},{10... | collective-permute-start | bytes 1966088 | tf_op jit(solution)/shard_map/ppermute | solution.py:950
  428.2 10.7 %collective-permute-start.28 = (bf16[640,512]{1,0:T(8,128)(2,1)S(1)}, bf16[640,512]{1,0:T(8,128)(2,1)}, u32[]{:S(2)}, u32[]{:S(2)}) collective-permute-start(bf16[640,512]{1,0:T(8,128)(2,1)S(1)} %slice.241), channel_id=1, source_target_pairs={{0,16},{16,0},{8,24},{24,8},{1,17},{17,1},{9,25},{25,9},{2,18},{18... | collective-permute-start | bytes 1966088 | tf_op jit(solution)/shard_map/ppermute | solution.py:950
  475.5 140.4 %reduce-scatter.9.cloned.1.call-start = ((), (), s32[]{:S(2)}) async-start(), calls=%async_computation.10 | async-start | bytes 4718592 | tf_op jit(solution)/shard_map/reduce_scatter | solution.py:1052
  475.6 28.8 %collective-permute-start.30 = (bf16[2,640,512]{2,1,0:T(8,128)(2,1)}, bf16[2,640,512]{2,1,0:T(8,128)(2,1)}, u32[]{:S(2)}, u32[]{:S(2)}) collective-permute-start(bf16[2,640,512]{2,1,0:T(8,128)(2,1)} %get-tuple-element.202), channel_id=1, source_target_pairs={{0,8},{8,0},{16,24},{24,16},{1,9},{9,1},{17,25},{25,17},{2,10},{10... | collective-permute-start | bytes 3932168 | tf_op jit(solution)/shard_map/ppermute | solution.py:950
  477.1 28.4 %collective-permute-start.31 = (bf16[2,640,512]{2,1,0:T(8,128)(2,1)}, bf16[2,640,512]{2,1,0:T(8,128)(2,1)}, u32[]{:S(2)}, u32[]{:S(2)}) collective-permute-start(bf16[2,640,512]{2,1,0:T(8,128)(2,1)} %get-tuple-element.203), channel_id=1, source_target_pairs={{0,16},{16,0},{8,24},{24,8},{1,17},{17,1},{9,25},{25,9},{2,18},{18... | collective-permute-start | bytes 3932168 | tf_op jit(solution)/shard_map/ppermute | solution.py:950
  557.4 146.2 %reduce-scatter.11.cloned.1.call-start = ((), (), s32[]{:S(2)}) async-start(), calls=%async_computation.11 | async-start | bytes 5242880 | tf_op jit(solution)/shard_map/reduce_scatter | solution.py:1054
  586.9 28.9 %collective-permute-start.34 = (bf16[2,640,512]{2,1,0:T(8,128)(2,1)}, bf16[2,640,512]{2,1,0:T(8,128)(2,1)}, u32[]{:S(2)}, u32[]{:S(2)}) collective-permute-start(bf16[2,640,512]{2,1,0:T(8,128)(2,1)} %get-tuple-element.238), channel_id=1, source_target_pairs={{0,8},{8,0},{16,24},{24,16},{1,9},{9,1},{17,25},{25,17},{2,10},{10... | collective-permute-start | bytes 3932168 | tf_op jit(solution)/shard_map/ppermute | solution.py:950
  587.9 28.0 %collective-permute-start.35 = (bf16[2,640,512]{2,1,0:T(8,128)(2,1)}, bf16[2,640,512]{2,1,0:T(8,128)(2,1)}, u32[]{:S(2)}, u32[]{:S(2)}) collective-permute-start(bf16[2,640,512]{2,1,0:T(8,128)(2,1)} %get-tuple-element.239), channel_id=1, source_target_pairs={{0,16},{16,0},{8,24},{24,8},{1,17},{17,1},{9,25},{25,9},{2,18},{18... | collective-permute-start | bytes 3932168 | tf_op jit(solution)/shard_map/ppermute | solution.py:950
  623.8 22.3 %collective-permute-start.32 = (bf16[640,512]{1,0:T(8,128)(2,1)}, bf16[640,512]{1,0:T(8,128)(2,1)S(1)}, u32[]{:S(2)}, u32[]{:S(2)}) collective-permute-start(bf16[640,512]{1,0:T(8,128)(2,1)} %get-tuple-element.383), channel_id=1, source_target_pairs={{0,16},{16,0},{8,24},{24,8},{1,17},{17,1},{9,25},{25,9},{2,18},{18... | collective-permute-start | bytes 1966088 | tf_op jit(solution)/shard_map/ppermute | solution.py:950
  624.8 21.3 %collective-permute-start.33 = (bf16[640,512]{1,0:T(8,128)(2,1)}, bf16[640,512]{1,0:T(8,128)(2,1)}, u32[]{:S(2)}, u32[]{:S(2)}) collective-permute-start(bf16[640,512]{1,0:T(8,128)(2,1)} %get-tuple-element.384), channel_id=1, source_target_pairs={{0,8},{8,0},{16,24},{24,16},{1,9},{9,1},{17,25},{25,17},{2,10},{10... | collective-permute-start | bytes 1966088 | tf_op jit(solution)/shard_map/ppermute | solution.py:950
  643.3 15.5 %collective-permute-start.36 = (bf16[640,512]{1,0:T(8,128)(2,1)S(1)}, bf16[640,512]{1,0:T(8,128)(2,1)S(1)}, u32[]{:S(2)}, u32[]{:S(2)}) collective-permute-start(bf16[640,512]{1,0:T(8,128)(2,1)S(1)} %get-tuple-element.381), channel_id=1, source_target_pairs={{0,16},{16,0},{8,24},{24,8},{1,17},{17,1},{9,25},{25,9},{2,18},{18... | collective-permute-start | bytes 1966088 | tf_op jit(solution)/shard_map/ppermute | solution.py:950
  644.6 15.8 %collective-permute-start.37 = (bf16[640,512]{1,0:T(8,128)(2,1)S(1)}, bf16[640,512]{1,0:T(8,128)(2,1)S(1)}, u32[]{:S(2)}, u32[]{:S(2)}) collective-permute-start(bf16[640,512]{1,0:T(8,128)(2,1)S(1)} %get-tuple-element.382), channel_id=1, source_target_pairs={{0,8},{8,0},{16,24},{24,16},{1,9},{9,1},{17,25},{25,17},{2,10},{10... | collective-permute-start | bytes 1966088 | tf_op jit(solution)/shard_map/ppermute | solution.py:950
  664.4 13.8 %collective-permute-start.39 = (f32[2,1280]{1,0:T(2,128)S(1)}, f32[2,1280]{1,0:T(2,128)S(1)}, u32[]{:S(2)}, u32[]{:S(2)}) collective-permute-start(f32[2,1280]{1,0:T(2,128)S(1)} %pad_maximum_fusion.7), channel_id=1, source_target_pairs={{0,16},{16,0},{8,24},{24,8},{1,17},{17,1},{9,25},{25,9},{2,18},{18... | collective-permute-start | bytes 30728 | tf_op jit(solution)/shard_map/ppermute | solution.py:950
  665.3 12.7 %collective-permute-start.40 = (f32[2,1280]{1,0:T(2,128)S(1)}, f32[2,1280]{1,0:T(2,128)S(1)}, u32[]{:S(2)}, u32[]{:S(2)}) collective-permute-start(f32[2,1280]{1,0:T(2,128)S(1)} %pad_maximum_fusion.7), channel_id=1, source_target_pairs={{0,24},{24,0},{8,16},{16,8},{1,25},{25,1},{9,17},{17,9},{2,26},{26... | collective-permute-start | bytes 30728 | tf_op jit(solution)/shard_map/ppermute | solution.py:950
  667.3 15.3 %collective-permute-start.38 = (f32[2,1280]{1,0:T(2,128)S(1)}, f32[2,1280]{1,0:T(2,128)S(1)}, u32[]{:S(2)}, u32[]{:S(2)}) collective-permute-start(f32[2,1280]{1,0:T(2,128)S(1)} %pad_maximum_fusion.7), channel_id=1, source_target_pairs={{0,8},{8,0},{16,24},{24,16},{1,9},{9,1},{17,25},{25,17},{2,10},{10... | collective-permute-start | bytes 30728 | tf_op jit(solution)/shard_map/ppermute | solution.py:950
  683.0 6.8 collective-permute-start.42
  689.9 6.6 collective-permute-start.43
  (69 other events, 428.4 us)
Sparse Core Ops, SparseCore 0:
  10.2 84.7 all-gather.4
  96.6 52.1 all-gather.6
  150.9 47.2 all-gather.8
  200.3 86.4 all-gather.10
  365.9 106.7 reduce-scatter.4
  475.6 44.0 reduce-scatter.6
  557.5 56.2 reduce-scatter.8
  618.2 78.6 reduce-scatter.10

commit v6 on v5

--- a/solution.py
+++ b/solution.py
@@ -967,10 +967,13 @@
     return tuple(partial_blocks(values, weights, row, 2, (BF16, F32)))
 
 
-def reduce_row_finish(sends, values, weights, row, between=None, tied=None, rest=None):
+def reduce_row_finish(
+    sends, values, weights, row, between=None, tied=None, rest=None, delayed=False
+):
     if lax.axis_size("row") != 4:
         total = lax.psum_scatter(sends, "row", scatter_dimension=1, tiled=True).astype(F32)
-        return total, between(tied) if between else None
+        extra = between(tied) if between else None
+        return ((lambda first: (total, first)) if delayed else total), extra
     from_x = permute_row(sends[0], X_PAIRS)
     from_y = permute_row(sends[1], Y_PAIRS)
     keep, own = rest if rest is not None else reduce_row_rest(values, weights, row)
@@ -984,9 +987,17 @@
     next_x = (keep[1].astype(F32) + from_y[1].astype(F32)).astype(BF16)
     last_y = permute_row(next_y, Y_PAIRS)
     last_x = permute_row(next_x, X_PAIRS)
-    first_half = own[0] + from_x[0].astype(F32) + last_y.astype(F32)
-    second_half = own[1] + from_y[0].astype(F32) + last_x.astype(F32)
-    return jnp.concatenate([first_half, second_half], axis=0), extra
+
+    def add(last_y, last_x):
+        first_half = own[0] + from_x[0].astype(F32) + last_y.astype(F32)
+        second_half = own[1] + from_y[0].astype(F32) + last_x.astype(F32)
+        return jnp.concatenate([first_half, second_half], axis=0)
+
+    def add_after(first):
+        now_y, now_x, first = in_order(last_y, last_x, first)
+        return add(now_y, now_x), first
+
+    return (add_after if delayed else add(last_y, last_x)), extra
 
 
 def gather_row(value, between=None, later=None):
@@ -1049,10 +1060,9 @@
 
 def scatter_col(grad):
     if grad.ndim == 2:
-        return lax.psum_scatter(grad, "col", scatter_dimension=0, tiled=True).astype(F32)
+        return lax.psum_scatter(grad, "col", scatter_dimension=0, tiled=True)
     groups = [list(range(core, SLOTS, 2)) for core in range(2)]
-    total = lax.psum_scatter(grad, "col", scatter_dimension=0, axis_index_groups=groups)
-    return total.astype(F32)
+    return lax.psum_scatter(grad, "col", scatter_dimension=0, axis_index_groups=groups)
 
 
 class Exchange:
@@ -1510,7 +1520,7 @@
     out_partial, grad_wide = in_order(out_partial, grad_wide)
     out_partial, feed_grad = in_order(out_partial, feed_grad)
     out_grad = scatter_col(out_partial)
-    fed_out, gate_results = reduce_row_finish(
+    add_fed_out, gate_results = reduce_row_finish(
         fed_sends,
         [hidden],
         [down_part],
@@ -1521,9 +1531,8 @@
             )
         ),
         rest=fed_rest,
-    )
-    fed_out = fed_out + down_bias
-    layer_out = middle + fed_out
+        delayed=True,
+    )
     grad_gate, grad_retained, group_gain_grad, group_bias_grad, returns, first_state = gate_results
     own0, own1, own2, gate_partial = return_states(
         meta, rates, returns, first_state, first_wide, grad_gate, rows
@@ -1538,6 +1547,9 @@
     back_weights = [query_part, key_part, value_part, gate_part]
     sends = reduce_row_start(back_values, back_weights, row_ref)
     sends, grad_value = in_order(sends, grad_value)
+    fed_out, back_rest = add_fed_out(reduce_row_rest(back_values, back_weights, row_ref))
+    fed_out = fed_out + down_bias
+    layer_out = middle + fed_out
     first_back, project_partial = reduce_row_finish(
         sends,
         back_values,
@@ -1546,9 +1558,13 @@
         lambda _: column_grads(
             [(first_wide, grad_query), (first_wide, grad_key), (first_wide, grad_value)], 6
         ),
+        rest=back_rest,
     )
     project_partial, gate_grad = in_order(project_partial, gate_grad)
-    project_grad = scatter_col(project_partial)
+    project_grad = scatter_col(project_partial).astype(F32)
+    feed_grad, out_grad, gate_grad = (
+        grad.astype(F32) for grad in (feed_grad, out_grad, gate_grad)
+    )
 
     first_normal = (tokens.astype(F32) - first_average[:, :1]) * first_inverse[:, :1]
     grad_first, first_gain_grad, first_bias_grad = norm_backward(

time: 723 us -> 717 us (level)
    unnamed x128 -> x132, local copies, waits for them, and re-layouts: 21.3 us -> 21.3 us
  transfers between devices with their start and end apart: 55 -> 55, of which waited for: 27 -> 26; matrix products, arithmetic and copies ran while one was open for 11% -> 11% of each run, Pallas kernels for 42% -> 43%
where the time goes in v6:
time: 717 us; the launch traced here: 708 us
  Pallas kernels  328 us (46%)
  waiting for transfers between devices  199 us (28%)
  starting transfers between devices  63.5 us (9%)
  local copies, waits for them, and re-layouts  50.4 us (7%)
  other arithmetic  50.3 us (7%)
  between operations  16 us (2%)
    ppermute x44, waiting for transfers between devices, permute_row(): return lax.ppermute(value, 'row', pairs)  141 us
    pallas_call x8, Pallas kernels, partial_blocks(): pl.pallas_call(functools.partial(partial_kernel, count), grid_spec=pltpu....  80.1 us
    ppermute x44, starting transfers between devices, permute_row(): return lax.ppermute(value, 'row', pairs)  55.3 us
    pallas_call x1, Pallas kernels, return_states(): pl.pallas_call(functools.partial(return_kernel, rows), in_specs=[smem(),...  40.2 us
    all_gather x4, waiting for transfers between devices, gather_col(): return lax.all_gather(weight, 'col', axis=0, tiled=True)  39.2 us
    pallas_call x2, Pallas kernels, paired_grads(): pl.pallas_call(functools.partial(paired_grad_kernel, tuple(spans), tiles,...  39 us
    pallas_call x1, Pallas kernels, share_states(): pl.pallas_call(functools.partial(share_kernel, rows), in_specs=[smem(), s...  25.3 us
    pallas_call x1, Pallas kernels, project(): pl.pallas_call(functools.partial(project_kernel, heads, rows, chunks), gr...  21.3 us
  transfers between devices with their start and end apart: 55, of which 26 were waited for; matrix products, arithmetic and copies ran while one was open for 11% of the time, Pallas kernels for 43%

profile of v6, /device:TPU:0, one launch (start us, length us, event | category | flops | bytes accessed | tf_op | source)
XLA Modules:
  0.0 708.0 jit_solution(7939580839625845057)
XLA Ops:
  7.2 2.3 pad_maximum_fusion.3
  13.1 3.0 collective-permute-start.5
  23.5 24.5 %collective-permute-done.from_x = bf16[1280,512]{1,0:T(8,128)(2,1)} collective-permute-done((bf16[1280,512]{1,0:T(8,128)(2,1)S(1)}, bf16[1280,512]{1,0:T(8,128)(2,1)}, u32[]{:S(2)}, u32[]{:S(2)}) %collective-permute-start) | collective-permute-done | bytes 1310752 | tf_op jit(solution)/shard_map/ppermute | solution.py:950
  54.1 10.2 %collective-permute-done.2.far_a = bf16[640,512]{1,0:T(8,128)(2,1)S(1)} collective-permute-done((bf16[640,512]{1,0:T(8,128)(2,1)S(1)}, bf16[640,512]{1,0:T(8,128)(2,1)S(1)}, u32[]{:S(2)}, u32[]{:S(2)}) %collective-permute-start.2) | collective-permute-done | bytes 655392 | tf_op jit(solution)/shard_map/ppermute | solution.py:950
  64.2 2.2 collective-permute-done.3.far_b
  67.3 7.5 %join_norm.1 = (bf16[1280,2048]{1,0:T(8,128)(2,1)}, f32[1280,128]{1,0:T(8,128)}, f32[1280,128]{1,0:T(8,128)}) custom-call(s32[1]{0:T(128)} %bitcast.row, bf16[1280,512]{1,0:T(8,128)(2,1)} %own.1, bf16[1280,512]{1,0:T(8,128)(2,1)} %collective-permute-done.from_x, bf16[1280,512]{1,0:T(8,128)(2,1)} %collective-permute-done.1.from_y, ...), custom_call_target="tpu_custom_call" | custom-call | flops 20971520 | bytes 10485760 | tf_op jit(solution)/shard_map/join_norm/pallas_call | solution.py:491
  77.0 3.7 multiply_sine_fusion
  81.9 13.1 %all-gather.5.cloned.1.call-done.weight.refs_4_.refs_5_.refs_6_ = bf16[2048,2048]{1,0:T(8,128)(2,1)} async-done(((bf16[256,2048]{1,0:T(8,128)(2,1)}), bf16[2048,2048]{1,0:T(8,128)(2,1)}) %all-gather.5.cloned.1.call-update) | async-done | bytes 8388624 | tf_op jit(solution)/shard_map/all_gather | solution.py:1058
  95.0 21.3 %project.1 = (bf16[1280,512]{1,0:T(8,128)(2,1)}, bf16[1280,512]{1,0:T(8,128)(2,1)}, bf16[1280,1024]{1,0:T(8,128)(2,1)}, bf16[3,2,256,512]{3,2,1,0:T(8,128)(2,1)}) custom-call(s32[22]{0:T(128)} %pad_add_fusion.meta, f32[2]{0:T(128)} %subtract_log_fusion.rates, bf16[1280,2048]{1,0:T(8,128)(2,1)} %get-tuple-element.142.values.wide.left.refs_0_.refs_1_.refs_2_, ...), custom_call_target="tpu_custom_call" | custom-call | flops 10737418240 | bytes 13631488 | tf_op jit(solution)/shard_map/project/pallas_call | solution.py:554
  122.8 25.3 %share_states.1 = (bf16[8,2,256,512]{3,2,1,0:T(8,128)(2,1)S(1)}, bf16[2,256,512]{2,1,0:T(8,128)(2,1)S(1)}) custom-call(s32[22]{0:T(128)S(1)} %copy-done.5, f32[2]{0:T(128)S(1)} %copy-done.7, bf16[3,2,256,512]{3,2,1,0:T(8,128)(2,1)S(1)} %copy-done.3), custom_call_target="tpu_custom_call" | custom-call | bytes 104857600 | tf_op jit(solution)/shard_map/share_states/pallas_call | solution.py:1214
  150.9 21.3 %retention_forward.1 = (f32[1280,1024]{1,0:T(8,128)}, bf16[1280,1024]{1,0:T(8,128)(2,1)}, bf16[1280,1024]{1,0:T(8,128)(2,1)}, f32[2,1280,128]{2,1,0:T(8,128)}, bf16[2,5,256,512]{3,2,1,0:T(8,128)(2,1)}) custom-call(s32[22]{0:T(128)} %pad_add_fusion.meta, f32[2]{0:T(128)} %subtract_log_fusion.rates, bf16[1280,512]{1,0:T(8,128)(2,1)} %get-tuple-element.147.query, ...), custom_call_target="tpu_custom_call" | custom-call | flops 7717519360 | bytes 20971520 | tf_op jit(solution)/shard_map/retention_forward/pallas_call | solution.py:203
  172.2 26.0 %all-gather.9.cloned.1.call-done.refs_1_.weight = bf16[2048,1024]{1,0:T(8,128)(2,1)} async-done(((bf16[256,1024]{1,0:T(8,128)(2,1)}), bf16[2048,1024]{1,0:T(8,128)(2,1)}) %all-gather.9.cloned.1.call-update) | async-done | bytes 4194320 | tf_op jit(solution)/shard_map/all_gather | solution.py:1058
  198.3 8.1 %partial_blocks.9 = (bf16[2,640,512]{2,1,0:T(8,128)(2,1)}, bf16[2,640,512]{2,1,0:T(8,128)(2,1)}) custom-call(s32[1]{0:T(128)} %bitcast.row, bf16[1280,1024]{1,0:T(8,128)(2,1)} %get-tuple-element.158.refs_0_.refs_1_, bf16[2048,1024]{1,0:T(8,128)(2,1)} %all-gather.9.cloned.1.call-done.refs_1_.weight), custom_call_target="tpu_custom_call" | custom-call | flops 2684354560 | bytes 12058624 | tf_op jit(solution)/shard_map/partial_blocks/pallas_call | solution.py:930
  209.3 8.5 %partial_blocks.8 = (bf16[2,640,512]{2,1,0:T(8,128)(2,1)}, f32[2,640,512]{2,1,0:T(8,128)}) custom-call(s32[1]{0:T(128)} %bitcast.row, bf16[1280,1024]{1,0:T(8,128)(2,1)} %get-tuple-element.158.refs_0_.refs_1_, bf16[2048,1024]{1,0:T(8,128)(2,1)} %all-gather.9.cloned.1.call-done.refs_1_.weight), custom_call_target="tpu_custom_call" | custom-call | flops 2684354560 | bytes 12058624 | tf_op jit(solution)/shard_map/partial_blocks/pallas_call | solution.py:930
  217.8 19.7 %collective-permute-done.11 = bf16[2,640,512]{2,1,0:T(8,128)(2,1)S(1)} collective-permute-done((bf16[2,640,512]{2,1,0:T(8,128)(2,1)}, bf16[2,640,512]{2,1,0:T(8,128)(2,1)S(1)}, u32[]{:S(2)}, u32[]{:S(2)}) %collective-permute-start.11) | collective-permute-done | bytes 1310752 | tf_op jit(solution)/shard_map/ppermute | solution.py:950
  243.2 13.6 %collective-permute-done.12 = bf16[640,512]{1,0:T(8,128)(2,1)S(1)} collective-permute-done((bf16[640,512]{1,0:T(8,128)(2,1)S(1)}, bf16[640,512]{1,0:T(8,128)(2,1)S(1)}, u32[]{:S(2)}, u32[]{:S(2)}) %collective-permute-start.12) | collective-permute-done | bytes 655392 | tf_op jit(solution)/shard_map/ppermute | solution.py:950
  262.7 27.1 %collective-permute-done.16.refs_2_ = bf16[1280,512]{1,0:T(8,128)(2,1)S(1)} collective-permute-done((bf16[1280,512]{1,0:T(8,128)(2,1)S(1)}, bf16[1280,512]{1,0:T(8,128)(2,1)S(1)}, u32[]{:S(2)}, u32[]{:S(2)}) %collective-permute-start.16) | collective-permute-done | bytes 1310752 | tf_op jit(solution)/shard_map/ppermute | solution.py:950
  294.8 5.3 join.2.values.refs_0_
  300.1 9.9 %matmul.1.refs_9_ = bf16[1280,1024]{1,0:T(8,128)(2,1)} custom-call(bf16[1280,2048]{1,0:T(8,128)(2,1)} %join.2.values.refs_0_, bf16[2048,2048]{1,0:T(8,128)(2,1)} %all-gather.11.cloned.1.call-done.weight.refs_7_.refs_1_), custom_call_target="tpu_custom_call" | custom-call | flops 5368709120 | bytes 9437184 | tf_op jit(solution)/shard_map/matmul/pallas_call | solution.py:583
  310.0 19.3 %feed_up.1 = (bf16[1280,2048]{1,0:T(8,128)(2,1)}, f32[1280,128]{1,0:T(8,128)}, f32[1280,128]{1,0:T(8,128)}, bf16[1280,1024]{1,0:T(8,128)(2,1)}, bf16[1280,1024]{...) custom-call(s32[1]{0:T(128)} %bitcast.row, bf16[1280,512]{1,0:T(8,128)(2,1)} %copy-done.36, ...), custom_call_target="tpu_custom_call" | custom-call | flops 5368709120 | bytes 25165824 | tf_op jit(solution)/shard_map/feed_up/pallas_call | solution.py:849
  329.3 8.1 %partial_blocks.11 = (bf16[2,640,512]{2,1,0:T(8,128)(2,1)}, bf16[2,640,512]{2,1,0:T(8,128)(2,1)}) custom-call(s32[1]{0:T(128)} %bitcast.row, bf16[1280,1024]{1,0:T(8,128)(2,1)} %get-tuple-element.179.refs_0_.refs_3_, bf16[2048,2048]{1,0:T(8,128)(2,1)} %all-gather.11.cloned.1.call-done.weight.refs_7_.refs_1_), custom_call_target="tpu_custom_call" | custom-call | flops 2684354560 | bytes 12058624 | tf_op jit(solution)/shard_map/partial_blocks/pallas_call | solution.py:930
  338.7 8.3 %partial_blocks.10 = (bf16[2,640,512]{2,1,0:T(8,128)(2,1)}, f32[2,640,512]{2,1,0:T(8,128)}) custom-call(s32[1]{0:T(128)} %bitcast.row, bf16[1280,1024]{1,0:T(8,128)(2,1)} %get-tuple-element.179.refs_0_.refs_3_, bf16[2048,2048]{1,0:T(8,128)(2,1)} %all-gather.11.cloned.1.call-done.weight.refs_7_.refs_1_), custom_call_target="tpu_custom_call" | custom-call | flops 2684354560 | bytes 12058624 | tf_op jit(solution)/shard_map/partial_blocks/pallas_call | solution.py:930
  347.1 18.6 %weight_grads.1 = bf16[2048,2048]{1,0:T(8,128)(2,1)} custom-call(bf16[1280,2048]{1,0:T(8,128)(2,1)} %join.2.values.refs_0_, bf16[1280,2048]{1,0:T(8,128)(2,1)} %get-tuple-element.190.refs_1_, bf16[1280,1024]{1,0:T(8,128)(2,1)} %get-tuple-element.191.refs_2_.refs_0_, bf16[1280,1024]{1,0:T(8,128)(2,1)} %get-tuple-element.179.refs_0_.refs_3_), custom_call_target="tpu_custom_call" | custom-call | flops 10737418240 | bytes 18874368 | tf_op jit(solution)/shard_map/weight_grads/pallas_call | solution.py:641
  367.1 2.2 collective-permute-start.25
  381.6 8.1 %collective-permute-done.21 = bf16[640,512]{1,0:T(8,128)(2,1)S(1)} collective-permute-done((bf16[640,512]{1,0:T(8,128)(2,1)S(1)}, bf16[640,512]{1,0:T(8,128)(2,1)S(1)}, u32[]{:S(2)}, u32[]{:S(2)}) %collective-permute-start.21) | collective-permute-done | bytes 655392 | tf_op jit(solution)/shard_map/ppermute | solution.py:950
  392.7 3.7 fusion.35
  398.9 8.1 %partial_blocks.12 = (bf16[2,640,512]{2,1,0:T(8,128)(2,1)}, bf16[2,640,512]{2,1,0:T(8,128)(2,1)}) custom-call(s32[1]{0:T(128)} %bitcast.row, bf16[1280,1024]{1,0:T(8,128)(2,1)} %get-tuple-element.191.refs_2_.refs_0_, bf16[2048,2048]{1,0:T(8,128)(2,1)} %all-gather.11.cloned.1.call-done.weight.refs_7_.refs_1_), custom_call_target="tpu_custom_call" | custom-call | flops 2684354560 | bytes 12058624 | tf_op jit(solution)/shard_map/partial_blocks/pallas_call | solution.py:930
  407.0 8.5 %partial_blocks.13 = (bf16[2,640,512]{2,1,0:T(8,128)(2,1)}, f32[2,640,512]{2,1,0:T(8,128)}) custom-call(s32[1]{0:T(128)} %bitcast.row, bf16[1280,1024]{1,0:T(8,128)(2,1)} %get-tuple-element.191.refs_2_.refs_0_, bf16[2048,2048]{1,0:T(8,128)(2,1)} %all-gather.11.cloned.1.call-done.weight.refs_7_.refs_1_), custom_call_target="tpu_custom_call" | custom-call | flops 2684354560 | bytes 12058624 | tf_op jit(solution)/shard_map/partial_blocks/pallas_call | solution.py:930
  415.5 5.2 collective-permute-done.27.from_y
  420.8 3.2 collective-permute-done.26.from_x
  429.2 7.7 %collective-permute-done.29.far_b = bf16[640,512]{1,0:T(8,128)(2,1)S(1)} collective-permute-done((bf16[640,512]{1,0:T(8,128)(2,1)S(1)}, bf16[640,512]{1,0:T(8,128)(2,1)S(1)}, u32[]{:S(2)}, u32[]{:S(2)}) %collective-permute-start.29) | collective-permute-done | bytes 655392 | tf_op jit(solution)/shard_map/ppermute | solution.py:950
  438.8 5.2 join.3.refs_0_.wide
  444.0 12.2 %paired_grads.2 = bf16[4,256,1024]{2,1,0:T(8,128)(2,1)} custom-call(bf16[1280,2048]{1,0:T(8,128)(2,1)} %join.3.refs_0_.wide, bf16[1280,1024]{1,0:T(8,128)(2,1)} %get-tuple-element.158.refs_0_.refs_1_), custom_call_target="tpu_custom_call" | custom-call | flops 5368709120 | bytes 14680064 | tf_op jit(solution)/shard_map/paired_grads/pallas_call | solution.py:732
  456.2 16.3 %reduce-scatter.5.cloned.1.call-done = bf16[256,2048]{1,0:T(8,128)(2,1)} async-done(((bf16[2048,2048]{1,0:T(8,128)(2,1)}), bf16[256,2048]{1,0:T(8,128)(2,1)}) %reduce-scatter.5.cloned.1.call-update) | async-done | bytes 1048592 | tf_op jit(solution)/shard_map/reduce_scatter | solution.py:1063
  475.6 21.1 %gate_backward.1 = (bf16[1280,1024]{1,0:T(8,128)(2,1)}, bf16[1280,1024]{1,0:T(8,128)(2,1)}, f32[1,1024]{1,0:T(1,128)}, f32[1,1024]{1,0:T(1,128)}, bf16[8,2,256,5...) custom-call(s32[22]{0:T(128)} %pad_add_fusion.meta, f32[2]{0:T(128)} %subtract_log_fusion.rates, ...), custom_call_target="tpu_custom_call" | custom-call | flops 6039797760 | bytes 31457280 | tf_op jit(solution)/shard_map/gate_backward/pallas_call | solution.py:300
  496.7 4.6 collective-permute-done.30
  507.5 40.2 %return_states.1 = (bf16[2,256,512]{2,1,0:T(8,128)(2,1)S(1)}, bf16[2,256,512]{2,1,0:T(8,128)(2,1)S(1)}, bf16[2,256,512]{2,1,0:T(8,128)(2,1)S(1)}, bf16[2048,1024]{1,0:T(8,128)(2,1)S(1)}) custom-call(s32[22]{0:T(128)S(1)} %copy-done.6, f32[2]{0:T(128)S(1)} %copy-done.8, bf16[8,2,256,512]{3,2,1,0:T(8,128)(2,1)S(1)} %copy-done.1, ...), custom_call_target="tpu_custom_call" | custom-call | bytes 104857600 | tf_op jit(solution)/shard_map/return_states/pallas_call | solution.py:1343
  552.2 14.4 %retention_backward.1 = (bf16[1280,512]{1,0:T(8,128)(2,1)}, bf16[1280,512]{1,0:T(8,128)(2,1)}, bf16[1280,1024]{1,0:T(8,128)(2,1)}) custom-call(s32[22]{0:T(128)} %pad_add_fusion.meta, f32[2]{0:T(128)} %subtract_log_fusion.rates, bf16[1280,512]{1,0:T(8,128)(2,1)} %get-tuple-element.147.query, bf16[1280,512]{1,0:T(8,128)(2,1)} %get-tuple-element.148.key, ...), custom_call_target="tpu_custom_call" | custom-call | flops 5033164800 | bytes 15728640 | tf_op jit(solution)/shard_map/retention_backward/pallas_call | solution.py:395
  566.5 15.1 %partial_blocks.15 = (bf16[2,640,512]{2,1,0:T(8,128)(2,1)}, bf16[2,640,512]{2,1,0:T(8,128)(2,1)}) custom-call(s32[1]{0:T(128)} %bitcast.row, bf16[1280,512]{1,0:T(8,128)(2,1)} %get-tuple-element.235.refs_0_.refs_3_, bf16[1280,512]{1,0:T(8,128)(2,1)} %get-tuple-element.236.refs_1_.refs_4_, bf16[1280,1024]{1,0:T(8,128)(2,1)} %get-tuple-element.248.refs_2_.refs_5_, ...), custom_call_target="tpu_custom_call" | custom-call | flops 8053063680 | bytes 25690112 | tf_op jit(solution)/shard_map/partial_blocks/pallas_call | solution.py:930
  583.8 26.8 %paired_grads.3 = bf16[4,256,2048]{2,1,0:T(8,128)(2,1)} custom-call(bf16[1280,2048]{1,0:T(8,128)(2,1)} %get-tuple-element.142.values.wide.left.refs_0_.refs_1_.refs_2_, bf16[1280,2048]{1,0:T(8,128)(2,1)} %get-tuple-element.142.values.wide.left.refs_0_.refs_1_.refs_2_, bf16[1280,2048]{1,0:T(8,128)(2,1)} %get-tuple-element.142.values.wide.left.refs_0_.refs_1_.refs_2_, ...), custom_call_target="tpu_custom_call" | custom-call | flops 10737418240 | bytes 18874368 | tf_op jit(solution)/shard_map/paired_grads/pallas_call | solution.py:732
  613.8 2.8 fusion.18
  620.9 2.5 copy.88
  623.4 15.3 %partial_blocks.14 = (bf16[2,640,512]{2,1,0:T(8,128)(2,1)}, f32[2,640,512]{2,1,0:T(8,128)}) custom-call(s32[1]{0:T(128)} %bitcast.row, bf16[1280,512]{1,0:T(8,128)(2,1)} %get-tuple-element.235.refs_0_.refs_3_, bf16[1280,512]{1,0:T(8,128)(2,1)} %get-tuple-element.236.refs_1_.refs_4_, bf16[1280,1024]{1,0:T(8,128)(2,1)} %get-tuple-element.248.refs_2_.refs_5_, ...), custom_call_target="tpu_custom_call" | custom-call | flops 8053063680 | bytes 25690112 | tf_op jit(solution)/shard_map/partial_blocks/pallas_call | solution.py:930
  645.4 5.3 fusion.9
  650.7 5.7 collective-permute-done.36
  665.6 2.5 copy.87
  677.1 4.0 collective-permute-start.42
  685.7 3.9 fusion.7
  (310 shorter events, 140.3 us)
Async XLA Ops:
  7.2 87.8 %all-gather.5.cloned.1.call-start = ((), (), s32[]{:S(2)}) async-start(), calls=%async_computation.4 | async-start | bytes 9437184 | tf_op jit(solution)/shard_map/all_gather | solution.py:1058
  9.5 141.4 %all-gather.7.cloned.1.call-start = ((), (), s32[]{:S(2)}) async-start(), calls=%async_computation.5 | async-start | bytes 4718592 | tf_op jit(solution)/shard_map/all_gather | solution.py:1058
  10.3 187.9 %all-gather.9.cloned.1.call-start = ((), (), s32[]{:S(2)}) async-start(), calls=%async_computation.6 | async-start | bytes 4718592 | tf_op jit(solution)/shard_map/all_gather | solution.py:1058
  11.6 288.5 %all-gather.11.cloned.1.call-start = ((), (), s32[]{:S(2)}) async-start(), calls=%async_computation.7 | async-start | bytes 9437184 | tf_op jit(solution)/shard_map/all_gather | solution.py:1058
  13.0 459.5 %reduce-scatter.5.cloned.1.call-start = ((), (), s32[]{:S(2)}) async-start(), calls=%async_computation.8 | async-start | bytes 9437184 | tf_op jit(solution)/shard_map/reduce_scatter | solution.py:1063
  13.1 10.3 %collective-permute-start.5 = (f32[4,512]{1,0:T(4,128)S(1)}, f32[4,512]{1,0:T(4,128)S(1)}, u32[]{:S(2)}, u32[]{:S(2)}) collective-permute-start(f32[4,512]{1,0:T(4,128)S(1)} %get-tuple-element.420), channel_id=1, source_target_pairs={{0,16},{16,0},{8,24},{24,8},{1,17},{17,1},{9,25},{25,9},{2,18},{18... | collective-permute-start | bytes 24584 | tf_op jit(solution)/shard_map/ppermute | solution.py:950
  16.2 7.3 %collective-permute-start.4 = (f32[4,512]{1,0:T(4,128)S(1)}, f32[4,512]{1,0:T(4,128)S(1)}, u32[]{:S(2)}, u32[]{:S(2)}) collective-permute-start(f32[4,512]{1,0:T(4,128)S(1)} %get-tuple-element.420), channel_id=1, source_target_pairs={{0,8},{8,0},{16,24},{24,16},{1,9},{9,1},{17,25},{25,17},{2,10},{10... | collective-permute-start | bytes 24584 | tf_op jit(solution)/shard_map/ppermute | solution.py:950
  17.7 30.2 %collective-permute-start = (bf16[1280,512]{1,0:T(8,128)(2,1)S(1)}, bf16[1280,512]{1,0:T(8,128)(2,1)}, u32[]{:S(2)}, u32[]{:S(2)}) collective-permute-start(bf16[1280,512]{1,0:T(8,128)(2,1)S(1)} %copy-done.14), channel_id=1, source_target_pairs={{0,8},{8,0},{16,24},{24,16},{1,9},{9,1},{17,25},{25,17},{2,10},{10... | collective-permute-start | bytes 3932168 | tf_op jit(solution)/shard_map/ppermute | solution.py:950
  19.6 31.1 %collective-permute-start.1 = (bf16[1280,512]{1,0:T(8,128)(2,1)S(1)}, bf16[1280,512]{1,0:T(8,128)(2,1)}, u32[]{:S(2)}, u32[]{:S(2)}) collective-permute-start(bf16[1280,512]{1,0:T(8,128)(2,1)S(1)} %copy-done.14), channel_id=1, source_target_pairs={{0,16},{16,0},{8,24},{24,8},{1,17},{17,1},{9,25},{25,9},{2,18},{18... | collective-permute-start | bytes 3932168 | tf_op jit(solution)/shard_map/ppermute | solution.py:950
  49.1 15.2 %collective-permute-start.2 = (bf16[640,512]{1,0:T(8,128)(2,1)S(1)}, bf16[640,512]{1,0:T(8,128)(2,1)S(1)}, u32[]{:S(2)}, u32[]{:S(2)}) collective-permute-start(bf16[640,512]{1,0:T(8,128)(2,1)S(1)} %slice.269), channel_id=1, source_target_pairs={{0,16},{16,0},{8,24},{24,8},{1,17},{17,1},{9,25},{25,9},{2,18},{18... | collective-permute-start | bytes 1966088 | tf_op jit(solution)/shard_map/ppermute | solution.py:950
  51.9 14.6 %collective-permute-start.3 = (bf16[640,512]{1,0:T(8,128)(2,1)S(1)}, bf16[640,512]{1,0:T(8,128)(2,1)S(1)}, u32[]{:S(2)}, u32[]{:S(2)}) collective-permute-start(bf16[640,512]{1,0:T(8,128)(2,1)S(1)} %slice.270), channel_id=1, source_target_pairs={{0,8},{8,0},{16,24},{24,16},{1,9},{9,1},{17,25},{25,17},{2,10},{10... | collective-permute-start | bytes 1966088 | tf_op jit(solution)/shard_map/ppermute | solution.py:950
  74.8 41.5 %collective-permute-start.8 = (bf16[1280,512]{1,0:T(8,128)(2,1)S(1)}, bf16[1280,512]{1,0:T(8,128)(2,1)S(1)}, u32[]{:S(2)}, u32[]{:S(2)}) collective-permute-start(bf16[1280,512]{1,0:T(8,128)(2,1)S(1)} %multiply_convert_fusion.own), channel_id=1, source_target_pairs={{0,16},{16,0},{8,24},{24,8},{1,17},{17,1},{9,25},{25,9},{2,18},{18... | collective-permute-start | bytes 3932168 | tf_op jit(solution)/shard_map/ppermute | solution.py:950
  75.6 40.7 %collective-permute-start.7 = (bf16[1280,512]{1,0:T(8,128)(2,1)S(1)}, bf16[1280,512]{1,0:T(8,128)(2,1)}, u32[]{:S(2)}, u32[]{:S(2)}) collective-permute-start(bf16[1280,512]{1,0:T(8,128)(2,1)S(1)} %multiply_convert_fusion.own), channel_id=1, source_target_pairs={{0,8},{8,0},{16,24},{24,16},{1,9},{9,1},{17,25},{25,17},{2,10},{10... | collective-permute-start | bytes 3932168 | tf_op jit(solution)/shard_map/ppermute | solution.py:950
  119.7 31.2 %collective-permute-start.10 = (bf16[640,512]{1,0:T(8,128)(2,1)S(1)}, bf16[640,512]{1,0:T(8,128)(2,1)S(1)}, u32[]{:S(2)}, u32[]{:S(2)}) collective-permute-start(bf16[640,512]{1,0:T(8,128)(2,1)S(1)} %slice.210), channel_id=1, source_target_pairs={{0,8},{8,0},{16,24},{24,16},{1,9},{9,1},{17,25},{25,17},{2,10},{10... | collective-permute-start | bytes 1966088 | tf_op jit(solution)/shard_map/ppermute | solution.py:950
  121.3 29.6 %collective-permute-start.9 = (bf16[640,512]{1,0:T(8,128)(2,1)S(1)}, bf16[640,512]{1,0:T(8,128)(2,1)S(1)}, u32[]{:S(2)}, u32[]{:S(2)}) collective-permute-start(bf16[640,512]{1,0:T(8,128)(2,1)S(1)} %slice.209), channel_id=1, source_target_pairs={{0,16},{16,0},{8,24},{24,8},{1,17},{17,1},{9,25},{25,9},{2,18},{18... | collective-permute-start | bytes 1966088 | tf_op jit(solution)/shard_map/ppermute | solution.py:950
  206.4 31.2 %collective-permute-start.11 = (bf16[2,640,512]{2,1,0:T(8,128)(2,1)}, bf16[2,640,512]{2,1,0:T(8,128)(2,1)S(1)}, u32[]{:S(2)}, u32[]{:S(2)}) collective-permute-start(bf16[2,640,512]{2,1,0:T(8,128)(2,1)} %get-tuple-element.160), channel_id=1, source_target_pairs={{0,8},{8,0},{16,24},{24,16},{1,9},{9,1},{17,25},{25,17},{2,10},{10... | collective-permute-start | bytes 3932168 | tf_op jit(solution)/shard_map/ppermute | solution.py:950
  207.8 30.9 %collective-permute-start.13 = (bf16[2,640,512]{2,1,0:T(8,128)(2,1)}, bf16[2,640,512]{2,1,0:T(8,128)(2,1)S(1)}, u32[]{:S(2)}, u32[]{:S(2)}) collective-permute-start(bf16[2,640,512]{2,1,0:T(8,128)(2,1)} %get-tuple-element.162), channel_id=1, source_target_pairs={{0,16},{16,0},{8,24},{24,8},{1,17},{17,1},{9,25},{25,9},{2,18},{18... | collective-permute-start | bytes 3932168 | tf_op jit(solution)/shard_map/ppermute | solution.py:950
  240.9 15.9 %collective-permute-start.12 = (bf16[640,512]{1,0:T(8,128)(2,1)S(1)}, bf16[640,512]{1,0:T(8,128)(2,1)S(1)}, u32[]{:S(2)}, u32[]{:S(2)}) collective-permute-start(bf16[640,512]{1,0:T(8,128)(2,1)S(1)} %get-tuple-element.393), channel_id=1, source_target_pairs={{0,16},{16,0},{8,24},{24,8},{1,17},{17,1},{9,25},{25,9},{2,18},{18... | collective-permute-start | bytes 1966088 | tf_op jit(solution)/shard_map/ppermute | solution.py:950
  242.4 15.6 %collective-permute-start.14 = (bf16[640,512]{1,0:T(8,128)(2,1)S(1)}, bf16[640,512]{1,0:T(8,128)(2,1)S(1)}, u32[]{:S(2)}, u32[]{:S(2)}) collective-permute-start(bf16[640,512]{1,0:T(8,128)(2,1)S(1)} %get-tuple-element.394), channel_id=1, source_target_pairs={{0,8},{8,0},{16,24},{24,16},{1,9},{9,1},{17,25},{25,17},{2,10},{10... | collective-permute-start | bytes 1966088 | tf_op jit(solution)/shard_map/ppermute | solution.py:950
  261.1 28.8 %collective-permute-start.16 = (bf16[1280,512]{1,0:T(8,128)(2,1)S(1)}, bf16[1280,512]{1,0:T(8,128)(2,1)S(1)}, u32[]{:S(2)}, u32[]{:S(2)}) collective-permute-start(bf16[1280,512]{1,0:T(8,128)(2,1)S(1)} %fusion.30.refs_0_), channel_id=1, source_target_pairs={{0,16},{16,0},{8,24},{24,8},{1,17},{17,1},{9,25},{25,9},{2,18},{18... | collective-permute-start | bytes 3932168 | tf_op jit(solution)/shard_map/ppermute | solution.py:950
  261.6 28.5 %collective-permute-start.15 = (bf16[1280,512]{1,0:T(8,128)(2,1)S(1)}, bf16[1280,512]{1,0:T(8,128)(2,1)S(1)}, u32[]{:S(2)}, u32[]{:S(2)}) collective-permute-start(bf16[1280,512]{1,0:T(8,128)(2,1)S(1)} %fusion.30.refs_0_), channel_id=1, source_target_pairs={{0,8},{8,0},{16,24},{24,16},{1,9},{9,1},{17,25},{25,17},{2,10},{10... | collective-permute-start | bytes 3932168 | tf_op jit(solution)/shard_map/ppermute | solution.py:950
  291.3 18.7 %collective-permute-start.18 = (bf16[640,512]{1,0:T(8,128)(2,1)}, bf16[640,512]{1,0:T(8,128)(2,1)}, u32[]{:S(2)}, u32[]{:S(2)}) collective-permute-start(bf16[640,512]{1,0:T(8,128)(2,1)} %slice.220), channel_id=1, source_target_pairs={{0,8},{8,0},{16,24},{24,16},{1,9},{9,1},{17,25},{25,17},{2,10},{10... | collective-permute-start | bytes 1966088 | tf_op jit(solution)/shard_map/ppermute | solution.py:950
  292.7 17.3 %collective-permute-start.17 = (bf16[640,512]{1,0:T(8,128)(2,1)S(1)}, bf16[640,512]{1,0:T(8,128)(2,1)}, u32[]{:S(2)}, u32[]{:S(2)}) collective-permute-start(bf16[640,512]{1,0:T(8,128)(2,1)S(1)} %slice.219), channel_id=1, source_target_pairs={{0,16},{16,0},{8,24},{24,8},{1,17},{17,1},{9,25},{25,9},{2,18},{18... | collective-permute-start | bytes 1966088 | tf_op jit(solution)/shard_map/ppermute | solution.py:950
  337.4 28.2 %collective-permute-start.19 = (bf16[2,640,512]{2,1,0:T(8,128)(2,1)}, bf16[2,640,512]{2,1,0:T(8,128)(2,1)}, u32[]{:S(2)}, u32[]{:S(2)}) collective-permute-start(bf16[2,640,512]{2,1,0:T(8,128)(2,1)} %get-tuple-element.187), channel_id=1, source_target_pairs={{0,8},{8,0},{16,24},{24,16},{1,9},{9,1},{17,25},{25,17},{2,10},{10... | collective-permute-start | bytes 3932168 | tf_op jit(solution)/shard_map/ppermute | solution.py:950
  338.1 27.6 %collective-permute-start.20 = (bf16[2,640,512]{2,1,0:T(8,128)(2,1)}, bf16[2,640,512]{2,1,0:T(8,128)(2,1)}, u32[]{:S(2)}, u32[]{:S(2)}) collective-permute-start(bf16[2,640,512]{2,1,0:T(8,128)(2,1)} %get-tuple-element.188), channel_id=1, source_target_pairs={{0,16},{16,0},{8,24},{24,8},{1,17},{17,1},{9,25},{25,9},{2,18},{18... | collective-permute-start | bytes 3932168 | tf_op jit(solution)/shard_map/ppermute | solution.py:950
  365.7 186.4 %reduce-scatter.7.cloned.1.call-start = ((), (), s32[]{:S(2)}) async-start(), calls=%async_computation.9 | async-start | bytes 2621440 | tf_op jit(solution)/shard_map/reduce_scatter | solution.py:1065
  367.1 8.0 %collective-permute-start.25 = (f32[2,1280]{1,0:T(2,128)S(1)}, f32[2,1280]{1,0:T(2,128)S(1)}, u32[]{:S(2)}, u32[]{:S(2)}) collective-permute-start(f32[2,1280]{1,0:T(2,128)S(1)} %copy.77), channel_id=1, source_target_pairs={{0,24},{24,0},{8,16},{16,8},{1,25},{25,1},{9,17},{17,9},{2,26},{26... | collective-permute-start | bytes 30728 | tf_op jit(solution)/shard_map/ppermute | solution.py:950
  378.4 11.4 %collective-permute-start.21 = (bf16[640,512]{1,0:T(8,128)(2,1)S(1)}, bf16[640,512]{1,0:T(8,128)(2,1)S(1)}, u32[]{:S(2)}, u32[]{:S(2)}) collective-permute-start(bf16[640,512]{1,0:T(8,128)(2,1)S(1)} %get-tuple-element.391), channel_id=1, source_target_pairs={{0,16},{16,0},{8,24},{24,8},{1,17},{17,1},{9,25},{25,9},{2,18},{18... | collective-permute-start | bytes 1966088 | tf_op jit(solution)/shard_map/ppermute | solution.py:950
  379.8 10.9 %collective-permute-start.22 = (bf16[640,512]{1,0:T(8,128)(2,1)S(1)}, bf16[640,512]{1,0:T(8,128)(2,1)S(1)}, u32[]{:S(2)}, u32[]{:S(2)}) collective-permute-start(bf16[640,512]{1,0:T(8,128)(2,1)S(1)} %get-tuple-element.392), channel_id=1, source_target_pairs={{0,8},{8,0},{16,24},{24,16},{1,9},{9,1},{17,25},{25,17},{2,10},{10... | collective-permute-start | bytes 1966088 | tf_op jit(solution)/shard_map/ppermute | solution.py:950
  396.4 24.4 %collective-permute-start.27 = (bf16[1280,512]{1,0:T(8,128)(2,1)}, bf16[1280,512]{1,0:T(8,128)(2,1)}, u32[]{:S(2)}, u32[]{:S(2)}) collective-permute-start(bf16[1280,512]{1,0:T(8,128)(2,1)} %get-tuple-element.373.own), channel_id=1, source_target_pairs={{0,16},{16,0},{8,24},{24,8},{1,17},{17,1},{9,25},{25,9},{2,18},{18... | collective-permute-start | bytes 3932168 | tf_op jit(solution)/shard_map/ppermute | solution.py:950
  397.2 26.8 %collective-permute-start.26 = (bf16[1280,512]{1,0:T(8,128)(2,1)}, bf16[1280,512]{1,0:T(8,128)(2,1)}, u32[]{:S(2)}, u32[]{:S(2)}) collective-permute-start(bf16[1280,512]{1,0:T(8,128)(2,1)} %get-tuple-element.373.own), channel_id=1, source_target_pairs={{0,8},{8,0},{16,24},{24,16},{1,9},{9,1},{17,25},{25,17},{2,10},{10... | collective-permute-start | bytes 3932168 | tf_op jit(solution)/shard_map/ppermute | solution.py:950
  426.3 10.7 %collective-permute-start.29 = (bf16[640,512]{1,0:T(8,128)(2,1)S(1)}, bf16[640,512]{1,0:T(8,128)(2,1)S(1)}, u32[]{:S(2)}, u32[]{:S(2)}) collective-permute-start(bf16[640,512]{1,0:T(8,128)(2,1)S(1)} %slice.242), channel_id=1, source_target_pairs={{0,8},{8,0},{16,24},{24,16},{1,9},{9,1},{17,25},{25,17},{2,10},{10... | collective-permute-start | bytes 1966088 | tf_op jit(solution)/shard_map/ppermute | solution.py:950
  428.1 10.7 %collective-permute-start.28 = (bf16[640,512]{1,0:T(8,128)(2,1)S(1)}, bf16[640,512]{1,0:T(8,128)(2,1)}, u32[]{:S(2)}, u32[]{:S(2)}) collective-permute-start(bf16[640,512]{1,0:T(8,128)(2,1)S(1)} %slice.241), channel_id=1, source_target_pairs={{0,16},{16,0},{8,24},{24,8},{1,17},{17,1},{9,25},{25,9},{2,18},{18... | collective-permute-start | bytes 1966088 | tf_op jit(solution)/shard_map/ppermute | solution.py:950
  472.5 138.2 %reduce-scatter.9.cloned.1.call-start = ((), (), s32[]{:S(2)}) async-start(), calls=%async_computation.10 | async-start | bytes 4718592 | tf_op jit(solution)/shard_map/reduce_scatter | solution.py:1063
  472.5 28.8 %collective-permute-start.30 = (bf16[2,640,512]{2,1,0:T(8,128)(2,1)}, bf16[2,640,512]{2,1,0:T(8,128)(2,1)}, u32[]{:S(2)}, u32[]{:S(2)}) collective-permute-start(bf16[2,640,512]{2,1,0:T(8,128)(2,1)} %get-tuple-element.206), channel_id=1, source_target_pairs={{0,8},{8,0},{16,24},{24,16},{1,9},{9,1},{17,25},{25,17},{2,10},{10... | collective-permute-start | bytes 3932168 | tf_op jit(solution)/shard_map/ppermute | solution.py:950
  474.1 28.4 %collective-permute-start.31 = (bf16[2,640,512]{2,1,0:T(8,128)(2,1)}, bf16[2,640,512]{2,1,0:T(8,128)(2,1)}, u32[]{:S(2)}, u32[]{:S(2)}) collective-permute-start(bf16[2,640,512]{2,1,0:T(8,128)(2,1)} %get-tuple-element.207), channel_id=1, source_target_pairs={{0,16},{16,0},{8,24},{24,8},{1,17},{17,1},{9,25},{25,9},{2,18},{18... | collective-permute-start | bytes 3932168 | tf_op jit(solution)/shard_map/ppermute | solution.py:950
  552.1 145.3 %reduce-scatter.11.cloned.1.call-start = ((), (), s32[]{:S(2)}) async-start(), calls=%async_computation.11 | async-start | bytes 5242880 | tf_op jit(solution)/shard_map/reduce_scatter | solution.py:1065
  581.6 29.1 %collective-permute-start.34 = (bf16[2,640,512]{2,1,0:T(8,128)(2,1)}, bf16[2,640,512]{2,1,0:T(8,128)(2,1)}, u32[]{:S(2)}, u32[]{:S(2)}) collective-permute-start(bf16[2,640,512]{2,1,0:T(8,128)(2,1)} %get-tuple-element.246), channel_id=1, source_target_pairs={{0,8},{8,0},{16,24},{24,16},{1,9},{9,1},{17,25},{25,17},{2,10},{10... | collective-permute-start | bytes 3932168 | tf_op jit(solution)/shard_map/ppermute | solution.py:950
  582.6 28.1 %collective-permute-start.35 = (bf16[2,640,512]{2,1,0:T(8,128)(2,1)}, bf16[2,640,512]{2,1,0:T(8,128)(2,1)}, u32[]{:S(2)}, u32[]{:S(2)}) collective-permute-start(bf16[2,640,512]{2,1,0:T(8,128)(2,1)} %get-tuple-element.247), channel_id=1, source_target_pairs={{0,16},{16,0},{8,24},{24,8},{1,17},{17,1},{9,25},{25,9},{2,18},{18... | collective-permute-start | bytes 3932168 | tf_op jit(solution)/shard_map/ppermute | solution.py:950
  616.6 22.1 %collective-permute-start.33 = (bf16[640,512]{1,0:T(8,128)(2,1)}, bf16[640,512]{1,0:T(8,128)(2,1)S(1)}, u32[]{:S(2)}, u32[]{:S(2)}) collective-permute-start(bf16[640,512]{1,0:T(8,128)(2,1)} %get-tuple-element.389), channel_id=1, source_target_pairs={{0,8},{8,0},{16,24},{24,16},{1,9},{9,1},{17,25},{25,17},{2,10},{10... | collective-permute-start | bytes 1966088 | tf_op jit(solution)/shard_map/ppermute | solution.py:950
  617.2 21.5 %collective-permute-start.32 = (bf16[640,512]{1,0:T(8,128)(2,1)}, bf16[640,512]{1,0:T(8,128)(2,1)}, u32[]{:S(2)}, u32[]{:S(2)}) collective-permute-start(bf16[640,512]{1,0:T(8,128)(2,1)} %get-tuple-element.390), channel_id=1, source_target_pairs={{0,16},{16,0},{8,24},{24,8},{1,17},{17,1},{9,25},{25,9},{2,18},{18... | collective-permute-start | bytes 1966088 | tf_op jit(solution)/shard_map/ppermute | solution.py:950
  640.9 15.5 %collective-permute-start.36 = (bf16[640,512]{1,0:T(8,128)(2,1)S(1)}, bf16[640,512]{1,0:T(8,128)(2,1)S(1)}, u32[]{:S(2)}, u32[]{:S(2)}) collective-permute-start(bf16[640,512]{1,0:T(8,128)(2,1)S(1)} %get-tuple-element.387), channel_id=1, source_target_pairs={{0,16},{16,0},{8,24},{24,8},{1,17},{17,1},{9,25},{25,9},{2,18},{18... | collective-permute-start | bytes 1966088 | tf_op jit(solution)/shard_map/ppermute | solution.py:950
  641.8 15.2 %collective-permute-start.37 = (bf16[640,512]{1,0:T(8,128)(2,1)S(1)}, bf16[640,512]{1,0:T(8,128)(2,1)S(1)}, u32[]{:S(2)}, u32[]{:S(2)}) collective-permute-start(bf16[640,512]{1,0:T(8,128)(2,1)S(1)} %get-tuple-element.388), channel_id=1, source_target_pairs={{0,8},{8,0},{16,24},{24,16},{1,9},{9,1},{17,25},{25,17},{2,10},{10... | collective-permute-start | bytes 1966088 | tf_op jit(solution)/shard_map/ppermute | solution.py:950
  660.9 11.4 %collective-permute-start.39 = (f32[2,1280]{1,0:T(2,128)S(1)}, f32[2,1280]{1,0:T(2,128)S(1)}, u32[]{:S(2)}, u32[]{:S(2)}) collective-permute-start(f32[2,1280]{1,0:T(2,128)S(1)} %pad_maximum_fusion.7), channel_id=1, source_target_pairs={{0,16},{16,0},{8,24},{24,8},{1,17},{17,1},{9,25},{25,9},{2,18},{18... | collective-permute-start | bytes 30728 | tf_op jit(solution)/shard_map/ppermute | solution.py:950
  662.8 9.2 %collective-permute-start.40 = (f32[2,1280]{1,0:T(2,128)S(1)}, f32[2,1280]{1,0:T(2,128)S(1)}, u32[]{:S(2)}, u32[]{:S(2)}) collective-permute-start(f32[2,1280]{1,0:T(2,128)S(1)} %pad_maximum_fusion.7), channel_id=1, source_target_pairs={{0,24},{24,0},{8,16},{16,8},{1,25},{25,1},{9,17},{17,9},{2,26},{26... | collective-permute-start | bytes 30728 | tf_op jit(solution)/shard_map/ppermute | solution.py:950
  663.9 12.8 %collective-permute-start.38 = (f32[2,1280]{1,0:T(2,128)S(1)}, f32[2,1280]{1,0:T(2,128)S(1)}, u32[]{:S(2)}, u32[]{:S(2)}) collective-permute-start(f32[2,1280]{1,0:T(2,128)S(1)} %pad_maximum_fusion.7), channel_id=1, source_target_pairs={{0,8},{8,0},{16,24},{24,16},{1,9},{9,1},{17,25},{25,17},{2,10},{10... | collective-permute-start | bytes 30728 | tf_op jit(solution)/shard_map/ppermute | solution.py:950
  670.2 6.9 collective-permute-start.41
  677.1 6.5 collective-permute-start.42
  (71 other events, 449.4 us)
Sparse Core Ops, SparseCore 0:
  10.2 84.7 all-gather.4
  96.6 52.1 all-gather.6
  150.9 47.2 all-gather.8
  200.3 86.4 all-gather.10
  365.8 106.6 reduce-scatter.4
  474.6 41.8 reduce-scatter.6
  552.2 56.3 reduce-scatter.8
  611.0 78.1 reduce-scatter.10

commit v7 on v6

--- a/solution.py
+++ b/solution.py
@@ -605,14 +605,7 @@
 
         @pl.when((tile >= first) & (tile < last))
         def _():
-            height = 2 * GRAD_TILE
-
-            def part(index, _):
-                spot = pl.ds(pl.multiple_of(index * height, height), height)
-                out[spot, :] = mm_tn(left[:, spot], right[...]).astype(BF16)
-                return 0
-
-            lax.fori_loop(0, left.shape[1] // height, part, 0)
+            out[...] = mm_tn(left[...], right[...]).astype(BF16)
 
 
 def weight_grads(pairs):
@@ -892,22 +885,14 @@
     values, weights = refs[:count], refs[count : 2 * count]
     outs = refs[2 * count :]
     step = pl.program_id(0)
-    strip = values[0].shape[0] // 2
-
-    def part(number, _):
-        spot = pl.ds(pl.multiple_of(number * strip, strip), strip)
-        total = mm_nt(values[0][spot, :], weights[0][...])
-        for x, w in zip(values[1:], weights[1:]):
-            total = total + mm_nt(x[spot, :], w[...])
-        for index, out in enumerate(outs):
-
-            @pl.when(step // 2 == index)
-            def _():
-                out[0, spot, :] = total.astype(out.dtype)
-
-        return 0
-
-    lax.fori_loop(0, 2, part, 0)
+    total = mm_nt(values[0][...], weights[0][...])
+    for x, w in zip(values[1:], weights[1:]):
+        total = total + mm_nt(x[...], w[...])
+    for index, out in enumerate(outs):
+
+        @pl.when(step // 2 == index)
+        def _():
+            out[0] = total.astype(out.dtype)
 
 
 def partial_blocks(values, weights, row, first, kinds):

time: 717 us -> 714 us (level)
  transfers between devices with their start and end apart: 55 -> 55, of which waited for: 26 -> 29; matrix products, arithmetic and copies ran while one was open for 11% -> 11% of each run, Pallas kernels for 43% -> 42%
where the time goes in v7:
time: 714 us; the launch traced here: 705 us
  Pallas kernels  323 us (45%)
  waiting for transfers between devices  203 us (28%)
  starting transfers between devices  62.4 us (9%)
  other arithmetic  50.7 us (7%)
  local copies, waits for them, and re-layouts  50.4 us (7%)
  between operations  16 us (2%)
    ppermute x44, waiting for transfers between devices, permute_row(): return lax.ppermute(value, 'row', pairs)  145 us
    pallas_call x8, Pallas kernels, partial_blocks(): pl.pallas_call(functools.partial(partial_kernel, count), grid_spec=pltpu....  75.4 us
    ppermute x44, starting transfers between devices, permute_row(): return lax.ppermute(value, 'row', pairs)  54.6 us
    pallas_call x1, Pallas kernels, return_states(): pl.pallas_call(functools.partial(return_kernel, rows), in_specs=[smem(),...  40.2 us
    all_gather x4, waiting for transfers between devices, gather_col(): return lax.all_gather(weight, 'col', axis=0, tiled=True)  39.2 us
    pallas_call x2, Pallas kernels, paired_grads(): pl.pallas_call(functools.partial(paired_grad_kernel, tuple(spans), tiles,...  38.9 us
    pallas_call x1, Pallas kernels, share_states(): pl.pallas_call(functools.partial(share_kernel, rows), in_specs=[smem(), s...  25.3 us
    pallas_call x1, Pallas kernels, retain(): pl.pallas_call(functools.partial(retain_kernel, rows, chunks), grid=(head...  21.3 us
  transfers between devices with their start and end apart: 55, of which 29 were waited for; matrix products, arithmetic and copies ran while one was open for 11% of the time, Pallas kernels for 42%

profile of v7, /device:TPU:0, one launch (start us, length us, event | category | flops | bytes accessed | tf_op | source)
XLA Modules:
  0.0 705.3 jit_solution(16675616468754183680)
XLA Ops:
  7.2 2.3 pad_maximum_fusion.3
  13.1 3.0 collective-permute-start.5
  23.5 24.5 %collective-permute-done.from_x = bf16[1280,512]{1,0:T(8,128)(2,1)} collective-permute-done((bf16[1280,512]{1,0:T(8,128)(2,1)S(1)}, bf16[1280,512]{1,0:T(8,128)(2,1)}, u32[]{:S(2)}, u32[]{:S(2)}) %collective-permute-start) | collective-permute-done | bytes 1310752 | tf_op jit(solution)/shard_map/ppermute | solution.py:935
  54.1 10.2 %collective-permute-done.2.far_a = bf16[640,512]{1,0:T(8,128)(2,1)S(1)} collective-permute-done((bf16[640,512]{1,0:T(8,128)(2,1)S(1)}, bf16[640,512]{1,0:T(8,128)(2,1)S(1)}, u32[]{:S(2)}, u32[]{:S(2)}) %collective-permute-start.2) | collective-permute-done | bytes 655392 | tf_op jit(solution)/shard_map/ppermute | solution.py:935
  64.2 2.2 collective-permute-done.3.far_b
  67.3 7.5 %join_norm.1 = (bf16[1280,2048]{1,0:T(8,128)(2,1)}, f32[1280,128]{1,0:T(8,128)}, f32[1280,128]{1,0:T(8,128)}) custom-call(s32[1]{0:T(128)} %bitcast.row, bf16[1280,512]{1,0:T(8,128)(2,1)} %own.1, bf16[1280,512]{1,0:T(8,128)(2,1)} %collective-permute-done.from_x, bf16[1280,512]{1,0:T(8,128)(2,1)} %collective-permute-done.1.from_y, ...), custom_call_target="tpu_custom_call" | custom-call | flops 20971520 | bytes 10485760 | tf_op jit(solution)/shard_map/join_norm/pallas_call | solution.py:491
  77.0 3.7 multiply_sine_fusion
  81.9 13.1 %all-gather.5.cloned.1.call-done.weight.refs_4_.refs_5_.refs_6_ = bf16[2048,2048]{1,0:T(8,128)(2,1)} async-done(((bf16[256,2048]{1,0:T(8,128)(2,1)}), bf16[2048,2048]{1,0:T(8,128)(2,1)}) %all-gather.5.cloned.1.call-update) | async-done | bytes 8388624 | tf_op jit(solution)/shard_map/all_gather | solution.py:1043
  95.0 21.3 %project.1 = (bf16[1280,512]{1,0:T(8,128)(2,1)}, bf16[1280,512]{1,0:T(8,128)(2,1)}, bf16[1280,1024]{1,0:T(8,128)(2,1)}, bf16[3,2,256,512]{3,2,1,0:T(8,128)(2,1)}) custom-call(s32[22]{0:T(128)} %pad_add_fusion.meta, f32[2]{0:T(128)} %subtract_log_fusion.rates, bf16[1280,2048]{1,0:T(8,128)(2,1)} %get-tuple-element.142.values.wide.left.refs_0_.refs_1_.refs_2_, ...), custom_call_target="tpu_custom_call" | custom-call | flops 10737418240 | bytes 13631488 | tf_op jit(solution)/shard_map/project/pallas_call | solution.py:554
  122.8 25.3 %share_states.1 = (bf16[8,2,256,512]{3,2,1,0:T(8,128)(2,1)S(1)}, bf16[2,256,512]{2,1,0:T(8,128)(2,1)S(1)}) custom-call(s32[22]{0:T(128)S(1)} %copy-done.5, f32[2]{0:T(128)S(1)} %copy-done.7, bf16[3,2,256,512]{3,2,1,0:T(8,128)(2,1)S(1)} %copy-done.3), custom_call_target="tpu_custom_call" | custom-call | bytes 104857600 | tf_op jit(solution)/shard_map/share_states/pallas_call | solution.py:1199
  150.9 21.3 %retention_forward.1 = (f32[1280,1024]{1,0:T(8,128)}, bf16[1280,1024]{1,0:T(8,128)(2,1)}, bf16[1280,1024]{1,0:T(8,128)(2,1)}, f32[2,1280,128]{2,1,0:T(8,128)}, bf16[2,5,256,512]{3,2,1,0:T(8,128)(2,1)}) custom-call(s32[22]{0:T(128)} %pad_add_fusion.meta, f32[2]{0:T(128)} %subtract_log_fusion.rates, bf16[1280,512]{1,0:T(8,128)(2,1)} %get-tuple-element.147.query, ...), custom_call_target="tpu_custom_call" | custom-call | flops 7717519360 | bytes 20971520 | tf_op jit(solution)/shard_map/retention_forward/pallas_call | solution.py:203
  172.2 26.0 %all-gather.9.cloned.1.call-done.refs_1_.weight = bf16[2048,1024]{1,0:T(8,128)(2,1)} async-done(((bf16[256,1024]{1,0:T(8,128)(2,1)}), bf16[2048,1024]{1,0:T(8,128)(2,1)}) %all-gather.9.cloned.1.call-update) | async-done | bytes 4194320 | tf_op jit(solution)/shard_map/all_gather | solution.py:1043
  198.3 7.5 %partial_blocks.9 = (bf16[2,640,512]{2,1,0:T(8,128)(2,1)}, bf16[2,640,512]{2,1,0:T(8,128)(2,1)}) custom-call(s32[1]{0:T(128)} %bitcast.row, bf16[1280,1024]{1,0:T(8,128)(2,1)} %get-tuple-element.158.refs_0_.refs_1_, bf16[2048,1024]{1,0:T(8,128)(2,1)} %all-gather.9.cloned.1.call-done.refs_1_.weight), custom_call_target="tpu_custom_call" | custom-call | flops 2684354560 | bytes 12058624 | tf_op jit(solution)/shard_map/partial_blocks/pallas_call | solution.py:915
  208.7 8.0 %partial_blocks.8 = (bf16[2,640,512]{2,1,0:T(8,128)(2,1)}, f32[2,640,512]{2,1,0:T(8,128)}) custom-call(s32[1]{0:T(128)} %bitcast.row, bf16[1280,1024]{1,0:T(8,128)(2,1)} %get-tuple-element.158.refs_0_.refs_1_, bf16[2048,1024]{1,0:T(8,128)(2,1)} %all-gather.9.cloned.1.call-done.refs_1_.weight), custom_call_target="tpu_custom_call" | custom-call | flops 2684354560 | bytes 12058624 | tf_op jit(solution)/shard_map/partial_blocks/pallas_call | solution.py:915
  216.7 20.2 %collective-permute-done.11 = bf16[2,640,512]{2,1,0:T(8,128)(2,1)S(1)} collective-permute-done((bf16[2,640,512]{2,1,0:T(8,128)(2,1)}, bf16[2,640,512]{2,1,0:T(8,128)(2,1)S(1)}, u32[]{:S(2)}, u32[]{:S(2)}) %collective-permute-start.11) | collective-permute-done | bytes 1310752 | tf_op jit(solution)/shard_map/ppermute | solution.py:935
  242.6 13.6 %collective-permute-done.12 = bf16[640,512]{1,0:T(8,128)(2,1)S(1)} collective-permute-done((bf16[640,512]{1,0:T(8,128)(2,1)S(1)}, bf16[640,512]{1,0:T(8,128)(2,1)S(1)}, u32[]{:S(2)}, u32[]{:S(2)}) %collective-permute-start.12) | collective-permute-done | bytes 655392 | tf_op jit(solution)/shard_map/ppermute | solution.py:935
  262.1 27.1 %collective-permute-done.16.refs_2_ = bf16[1280,512]{1,0:T(8,128)(2,1)S(1)} collective-permute-done((bf16[1280,512]{1,0:T(8,128)(2,1)S(1)}, bf16[1280,512]{1,0:T(8,128)(2,1)S(1)}, u32[]{:S(2)}, u32[]{:S(2)}) %collective-permute-start.16) | collective-permute-done | bytes 1310752 | tf_op jit(solution)/shard_map/ppermute | solution.py:935
  294.1 5.3 join.2.values.refs_0_
  299.4 9.9 %matmul.1.refs_9_ = bf16[1280,1024]{1,0:T(8,128)(2,1)} custom-call(bf16[1280,2048]{1,0:T(8,128)(2,1)} %join.2.values.refs_0_, bf16[2048,2048]{1,0:T(8,128)(2,1)} %all-gather.11.cloned.1.call-done.weight.refs_7_.refs_1_), custom_call_target="tpu_custom_call" | custom-call | flops 5368709120 | bytes 9437184 | tf_op jit(solution)/shard_map/matmul/pallas_call | solution.py:583
  309.4 19.3 %feed_up.1 = (bf16[1280,2048]{1,0:T(8,128)(2,1)}, f32[1280,128]{1,0:T(8,128)}, f32[1280,128]{1,0:T(8,128)}, bf16[1280,1024]{1,0:T(8,128)(2,1)}, bf16[1280,1024]{...) custom-call(s32[1]{0:T(128)} %bitcast.row, bf16[1280,512]{1,0:T(8,128)(2,1)} %copy-done.36, ...), custom_call_target="tpu_custom_call" | custom-call | flops 5368709120 | bytes 25165824 | tf_op jit(solution)/shard_map/feed_up/pallas_call | solution.py:842
  328.7 7.5 %partial_blocks.11 = (bf16[2,640,512]{2,1,0:T(8,128)(2,1)}, bf16[2,640,512]{2,1,0:T(8,128)(2,1)}) custom-call(s32[1]{0:T(128)} %bitcast.row, bf16[1280,1024]{1,0:T(8,128)(2,1)} %get-tuple-element.179.refs_0_.refs_3_, bf16[2048,2048]{1,0:T(8,128)(2,1)} %all-gather.11.cloned.1.call-done.weight.refs_7_.refs_1_), custom_call_target="tpu_custom_call" | custom-call | flops 2684354560 | bytes 12058624 | tf_op jit(solution)/shard_map/partial_blocks/pallas_call | solution.py:915
  337.5 7.9 %partial_blocks.10 = (bf16[2,640,512]{2,1,0:T(8,128)(2,1)}, f32[2,640,512]{2,1,0:T(8,128)}) custom-call(s32[1]{0:T(128)} %bitcast.row, bf16[1280,1024]{1,0:T(8,128)(2,1)} %get-tuple-element.179.refs_0_.refs_3_, bf16[2048,2048]{1,0:T(8,128)(2,1)} %all-gather.11.cloned.1.call-done.weight.refs_7_.refs_1_), custom_call_target="tpu_custom_call" | custom-call | flops 2684354560 | bytes 12058624 | tf_op jit(solution)/shard_map/partial_blocks/pallas_call | solution.py:915
  345.5 17.3 %weight_grads.1 = bf16[2048,2048]{1,0:T(8,128)(2,1)} custom-call(bf16[1280,2048]{1,0:T(8,128)(2,1)} %join.2.values.refs_0_, bf16[1280,2048]{1,0:T(8,128)(2,1)} %get-tuple-element.190.refs_1_, bf16[1280,1024]{1,0:T(8,128)(2,1)} %get-tuple-element.191.refs_2_.refs_0_, bf16[1280,1024]{1,0:T(8,128)(2,1)} %get-tuple-element.179.refs_0_.refs_3_), custom_call_target="tpu_custom_call" | custom-call | flops 10737418240 | bytes 18874368 | tf_op jit(solution)/shard_map/weight_grads/pallas_call | solution.py:634
  379.6 8.2 %collective-permute-done.21 = bf16[640,512]{1,0:T(8,128)(2,1)S(1)} collective-permute-done((bf16[640,512]{1,0:T(8,128)(2,1)S(1)}, bf16[640,512]{1,0:T(8,128)(2,1)S(1)}, u32[]{:S(2)}, u32[]{:S(2)}) %collective-permute-start.21) | collective-permute-done | bytes 655392 | tf_op jit(solution)/shard_map/ppermute | solution.py:935
  390.5 4.0 fusion.35
  397.2 7.5 %partial_blocks.12 = (bf16[2,640,512]{2,1,0:T(8,128)(2,1)}, bf16[2,640,512]{2,1,0:T(8,128)(2,1)}) custom-call(s32[1]{0:T(128)} %bitcast.row, bf16[1280,1024]{1,0:T(8,128)(2,1)} %get-tuple-element.191.refs_2_.refs_0_, bf16[2048,2048]{1,0:T(8,128)(2,1)} %all-gather.11.cloned.1.call-done.weight.refs_7_.refs_1_), custom_call_target="tpu_custom_call" | custom-call | flops 2684354560 | bytes 12058624 | tf_op jit(solution)/shard_map/partial_blocks/pallas_call | solution.py:915
  404.7 7.8 %partial_blocks.13 = (bf16[2,640,512]{2,1,0:T(8,128)(2,1)}, f32[2,640,512]{2,1,0:T(8,128)}) custom-call(s32[1]{0:T(128)} %bitcast.row, bf16[1280,1024]{1,0:T(8,128)(2,1)} %get-tuple-element.191.refs_2_.refs_0_, bf16[2048,2048]{1,0:T(8,128)(2,1)} %all-gather.11.cloned.1.call-done.weight.refs_7_.refs_1_), custom_call_target="tpu_custom_call" | custom-call | flops 2684354560 | bytes 12058624 | tf_op jit(solution)/shard_map/partial_blocks/pallas_call | solution.py:915
  412.5 6.5 collective-permute-done.27.from_y
  419.0 3.3 collective-permute-done.26.from_x
  427.2 8.0 %collective-permute-done.29.far_b = bf16[640,512]{1,0:T(8,128)(2,1)S(1)} collective-permute-done((bf16[640,512]{1,0:T(8,128)(2,1)S(1)}, bf16[640,512]{1,0:T(8,128)(2,1)S(1)}, u32[]{:S(2)}, u32[]{:S(2)}) %collective-permute-start.29) | collective-permute-done | bytes 655392 | tf_op jit(solution)/shard_map/ppermute | solution.py:935
  437.0 5.2 join.3.refs_0_.wide
  442.3 12.2 %paired_grads.2 = bf16[4,256,1024]{2,1,0:T(8,128)(2,1)} custom-call(bf16[1280,2048]{1,0:T(8,128)(2,1)} %join.3.refs_0_.wide, bf16[1280,1024]{1,0:T(8,128)(2,1)} %get-tuple-element.158.refs_0_.refs_1_), custom_call_target="tpu_custom_call" | custom-call | flops 5368709120 | bytes 14680064 | tf_op jit(solution)/shard_map/paired_grads/pallas_call | solution.py:725
  454.4 16.3 %reduce-scatter.5.cloned.1.call-done = bf16[256,2048]{1,0:T(8,128)(2,1)} async-done(((bf16[2048,2048]{1,0:T(8,128)(2,1)}), bf16[256,2048]{1,0:T(8,128)(2,1)}) %reduce-scatter.5.cloned.1.call-update) | async-done | bytes 1048592 | tf_op jit(solution)/shard_map/reduce_scatter | solution.py:1048
  473.8 21.1 %gate_backward.1 = (bf16[1280,1024]{1,0:T(8,128)(2,1)}, bf16[1280,1024]{1,0:T(8,128)(2,1)}, f32[1,1024]{1,0:T(1,128)}, f32[1,1024]{1,0:T(1,128)}, bf16[8,2,256,5...) custom-call(s32[22]{0:T(128)} %pad_add_fusion.meta, f32[2]{0:T(128)} %subtract_log_fusion.rates, ...), custom_call_target="tpu_custom_call" | custom-call | flops 6039797760 | bytes 31457280 | tf_op jit(solution)/shard_map/gate_backward/pallas_call | solution.py:300
  494.9 4.6 collective-permute-done.30
  505.7 40.2 %return_states.1 = (bf16[2,256,512]{2,1,0:T(8,128)(2,1)S(1)}, bf16[2,256,512]{2,1,0:T(8,128)(2,1)S(1)}, bf16[2,256,512]{2,1,0:T(8,128)(2,1)S(1)}, bf16[2048,1024]{1,0:T(8,128)(2,1)S(1)}) custom-call(s32[22]{0:T(128)S(1)} %copy-done.6, f32[2]{0:T(128)S(1)} %copy-done.8, bf16[8,2,256,512]{3,2,1,0:T(8,128)(2,1)S(1)} %copy-done.1, ...), custom_call_target="tpu_custom_call" | custom-call | bytes 104857600 | tf_op jit(solution)/shard_map/return_states/pallas_call | solution.py:1328
  550.4 14.4 %retention_backward.1 = (bf16[1280,512]{1,0:T(8,128)(2,1)}, bf16[1280,512]{1,0:T(8,128)(2,1)}, bf16[1280,1024]{1,0:T(8,128)(2,1)}) custom-call(s32[22]{0:T(128)} %pad_add_fusion.meta, f32[2]{0:T(128)} %subtract_log_fusion.rates, bf16[1280,512]{1,0:T(8,128)(2,1)} %get-tuple-element.147.query, bf16[1280,512]{1,0:T(8,128)(2,1)} %get-tuple-element.148.key, ...), custom_call_target="tpu_custom_call" | custom-call | flops 5033164800 | bytes 15728640 | tf_op jit(solution)/shard_map/retention_backward/pallas_call | solution.py:395
  564.8 14.5 %partial_blocks.15 = (bf16[2,640,512]{2,1,0:T(8,128)(2,1)}, bf16[2,640,512]{2,1,0:T(8,128)(2,1)}) custom-call(s32[1]{0:T(128)} %bitcast.row, bf16[1280,512]{1,0:T(8,128)(2,1)} %get-tuple-element.235.refs_0_.refs_3_, bf16[1280,512]{1,0:T(8,128)(2,1)} %get-tuple-element.236.refs_1_.refs_4_, bf16[1280,1024]{1,0:T(8,128)(2,1)} %get-tuple-element.248.refs_2_.refs_5_, ...), custom_call_target="tpu_custom_call" | custom-call | flops 8053063680 | bytes 25690112 | tf_op jit(solution)/shard_map/partial_blocks/pallas_call | solution.py:915
  581.4 26.8 %paired_grads.3 = bf16[4,256,2048]{2,1,0:T(8,128)(2,1)} custom-call(bf16[1280,2048]{1,0:T(8,128)(2,1)} %get-tuple-element.142.values.wide.left.refs_0_.refs_1_.refs_2_, bf16[1280,2048]{1,0:T(8,128)(2,1)} %get-tuple-element.142.values.wide.left.refs_0_.refs_1_.refs_2_, bf16[1280,2048]{1,0:T(8,128)(2,1)} %get-tuple-element.142.values.wide.left.refs_0_.refs_1_.refs_2_, ...), custom_call_target="tpu_custom_call" | custom-call | flops 10737418240 | bytes 18874368 | tf_op jit(solution)/shard_map/paired_grads/pallas_call | solution.py:725
  611.3 2.8 fusion.18
  618.6 2.5 copy.88
  621.1 14.7 %partial_blocks.14 = (bf16[2,640,512]{2,1,0:T(8,128)(2,1)}, f32[2,640,512]{2,1,0:T(8,128)}) custom-call(s32[1]{0:T(128)} %bitcast.row, bf16[1280,512]{1,0:T(8,128)(2,1)} %get-tuple-element.235.refs_0_.refs_3_, bf16[1280,512]{1,0:T(8,128)(2,1)} %get-tuple-element.236.refs_1_.refs_4_, bf16[1280,1024]{1,0:T(8,128)(2,1)} %get-tuple-element.248.refs_2_.refs_5_, ...), custom_call_target="tpu_custom_call" | custom-call | flops 8053063680 | bytes 25690112 | tf_op jit(solution)/shard_map/partial_blocks/pallas_call | solution.py:915
  635.8 2.2 fusion.19
  642.4 5.5 fusion.9
  647.8 5.8 collective-permute-done.36
  662.5 2.5 copy.87
  674.0 3.9 collective-permute-start.42
  682.2 3.9 fusion.7
  (310 shorter events, 140.7 us)
Async XLA Ops:
  7.2 87.8 %all-gather.5.cloned.1.call-start = ((), (), s32[]{:S(2)}) async-start(), calls=%async_computation.4 | async-start | bytes 9437184 | tf_op jit(solution)/shard_map/all_gather | solution.py:1043
  9.5 141.4 %all-gather.7.cloned.1.call-start = ((), (), s32[]{:S(2)}) async-start(), calls=%async_computation.5 | async-start | bytes 4718592 | tf_op jit(solution)/shard_map/all_gather | solution.py:1043
  10.3 187.9 %all-gather.9.cloned.1.call-start = ((), (), s32[]{:S(2)}) async-start(), calls=%async_computation.6 | async-start | bytes 4718592 | tf_op jit(solution)/shard_map/all_gather | solution.py:1043
  11.6 287.9 %all-gather.11.cloned.1.call-start = ((), (), s32[]{:S(2)}) async-start(), calls=%async_computation.7 | async-start | bytes 9437184 | tf_op jit(solution)/shard_map/all_gather | solution.py:1043
  13.0 457.7 %reduce-scatter.5.cloned.1.call-start = ((), (), s32[]{:S(2)}) async-start(), calls=%async_computation.8 | async-start | bytes 9437184 | tf_op jit(solution)/shard_map/reduce_scatter | solution.py:1048
  13.1 10.3 %collective-permute-start.5 = (f32[4,512]{1,0:T(4,128)S(1)}, f32[4,512]{1,0:T(4,128)S(1)}, u32[]{:S(2)}, u32[]{:S(2)}) collective-permute-start(f32[4,512]{1,0:T(4,128)S(1)} %get-tuple-element.420), channel_id=1, source_target_pairs={{0,16},{16,0},{8,24},{24,8},{1,17},{17,1},{9,25},{25,9},{2,18},{18... | collective-permute-start | bytes 24584 | tf_op jit(solution)/shard_map/ppermute | solution.py:935
  16.2 7.3 %collective-permute-start.4 = (f32[4,512]{1,0:T(4,128)S(1)}, f32[4,512]{1,0:T(4,128)S(1)}, u32[]{:S(2)}, u32[]{:S(2)}) collective-permute-start(f32[4,512]{1,0:T(4,128)S(1)} %get-tuple-element.420), channel_id=1, source_target_pairs={{0,8},{8,0},{16,24},{24,16},{1,9},{9,1},{17,25},{25,17},{2,10},{10... | collective-permute-start | bytes 24584 | tf_op jit(solution)/shard_map/ppermute | solution.py:935
  17.7 30.2 %collective-permute-start = (bf16[1280,512]{1,0:T(8,128)(2,1)S(1)}, bf16[1280,512]{1,0:T(8,128)(2,1)}, u32[]{:S(2)}, u32[]{:S(2)}) collective-permute-start(bf16[1280,512]{1,0:T(8,128)(2,1)S(1)} %copy-done.14), channel_id=1, source_target_pairs={{0,8},{8,0},{16,24},{24,16},{1,9},{9,1},{17,25},{25,17},{2,10},{10... | collective-permute-start | bytes 3932168 | tf_op jit(solution)/shard_map/ppermute | solution.py:935
  19.6 31.1 %collective-permute-start.1 = (bf16[1280,512]{1,0:T(8,128)(2,1)S(1)}, bf16[1280,512]{1,0:T(8,128)(2,1)}, u32[]{:S(2)}, u32[]{:S(2)}) collective-permute-start(bf16[1280,512]{1,0:T(8,128)(2,1)S(1)} %copy-done.14), channel_id=1, source_target_pairs={{0,16},{16,0},{8,24},{24,8},{1,17},{17,1},{9,25},{25,9},{2,18},{18... | collective-permute-start | bytes 3932168 | tf_op jit(solution)/shard_map/ppermute | solution.py:935
  49.1 15.2 %collective-permute-start.2 = (bf16[640,512]{1,0:T(8,128)(2,1)S(1)}, bf16[640,512]{1,0:T(8,128)(2,1)S(1)}, u32[]{:S(2)}, u32[]{:S(2)}) collective-permute-start(bf16[640,512]{1,0:T(8,128)(2,1)S(1)} %slice.269), channel_id=1, source_target_pairs={{0,16},{16,0},{8,24},{24,8},{1,17},{17,1},{9,25},{25,9},{2,18},{18... | collective-permute-start | bytes 1966088 | tf_op jit(solution)/shard_map/ppermute | solution.py:935
  51.9 14.6 %collective-permute-start.3 = (bf16[640,512]{1,0:T(8,128)(2,1)S(1)}, bf16[640,512]{1,0:T(8,128)(2,1)S(1)}, u32[]{:S(2)}, u32[]{:S(2)}) collective-permute-start(bf16[640,512]{1,0:T(8,128)(2,1)S(1)} %slice.270), channel_id=1, source_target_pairs={{0,8},{8,0},{16,24},{24,16},{1,9},{9,1},{17,25},{25,17},{2,10},{10... | collective-permute-start | bytes 1966088 | tf_op jit(solution)/shard_map/ppermute | solution.py:935
  74.8 41.5 %collective-permute-start.8 = (bf16[1280,512]{1,0:T(8,128)(2,1)S(1)}, bf16[1280,512]{1,0:T(8,128)(2,1)S(1)}, u32[]{:S(2)}, u32[]{:S(2)}) collective-permute-start(bf16[1280,512]{1,0:T(8,128)(2,1)S(1)} %multiply_convert_fusion.own), channel_id=1, source_target_pairs={{0,16},{16,0},{8,24},{24,8},{1,17},{17,1},{9,25},{25,9},{2,18},{18... | collective-permute-start | bytes 3932168 | tf_op jit(solution)/shard_map/ppermute | solution.py:935
  75.6 40.7 %collective-permute-start.7 = (bf16[1280,512]{1,0:T(8,128)(2,1)S(1)}, bf16[1280,512]{1,0:T(8,128)(2,1)}, u32[]{:S(2)}, u32[]{:S(2)}) collective-permute-start(bf16[1280,512]{1,0:T(8,128)(2,1)S(1)} %multiply_convert_fusion.own), channel_id=1, source_target_pairs={{0,8},{8,0},{16,24},{24,16},{1,9},{9,1},{17,25},{25,17},{2,10},{10... | collective-permute-start | bytes 3932168 | tf_op jit(solution)/shard_map/ppermute | solution.py:935
  119.7 31.2 %collective-permute-start.10 = (bf16[640,512]{1,0:T(8,128)(2,1)S(1)}, bf16[640,512]{1,0:T(8,128)(2,1)S(1)}, u32[]{:S(2)}, u32[]{:S(2)}) collective-permute-start(bf16[640,512]{1,0:T(8,128)(2,1)S(1)} %slice.210), channel_id=1, source_target_pairs={{0,8},{8,0},{16,24},{24,16},{1,9},{9,1},{17,25},{25,17},{2,10},{10... | collective-permute-start | bytes 1966088 | tf_op jit(solution)/shard_map/ppermute | solution.py:935
  121.3 29.6 %collective-permute-start.9 = (bf16[640,512]{1,0:T(8,128)(2,1)S(1)}, bf16[640,512]{1,0:T(8,128)(2,1)S(1)}, u32[]{:S(2)}, u32[]{:S(2)}) collective-permute-start(bf16[640,512]{1,0:T(8,128)(2,1)S(1)} %slice.209), channel_id=1, source_target_pairs={{0,16},{16,0},{8,24},{24,8},{1,17},{17,1},{9,25},{25,9},{2,18},{18... | collective-permute-start | bytes 1966088 | tf_op jit(solution)/shard_map/ppermute | solution.py:935
  205.8 31.1 %collective-permute-start.11 = (bf16[2,640,512]{2,1,0:T(8,128)(2,1)}, bf16[2,640,512]{2,1,0:T(8,128)(2,1)S(1)}, u32[]{:S(2)}, u32[]{:S(2)}) collective-permute-start(bf16[2,640,512]{2,1,0:T(8,128)(2,1)} %get-tuple-element.160), channel_id=1, source_target_pairs={{0,8},{8,0},{16,24},{24,16},{1,9},{9,1},{17,25},{25,17},{2,10},{10... | collective-permute-start | bytes 3932168 | tf_op jit(solution)/shard_map/ppermute | solution.py:935
  207.2 30.9 %collective-permute-start.13 = (bf16[2,640,512]{2,1,0:T(8,128)(2,1)}, bf16[2,640,512]{2,1,0:T(8,128)(2,1)S(1)}, u32[]{:S(2)}, u32[]{:S(2)}) collective-permute-start(bf16[2,640,512]{2,1,0:T(8,128)(2,1)} %get-tuple-element.162), channel_id=1, source_target_pairs={{0,16},{16,0},{8,24},{24,8},{1,17},{17,1},{9,25},{25,9},{2,18},{18... | collective-permute-start | bytes 3932168 | tf_op jit(solution)/shard_map/ppermute | solution.py:935
  240.3 15.9 %collective-permute-start.12 = (bf16[640,512]{1,0:T(8,128)(2,1)S(1)}, bf16[640,512]{1,0:T(8,128)(2,1)S(1)}, u32[]{:S(2)}, u32[]{:S(2)}) collective-permute-start(bf16[640,512]{1,0:T(8,128)(2,1)S(1)} %get-tuple-element.393), channel_id=1, source_target_pairs={{0,16},{16,0},{8,24},{24,8},{1,17},{17,1},{9,25},{25,9},{2,18},{18... | collective-permute-start | bytes 1966088 | tf_op jit(solution)/shard_map/ppermute | solution.py:935
  241.8 15.6 %collective-permute-start.14 = (bf16[640,512]{1,0:T(8,128)(2,1)S(1)}, bf16[640,512]{1,0:T(8,128)(2,1)S(1)}, u32[]{:S(2)}, u32[]{:S(2)}) collective-permute-start(bf16[640,512]{1,0:T(8,128)(2,1)S(1)} %get-tuple-element.394), channel_id=1, source_target_pairs={{0,8},{8,0},{16,24},{24,16},{1,9},{9,1},{17,25},{25,17},{2,10},{10... | collective-permute-start | bytes 1966088 | tf_op jit(solution)/shard_map/ppermute | solution.py:935
  260.5 28.7 %collective-permute-start.16 = (bf16[1280,512]{1,0:T(8,128)(2,1)S(1)}, bf16[1280,512]{1,0:T(8,128)(2,1)S(1)}, u32[]{:S(2)}, u32[]{:S(2)}) collective-permute-start(bf16[1280,512]{1,0:T(8,128)(2,1)S(1)} %fusion.30.refs_0_), channel_id=1, source_target_pairs={{0,16},{16,0},{8,24},{24,8},{1,17},{17,1},{9,25},{25,9},{2,18},{18... | collective-permute-start | bytes 3932168 | tf_op jit(solution)/shard_map/ppermute | solution.py:935
  261.0 28.5 %collective-permute-start.15 = (bf16[1280,512]{1,0:T(8,128)(2,1)S(1)}, bf16[1280,512]{1,0:T(8,128)(2,1)S(1)}, u32[]{:S(2)}, u32[]{:S(2)}) collective-permute-start(bf16[1280,512]{1,0:T(8,128)(2,1)S(1)} %fusion.30.refs_0_), channel_id=1, source_target_pairs={{0,8},{8,0},{16,24},{24,16},{1,9},{9,1},{17,25},{25,17},{2,10},{10... | collective-permute-start | bytes 3932168 | tf_op jit(solution)/shard_map/ppermute | solution.py:935
  290.7 18.7 %collective-permute-start.18 = (bf16[640,512]{1,0:T(8,128)(2,1)}, bf16[640,512]{1,0:T(8,128)(2,1)}, u32[]{:S(2)}, u32[]{:S(2)}) collective-permute-start(bf16[640,512]{1,0:T(8,128)(2,1)} %slice.220), channel_id=1, source_target_pairs={{0,8},{8,0},{16,24},{24,16},{1,9},{9,1},{17,25},{25,17},{2,10},{10... | collective-permute-start | bytes 1966088 | tf_op jit(solution)/shard_map/ppermute | solution.py:935
  292.1 17.3 %collective-permute-start.17 = (bf16[640,512]{1,0:T(8,128)(2,1)S(1)}, bf16[640,512]{1,0:T(8,128)(2,1)}, u32[]{:S(2)}, u32[]{:S(2)}) collective-permute-start(bf16[640,512]{1,0:T(8,128)(2,1)S(1)} %slice.219), channel_id=1, source_target_pairs={{0,16},{16,0},{8,24},{24,8},{1,17},{17,1},{9,25},{25,9},{2,18},{18... | collective-permute-start | bytes 1966088 | tf_op jit(solution)/shard_map/ppermute | solution.py:935
  336.2 27.7 %collective-permute-start.19 = (bf16[2,640,512]{2,1,0:T(8,128)(2,1)}, bf16[2,640,512]{2,1,0:T(8,128)(2,1)}, u32[]{:S(2)}, u32[]{:S(2)}) collective-permute-start(bf16[2,640,512]{2,1,0:T(8,128)(2,1)} %get-tuple-element.187), channel_id=1, source_target_pairs={{0,8},{8,0},{16,24},{24,16},{1,9},{9,1},{17,25},{25,17},{2,10},{10... | collective-permute-start | bytes 3932168 | tf_op jit(solution)/shard_map/ppermute | solution.py:935
  336.9 27.1 %collective-permute-start.20 = (bf16[2,640,512]{2,1,0:T(8,128)(2,1)}, bf16[2,640,512]{2,1,0:T(8,128)(2,1)}, u32[]{:S(2)}, u32[]{:S(2)}) collective-permute-start(bf16[2,640,512]{2,1,0:T(8,128)(2,1)} %get-tuple-element.188), channel_id=1, source_target_pairs={{0,16},{16,0},{8,24},{24,8},{1,17},{17,1},{9,25},{25,9},{2,18},{18... | collective-permute-start | bytes 3932168 | tf_op jit(solution)/shard_map/ppermute | solution.py:935
  364.0 186.3 %reduce-scatter.7.cloned.1.call-start = ((), (), s32[]{:S(2)}) async-start(), calls=%async_computation.9 | async-start | bytes 2621440 | tf_op jit(solution)/shard_map/reduce_scatter | solution.py:1050
  365.4 8.2 %collective-permute-start.25 = (f32[2,1280]{1,0:T(2,128)S(1)}, f32[2,1280]{1,0:T(2,128)S(1)}, u32[]{:S(2)}, u32[]{:S(2)}) collective-permute-start(f32[2,1280]{1,0:T(2,128)S(1)} %copy.77), channel_id=1, source_target_pairs={{0,24},{24,0},{8,16},{16,8},{1,25},{25,1},{9,17},{17,9},{2,26},{26... | collective-permute-start | bytes 30728 | tf_op jit(solution)/shard_map/ppermute | solution.py:935
  376.9 10.9 %collective-permute-start.21 = (bf16[640,512]{1,0:T(8,128)(2,1)S(1)}, bf16[640,512]{1,0:T(8,128)(2,1)S(1)}, u32[]{:S(2)}, u32[]{:S(2)}) collective-permute-start(bf16[640,512]{1,0:T(8,128)(2,1)S(1)} %get-tuple-element.391), channel_id=1, source_target_pairs={{0,16},{16,0},{8,24},{24,8},{1,17},{17,1},{9,25},{25,9},{2,18},{18... | collective-permute-start | bytes 1966088 | tf_op jit(solution)/shard_map/ppermute | solution.py:935
  377.8 10.7 %collective-permute-start.22 = (bf16[640,512]{1,0:T(8,128)(2,1)S(1)}, bf16[640,512]{1,0:T(8,128)(2,1)S(1)}, u32[]{:S(2)}, u32[]{:S(2)}) collective-permute-start(bf16[640,512]{1,0:T(8,128)(2,1)S(1)} %get-tuple-element.392), channel_id=1, source_target_pairs={{0,8},{8,0},{16,24},{24,16},{1,9},{9,1},{17,25},{25,17},{2,10},{10... | collective-permute-start | bytes 1966088 | tf_op jit(solution)/shard_map/ppermute | solution.py:935
  394.5 24.4 %collective-permute-start.27 = (bf16[1280,512]{1,0:T(8,128)(2,1)}, bf16[1280,512]{1,0:T(8,128)(2,1)}, u32[]{:S(2)}, u32[]{:S(2)}) collective-permute-start(bf16[1280,512]{1,0:T(8,128)(2,1)} %get-tuple-element.373.own), channel_id=1, source_target_pairs={{0,16},{16,0},{8,24},{24,8},{1,17},{17,1},{9,25},{25,9},{2,18},{18... | collective-permute-start | bytes 3932168 | tf_op jit(solution)/shard_map/ppermute | solution.py:935
  395.7 26.6 %collective-permute-start.26 = (bf16[1280,512]{1,0:T(8,128)(2,1)}, bf16[1280,512]{1,0:T(8,128)(2,1)}, u32[]{:S(2)}, u32[]{:S(2)}) collective-permute-start(bf16[1280,512]{1,0:T(8,128)(2,1)} %get-tuple-element.373.own), channel_id=1, source_target_pairs={{0,8},{8,0},{16,24},{24,16},{1,9},{9,1},{17,25},{25,17},{2,10},{10... | collective-permute-start | bytes 3932168 | tf_op jit(solution)/shard_map/ppermute | solution.py:935
  424.6 10.7 %collective-permute-start.29 = (bf16[640,512]{1,0:T(8,128)(2,1)S(1)}, bf16[640,512]{1,0:T(8,128)(2,1)S(1)}, u32[]{:S(2)}, u32[]{:S(2)}) collective-permute-start(bf16[640,512]{1,0:T(8,128)(2,1)S(1)} %slice.242), channel_id=1, source_target_pairs={{0,8},{8,0},{16,24},{24,16},{1,9},{9,1},{17,25},{25,17},{2,10},{10... | collective-permute-start | bytes 1966088 | tf_op jit(solution)/shard_map/ppermute | solution.py:935
  426.3 10.7 %collective-permute-start.28 = (bf16[640,512]{1,0:T(8,128)(2,1)S(1)}, bf16[640,512]{1,0:T(8,128)(2,1)}, u32[]{:S(2)}, u32[]{:S(2)}) collective-permute-start(bf16[640,512]{1,0:T(8,128)(2,1)S(1)} %slice.241), channel_id=1, source_target_pairs={{0,16},{16,0},{8,24},{24,8},{1,17},{17,1},{9,25},{25,9},{2,18},{18... | collective-permute-start | bytes 1966088 | tf_op jit(solution)/shard_map/ppermute | solution.py:935
  470.7 137.5 %reduce-scatter.9.cloned.1.call-start = ((), (), s32[]{:S(2)}) async-start(), calls=%async_computation.10 | async-start | bytes 4718592 | tf_op jit(solution)/shard_map/reduce_scatter | solution.py:1048
  470.8 28.7 %collective-permute-start.30 = (bf16[2,640,512]{2,1,0:T(8,128)(2,1)}, bf16[2,640,512]{2,1,0:T(8,128)(2,1)}, u32[]{:S(2)}, u32[]{:S(2)}) collective-permute-start(bf16[2,640,512]{2,1,0:T(8,128)(2,1)} %get-tuple-element.206), channel_id=1, source_target_pairs={{0,8},{8,0},{16,24},{24,16},{1,9},{9,1},{17,25},{25,17},{2,10},{10... | collective-permute-start | bytes 3932168 | tf_op jit(solution)/shard_map/ppermute | solution.py:935
  472.3 28.4 %collective-permute-start.31 = (bf16[2,640,512]{2,1,0:T(8,128)(2,1)}, bf16[2,640,512]{2,1,0:T(8,128)(2,1)}, u32[]{:S(2)}, u32[]{:S(2)}) collective-permute-start(bf16[2,640,512]{2,1,0:T(8,128)(2,1)} %get-tuple-element.207), channel_id=1, source_target_pairs={{0,16},{16,0},{8,24},{24,8},{1,17},{17,1},{9,25},{25,9},{2,18},{18... | collective-permute-start | bytes 3932168 | tf_op jit(solution)/shard_map/ppermute | solution.py:935
  550.3 144.3 %reduce-scatter.11.cloned.1.call-start = ((), (), s32[]{:S(2)}) async-start(), calls=%async_computation.11 | async-start | bytes 5242880 | tf_op jit(solution)/shard_map/reduce_scatter | solution.py:1050
  579.3 28.9 %collective-permute-start.34 = (bf16[2,640,512]{2,1,0:T(8,128)(2,1)}, bf16[2,640,512]{2,1,0:T(8,128)(2,1)}, u32[]{:S(2)}, u32[]{:S(2)}) collective-permute-start(bf16[2,640,512]{2,1,0:T(8,128)(2,1)} %get-tuple-element.246), channel_id=1, source_target_pairs={{0,8},{8,0},{16,24},{24,16},{1,9},{9,1},{17,25},{25,17},{2,10},{10... | collective-permute-start | bytes 3932168 | tf_op jit(solution)/shard_map/ppermute | solution.py:935
  580.4 27.9 %collective-permute-start.35 = (bf16[2,640,512]{2,1,0:T(8,128)(2,1)}, bf16[2,640,512]{2,1,0:T(8,128)(2,1)}, u32[]{:S(2)}, u32[]{:S(2)}) collective-permute-start(bf16[2,640,512]{2,1,0:T(8,128)(2,1)} %get-tuple-element.247), channel_id=1, source_target_pairs={{0,16},{16,0},{8,24},{24,8},{1,17},{17,1},{9,25},{25,9},{2,18},{18... | collective-permute-start | bytes 3932168 | tf_op jit(solution)/shard_map/ppermute | solution.py:935
  614.1 21.7 %collective-permute-start.33 = (bf16[640,512]{1,0:T(8,128)(2,1)}, bf16[640,512]{1,0:T(8,128)(2,1)S(1)}, u32[]{:S(2)}, u32[]{:S(2)}) collective-permute-start(bf16[640,512]{1,0:T(8,128)(2,1)} %get-tuple-element.389), channel_id=1, source_target_pairs={{0,8},{8,0},{16,24},{24,16},{1,9},{9,1},{17,25},{25,17},{2,10},{10... | collective-permute-start | bytes 1966088 | tf_op jit(solution)/shard_map/ppermute | solution.py:935
  614.8 21.0 %collective-permute-start.32 = (bf16[640,512]{1,0:T(8,128)(2,1)}, bf16[640,512]{1,0:T(8,128)(2,1)}, u32[]{:S(2)}, u32[]{:S(2)}) collective-permute-start(bf16[640,512]{1,0:T(8,128)(2,1)} %get-tuple-element.390), channel_id=1, source_target_pairs={{0,16},{16,0},{8,24},{24,8},{1,17},{17,1},{9,25},{25,9},{2,18},{18... | collective-permute-start | bytes 1966088 | tf_op jit(solution)/shard_map/ppermute | solution.py:935
  638.0 15.6 %collective-permute-start.36 = (bf16[640,512]{1,0:T(8,128)(2,1)S(1)}, bf16[640,512]{1,0:T(8,128)(2,1)S(1)}, u32[]{:S(2)}, u32[]{:S(2)}) collective-permute-start(bf16[640,512]{1,0:T(8,128)(2,1)S(1)} %get-tuple-element.387), channel_id=1, source_target_pairs={{0,16},{16,0},{8,24},{24,8},{1,17},{17,1},{9,25},{25,9},{2,18},{18... | collective-permute-start | bytes 1966088 | tf_op jit(solution)/shard_map/ppermute | solution.py:935
  638.8 15.2 %collective-permute-start.37 = (bf16[640,512]{1,0:T(8,128)(2,1)S(1)}, bf16[640,512]{1,0:T(8,128)(2,1)S(1)}, u32[]{:S(2)}, u32[]{:S(2)}) collective-permute-start(bf16[640,512]{1,0:T(8,128)(2,1)S(1)} %get-tuple-element.388), channel_id=1, source_target_pairs={{0,8},{8,0},{16,24},{24,16},{1,9},{9,1},{17,25},{25,17},{2,10},{10... | collective-permute-start | bytes 1966088 | tf_op jit(solution)/shard_map/ppermute | solution.py:935
  657.8 11.4 %collective-permute-start.39 = (f32[2,1280]{1,0:T(2,128)S(1)}, f32[2,1280]{1,0:T(2,128)S(1)}, u32[]{:S(2)}, u32[]{:S(2)}) collective-permute-start(f32[2,1280]{1,0:T(2,128)S(1)} %pad_maximum_fusion.7), channel_id=1, source_target_pairs={{0,16},{16,0},{8,24},{24,8},{1,17},{17,1},{9,25},{25,9},{2,18},{18... | collective-permute-start | bytes 30728 | tf_op jit(solution)/shard_map/ppermute | solution.py:935
  659.8 9.1 %collective-permute-start.40 = (f32[2,1280]{1,0:T(2,128)S(1)}, f32[2,1280]{1,0:T(2,128)S(1)}, u32[]{:S(2)}, u32[]{:S(2)}) collective-permute-start(f32[2,1280]{1,0:T(2,128)S(1)} %pad_maximum_fusion.7), channel_id=1, source_target_pairs={{0,24},{24,0},{8,16},{16,8},{1,25},{25,1},{9,17},{17,9},{2,26},{26... | collective-permute-start | bytes 30728 | tf_op jit(solution)/shard_map/ppermute | solution.py:935
  660.5 13.1 %collective-permute-start.38 = (f32[2,1280]{1,0:T(2,128)S(1)}, f32[2,1280]{1,0:T(2,128)S(1)}, u32[]{:S(2)}, u32[]{:S(2)}) collective-permute-start(f32[2,1280]{1,0:T(2,128)S(1)} %pad_maximum_fusion.7), channel_id=1, source_target_pairs={{0,8},{8,0},{16,24},{24,16},{1,9},{9,1},{17,25},{25,17},{2,10},{10... | collective-permute-start | bytes 30728 | tf_op jit(solution)/shard_map/ppermute | solution.py:935
  667.0 6.9 collective-permute-start.41
  674.0 6.5 collective-permute-start.42
  (71 other events, 447.8 us)
Sparse Core Ops, SparseCore 0:
  10.2 84.7 all-gather.4
  96.6 52.1 all-gather.6
  150.9 47.2 all-gather.8
  200.3 86.4 all-gather.10
  364.1 106.5 reduce-scatter.4
  472.9 42.1 reduce-scatter.6
  550.5 56.2 reduce-scatter.8
  609.1 77.6 reduce-scatter.10
